TPU v7x, 32 devices: a whole 2x2x4 slice. The times are simulated.
32 devices in a mesh: section: 2 (over x), dp: 16 (over z, y, core).
Axes of the slice: x: 2, y: 2, z: 4, core: 2. Of those that a mesh axis runs over, the one named last changes fastest.
Arguments:
- edge_data: bfloat16 [2, 2, 1024, 960], P('section', None, 'dp'), may hold values from -6 to 6
- segment_ids: int32 [2, 1024], P(None, 'dp'), may hold values from 0 to 63, as said below
- attn_weight: bfloat16 [2, 960, 2560], P('section', None, 'dp'), may hold values from -0.1875 to 0.1875
- ffn_weight: bfloat16 [2, 3, 960, 2560], P('section', None, None, 'dp'), may hold values from -0.1875 to 0.1875
- gains: bfloat16 [2, 1920], P('section', 'dp'), may hold values from 0.5 to 1.5
Outputs:
- edge_out: bfloat16 [2, 2, 1024, 960], P('section', None, 'dp')
- attention_grad: float32 [2, 960, 2560], P('section', None, 'dp')
- ffn_grad: float32 [2, 3, 960, 2560], P('section', None, None, 'dp')
- gain_grad: float32 [2, 1920], P('section', 'dp')
Inputs may be any that keep to these rules, and one draw needn't show every extreme that they name: `segment_ids`: inside each aligned block of 64 tokens (one index of dp in one micro-batch) the ids start at 0 at the block's first token and rise by 0 or 1 from token to token; tokens of a block with equal ids form one sequence; no sequence crosses a block; some sequence fills a whole block, and some block holds only sequences of one token.
All inputs are finite; a program needn't handle non-finite values.
Results may differ from a plain program's by a relative error of at most 0.02.
Values may be sent and summed in bfloat16 or wider, within the bound.
No kernel may reach another device: no remote copies, remote signals or barrier semaphores. Data moves between devices by JAX's collectives and lax.ppermute only.
A program may use at most 256 MiB of HBM per device.

v0:
```python
import jax
import jax.numpy as jnp
from jax import lax
from jax.sharding import PartitionSpec as P

QUERY_HEADS = 15
KEY_VALUE_HEADS = 5
HEAD_SIZE = 64


epsilon = 1e-05
theta_base = 100000.0
contract_last = (((1,), (1,)), ((), ()))
contract_first = (((0,), (0,)), ((), ()))


def passed_along(array, axis, by):
    length = lax.axis_size(axis)
    pairs = [(i, i + by) for i in range(length) if 0 <= i + by < length]
    return lax.ppermute(array, axis, pairs)


def matmul(left_op, right_op):
    return jnp.dot(left_op, right_op, preferred_element_type=jnp.float32)


def right_trans(left_op, right_op):
    return lax.dot_general(left_op, right_op, contract_last, preferred_element_type=jnp.float32)


def left_trans(left_op, right_op):
    return lax.dot_general(left_op, right_op, contract_first, preferred_element_type=jnp.float32)


def norm_rows(rows, gain):
    return rows * lax.rsqrt(jnp.mean(rows * rows, axis=-1, keepdims=True) + epsilon) * gain


def rotary_apply(rows, cosine_table, sine_values):
    half_size = rows.shape[-1] // 2
    front_part = rows[..., :half_size]
    back_part = rows[..., half_size:]
    return jnp.concatenate(
        [
            front_part * cosine_table - back_part * sine_values,
            back_part * cosine_table + front_part * sine_values,
        ],
        axis=-1,
    )


def block_tables(segments):
    block_len = segments.shape[-1]
    offsets = jnp.arange(block_len, dtype=jnp.int32)
    same_segment = segments[..., :, None] == segments[..., None, :]
    segment_start = jnp.min(jnp.where(same_segment, offsets, block_len), axis=-1)
    positions = (offsets - segment_start).astype(jnp.float32)
    half_size = HEAD_SIZE // 2
    frequency = theta_base ** (-(2.0 * jnp.arange(half_size, dtype=jnp.float32)) / HEAD_SIZE)
    angles = positions[..., None] * frequency
    allowed = same_segment & (offsets[:, None] >= offsets[None, :])
    return (jnp.cos(angles), jnp.sin(angles), allowed)


def attention_scores(query_matrix, key_matrix_rows, allowed):
    scores = jnp.einsum(
        "tgrd,ugd->grtu", query_matrix, key_matrix_rows, preferred_element_type=jnp.float32
    ) * HEAD_SIZE ** (-0.5)
    return jnp.where(allowed, scores, -1000000000.0)


def layer_forward(layer_in, qkv_w, out_w, ffn_w, gain_row, cosine_table, sine_values, allowed):
    sequence_length, model_width = layer_in.shape
    head_column_width = QUERY_HEADS * HEAD_SIZE
    key_value_width = KEY_VALUE_HEADS * HEAD_SIZE
    query_group_count = QUERY_HEADS // KEY_VALUE_HEADS
    residual = layer_in.astype(jnp.float32)
    normed = norm_rows(residual, gain_row[:model_width].astype(jnp.float32)).astype(jnp.bfloat16)
    projected_rows = matmul(normed, qkv_w)
    query_matrix = rotary_apply(
        projected_rows[:, :head_column_width].reshape(
            sequence_length, KEY_VALUE_HEADS, query_group_count, HEAD_SIZE
        ),
        cosine_table[:, None, None, :],
        sine_values[:, None, None, :],
    ).astype(jnp.bfloat16)
    key_matrix_rows = rotary_apply(
        projected_rows[:, head_column_width : head_column_width + key_value_width].reshape(
            sequence_length, KEY_VALUE_HEADS, HEAD_SIZE
        ),
        cosine_table[:, None, :],
        sine_values[:, None, :],
    ).astype(jnp.bfloat16)
    value_matrix_rows = (
        projected_rows[:, head_column_width + key_value_width :]
        .reshape(sequence_length, KEY_VALUE_HEADS, HEAD_SIZE)
        .astype(jnp.bfloat16)
    )
    masked = attention_scores(query_matrix, key_matrix_rows, allowed)
    peak_score = jnp.max(masked, axis=-1, keepdims=True)
    log_total = peak_score + jnp.log(jnp.sum(jnp.exp(masked - peak_score), axis=-1, keepdims=True))
    prob_low = jnp.exp(masked - log_total).astype(jnp.bfloat16)
    attended = jnp.einsum(
        "grtu,ugd->tgrd", prob_low, value_matrix_rows, preferred_element_type=jnp.float32
    )
    attended = attended.reshape(sequence_length, head_column_width).astype(jnp.bfloat16)
    hidden = residual + right_trans(attended, out_w)
    normed_two = norm_rows(hidden, gain_row[model_width:].astype(jnp.float32)).astype(jnp.bfloat16)
    gate_proj = matmul(normed_two, ffn_w[0])
    upward = matmul(normed_two, ffn_w[1])
    active = (jax.nn.silu(gate_proj) * upward).astype(jnp.bfloat16)
    output = hidden + right_trans(active, ffn_w[2])
    saved_state = (
        residual,
        normed,
        query_matrix,
        key_matrix_rows,
        value_matrix_rows,
        log_total,
        attended,
        hidden,
        normed_two,
        gate_proj,
        upward,
        active,
    )
    return (output, saved_state)


def layer_backward(
    grad_out, saved_state, qkv_w, out_w, ffn_w, gain_row, cosine_table, sine_values, allowed
):
    (
        residual,
        normed,
        query_matrix,
        key_matrix_rows,
        value_matrix_rows,
        log_total,
        attended,
        hidden,
        normed_two,
        gate_proj,
        upward,
        active,
    ) = saved_state
    sequence_length, model_width = residual.shape
    head_column_width = QUERY_HEADS * HEAD_SIZE
    key_value_width = KEY_VALUE_HEADS * HEAD_SIZE
    query_group_count = QUERY_HEADS // KEY_VALUE_HEADS
    branch_grad = grad_out.astype(jnp.bfloat16)
    active_grad = matmul(branch_grad, ffn_w[2])
    _, pull_back = jax.vjp(lambda gate_in, up_in: jax.nn.silu(gate_in) * up_in, gate_proj, upward)
    gate_grad, up_grad = pull_back(active_grad)
    gate_grad = gate_grad.astype(jnp.bfloat16)
    up_grad = up_grad.astype(jnp.bfloat16)
    normed_two_grad = right_trans(gate_grad, ffn_w[0]) + right_trans(up_grad, ffn_w[1])
    _, pull_back = jax.vjp(norm_rows, hidden, gain_row[model_width:].astype(jnp.float32))
    hidden_part, gain_two_grad = pull_back(normed_two_grad)
    hidden_grad = grad_out + hidden_part
    mixed_grad = hidden_grad.astype(jnp.bfloat16)
    attended_grad = (
        matmul(mixed_grad, out_w)
        .reshape(sequence_length, KEY_VALUE_HEADS, query_group_count, HEAD_SIZE)
        .astype(jnp.bfloat16)
    )
    prob_full = jnp.exp(attention_scores(query_matrix, key_matrix_rows, allowed) - log_total)
    prob_low = prob_full.astype(jnp.bfloat16)
    value_grad = jnp.einsum(
        "grtu,tgrd->ugd", prob_low, attended_grad, preferred_element_type=jnp.float32
    )
    prob_grad = jnp.einsum(
        "tgrd,ugd->grtu", attended_grad, value_matrix_rows, preferred_element_type=jnp.float32
    )
    scores_grad = (
        prob_full * (prob_grad - jnp.sum(prob_grad * prob_full, axis=-1, keepdims=True))
    ).astype(jnp.bfloat16)
    query_grad = jnp.einsum(
        "grtu,ugd->tgrd", scores_grad, key_matrix_rows, preferred_element_type=jnp.float32
    ) * HEAD_SIZE ** (-0.5)
    key_grad = jnp.einsum(
        "grtu,tgrd->ugd", scores_grad, query_matrix, preferred_element_type=jnp.float32
    ) * HEAD_SIZE ** (-0.5)
    _, pull_back = jax.vjp(
        lambda rows: rotary_apply(
            rows, cosine_table[:, None, None, :], sine_values[:, None, None, :]
        ),
        query_grad,
    )
    (query_grad,) = pull_back(query_grad)
    _, pull_back = jax.vjp(
        lambda rows: rotary_apply(rows, cosine_table[:, None, :], sine_values[:, None, :]), key_grad
    )
    (key_grad,) = pull_back(key_grad)
    qkv_grad = jnp.concatenate(
        [
            query_grad.reshape(sequence_length, head_column_width),
            key_grad.reshape(sequence_length, key_value_width),
            value_grad.reshape(sequence_length, key_value_width),
        ],
        axis=1,
    ).astype(jnp.bfloat16)
    normed_grad = right_trans(qkv_grad, qkv_w)
    _, pull_back = jax.vjp(norm_rows, residual, gain_row[:model_width].astype(jnp.float32))
    input_part, gain_one_grad = pull_back(normed_grad)
    input_grad = hidden_grad + input_part
    pieces = (
        normed,
        qkv_grad,
        mixed_grad,
        attended,
        normed_two,
        gate_grad,
        up_grad,
        branch_grad,
        active,
    )
    return (input_grad, pieces, jnp.concatenate([gain_one_grad, gain_two_grad]))


def owner_rows_maker(piece_group, owners):
    joined = tuple(
        (jnp.concatenate([pieces[member] for pieces in piece_group], axis=0) for member in range(9))
    )
    normed, qkv_grad, mixed_grad, attended, normed_two, gate_grad, up_grad, branch_grad, active = (
        joined
    )
    token_count = normed.shape[0]
    qkv_cols = qkv_grad.shape[1]
    out_cols = attended.shape[1]
    qkv_padded = jnp.concatenate(
        [qkv_grad, jnp.zeros((token_count, out_cols), jnp.bfloat16)], axis=1
    )
    out_padded = jnp.concatenate(
        [jnp.zeros((token_count, qkv_cols), jnp.bfloat16), attended], axis=1
    )
    attn_share = (qkv_cols + out_cols) // owners
    ffn_share = gate_grad.shape[1] // owners
    owner_width = attn_share + 3 * ffn_share

    def one_owner(owner):
        attn_first = lax.dynamic_slice_in_dim(qkv_padded, owner * attn_share, attn_share, 1)
        attn_second = lax.dynamic_slice_in_dim(out_padded, owner * attn_share, attn_share, 1)
        attn_rows = left_trans(attn_first, normed) + left_trans(attn_second, mixed_grad)
        gate_rows = left_trans(
            lax.dynamic_slice_in_dim(gate_grad, owner * ffn_share, ffn_share, 1), normed_two
        )
        up_rows = left_trans(
            lax.dynamic_slice_in_dim(up_grad, owner * ffn_share, ffn_share, 1), normed_two
        )
        down_rows = left_trans(
            lax.dynamic_slice_in_dim(active, owner * ffn_share, ffn_share, 1), branch_grad
        )
        return jnp.concatenate([attn_rows, gate_rows, up_rows, down_rows], axis=0)

    def owner_rows(start, count):
        block_total = count // owner_width
        first_owner = start // owner_width
        owner_list = jnp.arange(block_total, dtype=jnp.int32)
        stacked = lax.map(one_owner, owner_list)
        return stacked.reshape(count, stacked.shape[-1])

    return (owner_rows, owner_width, attn_share, ffn_share)


def unpack_shard(shard, attn_share, ffn_share):
    attention_shard = shard[:attn_share].T[None]
    gate_part = shard[attn_share : attn_share + ffn_share].T
    up_part = shard[attn_share + ffn_share : attn_share + 2 * ffn_share].T
    down_part = shard[attn_share + 2 * ffn_share :].T
    return (attention_shard, jnp.stack([gate_part, up_part, down_part])[None])


def pick_section(leading, first_tree, second_tree):
    return jax.tree.map(
        lambda one_val, two_val: jnp.where(leading, one_val, two_val), first_tree, second_tree
    )


def local(edge_data, segment_ids, attn_weight, ffn_weight, gains):
    micro_count = segment_ids.shape[0]
    owners = lax.axis_size("dp")
    split_at = QUERY_HEADS * HEAD_SIZE + 2 * KEY_VALUE_HEADS * HEAD_SIZE
    leading = lax.axis_index("section") == 0
    table_list = [block_tables(segment_ids[mb_num]) for mb_num in range(micro_count)]
    gathered = (
        lax.all_gather(attn_weight, "dp", axis=2, tiled=True),
        lax.all_gather(ffn_weight, "dp", axis=3, tiled=True),
        lax.all_gather(gains, "dp", axis=1, tiled=True),
    )
    qkv_w = gathered[0][0][:, :split_at]
    out_w = gathered[0][0][:, split_at:]
    ffn_w, gain_row = (gathered[1][0], gathered[2][0])
    received = jnp.zeros_like(edge_data[0, 0])
    saved_list = []
    output_list = []
    for tick_num in range(micro_count + 1):
        own_input = edge_data[0, min(tick_num, micro_count - 1)]
        layer_in = jnp.where(leading, own_input, received)
        cosine_table, sine_values, allowed = pick_section(
            leading, table_list[min(tick_num, micro_count - 1)], table_list[max(tick_num - 1, 0)]
        )
        output, saved_state = layer_forward(
            layer_in, qkv_w, out_w, ffn_w, gain_row, cosine_table, sine_values, allowed
        )
        saved_list.append(saved_state)
        output_list.append(output)
        if tick_num < micro_count:
            received = passed_along(output.astype(jnp.bfloat16), "section", 1)
    back_weights = (
        lax.all_gather(attn_weight, "dp", axis=2, tiled=True),
        lax.all_gather(ffn_weight, "dp", axis=3, tiled=True),
        lax.all_gather(gains, "dp", axis=1, tiled=True),
    )
    qkv_w = back_weights[0][0][:, :split_at]
    out_w = back_weights[0][0][:, split_at:]
    ffn_w, gain_row = (back_weights[1][0], back_weights[2][0])
    grad_received = jnp.zeros_like(edge_data[0, 0])
    piece_list = []
    input_grad_list = []
    gain_total = jnp.zeros(gain_row.shape, jnp.float32)
    for tick_num in range(micro_count + 1):
        saved_state = pick_section(
            leading, saved_list[max(tick_num - 1, 0)], saved_list[min(tick_num + 1, micro_count)]
        )
        cosine_table, sine_values, allowed = pick_section(
            leading, table_list[max(tick_num - 1, 0)], table_list[min(tick_num, micro_count - 1)]
        )
        cotangent = edge_data[1, min(tick_num, micro_count - 1)]
        incoming = jnp.where(leading, grad_received, cotangent).astype(jnp.float32)
        is_valid = jnp.where(leading, tick_num >= 1, tick_num < micro_count)
        incoming = jnp.where(is_valid, incoming, 0.0)
        input_grad, pieces, gain_grad = layer_backward(
            incoming, saved_state, qkv_w, out_w, ffn_w, gain_row, cosine_table, sine_values, allowed
        )
        input_grad_list.append(input_grad)
        gain_total = gain_total + gain_grad
        piece_list.append(pieces)
        if tick_num < micro_count:
            grad_received = passed_along(input_grad.astype(jnp.bfloat16), "section", -1)
    owner_rows, owner_width, attn_share, ffn_share = owner_rows_maker(piece_list, owners)
    total_shard = lax.psum_scatter(
        owner_rows(jnp.int32(0), owner_width * lax.axis_size("dp")),
        "dp",
        scatter_dimension=0,
        tiled=True,
    )
    attention_shard, ffn_shard = unpack_shard(total_shard, attn_share, ffn_share)
    gain_shard = lax.psum_scatter(gain_total[None], "dp", scatter_dimension=1, tiled=True)
    edge_out = jnp.stack(
        [
            jnp.where(leading, input_grad_list[mb_num + 1], output_list[mb_num + 1])
            for mb_num in range(micro_count)
        ]
    ).astype(jnp.bfloat16)
    return (edge_out[None], attention_shard, ffn_shard, gain_shard)


def solution(mesh):
    in_specs = (
        P("section", None, "dp", None),
        P(None, "dp"),
        P("section", None, "dp"),
        P("section", None, None, "dp"),
        P("section", "dp"),
    )
    out_specs = (
        P("section", None, "dp", None),
        P("section", None, "dp"),
        P("section", None, None, "dp"),
        P("section", "dp"),
    )
    return jax.shard_map(local, mesh=mesh, in_specs=in_specs, out_specs=out_specs, check_vma=False)
```

profile of v0, /device:TPU:0, one launch (start us, length us, event | category | flops | bytes accessed | tf_op | source)
XLA Modules:
  0.0 898.2 jit_solution(8501034763040781893)
XLA Ops:
  8.7 1.3 fusion.218
  11.6 35.4 %all-reduce.14 = bf16[1920]{0:T(1024)(128)(2,1)S(1)} all-reduce(bf16[1920]{0:T(1024)(128)(2,1)S(1)} %dynamic-update-slice), channel_id=1, replica_groups=mesh['section'=2,'dp'=16] {'dp'}, use_global_device_ids=true, to_apply=%add.14 | all-reduce | flops 1920 | bytes 7680
  50.7 18.4 %all-gather.5.cloned.1.call-done = bf16[1,960,2560]{1,2,0:T(8,128)(2,1)} async-done(((bf16[1,960,160]{1,2,0:T(8,128)(2,1)}), bf16[1,960,2560]{1,2,0:T(8,128)(2,1)}) %all-gather.5.cloned.1.call-update) | async-done | bytes 4915216 | tf_op jit(solution)/shard_map/all_gather | solution.py:287
  69.1 3.1 fusion.55
  74.7 2.1 multiply_reduce_fusion.23
  76.9 113.4 %all-gather.3.cloned.1.call-done = bf16[1,3,960,2560]{2,3,1,0:T(8,128)(2,1)} async-done(((bf16[1,3,960,160]{2,3,1,0:T(8,128)(2,1)}), bf16[1,3,960,2560]{2,3,1,0:T(8,128)(2,1)}) %all-gather.3.cloned.1.call-update) | async-done | bytes 14745616 | tf_op jit(solution)/shard_map/all_gather | solution.py:312
  190.3 4.2 fusion.41
  194.5 5.3 multiply_convert_fusion.5
  199.8 3.6 fusion.92
  203.4 3.6 collective-permute-start
  208.6 1.4 collective-permute-done
  210.8 3.1 fusion.53
  216.7 2.3 multiply_reduce_fusion.21
  219.8 4.3 fusion.40
  224.2 5.4 broadcast_select_fusion.2
  229.6 4.6 fusion.112
  235.3 1.7 multiply_reduce_fusion.7
  237.9 2.3 convolution_convert_fusion.5
  243.8 4.2 fusion.90
  247.9 4.4 collective-permute-start.2
  252.4 2.5 collective-permute-done.2
  254.9 4.1 multiply_reduce_fusion.8
  264.1 2.9 multiply_reduce_fusion.16
  269.5 1.7 fusion.136
  271.3 1.3 collective-permute-start.1
  274.6 4.3 fusion.38
  279.1 4.6 broadcast_select_fusion.1
  287.1 4.3 fusion.91
  292.0 1.7 broadcast_select_fusion.19
  293.7 4.5 fusion.115
  299.4 1.7 multiply_reduce_fusion.5
  301.8 2.3 convolution_convert_fusion.4
  310.7 3.4 multiply_reduce_fusion.6
  315.2 1.5 collective-permute-start.3
  318.2 4.4 collective-permute-done.3
  322.7 4.7 fusion.118
  327.5 3.8 fusion.30
  331.3 4.2 multiply_reduce_fusion.3
  336.4 2.3 convolution_convert_fusion.3
  340.8 2.4 pad_maximum_fusion
  346.0 5.3 fusion.60
  351.3 2.8 multiply_reduce_fusion.4
  355.6 133.8 %while.10 = (s32[]{:T(128)}, f32[16,640,960]{2,1,0:T(8,128)}, s32[16]{0:T(128)S(1)}, bf16[192,2560]{0,1:T(8,128)(2,1)}, bf16[192,960]{1,0:T(8,128)(2,1)S(1)}, /*...) while((s32[]{:T(128)}, f32[16,640,960]{2,1,0:T(8,128)}, ...), condition=%wide.region_30.31_spmd, body=%wide.region_29.30_spmd.sunk | while | flops 296908800 | bytes 11109091 | solution.py:260
  362.1 1.8 fusion.297
  370.4 1.8 fusion.297
  374.6 1.3 convolution_add_fusion.5
  378.8 1.9 fusion.297
  387.2 1.8 fusion.297
  395.5 1.9 fusion.297
  403.9 1.8 fusion.297
  412.3 1.8 fusion.297
  420.6 1.9 fusion.297
  429.0 1.8 fusion.297
  437.4 1.9 fusion.297
  445.8 1.9 fusion.297
  454.2 1.8 fusion.297
  462.6 1.8 fusion.297
  470.9 1.9 fusion.297
  479.3 1.8 fusion.297
  487.6 1.8 fusion.297
  490.3 30.0 %all-reduce.15 = f32[1,1920]{1,0:T(1,128)S(1)} all-reduce(f32[1,1920]{1,0:T(1,128)S(1)} %fusion.191), channel_id=3, replica_groups=mesh['section'=2,'dp'=16] {'dp'}, use_global_device_ids=true, to_apply=%region_38.39.clone | all-reduce | flops 1920 | bytes 15360
  521.6 365.7 %reduce-scatter.3.cloned.1.call-done = f32[640,960]{1,0:T(8,128)} async-done(((f32[10240,960]{1,0:T(8,128)}), f32[640,960]{1,0:T(8,128)}) %reduce-scatter.3.cloned.1.call-update) | async-done | bytes 2457616 | tf_op jit(solution)/shard_map/reduce_scatter | solution.py:342
  887.3 2.7 slice_bitcast_fusion.37
  890.1 1.4 maximum_bitcast_fusion.1
  (501 shorter events, 144.1 us)
Async XLA Ops:
  7.2 61.9 %all-gather.5.cloned.1.call-start = ((), (), s32[]{:S(2)}) async-start(), calls=%async_computation.2 | async-start | bytes 5570560 | tf_op jit(solution)/shard_map/all_gather | solution.py:287
  7.9 182.4 %all-gather.3.cloned.1.call-start = ((), (), s32[]{:S(2)}) async-start(), calls=%async_computation.1 | async-start | bytes 16711680 | tf_op jit(solution)/shard_map/all_gather | solution.py:312
  8.6 878.7 %reduce-scatter.3.cloned.1.call-start = ((), (), s32[]{:S(2)}) async-start(), calls=%async_computation.3 | async-start | bytes 44564480 | tf_op jit(solution)/shard_map/reduce_scatter | solution.py:342
  49.0 23.5 %copy-start.73 = (f32[64]{0:T(128)}, f32[64]{0:T(128)S(1)}, u32[]{:S(2)}) copy-start(f32[64]{0:T(128)S(1)} %add_rsqrt_fusion.5) | copy-start | bytes 772
  49.1 161.7 %copy-start.58 = (f32[1,960]{1,0:T(1,128)}, f32[1,960]{1,0:T(1,128)S(1)}, u32[]{:S(2)}) copy-start(f32[1,960]{1,0:T(1,128)S(1)} %get-tuple-element.217) | copy-start | bytes 11524
  49.1 224.8 %copy-start.55 = (f32[1,960]{1,0:T(1,128)}, f32[1,960]{1,0:T(1,128)S(1)}, u32[]{:S(2)}) copy-start(f32[1,960]{1,0:T(1,128)S(1)} %get-tuple-element.216) | copy-start | bytes 11524
  50.7 210.8 %copy-start.15 = (f32[64,32]{1,0:T(8,128)}, f32[64,32]{1,0:T(8,128)S(1)}, u32[]{:S(2)}) copy-start(f32[64,32]{1,0:T(8,128)S(1)} %get-tuple-element.224) | copy-start | bytes 24580
  50.7 210.8 %copy-start.18 = (f32[64,32]{1,0:T(8,128)}, f32[64,32]{1,0:T(8,128)S(1)}, u32[]{:S(2)}) copy-start(f32[64,32]{1,0:T(8,128)S(1)} %get-tuple-element.225) | copy-start | bytes 24580
  76.9 142.1 %copy-start.83 = (f32[64]{0:T(128)}, f32[64]{0:T(128)S(1)}, u32[]{:S(2)}) copy-start(f32[64]{0:T(128)S(1)} %add_rsqrt_fusion.4) | copy-start | bytes 772
  194.5 8.9 copy-start.96
  199.8 14.0 %copy-start.101 = (bf16[64,2560]{1,0:T(8,128)(2,1)}, bf16[64,2560]{1,0:T(8,128)(2,1)S(1)}, u32[]{:S(2)}) copy-start(bf16[64,2560]{1,0:T(8,128)(2,1)S(1)} %get-tuple-element.238) | copy-start | bytes 983044
  203.4 6.5 collective-permute-start
  208.6 32.0 %copy-start.21 = (bf16[64,5,64]{2,0,1:T(8,128)(2,1)}, bf16[64,5,64]{2,0,1:T(8,128)(2,1)S(1)}, u32[]{:S(2)}) copy-start(bf16[64,5,64]{2,0,1:T(8,128)(2,1)S(1)} %copy.141) | copy-start | bytes 122884
  216.7 17.6 %slice-start.2 = ((s8[15728640]{0:T(1024)(128)(4,1)}), s8[4194304]{0:T(1024)(128)(4,1)S(1)}, s32[]{:S(2)}) async-start(s8[15728640]{0:T(1024)(128)(4,1)} %bitcast.493), calls=%async_computation.6 | async-start | bytes 8388608
  219.8 9.8 %copy-start.31 = (bf16[64,960]{1,0:T(8,128)(2,1)}, bf16[64,960]{1,0:T(8,128)(2,1)S(1)}, u32[]{:S(2)}) copy-start(bf16[64,960]{1,0:T(8,128)(2,1)S(1)} %get-tuple-element.137) | copy-start | bytes 368644
  219.8 14.5 %slice-start.3 = ((s8[15728640]{0:T(1024)(128)(4,1)}), s8[4194304]{0:T(1024)(128)(4,1)S(1)}, s32[]{:S(2)}) async-start(s8[15728640]{0:T(1024)(128)(4,1)} %bitcast.493), calls=%async_computation.7 | async-start | bytes 8388608
  224.1 10.1 %copy-start.99 = (f32[64,2560]{1,0:T(8,128)}, f32[64,2560]{1,0:T(8,128)S(1)}, u32[]{:S(2)}) copy-start(f32[64,2560]{1,0:T(8,128)S(1)} %fusion.40) | copy-start | bytes 1966084
  224.2 10.1 %slice-start.4 = ((s8[15728640]{0:T(1024)(128)(4,1)}), s8[4194304]{0:T(1024)(128)(4,1)S(1)}, s32[]{:S(2)}) async-start(s8[15728640]{0:T(1024)(128)(4,1)} %bitcast.493), calls=%async_computation.8 | async-start | bytes 8388608
  242.0 12.9 %copy-start.40 = (bf16[5,64,64]{2,1,0:T(8,128)(2,1)}, bf16[5,64,64]{2,1,0:T(8,128)(2,1)S(1)}, u32[]{:S(2)}) copy-start(bf16[5,64,64]{2,1,0:T(8,128)(2,1)S(1)} %fusion.99) | copy-start | bytes 122884
  243.0 9.4 %copy-start.91 = (f32[64]{0:T(128)S(1)}, f32[64]{0:T(128)}, u32[]{:S(2)}) copy-start(f32[64]{0:T(128)} %get-tuple-element.106) | copy-start | bytes 772
  243.0 11.9 %copy-start.59 = (f32[1,960]{1,0:T(1,128)S(1)}, f32[1,960]{1,0:T(1,128)}, u32[]{:S(2)}) copy-start(f32[1,960]{1,0:T(1,128)} %copy-done.58) | copy-start | bytes 11524
  243.4 15.6 %copy-start.13 = (bf16[64,5,3,64]{0,3,2,1:T(8,128)(2,1)}, bf16[64,5,3,64]{0,3,2,1:T(8,128)(2,1)S(1)}, u32[]{:S(2)}) copy-start(bf16[64,5,3,64]{0,3,2,1:T(8,128)(2,1)S(1)} %copy.148) | copy-start | bytes 368644
  243.8 15.2 %copy-start.42 = (bf16[64,5,64]{0,2,1:T(8,128)(2,1)}, bf16[64,5,64]{0,2,1:T(8,128)(2,1)S(1)}, u32[]{:S(2)}) copy-start(bf16[64,5,64]{0,2,1:T(8,128)(2,1)S(1)} %copy.152) | copy-start | bytes 122884
  243.8 15.2 %slice-start = ((s8[5242880]{0:T(1024)(128)(4,1)}), s8[4194304]{0:T(1024)(128)(4,1)S(1)}, s32[]{:S(2)}) async-start(s8[5242880]{0:T(1024)(128)(4,1)} %bitcast.421), calls=%async_computation.4 | async-start | bytes 8388608
  243.8 15.2 %slice-start.1 = ((s8[5242880]{0:T(1024)(128)(4,1)}), s8[1048576]{0:T(1024)(128)(4,1)S(1)}, s32[]{:S(2)}) async-start(s8[5242880]{0:T(1024)(128)(4,1)} %bitcast.421), calls=%async_computation.5 | async-start | bytes 2097152
  247.9 6.9 collective-permute-start.2
  261.4 8.1 copy-start.9
  261.5 44.0 %copy-start.1 = (bf16[64,5,64]{2,0,1:T(8,128)(2,1)}, bf16[64,5,64]{2,0,1:T(8,128)(2,1)S(1)}, u32[]{:S(2)}) copy-start(bf16[64,5,64]{2,0,1:T(8,128)(2,1)S(1)} %pad_maximum_fusion.13) | copy-start | bytes 122884
  261.5 11.8 %copy-start.94 = (f32[64]{0:T(128)S(1)}, f32[64]{0:T(128)}, u32[]{:S(2)}) copy-start(f32[64]{0:T(128)} %get-tuple-element.103) | copy-start | bytes 772
  261.5 12.3 %copy-start.84 = (f32[64]{0:T(128)S(1)}, f32[64]{0:T(128)}, u32[]{:S(2)}) copy-start(f32[64]{0:T(128)} %copy-done.83) | copy-start | bytes 772
  267.0 16.6 %copy-start.7 = (f32[64,960]{1,0:T(8,128)}, f32[64,960]{1,0:T(8,128)S(1)}, u32[]{:S(2)}) copy-start(f32[64,960]{1,0:T(8,128)S(1)} %get-tuple-element.250) | copy-start | bytes 737284
  267.0 24.4 %copy-start.87 = (f32[64]{0:T(128)}, f32[64]{0:T(128)S(1)}, u32[]{:S(2)}) copy-start(f32[64]{0:T(128)S(1)} %get-tuple-element.197) | copy-start | bytes 772
  271.3 20.7 %collective-permute-start.1 = (bf16[64,960]{1,0:T(8,128)(2,1)}, bf16[64,960]{1,0:T(8,128)(2,1)}, u32[]{:S(2)}, u32[]{:S(2)}) collective-permute-start(bf16[64,960]{1,0:T(8,128)(2,1)} %fusion.136), channel_id=1, source_target_pairs={{16,0},{17,1},{18,2},{19,3},{20,4},{21,5},{22,6},{23,7},{24,8},{25... | collective-permute-start | bytes 368648 | tf_op jit(solution)/shard_map/ppermute | solution.py:20
  272.6 28.5 %copy-start.79 = (f32[64]{0:T(128)}, f32[64]{0:T(128)S(1)}, u32[]{:S(2)}) copy-start(f32[64]{0:T(128)S(1)} %fusion.194) | copy-start | bytes 772
  274.6 23.6 %slice-start.6 = ((s8[15728640]{0:T(1024)(128)(4,1)}), s8[4194304]{0:T(1024)(128)(4,1)S(1)}, s32[]{:S(2)}) async-start(s8[15728640]{0:T(1024)(128)(4,1)} %bitcast.495), calls=%async_computation.10 | async-start | bytes 8388608
  279.0 14.7 %copy-start.100 = (f32[64,2560]{1,0:T(8,128)}, f32[64,2560]{1,0:T(8,128)S(1)}, u32[]{:S(2)}) copy-start(f32[64,2560]{1,0:T(8,128)S(1)} %fusion.38) | copy-start | bytes 1966084
  279.1 19.2 %slice-start.7 = ((s8[15728640]{0:T(1024)(128)(4,1)}), s8[4194304]{0:T(1024)(128)(4,1)S(1)}, s32[]{:S(2)}) async-start(s8[15728640]{0:T(1024)(128)(4,1)} %bitcast.495), calls=%async_computation.11 | async-start | bytes 8388608
  283.7 10.0 %copy-start.104 = (f32[64,2560]{1,0:T(8,128)}, f32[64,2560]{1,0:T(8,128)S(1)}, u32[]{:S(2)}) copy-start(f32[64,2560]{1,0:T(8,128)S(1)} %get-tuple-element.251) | copy-start | bytes 1966084
  284.1 7.9 copy-start.60
  284.1 7.9 copy-start.71
  284.1 7.9 copy-start.74
  285.2 8.5 copy-start.98
  285.2 8.5 copy-start.106
  285.2 13.1 %slice-start.8 = ((s8[15728640]{0:T(1024)(128)(4,1)}), s8[4194304]{0:T(1024)(128)(4,1)S(1)}, s32[]{:S(2)}) async-start(s8[15728640]{0:T(1024)(128)(4,1)} %bitcast.495), calls=%async_computation.12 | async-start | bytes 8388608
  306.3 8.9 copy-start.41
  306.3 7.8 copy-start.4
  306.3 7.8 copy-start.12
  307.5 9.1 %copy-start.92 = (f32[64]{0:T(128)S(1)}, f32[64]{0:T(128)}, u32[]{:S(2)}) copy-start(f32[64]{0:T(128)} %get-tuple-element.104) | copy-start | bytes 772
  310.7 12.0 %copy-start.43 = (bf16[64,5,64]{0,2,1:T(8,128)(2,1)}, bf16[64,5,64]{0,2,1:T(8,128)(2,1)S(1)}, u32[]{:S(2)}) copy-start(bf16[64,5,64]{0,2,1:T(8,128)(2,1)S(1)} %copy.173) | copy-start | bytes 122884
  315.2 7.4 collective-permute-start.3
  327.4 8.1 copy-start.50
  327.4 8.1 copy-start.52
  327.4 8.1 copy-start.88
  331.3 8.0 copy-start.2
  340.8 10.6 %copy-start.5 = (bf16[64,960]{1,0:T(8,128)(2,1)S(1)}, bf16[64,960]{1,0:T(8,128)(2,1)}, u32[]{:S(2)}) copy-start(bf16[64,960]{1,0:T(8,128)(2,1)} %copy-done.3) | copy-start | bytes 368644
  340.8 10.6 %copy-start.62 = (f32[1,960]{1,0:T(1,128)S(1)}, f32[1,960]{1,0:T(1,128)}, u32[]{:S(2)}) copy-start(f32[1,960]{1,0:T(1,128)} %copy-done.58) | copy-start | bytes 11524
  340.8 10.6 %copy-start.89 = (f32[64]{0:T(128)S(1)}, f32[64]{0:T(128)}, u32[]{:S(2)}) copy-start(f32[64]{0:T(128)} %fusion.197) | copy-start | bytes 772
  343.5 10.7 %copy-start.93 = (f32[64]{0:T(128)S(1)}, f32[64]{0:T(128)}, u32[]{:S(2)}) copy-start(f32[64]{0:T(128)} %get-tuple-element.104) | copy-start | bytes 772
  343.6 10.7 %copy-start.72 = (f32[64]{0:T(128)S(1)}, f32[64]{0:T(128)}, u32[]{:S(2)}) copy-start(f32[64]{0:T(128)} %copy-done.70) | copy-start | bytes 772
  343.6 10.7 %copy-start.78 = (f32[64]{0:T(128)S(1)}, f32[64]{0:T(128)}, u32[]{:S(2)}) copy-start(f32[64]{0:T(128)} %copy-done.76) | copy-start | bytes 772
  344.5 9.8 %copy-start.10 = (f32[64,960]{1,0:T(8,128)S(1)}, f32[64,960]{1,0:T(8,128)}, u32[]{:S(2)}) copy-start(f32[64,960]{1,0:T(8,128)} %get-tuple-element.145) | copy-start | bytes 737284
  344.5 10.0 %copy-start.28 = (bf16[64,960]{1,0:T(8,128)(2,1)S(1)}, bf16[64,960]{1,0:T(8,128)(2,1)}, u32[]{:S(2)}) copy-start(bf16[64,960]{1,0:T(8,128)(2,1)} %bitcast_convert_fusion) | copy-start | bytes 368644
  344.5 10.0 %copy-start.30 = (bf16[64,960]{1,0:T(8,128)(2,1)S(1)}, bf16[64,960]{1,0:T(8,128)(2,1)}, u32[]{:S(2)}) copy-start(bf16[64,960]{1,0:T(8,128)(2,1)} %copy-done.29) | copy-start | bytes 368644
  489.4 31.4 %copy-start.39 = (bf16[1,1,64,960]{3,2,1,0:T(8,128)(2,1)S(1)}, bf16[1,1,64,960]{3,2,1,0:T(8,128)(2,1)}, u32[]{:S(2)}) copy-start(bf16[1,1,64,960]{3,2,1,0:T(8,128)(2,1)} %get-tuple-element.140) | copy-start | bytes 368644
  (60 other events, 261.1 us)
Sparse Core Ops, SparseCore 0:
  10.3 58.7 all-gather.4
  71.4 118.8 all-gather.2
  489.6 397.7 reduce-scatter.2
where the time goes:
time: 906 us; the launch traced here: 898 us
  waiting for transfers between devices  507 us (56%)
  matrix products  192 us (21%)
  other arithmetic  67 us (7%)
  blocking collectives  65.3 us (7%)
  local copies, waits for them, and re-layouts  27.3 us (3%)
  between operations  17.5 us (2%)
  loops' own time  11.2 us (1%)
  starting transfers between devices  10.8 us (1%)
    reduce_scatter x1, waiting for transfers between devices, local(): lax.psum_scatter(owner_rows(jnp.int32(0), owner_width * lax.axis_size('dp...  366 us
    all_gather x1, waiting for transfers between devices, local(): lax.all_gather(ffn_weight, 'dp', axis=3, tiled=True)  113 us
    dot_general x80, matrix products, left_trans(): lax.dot_general(left_op, right_op, contract_first, preferred_element_type...  83.9 us
    unnamed x2, blocking collectives  65.3 us
    dot_general x15, matrix products, matmul(): return jnp.dot(left_op, right_op, preferred_element_type=jnp.float32)  56.3 us
    dot_general x15, matrix products, right_trans(): lax.dot_general(left_op, right_op, contract_last, preferred_element_type=...  43.2 us
    dynamic_update_slice x16, other arithmetic, owner_rows(): stacked = lax.map(one_owner, owner_list)  29.5 us
    all_gather x1, waiting for transfers between devices, local(): lax.all_gather(attn_weight, 'dp', axis=2, tiled=True)  18.4 us
  transfers between devices with their start and end apart: 7, of which 6 were waited for; matrix products, arithmetic and copies ran while one was open for 4% of the time, Pallas kernels for 0%

commit v1 on v0

v1 whole, which is shorter than its diff:
```python
import jax
import jax.numpy as jnp
from jax import lax
from jax.sharding import PartitionSpec as P

QUERY_HEADS = 15
KEY_VALUE_HEADS = 5
HEAD_SIZE = 64
GROUP = QUERY_HEADS // KEY_VALUE_HEADS
Q_COLS = QUERY_HEADS * HEAD_SIZE
KV_COLS = KEY_VALUE_HEADS * HEAD_SIZE
QKV_COLS = Q_COLS + 2 * KV_COLS

epsilon = 1e-05
theta_base = 100000.0
bf16 = jnp.bfloat16
f32 = jnp.float32


def dot_nn(a, b):
    return lax.dot_general(a, b, (((1,), (0,)), ((), ())), preferred_element_type=f32)


def dot_nt(a, b):
    return lax.dot_general(a, b, (((1,), (1,)), ((), ())), preferred_element_type=f32)


def rope(rows, cosine, sine):
    half = rows.shape[-1] // 2
    a, b = rows[..., :half], rows[..., half:]
    return jnp.concatenate([a * cosine - b * sine, b * cosine + a * sine], axis=-1)


def block_tables(segments):
    micro, block_len = segments.shape
    offsets = jnp.arange(block_len, dtype=jnp.int32)
    same = segments[:, :, None] == segments[:, None, :]
    start = jnp.min(jnp.where(same, offsets, block_len), axis=-1)
    positions = (offsets - start).astype(f32).reshape(-1)
    half = HEAD_SIZE // 2
    frequency = theta_base ** (-(2.0 * jnp.arange(half, dtype=f32)) / HEAD_SIZE)
    angles = positions[:, None] * frequency
    allowed = same & (offsets[:, None] >= offsets[None, :])
    eye = jnp.eye(micro, dtype=bool)
    full = allowed[:, :, None, :] & eye[:, None, :, None]
    total = micro * block_len
    return jnp.cos(angles), jnp.sin(angles), full.reshape(total, total)


def scores_of(q, k, allowed):
    s = jnp.einsum("tgrd,ugd->grtu", q, k, preferred_element_type=f32) * HEAD_SIZE**-0.5
    return jnp.where(allowed, s, -1000000000.0)


def forward(u, weights, tables):
    qkv_w, out_w, gate_w, up_w, down_w, gain_one, gain_two = weights
    cosine, sine, allowed = tables
    tokens = u.shape[0]
    u = u.astype(f32)
    r1 = lax.rsqrt(jnp.mean(u * u, axis=-1, keepdims=True) + epsilon)
    n = (u * r1 * gain_one).astype(bf16)
    proj = dot_nt(n, qkv_w)
    q = rope(
        proj[:, :Q_COLS].reshape(tokens, KEY_VALUE_HEADS, GROUP, HEAD_SIZE),
        cosine[:, None, None, :],
        sine[:, None, None, :],
    ).astype(bf16)
    k = rope(
        proj[:, Q_COLS : Q_COLS + KV_COLS].reshape(tokens, KEY_VALUE_HEADS, HEAD_SIZE),
        cosine[:, None, :],
        sine[:, None, :],
    ).astype(bf16)
    v = proj[:, Q_COLS + KV_COLS :].reshape(tokens, KEY_VALUE_HEADS, HEAD_SIZE).astype(bf16)
    masked = scores_of(q, k, allowed)
    peak = jnp.max(masked, axis=-1, keepdims=True)
    lse = peak + jnp.log(jnp.sum(jnp.exp(masked - peak), axis=-1, keepdims=True))
    prob = jnp.exp(masked - lse).astype(bf16)
    o = jnp.einsum("grtu,ugd->tgrd", prob, v, preferred_element_type=f32)
    o = o.reshape(tokens, Q_COLS).astype(bf16)
    h1 = u + dot_nn(o, out_w)
    r2 = lax.rsqrt(jnp.mean(h1 * h1, axis=-1, keepdims=True) + epsilon)
    m = (h1 * r2 * gain_two).astype(bf16)
    gate = dot_nt(m, gate_w)
    up = dot_nt(m, up_w)
    act = (jax.nn.silu(gate) * up).astype(bf16)
    out = h1 + dot_nn(act, down_w)
    return out, (u, r1, n, q, k, v, lse, o, h1, r2, m, gate, up, act)


def norm_back(grad, rows, r, gain):
    scaled = grad * gain
    part = r * scaled - rows * (r * r * r) * jnp.mean(scaled * rows, axis=-1, keepdims=True)
    return part, jnp.sum(grad * rows * r, axis=0)


def backward(e, state, weights, tables):
    qkv_w, out_w, gate_w, up_w, down_w, gain_one, gain_two = weights
    cosine, sine, allowed = tables
    u, r1, n, q, k, v, lse, o, h1, r2, m, gate, up, act = state
    tokens = u.shape[0]
    eb = e.astype(bf16)
    e = e.astype(f32)
    da = dot_nt(eb, down_w)
    sig = jax.nn.sigmoid(gate)
    dgate = (da * up * sig * (1.0 + gate * (1.0 - sig))).astype(bf16)
    dup = (da * gate * sig).astype(bf16)
    dm = dot_nn(dgate, gate_w) + dot_nn(dup, up_w)
    part, gain_two_grad = norm_back(dm, h1, r2, gain_two)
    dh1 = e + part
    dz = dh1.astype(bf16)
    do = dot_nt(dz, out_w).reshape(tokens, KEY_VALUE_HEADS, GROUP, HEAD_SIZE).astype(bf16)
    prob = jnp.exp(scores_of(q, k, allowed) - lse)
    dv = jnp.einsum("grtu,tgrd->ugd", prob.astype(bf16), do, preferred_element_type=f32)
    dp = jnp.einsum("tgrd,ugd->grtu", do, v, preferred_element_type=f32)
    ds = (prob * (dp - jnp.sum(dp * prob, axis=-1, keepdims=True))).astype(bf16)
    dq = jnp.einsum("grtu,ugd->tgrd", ds, k, preferred_element_type=f32) * HEAD_SIZE**-0.5
    dk = jnp.einsum("grtu,tgrd->ugd", ds, q, preferred_element_type=f32) * HEAD_SIZE**-0.5
    dq = rope(dq, cosine[:, None, None, :], -sine[:, None, None, :])
    dk = rope(dk, cosine[:, None, :], -sine[:, None, :])
    dproj = jnp.concatenate(
        [dq.reshape(tokens, Q_COLS), dk.reshape(tokens, KV_COLS), dv.reshape(tokens, KV_COLS)],
        axis=1,
    ).astype(bf16)
    dn = dot_nn(dproj, qkv_w)
    part, gain_one_grad = norm_back(dn, u, r1, gain_one)
    du = dh1 + part
    gain_grad = jnp.concatenate([gain_one_grad, gain_two_grad])
    return du, (n, dproj, o, dz, m, dgate, dup, eb, act), gain_grad


def flip(x, bit):
    size = lax.axis_size("dp")
    return lax.ppermute(x, "dp", [(i, i ^ bit) for i in range(size)])


def gather_small(row):
    size = lax.axis_size("dp")
    me = lax.axis_index("dp")
    bit = 1
    while bit < size:
        other = flip(row, bit)
        high = (me & bit) != 0
        row = jnp.concatenate([jnp.where(high, other, row), jnp.where(high, row, other)])
        bit *= 2
    return row


def scatter_small(row):
    size = lax.axis_size("dp")
    me = lax.axis_index("dp")
    bit = size // 2
    while bit >= 1:
        half = row.shape[0] // 2
        low, top = row[:half], row[half:]
        high = (me & bit) != 0
        row = jnp.where(high, top, low) + flip(jnp.where(high, low, top), bit)
        bit //= 2
    return row


def grads_generic(pieces):
    n, dproj, o, dz, m, dgate, dup, eb, act = pieces
    attn = jnp.concatenate([dot_nn(dproj.T, n), dot_nn(o.T, dz)], axis=0)
    both = [
        lax.psum_scatter(g, "dp", scatter_dimension=0, tiled=True)
        for g in (attn, dot_nn(dgate.T, m), dot_nn(dup.T, m), dot_nn(act.T, eb))
    ]
    return both[0], jnp.stack(both[1:])


def plane_rows(x, y_bit, core_bit):
    x = jnp.concatenate([x, flip(x, y_bit)], axis=0)
    return jnp.concatenate([x, flip(x, core_bit)], axis=0)


def plane_cols(cols, y, core, y_bit, core_bit):
    keep = lax.dynamic_index_in_dim(cols, y, 2, keepdims=False)
    send = lax.dynamic_index_in_dim(cols, 1 - y, 2, keepdims=False)
    cols = jnp.concatenate([keep, flip(send, y_bit)], axis=-1)
    keep = lax.dynamic_index_in_dim(cols, core, 2, keepdims=False)
    send = lax.dynamic_index_in_dim(cols, 1 - core, 2, keepdims=False)
    return jnp.concatenate([keep, flip(send, core_bit)], axis=-1)


def line_sum(parts, z):
    def shift(x, pairs):
        return lax.ppermute(x, "dp", [(4 * a + i, 4 * b + i) for a, b in pairs for i in range(4)])

    def pick(indices):
        return lax.dynamic_index_in_dim(parts, jnp.array(indices, jnp.int32)[z], 0, keepdims=False)

    def plus(x, recv):
        return (x.astype(f32) + recv.astype(f32)).astype(bf16)

    first = pick([3, 3, 0, 0])
    right = shift(first, [(0, 1)])
    left = shift(first, [(3, 2)])
    send_right = plus(pick([2, 3, 3, 3]), right)
    send_left = plus(pick([0, 0, 0, 1]), left)
    right = shift(send_right, [(0, 1), (1, 2)])
    left = shift(send_left, [(3, 2), (2, 1)])
    send_right = plus(pick([1, 2, 3, 3]), right)
    send_left = plus(pick([0, 0, 1, 2]), left)
    right = shift(send_right, [(0, 1), (1, 2), (2, 3)])
    left = shift(send_left, [(3, 2), (2, 1), (1, 0)])
    own = lax.dynamic_index_in_dim(parts, z, 0, keepdims=False)
    return own.astype(f32) + right.astype(f32) + left.astype(f32)


def grads_planes(pieces):
    n, dproj, o, dz, m, dgate, dup, eb, act = pieces
    me = lax.axis_index("dp")
    z, y, core = me // 4, (me // 2) % 2, me % 2
    y_bit, core_bit = 2, 1
    tokens = n.shape[0]
    share = act.shape[1] // 16
    m_all = plane_rows(m, y_bit, core_bit)
    eb_all = plane_rows(eb, y_bit, core_bit)
    n_all = plane_rows(n, y_bit, core_bit)

    def cols(*arrays):
        stacked = jnp.stack([a.T.reshape(4, 2, 2, share, tokens) for a in arrays])
        return plane_cols(stacked, y, core, y_bit, core_bit)

    act_c = cols(act)
    gu_c = cols(dgate, dup)
    dz_all = plane_rows(dz, y_bit, core_bit)
    attn_c = cols(jnp.concatenate([dproj, o], axis=1))
    wide = 4 * tokens
    down = dot_nn(act_c.reshape(4 * share, wide), eb_all)
    gate_up = dot_nn(gu_c.reshape(8 * share, wide), m_all).reshape(2, 4, share, -1)
    ffn = jnp.concatenate([gate_up, down.reshape(1, 4, share, -1)], axis=0).astype(bf16)
    ffn = ffn.transpose(1, 0, 2, 3).reshape(4, 3 * share, -1)
    ffn_total = line_sum(ffn, z)
    owners = jnp.arange(4, dtype=jnp.int32) * 4 + y * 2 + core
    is_qkv = owners * share < QKV_COLS
    from_n = dot_nn(attn_c.reshape(4 * share, wide), n_all).reshape(4, share, -1)
    from_dz = dot_nn(attn_c.reshape(4 * share, wide), dz_all).reshape(4, share, -1)
    attn = jnp.where(is_qkv[:, None, None], from_n, from_dz).astype(bf16)
    attn_total = line_sum(attn, z)
    return attn_total, ffn_total.reshape(3, share, -1)


def local(edge_data, segment_ids, attn_weight, ffn_weight, gains):
    micro = segment_ids.shape[0]
    leading = lax.axis_index("section") == 0
    tables = block_tables(segment_ids)
    block, width = edge_data.shape[2], edge_data.shape[3]
    x = edge_data[0].reshape(micro * block, width)
    attn_t = lax.all_gather(attn_weight[0].T, "dp", axis=0, tiled=True)
    ffn_t = lax.all_gather(ffn_weight[0].swapaxes(1, 2), "dp", axis=1, tiled=True)
    gain_row = gather_small(gains[0]).astype(f32)
    weights = (
        attn_t[:QKV_COLS],
        attn_t[QKV_COLS:],
        ffn_t[0],
        ffn_t[1],
        ffn_t[2],
        gain_row[:width],
        gain_row[width:],
    )
    first, _ = forward(x, weights, tables)
    received = lax.ppermute(first.astype(bf16), "section", [(0, 1)])
    u = jnp.where(leading, x, received)
    out, state = forward(u, weights, tables)
    first_grad, _, _ = backward(x, state, weights, tables)
    received = lax.ppermute(first_grad.astype(bf16), "section", [(1, 0)])
    e = jnp.where(leading, received, x)
    du, pieces, gain_grad = backward(e, state, weights, tables)
    if lax.axis_size("dp") == 16:
        attn_rows, ffn_rows = grads_planes(pieces)
    else:
        attn_rows, ffn_rows = grads_generic(pieces)
    gain_shard = scatter_small(gain_grad)
    edge_out = jnp.where(leading, du, out).astype(bf16).reshape(micro, block, width)
    return (
        edge_out[None],
        attn_rows.T[None],
        ffn_rows.swapaxes(1, 2)[None],
        gain_shard[None],
    )


def solution(mesh):
    in_specs = (
        P("section", None, "dp", None),
        P(None, "dp"),
        P("section", None, "dp"),
        P("section", None, None, "dp"),
        P("section", "dp"),
    )
    out_specs = (
        P("section", None, "dp", None),
        P("section", None, "dp"),
        P("section", None, None, "dp"),
        P("section", "dp"),
    )
    return jax.shard_map(local, mesh=mesh, in_specs=in_specs, out_specs=out_specs, check_vma=False)
```

time: 906 us -> 458 us (0.51)
  waiting for transfers between devices: 507 us -> 243 us
  matrix products: 192 us -> 79.6 us
  blocking collectives: 65.3 us -> 0 us
  starting transfers between devices: 10.8 us -> 73 us
  other arithmetic: 67 us -> 22.7 us
  local copies, waits for them, and re-layouts: 27.3 us -> 7.63 us
  loops' own time: 11.2 us -> 0 us
    reduce_scatter x1 -> x0, waiting for transfers between devices: 366 us -> none  [local(): lax.psum_scatter(owner_rows(jnp.int32(0), owner_width * lax.axis_size('dp...]
    dot_general x131 -> x35, matrix products: 192 us -> 79.6 us  [the longest x14 42.7 us: dot_nn(): lax.dot_general(a, b, (((1,), (0,)), ((), ())), preferred_element_type=f32)]
    ppermute x4 -> x36, waiting for transfers between devices: 8.24 us -> 81 us  [the longest x22 44.4 us: flip(): return lax.ppermute(x, 'dp', [(i, i ^ bit) for i in range(size)])]
    unnamed x2 -> x0, blocking collectives: 65.3 us -> none
    ppermute x4 -> x36, starting transfers between devices: 10.7 us -> 72.9 us  [the longest x12 49.7 us: shift(): lax.ppermute(x, 'dp', [(4 * a + i, 4 * b + i) for a, b in pairs for i in...]
    dynamic_update_slice x16 -> x0, other arithmetic: 29.5 us -> none  [owner_rows(): stacked = lax.map(one_owner, owner_list)]
    all_gather x2, waiting for transfers between devices: 132 us -> 160 us  [the longest x1 115 us: local(): lax.all_gather(ffn_weight[0].swapaxes(1, 2), 'dp', axis=1, tiled=True)]
    another operation x1 -> x0, loops' own time: 11.2 us -> none  [owner_rows(): stacked = lax.map(one_owner, owner_list)]
  transfers between devices with their start and end apart: 7 -> 38, of which waited for: 6 -> 16; matrix products, arithmetic and copies ran while one was open for 4% -> 16% of each run, Pallas kernels for 0% -> 0%
where the time goes in v1:
time: 458 us; the launch traced here: 451 us
  waiting for transfers between devices  243 us (53%)
  matrix products  79.6 us (17%)
  starting transfers between devices  73 us (16%)
  between operations  25.2 us (6%)
  other arithmetic  22.7 us (5%)
  local copies, waits for them, and re-layouts  7.63 us (2%)
    all_gather x1, waiting for transfers between devices, local(): lax.all_gather(ffn_weight[0].swapaxes(1, 2), 'dp', axis=1, tiled=True)  115 us
    ppermute x12, starting transfers between devices, shift(): lax.ppermute(x, 'dp', [(4 * a + i, 4 * b + i) for a, b in pairs for i in...  49.7 us
    all_gather x1, waiting for transfers between devices, local(): attn_t = lax.all_gather(attn_weight[0].T, 'dp', axis=0, tiled=True)  45.8 us
    ppermute x22, waiting for transfers between devices, flip(): return lax.ppermute(x, 'dp', [(i, i ^ bit) for i in range(size)])  44.4 us
    dot_general x14, matrix products, dot_nn(): lax.dot_general(a, b, (((1,), (0,)), ((), ())), preferred_element_type=f32)  42.7 us
    ppermute x12, waiting for transfers between devices, shift(): lax.ppermute(x, 'dp', [(4 * a + i, 4 * b + i) for a, b in pairs for i in...  35.7 us
    dot_general x9, matrix products, dot_nt(): lax.dot_general(a, b, (((1,), (1,)), ((), ())), preferred_element_type=f32)  32.7 us
    ppermute x22, starting transfers between devices, flip(): return lax.ppermute(x, 'dp', [(i, i ^ bit) for i in range(size)])  18.4 us
  transfers between devices with their start and end apart: 38, of which 16 were waited for; matrix products, arithmetic and copies ran while one was open for 16% of the time, Pallas kernels for 0%

profile of v1, /device:TPU:0, one launch (start us, length us, event | category | flops | bytes accessed | tf_op | source)
XLA Modules:
  0.0 451.0 jit_solution(17582125426785070834)
XLA Ops:
  10.1 2.8 collective-permute-start.1
  13.1 1.4 collective-permute-done.1
  14.6 2.1 collective-permute-start.2
  16.8 1.4 collective-permute-done.2
  18.4 3.0 collective-permute-start.3
  21.9 1.0 collective-permute-done.3
  23.2 45.8 %all-gather.3.cloned.1.call-done = bf16[2560,960]{1,0:T(8,128)(2,1)} async-done(((bf16[160,960]{1,0:T(8,128)(2,1)}), bf16[2560,960]{1,0:T(8,128)(2,1)}) %all-gather.3.cloned.1.call-update) | async-done | bytes 4915216 | tf_op jit(solution)/shard_map/all_gather | solution.py:250
  69.0 3.1 fusion.16
  73.1 2.4 multiply_reduce_fusion.7
  75.6 114.7 %all-gather.5.cloned.1.call-done = bf16[3,2560,960]{2,1,0:T(8,128)(2,1)} async-done(((bf16[3,160,960]{2,1,0:T(8,128)(2,1)}), bf16[3,2560,960]{2,1,0:T(8,128)(2,1)}) %all-gather.5.cloned.1.call-update) | async-done | bytes 14745616 | tf_op jit(solution)/shard_map/all_gather | solution.py:251
  190.3 4.6 %fusion.4 = f32[128,2560]{1,0:T(8,128)S(1)} fusion(bf16[3,2560,960]{2,1,0:T(8,128)(2,1)} %all-gather.5.cloned.1.call-done, f32[128,960]{0,1:T(8,128)S(1)} %get-tuple-element.69, f32[960]{0:T(1024)S(1)} %get-tuple-element.49, f32[128]{0:T(128)S(1)} %add_rsqrt_fusion.3), kind=kOutput, calls=%fused_computation.9 | convolution fusion | flops 629514240 | bytes 7049472 | tf_op jit(solution)/shard_map/dot_general | solution.py:25
  194.8 7.4 %fusion.72 = bf16[128,960]{0,1:T(8,128)(2,1)S(1)} fusion(f32[128,960]{0,1:T(8,128)S(1)} %get-tuple-element.69, bf16[3,2560,960]{2,1,0:T(8,128)(2,1)} %all-gather.5.cloned.1.call-done, f32[128,2560]{1,0:T(8,128)S(1)} %fusion.4, f32[960]{0:T(1024)S(1)} %get-tuple-element.49, f32[128]{0:T(128)S(1)} %add_rsqrt_fusion.3), kind=kOutput, calls=%fused_computation.112 | convolution fusion | flops 1260871680 | bytes 13029888 | tf_op jit(solution)/shard_map/dot_general | solution.py:21
  202.3 3.6 collective-permute-start.4
  205.8 4.5 fusion.10
  210.3 0.9 collective-permute-done.4
  211.4 0.9 fusion.135
  212.3 3.2 fusion.18
  216.8 0.9 multiply_reduce_fusion.6
  217.7 0.9 multiply_convert_fusion.12
  218.6 4.5 fusion.3
  223.2 3.1 fusion.7
  226.3 2.3 fusion.2
  228.6 2.0 multiply_reduce_fusion.5
  233.5 1.4 fusion.136
  235.3 1.3 collective-permute-start.5
  250.4 1.5 collective-permute-start.20
  251.9 6.8 %fusion.40 = (bf16[2560,128]{0,1:T(8,128)(2,1)}, bf16[2560,128]{0,1:T(8,128)(2,1)}, bf16[2560,128]{0,1:T(8,128)(2,1)}, f32[128,2560]{1,0:T(8,128)S(1)}) fusion(f32[128,2560]{1,0:T(8,128)} %copy-done.33, f32[128,2560]{1,0:T(8,128)} %copy-done.36, bf16[128,960]{0,1:T(8,128)(2,1)S(1)} %broadcast_select_fusion, ...), kind=kOutput, calls=%fused_computation.69 | convolution fusion | flops 634388480 | bytes 11386880 | tf_op jit(solution)/shard_map/dot_general | solution.py:25
  258.7 4.7 %fusion.1 = f32[128,960]{0,1:T(8,128)S(1)} fusion(bf16[3,2560,960]{2,1,0:T(8,128)(2,1)} %all-gather.5.cloned.1.call-done, f32[128,2560]{1,0:T(8,128)S(1)} %get-tuple-element.84, f32[128,2560]{1,0:T(8,128)S(1)} %copy-done.37, f32[128,2560]{1,0:T(8,128)S(1)} %copy-done.34), kind=kOutput, calls=%fused_computation.6 | convolution fusion | flops 632422400 | bytes 9666560 | tf_op jit(solution)/shard_map/dot_general | solution.py:21
  263.4 5.2 %multiply_reduce_fusion.3 = (f32[960]{0:T(1024)}, f32[128]{0:T(128)S(1)}, f32[128,960]{0,1:T(8,128)S(1)}) fusion(f32[128,960]{0,1:T(8,128)S(1)} %get-tuple-element.73, f32[128]{0:T(128)S(1)} %get-tuple-element.65, f32[960]{0:T(1024)S(1)} %get-tuple-element.49, f32[128,960]{0,1:T(8,128)S(1)} %fusion.1, ...), kind=kOutput, calls=%fused_computation.218 | convolution fusion | flops 631970752 | bytes 9347584 | tf_op jit(solution)/shard_map/dot_general | solution.py:21
  268.7 0.9 fusion.196
  269.6 2.2 fusion.73
  274.0 1.5 collective-permute-start.24
  276.9 1.4 copy.48
  279.2 3.5 fusion.139
  282.8 5.1 %collective-permute-done.24 = bf16[128,960]{0,1:T(8,128)(2,1)} collective-permute-done((bf16[128,960]{0,1:T(8,128)(2,1)S(1)}, bf16[128,960]{0,1:T(8,128)(2,1)}, u32[]{:S(2)}, u32[]{:S(2)}) %collective-permute-start.24) | collective-permute-done | bytes 245792 | tf_op jit(solution)/shard_map/ppermute | solution.py:133
  288.5 1.0 pad_maximum_fusion.5
  289.5 12.4 %collective-permute-done.18 = bf16[2,4,2,160,128]{4,3,2,1,0:T(8,128)(2,1)S(1)} collective-permute-done((bf16[2,4,2,160,128]{4,3,2,1,0:T(8,128)(2,1)S(1)}, bf16[2,4,2,160,128]{4,3,2,1,0:T(8,128)(2,1)S(1)}, u32[]{:S(2)}, u32[]{:S(2)}) %collective-permute-start.18) | collective-permute-done | bytes 655392 | tf_op jit(solution)/shard_map/ppermute | solution.py:133
  302.6 1.1 pad_maximum_fusion.4
  303.8 2.9 collective-permute-done.22
  307.4 1.1 pad_maximum_fusion.2
  309.8 1.8 fusion.25
  311.7 2.6 convolution_convert_fusion
  315.2 1.6 collective-permute-start.26
  317.5 1.0 pad_maximum_fusion.3
  319.3 19.3 %collective-permute-done.32 = f32[960]{0:T(1024)S(1)} collective-permute-done((f32[960]{0:T(1024)S(1)}, f32[960]{0:T(1024)S(1)}, u32[]{:S(2)}, u32[]{:S(2)}) %collective-permute-start.32) | collective-permute-done | bytes 3872 | tf_op jit(solution)/shard_map/ppermute | solution.py:133
  338.6 1.8 fusion.89
  341.6 4.0 collective-permute-start.27
  345.6 1.9 select_convert_fusion
  347.6 4.4 collective-permute-start.12
  352.1 1.5 collective-permute-start.34
  354.3 18.8 %collective-permute-done.12 = bf16[160,960]{1,0:T(8,128)(2,1)S(1)} collective-permute-done((bf16[160,960]{1,0:T(8,128)(2,1)S(1)}, bf16[160,960]{1,0:T(8,128)(2,1)S(1)}, u32[]{:S(2)}, u32[]{:S(2)}) %collective-permute-start.12) | collective-permute-done | bytes 307232 | tf_op jit(solution)/shard_map/ppermute | solution.py:187
  373.2 4.4 collective-permute-start.13
  377.7 1.9 fusion.23
  380.2 3.0 collective-permute-done.13
  384.3 5.0 %collective-permute-start.14 = (bf16[160,960]{1,0:T(8,128)(2,1)S(1)}, bf16[160,960]{1,0:T(8,128)(2,1)S(1)}, u32[]{:S(2)}, u32[]{:S(2)}) collective-permute-start(bf16[160,960]{1,0:T(8,128)(2,1)S(1)} %get-tuple-element.23), channel_id=1, source_target_pairs={{0,4},{1,5},{2,6},{3,7},{4,8},{5,9},{6,10},{7,11},{8,12},{9,13},{1... | collective-permute-start | bytes 921608 | tf_op jit(solution)/shard_map/ppermute | solution.py:187
  389.5 1.4 collective-permute-start.17
  391.0 24.8 %collective-permute-start.28 = (bf16[480,960]{1,0:T(8,128)(2,1)}, bf16[480,960]{1,0:T(8,128)(2,1)}, u32[]{:S(2)}, u32[]{:S(2)}) collective-permute-start(bf16[480,960]{1,0:T(8,128)(2,1)} %get-tuple-element.14), channel_id=1, source_target_pairs={{0,4},{1,5},{2,6},{3,7},{4,8},{5,9},{6,10},{7,11},{8,12},{9,13},{1... | collective-permute-start | bytes 2764808 | tf_op jit(solution)/shard_map/ppermute | solution.py:187
  415.8 1.4 fusion.21
  417.2 1.3 collective-permute-start.31
  418.6 4.5 fusion.130
  424.5 2.0 fusion.117
  426.5 7.4 %collective-permute-done.28 = bf16[480,960]{1,0:T(8,128)(2,1)} collective-permute-done((bf16[480,960]{1,0:T(8,128)(2,1)}, bf16[480,960]{1,0:T(8,128)(2,1)}, u32[]{:S(2)}, u32[]{:S(2)}) %collective-permute-start.28) | collective-permute-done | bytes 921632 | tf_op jit(solution)/shard_map/ppermute | solution.py:187
  433.9 6.5 %collective-permute-done.31 = bf16[480,960]{1,0:T(8,128)(2,1)} collective-permute-done((bf16[480,960]{1,0:T(8,128)(2,1)}, bf16[480,960]{1,0:T(8,128)(2,1)}, u32[]{:S(2)}, u32[]{:S(2)}) %collective-permute-start.31) | collective-permute-done | bytes 921632 | tf_op jit(solution)/shard_map/ppermute | solution.py:187
  440.4 3.6 fusion.24
  (246 shorter events, 29.2 us)
Async XLA Ops:
  7.2 9.5 %copy-start.1 = (bf16[1,2,64,960]{3,2,1,0:T(8,128)(2,1)S(1)}, bf16[1,2,64,960]{3,2,1,0:T(8,128)(2,1)}, u32[]{:S(2)}) copy-start(bf16[1,2,64,960]{3,2,1,0:T(8,128)(2,1)} %param.15) | copy-start | bytes 737284
  7.2 61.8 %all-gather.3.cloned.1.call-start = ((), (), s32[]{:S(2)}) async-start(), calls=%async_computation | async-start | bytes 5570560 | tf_op jit(solution)/shard_map/all_gather | solution.py:250
  7.9 182.3 %all-gather.5.cloned.1.call-start = ((), (), s32[]{:S(2)}) async-start(), calls=%async_computation.1 | async-start | bytes 16711680 | tf_op jit(solution)/shard_map/all_gather | solution.py:251
  8.7 1.3 collective-permute-start
  10.1 4.3 collective-permute-start.1
  14.6 3.6 collective-permute-start.2
  18.4 4.6 %collective-permute-start.3 = (bf16[960]{0:T(1024)(128)(2,1)S(1)}, bf16[960]{0:T(1024)(128)(2,1)S(1)}, u32[]{:S(2)}, u32[]{:S(2)}) collective-permute-start(bf16[960]{0:T(1024)(128)(2,1)S(1)} %pad_maximum_fusion.16), channel_id=1, source_target_pairs={{0,8},{1,9},{2,10},{3,11},{4,12},{5,13},{6,14},{7,15},{8,0},{9,1},... | collective-permute-start | bytes 5768 | tf_op jit(solution)/shard_map/ppermute | solution.py:133
  23.2 210.3 %copy-start.12 = (f32[960]{0:T(1024)}, f32[960]{0:T(1024)S(1)}, u32[]{:S(2)}) copy-start(f32[960]{0:T(1024)S(1)} %get-tuple-element.50) | copy-start | bytes 11524
  23.2 245.4 %copy-start.10 = (f32[960]{0:T(1024)}, f32[960]{0:T(1024)S(1)}, u32[]{:S(2)}) copy-start(f32[960]{0:T(1024)S(1)} %get-tuple-element.49) | copy-start | bytes 11524
  202.3 9.0 %collective-permute-start.4 = (bf16[128,960]{0,1:T(8,128)(2,1)S(1)}, bf16[128,960]{0,1:T(8,128)(2,1)S(1)}, u32[]{:S(2)}, u32[]{:S(2)}) collective-permute-start(bf16[128,960]{0,1:T(8,128)(2,1)S(1)} %fusion.72), channel_id=1, source_target_pairs={{0,16},{1,17},{2,18},{3,19},{4,20},{5,21},{6,22},{7,23},{8,24},{9,... | collective-permute-start | bytes 737288 | tf_op jit(solution)/shard_map/ppermute | solution.py:263
  205.8 17.3 %slice-start = ((s8[15728640]{0:T(1024)(128)(4,1)}), s8[4194304]{0:T(1024)(128)(4,1)S(1)}, s32[]{:S(2)}) async-start(s8[15728640]{0:T(1024)(128)(4,1)} %bitcast.358), calls=%async_computation.2 | async-start | bytes 8388608
  211.3 5.5 %slice-start.4 = ((s8[5242880]{0:T(1024)(128)(4,1)}), s8[4194304]{0:T(1024)(128)(4,1)S(1)}, s32[]{:S(2)}) async-start(s8[5242880]{0:T(1024)(128)(4,1)} %bitcast.360), calls=%async_computation.6 | async-start | bytes 8388608
  211.4 23.6 %copy-start.18 = (f32[128]{0:T(128)}, f32[128]{0:T(128)S(1)}, u32[]{:S(2)}) copy-start(f32[128]{0:T(128)S(1)} %get-tuple-element.63) | copy-start | bytes 1540
  211.4 23.6 %copy-start.22 = (f32[128]{0:T(128)}, f32[128]{0:T(128)S(1)}, u32[]{:S(2)}) copy-start(f32[128]{0:T(128)S(1)} %get-tuple-element.62) | copy-start | bytes 1540
  212.3 10.8 %slice-start.1 = ((s8[15728640]{0:T(1024)(128)(4,1)}), s8[4194304]{0:T(1024)(128)(4,1)S(1)}, s32[]{:S(2)}) async-start(s8[15728640]{0:T(1024)(128)(4,1)} %bitcast.358), calls=%async_computation.3 | async-start | bytes 8388608
  215.6 7.6 %slice-start.2 = ((s8[15728640]{0:T(1024)(128)(4,1)}), s8[4194304]{0:T(1024)(128)(4,1)S(1)}, s32[]{:S(2)}) async-start(s8[15728640]{0:T(1024)(128)(4,1)} %bitcast.358), calls=%async_computation.4 | async-start | bytes 8388608
  216.8 6.4 %slice-start.3 = ((s8[15728640]{0:T(1024)(128)(4,1)}), s8[3145728]{0:T(1024)(128)(4,1)S(1)}, s32[]{:S(2)}) async-start(s8[15728640]{0:T(1024)(128)(4,1)} %bitcast.358), calls=%async_computation.5 | async-start | bytes 6291456
  217.7 51.0 %copy-start.16 = (f32[128]{0:T(128)}, f32[128]{0:T(128)S(1)}, u32[]{:S(2)}) copy-start(f32[128]{0:T(128)S(1)} %get-tuple-element.65) | copy-start | bytes 1540
  217.7 51.0 %copy-start.20 = (f32[128]{0:T(128)}, f32[128]{0:T(128)S(1)}, u32[]{:S(2)}) copy-start(f32[128]{0:T(128)S(1)} %get-tuple-element.64) | copy-start | bytes 1540
  234.9 5.5 %copy-start.29 = (s32[4]{0:T(128)S(1)}, s32[4]{0:T(128)}, u32[]{:S(2)}) copy-start(s32[4]{0:T(128)} %constant.170.clone) | copy-start | bytes 52
  235.0 7.5 %copy-start.28 = (s32[4]{0:T(128)S(1)}, s32[4]{0:T(128)}, u32[]{:S(2)}) copy-start(s32[4]{0:T(128)} %constant.169.clone) | copy-start | bytes 52
  235.0 9.4 %copy-start.27 = (s32[4]{0:T(128)S(1)}, s32[4]{0:T(128)}, u32[]{:S(2)}) copy-start(s32[4]{0:T(128)} %constant.171.clone) | copy-start | bytes 52
  235.3 16.6 %collective-permute-start.5 = (bf16[128,960]{0,1:T(8,128)(2,1)S(1)}, bf16[128,960]{0,1:T(8,128)(2,1)S(1)}, u32[]{:S(2)}, u32[]{:S(2)}) collective-permute-start(bf16[128,960]{0,1:T(8,128)(2,1)S(1)} %fusion.126), channel_id=1, source_target_pairs={{16,0},{17,1},{18,2},{19,3},{20,4},{21,5},{22,6},{23,7},{24,8},{25... | collective-permute-start | bytes 737288 | tf_op jit(solution)/shard_map/ppermute | solution.py:267
  249.8 57.0 %collective-permute-start.8 = (bf16[128,960]{0,1:T(8,128)(2,1)}, bf16[128,960]{0,1:T(8,128)(2,1)}, u32[]{:S(2)}, u32[]{:S(2)}) collective-permute-start(bf16[128,960]{0,1:T(8,128)(2,1)} %fusion.135), channel_id=1, source_target_pairs={{0,2},{1,3},{2,0},{3,1},{4,6},{5,7},{6,4},{7,5},{8,10},{9,11},{10,... | collective-permute-start | bytes 737288 | tf_op jit(solution)/shard_map/ppermute | solution.py:133
  250.4 51.7 %collective-permute-start.20 = (bf16[128,960]{0,1:T(8,128)(2,1)}, bf16[128,960]{0,1:T(8,128)(2,1)}, u32[]{:S(2)}, u32[]{:S(2)}) collective-permute-start(bf16[128,960]{0,1:T(8,128)(2,1)} %multiply_convert_fusion.12), channel_id=1, source_target_pairs={{0,2},{1,3},{2,0},{3,1},{4,6},{5,7},{6,4},{7,5},{8,10},{9,11},{10,... | collective-permute-start | bytes 737288 | tf_op jit(solution)/shard_map/ppermute | solution.py:133
  251.9 6.8 %copy-start.34 = (f32[128,2560]{1,0:T(8,128)S(1)}, f32[128,2560]{1,0:T(8,128)}, u32[]{:S(2)}) copy-start(f32[128,2560]{1,0:T(8,128)} %copy-done.33) | copy-start | bytes 3932164
  251.9 6.8 %copy-start.37 = (f32[128,2560]{1,0:T(8,128)S(1)}, f32[128,2560]{1,0:T(8,128)}, u32[]{:S(2)}) copy-start(f32[128,2560]{1,0:T(8,128)} %copy-done.36) | copy-start | bytes 3932164
  273.4 44.1 %collective-permute-start.10 = (bf16[128,960]{0,1:T(8,128)(2,1)}, bf16[128,960]{0,1:T(8,128)(2,1)S(1)}, u32[]{:S(2)}, u32[]{:S(2)}) collective-permute-start(bf16[128,960]{0,1:T(8,128)(2,1)} %fusion.196), channel_id=1, source_target_pairs={{0,2},{1,3},{2,0},{3,1},{4,6},{5,7},{6,4},{7,5},{8,10},{9,11},{10,... | collective-permute-start | bytes 737288 | tf_op jit(solution)/shard_map/ppermute | solution.py:133
  274.0 13.9 %collective-permute-start.24 = (bf16[128,960]{0,1:T(8,128)(2,1)S(1)}, bf16[128,960]{0,1:T(8,128)(2,1)}, u32[]{:S(2)}, u32[]{:S(2)}) collective-permute-start(bf16[128,960]{0,1:T(8,128)(2,1)S(1)} %broadcast_select_fusion), channel_id=1, source_target_pairs={{0,2},{1,3},{2,0},{3,1},{4,6},{5,7},{6,4},{7,5},{8,10},{9,11},{10,... | collective-permute-start | bytes 737288 | tf_op jit(solution)/shard_map/ppermute | solution.py:133
  278.5 23.4 %collective-permute-start.18 = (bf16[2,4,2,160,128]{4,3,2,1,0:T(8,128)(2,1)S(1)}, bf16[2,4,2,160,128]{4,3,2,1,0:T(8,128)(2,1)S(1)}, u32[]{:S(2)}, u32[]{:S(2)}) collective-permute-start(bf16[2,4,2,160,128]{4,3,2,1,0:T(8,128)(2,1)S(1)} %get-tuple-element.21), channel_id=1, source_target_pairs={{0,2},{1,3},{2,0},{3,1},{4,6},{5,7},{6,4},{7,5},{8,10},{9,11},{10,... | collective-permute-start | bytes 1966088 | tf_op jit(solution)/shard_map/ppermute | solution.py:133
  287.9 18.8 %collective-permute-start.22 = (bf16[1,4,2,160,128]{4,3,2,1,0:T(8,128)(2,1)S(1)}, bf16[1,4,2,160,128]{4,3,2,1,0:T(8,128)(2,1)S(1)}, u32[]{:S(2)}, u32[]{:S(2)}) collective-permute-start(bf16[1,4,2,160,128]{4,3,2,1,0:T(8,128)(2,1)S(1)} %get-tuple-element.27), channel_id=1, source_target_pairs={{0,2},{1,3},{2,0},{3,1},{4,6},{5,7},{6,4},{7,5},{8,10},{9,11},{10,... | collective-permute-start | bytes 983048 | tf_op jit(solution)/shard_map/ppermute | solution.py:133
  301.9 7.7 %collective-permute-start.25 = (bf16[256,960]{0,1:T(8,128)(2,1)S(1)}, bf16[256,960]{0,1:T(8,128)(2,1)S(1)}, u32[]{:S(2)}, u32[]{:S(2)}) collective-permute-start(bf16[256,960]{0,1:T(8,128)(2,1)S(1)} %pad_maximum_fusion.5), channel_id=1, source_target_pairs={{0,1},{1,0},{2,3},{3,2},{4,5},{5,4},{6,7},{7,6},{8,9},{9,8},{10,11... | collective-permute-start | bytes 1474568 | tf_op jit(solution)/shard_map/ppermute | solution.py:133
  302.1 9.6 %collective-permute-start.19 = (bf16[2,4,160,256]{3,2,1,0:T(8,128)(2,1)S(1)}, bf16[2,4,160,256]{3,2,1,0:T(8,128)(2,1)S(1)}, u32[]{:S(2)}, u32[]{:S(2)}) collective-permute-start(bf16[2,4,160,256]{3,2,1,0:T(8,128)(2,1)S(1)} %get-tuple-element.20), channel_id=1, source_target_pairs={{0,1},{1,0},{2,3},{3,2},{4,5},{5,4},{6,7},{7,6},{8,9},{9,8},{10,11... | collective-permute-start | bytes 1966088 | tf_op jit(solution)/shard_map/ppermute | solution.py:133
  306.8 4.9 %collective-permute-start.21 = (bf16[256,960]{0,1:T(8,128)(2,1)S(1)}, bf16[256,960]{0,1:T(8,128)(2,1)S(1)}, u32[]{:S(2)}, u32[]{:S(2)}) collective-permute-start(bf16[256,960]{0,1:T(8,128)(2,1)S(1)} %pad_maximum_fusion.4), channel_id=1, source_target_pairs={{0,1},{1,0},{2,3},{3,2},{4,5},{5,4},{6,7},{7,6},{8,9},{9,8},{10,11... | collective-permute-start | bytes 1474568 | tf_op jit(solution)/shard_map/ppermute | solution.py:133
  306.8 2.2 collective-permute-start.23
  309.1 9.8 %collective-permute-start.6 = (bf16[1,4,2,160,128]{4,3,1,2,0:T(8,128)(2,1)S(1)}, bf16[1,4,2,160,128]{4,3,1,2,0:T(8,128)(2,1)S(1)}, u32[]{:S(2)}, u32[]{:S(2)}) collective-permute-start(bf16[1,4,2,160,128]{4,3,1,2,0:T(8,128)(2,1)S(1)} %bitcast.351), channel_id=1, source_target_pairs={{0,2},{1,3},{2,0},{3,1},{4,6},{5,7},{6,4},{7,5},{8,10},{9,11},{10,... | collective-permute-start | bytes 983048 | tf_op jit(solution)/shard_map/ppermute | solution.py:133
  309.6 35.9 %collective-permute-start.9 = (bf16[256,960]{0,1:T(8,128)(2,1)S(1)}, bf16[256,960]{0,1:T(8,128)(2,1)S(1)}, u32[]{:S(2)}, u32[]{:S(2)}) collective-permute-start(bf16[256,960]{0,1:T(8,128)(2,1)S(1)} %pad_maximum_fusion.2), channel_id=1, source_target_pairs={{0,1},{1,0},{2,3},{3,2},{4,5},{5,4},{6,7},{7,6},{8,9},{9,8},{10,11... | collective-permute-start | bytes 1474568 | tf_op jit(solution)/shard_map/ppermute | solution.py:133
  315.1 100.7 %copy-start = (bf16[4,3,160,960]{3,2,1,0:T(8,128)(2,1)}, bf16[4,3,160,960]{3,2,1,0:T(8,128)(2,1)S(1)}, u32[]{:S(2)}) copy-start(bf16[4,3,160,960]{3,2,1,0:T(8,128)(2,1)S(1)} %copy.50) | copy-start | bytes 11059204
  315.2 26.0 %collective-permute-start.26 = (bf16[480,960]{1,0:T(8,128)(2,1)S(1)}, bf16[480,960]{1,0:T(8,128)(2,1)S(1)}, u32[]{:S(2)}, u32[]{:S(2)}) collective-permute-start(bf16[480,960]{1,0:T(8,128)(2,1)S(1)} %dynamic-slice_bitcast_fusion), channel_id=1, source_target_pairs={{0,4},{1,5},{2,6},{3,7},{16,20},{17,21},{18,22},{19,23}} | collective-permute-start | bytes 2764808 | tf_op jit(solution)/shard_map/ppermute | solution.py:187
  316.9 21.7 %collective-permute-start.32 = (f32[960]{0:T(1024)S(1)}, f32[960]{0:T(1024)S(1)}, u32[]{:S(2)}, u32[]{:S(2)}) collective-permute-start(f32[960]{0:T(1024)S(1)} %broadcast_select_fusion.2), channel_id=1, source_target_pairs={{0,8},{1,9},{2,10},{3,11},{4,12},{5,13},{6,14},{7,15},{8,0},{9,1},... | collective-permute-start | bytes 11528 | tf_op jit(solution)/shard_map/ppermute | solution.py:133
  318.5 20.1 %collective-permute-start.11 = (bf16[256,960]{0,1:T(8,128)(2,1)S(1)}, bf16[256,960]{0,1:T(8,128)(2,1)S(1)}, u32[]{:S(2)}, u32[]{:S(2)}) collective-permute-start(bf16[256,960]{0,1:T(8,128)(2,1)S(1)} %pad_maximum_fusion.3), channel_id=1, source_target_pairs={{0,1},{1,0},{2,3},{3,2},{4,5},{5,4},{6,7},{7,6},{8,9},{9,8},{10,11... | collective-permute-start | bytes 1474568 | tf_op jit(solution)/shard_map/ppermute | solution.py:133
  318.9 19.7 %collective-permute-start.7 = (bf16[1,4,160,256]{3,2,1,0:T(8,128)(2,1)S(1)}, bf16[1,4,160,256]{3,2,1,0:T(8,128)(2,1)S(1)}, u32[]{:S(2)}, u32[]{:S(2)}) collective-permute-start(bf16[1,4,160,256]{3,2,1,0:T(8,128)(2,1)S(1)} %get-tuple-element.30), channel_id=1, source_target_pairs={{0,1},{1,0},{2,3},{3,2},{4,5},{5,4},{6,7},{7,6},{8,9},{9,8},{10,11... | collective-permute-start | bytes 983048 | tf_op jit(solution)/shard_map/ppermute | solution.py:133
  338.6 13.4 %collective-permute-start.33 = (f32[480]{0:T(512)S(1)}, f32[480]{0:T(512)S(1)}, u32[]{:S(2)}, u32[]{:S(2)}) collective-permute-start(f32[480]{0:T(512)S(1)} %slice_select_fusion), channel_id=1, source_target_pairs={{0,4},{1,5},{2,6},{3,7},{4,0},{5,1},{6,2},{7,3},{8,12},{9,13},{10,... | collective-permute-start | bytes 5768 | tf_op jit(solution)/shard_map/ppermute | solution.py:133
  340.5 37.2 %collective-permute-start.29 = (bf16[480,960]{1,0:T(8,128)(2,1)S(1)}, bf16[480,960]{1,0:T(8,128)(2,1)S(1)}, u32[]{:S(2)}, u32[]{:S(2)}) collective-permute-start(bf16[480,960]{1,0:T(8,128)(2,1)S(1)} %dynamic-slice_bitcast_fusion), channel_id=1, source_target_pairs={{12,8},{13,9},{14,10},{15,11},{28,24},{29,25},{30,26},{31,27}} | collective-permute-start | bytes 2764808 | tf_op jit(solution)/shard_map/ppermute | solution.py:187
  341.6 36.1 %collective-permute-start.27 = (bf16[480,960]{1,0:T(8,128)(2,1)S(1)}, bf16[480,960]{1,0:T(8,128)(2,1)S(1)}, u32[]{:S(2)}, u32[]{:S(2)}) collective-permute-start(bf16[480,960]{1,0:T(8,128)(2,1)S(1)} %fusion.22), channel_id=1, source_target_pairs={{0,4},{1,5},{2,6},{3,7},{4,8},{5,9},{6,10},{7,11},{16,20},{17,21},... | collective-permute-start | bytes 2764808 | tf_op jit(solution)/shard_map/ppermute | solution.py:187
  347.6 25.5 %collective-permute-start.12 = (bf16[160,960]{1,0:T(8,128)(2,1)S(1)}, bf16[160,960]{1,0:T(8,128)(2,1)S(1)}, u32[]{:S(2)}, u32[]{:S(2)}) collective-permute-start(bf16[160,960]{1,0:T(8,128)(2,1)S(1)} %dynamic-slice_bitcast_fusion.3), channel_id=1, source_target_pairs={{0,4},{1,5},{2,6},{3,7},{16,20},{17,21},{18,22},{19,23}} | collective-permute-start | bytes 921608 | tf_op jit(solution)/shard_map/ppermute | solution.py:187
  352.1 32.0 %collective-permute-start.34 = (f32[240]{0:T(256)S(1)}, f32[240]{0:T(256)S(1)}, u32[]{:S(2)}, u32[]{:S(2)}) collective-permute-start(f32[240]{0:T(256)S(1)} %broadcast_select_fusion.9), channel_id=1, source_target_pairs={{0,2},{1,3},{2,0},{3,1},{4,6},{5,7},{6,4},{7,5},{8,10},{9,11},{10,... | collective-permute-start | bytes 2888 | tf_op jit(solution)/shard_map/ppermute | solution.py:133
  353.6 26.6 %collective-permute-start.15 = (bf16[160,960]{1,0:T(8,128)(2,1)S(1)}, bf16[160,960]{1,0:T(8,128)(2,1)S(1)}, u32[]{:S(2)}, u32[]{:S(2)}) collective-permute-start(bf16[160,960]{1,0:T(8,128)(2,1)S(1)} %dynamic-slice_bitcast_fusion.3), channel_id=1, source_target_pairs={{12,8},{13,9},{14,10},{15,11},{28,24},{29,25},{30,26},{31,27}} | collective-permute-start | bytes 921608 | tf_op jit(solution)/shard_map/ppermute | solution.py:187
  373.2 10.0 %collective-permute-start.13 = (bf16[160,960]{1,0:T(8,128)(2,1)S(1)}, bf16[160,960]{1,0:T(8,128)(2,1)S(1)}, u32[]{:S(2)}, u32[]{:S(2)}) collective-permute-start(bf16[160,960]{1,0:T(8,128)(2,1)S(1)} %fusion.114), channel_id=1, source_target_pairs={{0,4},{1,5},{2,6},{3,7},{4,8},{5,9},{6,10},{7,11},{16,20},{17,21},... | collective-permute-start | bytes 921608 | tf_op jit(solution)/shard_map/ppermute | solution.py:187
  379.5 36.3 %collective-permute-start.30 = (bf16[480,960]{1,0:T(8,128)(2,1)S(1)}, bf16[480,960]{1,0:T(8,128)(2,1)S(1)}, u32[]{:S(2)}, u32[]{:S(2)}) collective-permute-start(bf16[480,960]{1,0:T(8,128)(2,1)S(1)} %get-tuple-element.15), channel_id=1, source_target_pairs={{12,8},{13,9},{14,10},{15,11},{8,4},{9,5},{10,6},{11,7},{28,24},{2... | collective-permute-start | bytes 2764808 | tf_op jit(solution)/shard_map/ppermute | solution.py:187
  383.5 5.9 %collective-permute-start.16 = (bf16[160,960]{1,0:T(8,128)(2,1)S(1)}, bf16[160,960]{1,0:T(8,128)(2,1)S(1)}, u32[]{:S(2)}, u32[]{:S(2)}) collective-permute-start(bf16[160,960]{1,0:T(8,128)(2,1)S(1)} %get-tuple-element.24), channel_id=1, source_target_pairs={{12,8},{13,9},{14,10},{15,11},{8,4},{9,5},{10,6},{11,7},{28,24},{2... | collective-permute-start | bytes 921608 | tf_op jit(solution)/shard_map/ppermute | solution.py:187
  384.3 39.6 %collective-permute-start.35 = (f32[120]{0:T(128)S(1)}, f32[120]{0:T(128)S(1)}, u32[]{:S(2)}, u32[]{:S(2)}) collective-permute-start(f32[120]{0:T(128)S(1)} %broadcast_select_fusion.5), channel_id=1, source_target_pairs={{0,1},{1,0},{2,3},{3,2},{4,5},{5,4},{6,7},{7,6},{8,9},{9,8},{10,11... | collective-permute-start | bytes 1448 | tf_op jit(solution)/shard_map/ppermute | solution.py:133
  384.3 40.2 %collective-permute-start.14 = (bf16[160,960]{1,0:T(8,128)(2,1)S(1)}, bf16[160,960]{1,0:T(8,128)(2,1)S(1)}, u32[]{:S(2)}, u32[]{:S(2)}) collective-permute-start(bf16[160,960]{1,0:T(8,128)(2,1)S(1)} %get-tuple-element.23), channel_id=1, source_target_pairs={{0,4},{1,5},{2,6},{3,7},{4,8},{5,9},{6,10},{7,11},{8,12},{9,13},{1... | collective-permute-start | bytes 921608 | tf_op jit(solution)/shard_map/ppermute | solution.py:187
  389.3 29.2 %copy-start.38 = (f32[128,2560]{1,0:T(8,128)S(1)}, f32[128,2560]{1,0:T(8,128)}, u32[]{:S(2)}) copy-start(f32[128,2560]{1,0:T(8,128)} %copy-done.36) | copy-start | bytes 3932164
  389.5 35.1 %collective-permute-start.17 = (bf16[160,960]{1,0:T(8,128)(2,1)S(1)}, bf16[160,960]{1,0:T(8,128)(2,1)}, u32[]{:S(2)}, u32[]{:S(2)}) collective-permute-start(bf16[160,960]{1,0:T(8,128)(2,1)S(1)} %fusion.113), channel_id=1, source_target_pairs={{12,8},{13,9},{14,10},{15,11},{8,4},{9,5},{10,6},{11,7},{4,0},{5,1... | collective-permute-start | bytes 921608 | tf_op jit(solution)/shard_map/ppermute | solution.py:187
  390.9 27.6 %copy-start.7 = (f32[128,960]{0,1:T(8,128)S(1)}, f32[128,960]{0,1:T(8,128)}, u32[]{:S(2)}) copy-start(f32[128,960]{0,1:T(8,128)} %copy-done.6) | copy-start | bytes 1474564
  390.9 27.6 %copy-start.11 = (f32[960]{0:T(1024)S(1)}, f32[960]{0:T(1024)}, u32[]{:S(2)}) copy-start(f32[960]{0:T(1024)} %copy-done.10) | copy-start | bytes 11524
  390.9 27.6 %copy-start.17 = (f32[128]{0:T(128)S(1)}, f32[128]{0:T(128)}, u32[]{:S(2)}) copy-start(f32[128]{0:T(128)} %copy-done.16) | copy-start | bytes 1540
  390.9 27.6 %copy-start.21 = (f32[128]{0:T(128)S(1)}, f32[128]{0:T(128)}, u32[]{:S(2)}) copy-start(f32[128]{0:T(128)} %copy-done.20) | copy-start | bytes 1540
  390.9 27.6 %copy-start.23 = (f32[128]{0:T(128)S(1)}, f32[128]{0:T(128)}, u32[]{:S(2)}) copy-start(f32[128]{0:T(128)} %copy-done.22) | copy-start | bytes 1540
  390.9 27.6 %copy-start.25 = (f32[128]{0:T(128)S(1)}, f32[128]{0:T(128)}, u32[]{:S(2)}) copy-start(f32[128]{0:T(128)} %copy-done.24) | copy-start | bytes 1540
  391.0 27.6 %copy-start.35 = (f32[128,2560]{1,0:T(8,128)S(1)}, f32[128,2560]{1,0:T(8,128)}, u32[]{:S(2)}) copy-start(f32[128,2560]{1,0:T(8,128)} %copy-done.33) | copy-start | bytes 3932164
  391.0 43.0 %collective-permute-start.28 = (bf16[480,960]{1,0:T(8,128)(2,1)}, bf16[480,960]{1,0:T(8,128)(2,1)}, u32[]{:S(2)}, u32[]{:S(2)}) collective-permute-start(bf16[480,960]{1,0:T(8,128)(2,1)} %get-tuple-element.14), channel_id=1, source_target_pairs={{0,4},{1,5},{2,6},{3,7},{4,8},{5,9},{6,10},{7,11},{8,12},{9,13},{1... | collective-permute-start | bytes 2764808 | tf_op jit(solution)/shard_map/ppermute | solution.py:187
  417.2 23.2 %collective-permute-start.31 = (bf16[480,960]{1,0:T(8,128)(2,1)}, bf16[480,960]{1,0:T(8,128)(2,1)}, u32[]{:S(2)}, u32[]{:S(2)}) collective-permute-start(bf16[480,960]{1,0:T(8,128)(2,1)} %fusion.21), channel_id=1, source_target_pairs={{12,8},{13,9},{14,10},{15,11},{8,4},{9,5},{10,6},{11,7},{4,0},{5,1... | collective-permute-start | bytes 2764808 | tf_op jit(solution)/shard_map/ppermute | solution.py:187
  (19 other events, 48.5 us)
Sparse Core Ops, SparseCore 0:
  10.3 58.6 all-gather.2
  71.3 118.8 all-gather.4

commit v2 on v1

--- a/solution.py
+++ b/solution.py
@@ -13,6 +13,7 @@
 
 epsilon = 1e-05
 theta_base = 100000.0
+Z2_BIT, Z1_BIT, Y_BIT, CORE_BIT = 8, 4, 2, 1
 bf16 = jnp.bfloat16
 f32 = jnp.float32
 
@@ -168,77 +169,88 @@
     return both[0], jnp.stack(both[1:])
 
 
-def plane_rows(x, y_bit, core_bit):
-    x = jnp.concatenate([x, flip(x, y_bit)], axis=0)
-    return jnp.concatenate([x, flip(x, core_bit)], axis=0)
-
-
-def plane_cols(cols, y, core, y_bit, core_bit):
-    keep = lax.dynamic_index_in_dim(cols, y, 2, keepdims=False)
-    send = lax.dynamic_index_in_dim(cols, 1 - y, 2, keepdims=False)
-    cols = jnp.concatenate([keep, flip(send, y_bit)], axis=-1)
-    keep = lax.dynamic_index_in_dim(cols, core, 2, keepdims=False)
-    send = lax.dynamic_index_in_dim(cols, 1 - core, 2, keepdims=False)
-    return jnp.concatenate([keep, flip(send, core_bit)], axis=-1)
-
-
-def line_sum(parts, z):
-    def shift(x, pairs):
-        return lax.ppermute(x, "dp", [(4 * a + i, 4 * b + i) for a, b in pairs for i in range(4)])
-
-    def pick(indices):
-        return lax.dynamic_index_in_dim(parts, jnp.array(indices, jnp.int32)[z], 0, keepdims=False)
-
-    def plus(x, recv):
-        return (x.astype(f32) + recv.astype(f32)).astype(bf16)
-
-    first = pick([3, 3, 0, 0])
-    right = shift(first, [(0, 1)])
-    left = shift(first, [(3, 2)])
-    send_right = plus(pick([2, 3, 3, 3]), right)
-    send_left = plus(pick([0, 0, 0, 1]), left)
-    right = shift(send_right, [(0, 1), (1, 2)])
-    left = shift(send_left, [(3, 2), (2, 1)])
-    send_right = plus(pick([1, 2, 3, 3]), right)
-    send_left = plus(pick([0, 0, 1, 2]), left)
-    right = shift(send_right, [(0, 1), (1, 2), (2, 3)])
-    left = shift(send_left, [(3, 2), (2, 1), (1, 0)])
-    own = lax.dynamic_index_in_dim(parts, z, 0, keepdims=False)
-    return own.astype(f32) + right.astype(f32) + left.astype(f32)
-
-
-def grads_planes(pieces):
+def plane_rows(x):
+    x = jnp.concatenate([x, flip(x, Y_BIT)], axis=0)
+    return jnp.concatenate([x, flip(x, CORE_BIT)], axis=0)
+
+
+def doubled(block, bits):
+    block = block[None]
+    for bit in bits:
+        block = jnp.concatenate([block, flip(block, bit)], axis=0)
+    return block
+
+
+def doubled_in_order(block, bits, me):
+    rows, width = block.shape
+    have = []
+    for bit in bits:
+        other = flip(block, bit)
+        high = (me & bit) != 0
+        have = sorted(have + [bit], reverse=True)
+        block = jnp.stack(
+            [jnp.where(high, other, block), jnp.where(high, block, other)], axis=have.index(bit)
+        )
+    return block.reshape(-1, width)
+
+
+def ffn_cols(*arrays):
+    tokens, cols = arrays[0].shape
+    share = cols // 16
+    x = jnp.stack([a.T.reshape(2, 2, 2, 2, share, tokens) for a in arrays])
+    x = jnp.concatenate([x[:, :, 0], flip(x[:, :, 1], Y_BIT)], axis=-1)
+    return jnp.concatenate([x[:, 0], flip(x[:, 1], CORE_BIT)], axis=-1)
+
+
+def attn_cols(array, y, core):
+    tokens, cols = array.shape
+    share = cols // 16
+    x = array.T.reshape(2, 2, 2, 2, share, tokens)
+    pick = lambda v, i: lax.dynamic_index_in_dim(v, i, 2, keepdims=False)
+    x = jnp.concatenate([pick(x, y), flip(pick(x, 1 - y), Y_BIT)], axis=-1)
+    return jnp.concatenate([pick(x, core), flip(pick(x, 1 - core), CORE_BIT)], axis=-1)
+
+
+def halved(keep, send, bit):
+    return keep.astype(f32) + flip(send.astype(bf16), bit).astype(f32)
+
+
+def ffn_sum(parts):
+    x = halved(parts[0], parts[1], Z1_BIT)
+    return halved(x[0], x[1], Z2_BIT)
+
+
+def attn_sum(parts, z2, z1):
+    pick = lambda v, i, axis: lax.dynamic_index_in_dim(v, i, axis, keepdims=False)
+    x = halved(pick(parts, z1, 1), pick(parts, 1 - z1, 1), Z1_BIT)
+    return halved(pick(x, z2, 0), pick(x, 1 - z2, 0), Z2_BIT)
+
+
+def grads_planes(pieces, me):
     n, dproj, o, dz, m, dgate, dup, eb, act = pieces
-    me = lax.axis_index("dp")
-    z, y, core = me // 4, (me // 2) % 2, me % 2
-    y_bit, core_bit = 2, 1
+    z2, z1, y, core = (me >> 3) & 1, (me >> 2) & 1, (me >> 1) & 1, me & 1
     tokens = n.shape[0]
     share = act.shape[1] // 16
-    m_all = plane_rows(m, y_bit, core_bit)
-    eb_all = plane_rows(eb, y_bit, core_bit)
-    n_all = plane_rows(n, y_bit, core_bit)
-
-    def cols(*arrays):
-        stacked = jnp.stack([a.T.reshape(4, 2, 2, share, tokens) for a in arrays])
-        return plane_cols(stacked, y, core, y_bit, core_bit)
-
-    act_c = cols(act)
-    gu_c = cols(dgate, dup)
-    dz_all = plane_rows(dz, y_bit, core_bit)
-    attn_c = cols(jnp.concatenate([dproj, o], axis=1))
     wide = 4 * tokens
-    down = dot_nn(act_c.reshape(4 * share, wide), eb_all)
-    gate_up = dot_nn(gu_c.reshape(8 * share, wide), m_all).reshape(2, 4, share, -1)
-    ffn = jnp.concatenate([gate_up, down.reshape(1, 4, share, -1)], axis=0).astype(bf16)
-    ffn = ffn.transpose(1, 0, 2, 3).reshape(4, 3 * share, -1)
-    ffn_total = line_sum(ffn, z)
-    owners = jnp.arange(4, dtype=jnp.int32) * 4 + y * 2 + core
+    m_all = plane_rows(m)
+    n_all = plane_rows(n)
+    act_c = ffn_cols(act)[0]
+    o_c = attn_cols(jnp.concatenate([dproj, o], axis=1), y, core)
+    eb_all = plane_rows(eb)
+
+    def product(cols, rows):
+        return dot_nn(cols.reshape(4 * share, wide), rows).reshape(2, 2, share, -1)
+
+    down = ffn_sum(product(act_c, eb_all))
+    gu_c = ffn_cols(dgate, dup)
+    gate = ffn_sum(product(gu_c[0], m_all))
+    up = ffn_sum(product(gu_c[1], m_all))
+    dz_all = plane_rows(dz)
+    owners = (jnp.arange(4, dtype=jnp.int32) * 4 + y * 2 + core).reshape(2, 2, 1, 1)
     is_qkv = owners * share < QKV_COLS
-    from_n = dot_nn(attn_c.reshape(4 * share, wide), n_all).reshape(4, share, -1)
-    from_dz = dot_nn(attn_c.reshape(4 * share, wide), dz_all).reshape(4, share, -1)
-    attn = jnp.where(is_qkv[:, None, None], from_n, from_dz).astype(bf16)
-    attn_total = line_sum(attn, z)
-    return attn_total, ffn_total.reshape(3, share, -1)
+    attn = jnp.where(is_qkv, product(o_c, n_all), product(o_c, dz_all))
+    attn = attn_sum(attn, z2, z1)
+    return attn, jnp.stack([gate, up, down])
 
 
 def local(edge_data, segment_ids, attn_weight, ffn_weight, gains):
@@ -247,8 +259,18 @@
     tables = block_tables(segment_ids)
     block, width = edge_data.shape[2], edge_data.shape[3]
     x = edge_data[0].reshape(micro * block, width)
-    attn_t = lax.all_gather(attn_weight[0].T, "dp", axis=0, tiled=True)
-    ffn_t = lax.all_gather(ffn_weight[0].swapaxes(1, 2), "dp", axis=1, tiled=True)
+    planes = lax.axis_size("dp") == 16
+    me = lax.axis_index("dp")
+    attn_own = attn_weight[0].T
+    ffn_own = ffn_weight[0].swapaxes(1, 2)
+    if planes:
+        attn_t = doubled_in_order(attn_own, (Z2_BIT, Y_BIT, Z1_BIT, CORE_BIT), me)
+        ffn_t = [
+            doubled(ffn_own[i], (Z2_BIT, Z1_BIT, Y_BIT, CORE_BIT)).reshape(-1, width) for i in range(3)
+        ]
+    else:
+        attn_t = lax.all_gather(attn_own, "dp", axis=0, tiled=True)
+        ffn_t = lax.all_gather(ffn_own, "dp", axis=1, tiled=True)
     gain_row = gather_small(gains[0]).astype(f32)
     weights = (
         attn_t[:QKV_COLS],
@@ -267,8 +289,8 @@
     received = lax.ppermute(first_grad.astype(bf16), "section", [(1, 0)])
     e = jnp.where(leading, received, x)
     du, pieces, gain_grad = backward(e, state, weights, tables)
-    if lax.axis_size("dp") == 16:
-        attn_rows, ffn_rows = grads_planes(pieces)
+    if planes:
+        attn_rows, ffn_rows = grads_planes(pieces, me)
     else:
         attn_rows, ffn_rows = grads_generic(pieces)
     gain_shard = scatter_small(gain_grad)

time: 458 us -> 458 us (level)
  local copies, waits for them, and re-layouts: 7.63 us -> 48.2 us
  between operations: 25.2 us -> 2.47 us
  starting transfers between devices: 73 us -> 56.5 us
  other arithmetic: 22.7 us -> 39.1 us
  waiting for transfers between devices: 243 us -> 230 us
    ppermute x22 -> x46, waiting for transfers between devices: 44.4 us -> 223 us  [flip(): return lax.ppermute(x, 'dp', [(i, i ^ bit) for i in range(size)])]
    all_gather x2 -> x0, waiting for transfers between devices: 160 us -> none  [the longest x1 115 us: local(): lax.all_gather(ffn_weight[0].swapaxes(1, 2), 'dp', axis=1, tiled=True)]
    ppermute x12 -> x0, starting transfers between devices: 49.7 us -> none  [shift(): lax.ppermute(x, 'dp', [(4 * a + i, 4 * b + i) for a, b in pairs for i in...]
    ppermute x12 -> x0, waiting for transfers between devices: 35.7 us -> none  [shift(): lax.ppermute(x, 'dp', [(4 * a + i, 4 * b + i) for a, b in pairs for i in...]
    ppermute x22 -> x46, starting transfers between devices: 18.4 us -> 51.4 us  [flip(): return lax.ppermute(x, 'dp', [(i, i ^ bit) for i in range(size)])]
    slice x0 -> x13, local copies, waits for them, and re-layouts: none -> 22.8 us  [the longest x12 20.5 us: ffn_sum(): x = halved(parts[0], parts[1], Z1_BIT)]
    concatenate x0 -> x3, local copies, waits for them, and re-layouts: none -> 8.03 us  [doubled(): block = jnp.concatenate([block, flip(block, bit)], axis=0)]
    concatenate x8 -> x17, other arithmetic: 4.6 us -> 12.2 us  [the longest x9 5.7 us: doubled(): block = jnp.concatenate([block, flip(block, bit)], axis=0)]
  transfers between devices with their start and end apart: 38 -> 48, of which waited for: 16 -> 18; matrix products, arithmetic and copies ran while one was open for 16% -> 28% of each run, Pallas kernels for 0% -> 0%
where the time goes in v2:
time: 458 us; the launch traced here: 453 us
  waiting for transfers between devices  230 us (50%)
  matrix products  76.8 us (17%)
  starting transfers between devices  56.5 us (12%)
  local copies, waits for them, and re-layouts  48.2 us (11%)
  other arithmetic  39.1 us (9%)
    ppermute x46, waiting for transfers between devices, flip(): return lax.ppermute(x, 'dp', [(i, i ^ bit) for i in range(size)])  223 us
    ppermute x46, starting transfers between devices, flip(): return lax.ppermute(x, 'dp', [(i, i ^ bit) for i in range(size)])  51.4 us
    dot_general x15, matrix products, dot_nn(): lax.dot_general(a, b, (((1,), (0,)), ((), ())), preferred_element_type=f32)  46.5 us
    dot_general x9, matrix products, dot_nt(): lax.dot_general(a, b, (((1,), (1,)), ((), ())), preferred_element_type=f32)  26.3 us
    slice x12, local copies, waits for them, and re-layouts, ffn_sum(): x = halved(parts[0], parts[1], Z1_BIT)  20.5 us
  transfers between devices with their start and end apart: 48, of which 18 were waited for; matrix products, arithmetic and copies ran while one was open for 28% of the time, Pallas kernels for 0%

profile of v2, /device:TPU:0, one launch (start us, length us, event | category | flops | bytes accessed | tf_op | source)
XLA Modules:
  0.0 452.8 jit_solution(1169035461012674542)
XLA Ops:
  0.6 4.1 collective-permute-start.4
  4.7 2.3 fusion.170
  7.2 2.8 collective-permute-start.12
  12.0 29.5 %collective-permute-done.4 = bf16[160,960]{1,0:T(8,128)(2,1)S(1)} collective-permute-done((bf16[160,960]{1,0:T(8,128)(2,1)}, bf16[160,960]{1,0:T(8,128)(2,1)S(1)}, u32[]{:S(2)}, u32[]{:S(2)}) %collective-permute-start.4) | collective-permute-done | bytes 307232 | tf_op jit(solution)/shard_map/ppermute | solution.py:134
  42.5 1.9 collective-permute-start.5
  45.3 12.3 %collective-permute-done.1 = bf16[240]{0:T(256)(128)(2,1)S(1)} collective-permute-done((bf16[240]{0:T(256)(128)(2,1)S(1)}, bf16[240]{0:T(256)(128)(2,1)S(1)}, u32[]{:S(2)}, u32[]{:S(2)}) %collective-permute-start.1) | collective-permute-done | bytes 512 | tf_op jit(solution)/shard_map/ppermute | solution.py:134
  63.2 2.8 collective-permute-start.3
  69.4 20.1 %collective-permute-done.3 = bf16[960]{0:T(1024)(128)(2,1)} collective-permute-done((bf16[960]{0:T(1024)(128)(2,1)}, bf16[960]{0:T(1024)(128)(2,1)}, u32[]{:S(2)}, u32[]{:S(2)}) %collective-permute-start.3) | collective-permute-done | bytes 1952 | tf_op jit(solution)/shard_map/ppermute | solution.py:134
  90.5 6.2 %collective-permute-start.17 = (bf16[2,160,960]{2,1,0:T(8,128)(2,1)S(1)}, bf16[2,160,960]{2,1,0:T(8,128)(2,1)S(1)}, u32[]{:S(2)}, u32[]{:S(2)}) collective-permute-start(bf16[2,160,960]{2,1,0:T(8,128)(2,1)S(1)} %pad_maximum_fusion.16), channel_id=1, source_target_pairs={{0,4},{1,5},{2,6},{3,7},{4,0},{5,1},{6,2},{7,3},{8,12},{9,13},{10,... | collective-permute-start | bytes 1843208 | tf_op jit(solution)/shard_map/ppermute | solution.py:134
  96.9 2.1 collective-permute-start.9
  99.0 1.7 select_bitcast_fusion.3
  101.0 11.3 %collective-permute-done.17 = bf16[2,160,960]{2,1,0:T(8,128)(2,1)S(1)} collective-permute-done((bf16[2,160,960]{2,1,0:T(8,128)(2,1)S(1)}, bf16[2,160,960]{2,1,0:T(8,128)(2,1)S(1)}, u32[]{:S(2)}, u32[]{:S(2)}) %collective-permute-start.17) | collective-permute-done | bytes 614432 | tf_op jit(solution)/shard_map/ppermute | solution.py:134
  112.5 1.6 collective-permute-start.18
  114.1 12.3 %collective-permute-done.13 = bf16[2,160,960]{2,1,0:T(8,128)(2,1)S(1)} collective-permute-done((bf16[2,160,960]{2,1,0:T(8,128)(2,1)S(1)}, bf16[2,160,960]{2,1,0:T(8,128)(2,1)S(1)}, u32[]{:S(2)}, u32[]{:S(2)}) %collective-permute-start.13) | collective-permute-done | bytes 614432 | tf_op jit(solution)/shard_map/ppermute | solution.py:134
  128.1 8.5 %collective-permute-done.9 = bf16[2,160,960]{2,1,0:T(8,128)(2,1)S(1)} collective-permute-done((bf16[2,160,960]{2,1,0:T(8,128)(2,1)S(1)}, bf16[2,160,960]{2,1,0:T(8,128)(2,1)S(1)}, u32[]{:S(2)}, u32[]{:S(2)}) %collective-permute-start.9) | collective-permute-done | bytes 614432 | tf_op jit(solution)/shard_map/ppermute | solution.py:134
  140.9 3.4 collective-permute-done.18
  144.3 1.8 pad_maximum_fusion.4
  146.0 26.3 %collective-permute-done.14 = bf16[4,160,960]{2,1,0:T(8,128)(2,1)S(1)} collective-permute-done((bf16[4,160,960]{2,1,0:T(8,128)(2,1)S(1)}, bf16[4,160,960]{2,1,0:T(8,128)(2,1)S(1)}, u32[]{:S(2)}, u32[]{:S(2)}) %collective-permute-start.14) | collective-permute-done | bytes 1228832 | tf_op jit(solution)/shard_map/ppermute | solution.py:134
  172.3 1.6 pad_maximum_fusion.3
  174.0 17.9 %collective-permute-done.10 = bf16[4,160,960]{2,1,0:T(8,128)(2,1)S(1)} collective-permute-done((bf16[4,160,960]{2,1,0:T(8,128)(2,1)S(1)}, bf16[4,160,960]{2,1,0:T(8,128)(2,1)S(1)}, u32[]{:S(2)}, u32[]{:S(2)}) %collective-permute-start.10) | collective-permute-done | bytes 1228832 | tf_op jit(solution)/shard_map/ppermute | solution.py:134
  191.9 1.7 pad_maximum_fusion.2
  199.1 2.1 constant_dynamic-update-slice_fusion.10
  201.3 4.0 constant_dynamic-update-slice_fusion.5
  206.6 2.1 fusion.167
  208.7 1.9 constant_dynamic-update-slice_fusion
  210.6 7.5 %fusion.42 = bf16[128,960]{0,1:T(8,128)(2,1)S(1)} fusion(f32[128,960]{0,1:T(8,128)S(1)} %get-tuple-element.81, bf16[2560,960]{1,0:T(8,128)(2,1)} %bitcast.321, f32[128,2560]{1,0:T(8,128)S(1)} %fusion.167, bf16[2560,960]{1,0:T(8,128)(2,1)} %bitcast.26, f32[960]{0:T(1024)S(1)} %copy-done.34, f32[128]{0:T(128)S(1)} %add_rsqrt_fusion.3), kind=kOutput, calls=%fused_computation.96 | convolution fusion | flops 1260871680 | bytes 11882752 | tf_op jit(solution)/shard_map/dot_general | solution.py:22
  218.1 3.8 collective-permute-start.20
  221.9 4.3 convolution_bitcast_fusion
  228.4 3.3 fusion.6
  234.7 4.3 fusion.175
  239.1 1.9 fusion.174
  241.0 2.2 fusion.70
  243.3 4.8 %multiply_reduce_fusion.5 = (f32[128]{0:T(128)S(1)}, f32[128,960]{0,1:T(8,128)S(1)}) fusion(f32[128,960]{0,1:T(8,128)S(1)} %get-tuple-element.85, f32[960]{0:T(1024)S(1)} %copy-done.35, f32[128,960]{0,1:T(8,128)S(1)} %fusion.70, bf16[2560,960]{1,0:T(8,128)(2,1)} %bitcast.26, f32[128,2560]{1,0:T(8,128)S(1)} %convolution_bitcast_fusion, ...), kind=kOutput, calls=%fused_computation.214 | convolution fusion | flops 632913792 | bytes 10326272 | tf_op jit(solution)/shard_map/dot_general | solution.py:22
  257.2 5.9 %collective-permute-done.21 = bf16[128,960]{0,1:T(8,128)(2,1)S(1)} collective-permute-done((bf16[128,960]{0,1:T(8,128)(2,1)}, bf16[128,960]{0,1:T(8,128)(2,1)S(1)}, u32[]{:S(2)}, u32[]{:S(2)}) %collective-permute-start.21) | collective-permute-done | bytes 245792 | tf_op jit(solution)/shard_map/ppermute | solution.py:289
  263.8 6.8 %fusion.17 = (bf16[2560,128]{0,1:T(8,128)(2,1)}, bf16[2560,128]{0,1:T(8,128)(2,1)}, bf16[2560,128]{0,1:T(8,128)(2,1)}, f32[128,2560]{1,0:T(8,128)S(1)}) fusion(f32[128,2560]{1,0:T(8,128)} %copy-done.11, f32[128,2560]{1,0:T(8,128)} %copy-done.13, bf16[128,960]{0,1:T(8,128)(2,1)} %broadcast_select_fusion, bf16[2560,960]{1,0:T(8,128)(2,1)} %bitcast.323), kind=kOutput, calls=%fused_computation.48 | convolution fusion | flops 634388480 | bytes 11059200 | tf_op jit(solution)/shard_map/dot_general | solution.py:26
  270.7 4.8 %fusion.71 = f32[128,960]{0,1:T(8,128)S(1)} fusion(bf16[2560,960]{1,0:T(8,128)(2,1)} %bitcast.314, f32[128,2560]{1,0:T(8,128)S(1)} %get-tuple-element.96, f32[128,2560]{1,0:T(8,128)S(1)} %copy-done.12), kind=kOutput, calls=%fused_computation.144 | convolution fusion | flops 631111680 | bytes 8028160 | tf_op jit(solution)/shard_map/dot_general | solution.py:22
  275.6 5.4 %multiply_reduce_fusion.3 = (f32[960]{0:T(1024)}, f32[128]{0:T(128)S(1)}, f32[128,960]{0,1:T(8,128)S(1)}) fusion(f32[128,960]{0,1:T(8,128)S(1)} %get-tuple-element.85, f32[128]{0:T(128)S(1)} %get-tuple-element.77, f32[960]{0:T(1024)S(1)} %copy-done.36, f32[128,960]{0,1:T(8,128)S(1)} %fusion.71, bf16[2560,960]{1,0:T(8,128)(2,1)} %bitcast.26, ...), kind=kOutput, calls=%fused_computation.211 | convolution fusion | flops 633281472 | bytes 10330624 | tf_op jit(solution)/shard_map/dot_general | solution.py:22
  281.0 2.0 fusion.169
  283.1 1.6 fusion.43
  288.7 2.2 fusion.111
  297.4 6.4 %fusion.102 = bf16[128,960]{0,1:T(8,128)(2,1)} fusion(bf16[128,960]{0,1:T(8,128)(2,1)S(1)} %copy-done.10, f32[128,960]{0,1:T(8,128)} %get-tuple-element.95, f32[128]{0:T(128)S(1)} %broadcast_multiply_fusion, f32[128]{0:T(128)S(1)} %copy-done.56, f32[128]{0:T(128)S(1)} %copy-done.52, f32[960]{0:T(1024)S(1)} %copy-done.40, pred[]{:T(512)S(6)} %eq.27, ...), kind=kOutput, calls=%fused_computation.197 | convolution fusion | flops 633200640 | bytes 9759233 | tf_op jit(solution)/shard_map/dot_general | solution.py:22
  304.9 1.8 pad_maximum_fusion.21
  312.5 10.1 %collective-permute-done.46 = f32[240]{0:T(256)S(1)} collective-permute-done((f32[240]{0:T(256)S(1)}, f32[240]{0:T(256)S(1)}, u32[]{:S(2)}, u32[]{:S(2)}) %collective-permute-start.46) | collective-permute-done | bytes 992 | tf_op jit(solution)/shard_map/ppermute | solution.py:134
  328.7 7.9 %collective-permute-done.30 = bf16[2,2,2,2,160,128]{5,4,3,2,1,0:T(8,128)(2,1)S(1)} collective-permute-done((bf16[2,2,2,2,160,128]{5,4,3,2,1,0:T(8,128)(2,1)S(1)}, bf16[2,2,2,2,160,128]{5,4,3,2,1,0:T(8,128)(2,1)S(1)}, u32[]{:S(2)}, u32[]{:S(2)}) %collective-permute-start.30) | collective-permute-done | bytes 655392 | tf_op jit(solution)/shard_map/ppermute | solution.py:134
  338.2 2.0 fusion.64
  342.6 1.9 fusion.59
  344.5 1.9 convolution_select_fusion
  347.4 1.7 collective-permute-start.28
  349.1 2.9 copy.59
  352.0 2.2 copy.60
  355.7 2.1 fusion.123
  357.8 2.1 fusion.124
  363.7 2.9 copy.55
  366.6 2.3 copy.56
  368.9 1.7 collective-permute-start.36
  370.6 2.9 copy.53
  374.9 4.4 collective-permute-done.42
  379.3 1.6 convert_add_fusion
  381.0 2.6 collective-permute-start.43
  385.4 28.1 %collective-permute-done.43 = bf16[160,960]{1,0:T(8,128)(2,1)S(1)} collective-permute-done((bf16[160,960]{1,0:T(8,128)(2,1)S(1)}, bf16[160,960]{1,0:T(8,128)(2,1)S(1)}, u32[]{:S(2)}, u32[]{:S(2)}) %collective-permute-start.43) | collective-permute-done | bytes 307232 | tf_op jit(solution)/shard_map/ppermute | solution.py:134
  415.1 3.4 collective-permute-start.37
  418.6 2.4 collective-permute-done.34
  423.0 21.0 %collective-permute-done.37 = bf16[160,960]{1,0:T(8,128)(2,1)S(1)} collective-permute-done((bf16[160,960]{1,0:T(8,128)(2,1)S(1)}, bf16[160,960]{1,0:T(8,128)(2,1)S(1)}, u32[]{:S(2)}, u32[]{:S(2)}) %collective-permute-start.37) | collective-permute-done | bytes 307232 | tf_op jit(solution)/shard_map/ppermute | solution.py:134
  444.1 6.8 %collective-permute-done.35 = bf16[160,960]{1,0:T(8,128)(2,1)S(1)} collective-permute-done((bf16[160,960]{1,0:T(8,128)(2,1)S(1)}, bf16[160,960]{1,0:T(8,128)(2,1)S(1)}, u32[]{:S(2)}, u32[]{:S(2)}) %collective-permute-start.35) | collective-permute-done | bytes 307232 | tf_op jit(solution)/shard_map/ppermute | solution.py:134
  (361 shorter events, 83.6 us)
Async XLA Ops:
  0.6 40.9 %collective-permute-start.4 = (bf16[160,960]{1,0:T(8,128)(2,1)}, bf16[160,960]{1,0:T(8,128)(2,1)S(1)}, u32[]{:S(2)}, u32[]{:S(2)}) collective-permute-start(bf16[160,960]{1,0:T(8,128)(2,1)} %bitcast.375), channel_id=1, source_target_pairs={{0,8},{1,9},{2,10},{3,11},{4,12},{5,13},{6,14},{7,15},{8,0},{9,1},... | collective-permute-start | bytes 921608 | tf_op jit(solution)/shard_map/ppermute | solution.py:134
  4.7 39.6 %collective-permute-start = (bf16[120]{0:T(256)(128)(2,1)}, bf16[120]{0:T(256)(128)(2,1)S(1)}, u32[]{:S(2)}, u32[]{:S(2)}) collective-permute-start(bf16[120]{0:T(256)(128)(2,1)} %bitcast.381), channel_id=1, source_target_pairs={{0,1},{1,0},{2,3},{3,2},{4,5},{5,4},{6,7},{7,6},{8,9},{9,8},{10,11... | collective-permute-start | bytes 728 | tf_op jit(solution)/shard_map/ppermute | solution.py:134
  4.7 36.8 %copy-start.32 = (bf16[1,960,160]{1,2,0:T(8,128)(2,1)S(1)}, bf16[1,960,160]{1,2,0:T(8,128)(2,1)}, u32[]{:S(2)}) copy-start(bf16[1,960,160]{1,2,0:T(8,128)(2,1)} %param.7) | copy-start | bytes 921604
  7.1 37.3 %copy-start.59 = (bf16[1,120]{1,0:T(2,128)(2,1)S(1)}, bf16[1,120]{1,0:T(2,128)(2,1)}, u32[]{:S(2)}) copy-start(bf16[1,120]{1,0:T(2,128)(2,1)} %param.9) | copy-start | bytes 724
  7.1 37.6 %copy-start.7 = (bf16[1,2,64,960]{3,2,1,0:T(8,128)(2,1)S(1)}, bf16[1,2,64,960]{3,2,1,0:T(8,128)(2,1)}, u32[]{:S(2)}) copy-start(bf16[1,2,64,960]{3,2,1,0:T(8,128)(2,1)} %param.5) | copy-start | bytes 737284
  7.1 83.4 %collective-permute-start.16 = (bf16[1,160,960]{2,1,0:T(8,128)(2,1)S(1)}, bf16[1,160,960]{2,1,0:T(8,128)(2,1)S(1)}, u32[]{:S(2)}, u32[]{:S(2)}) collective-permute-start(bf16[1,160,960]{2,1,0:T(8,128)(2,1)S(1)} %get-tuple-element.33), channel_id=1, source_target_pairs={{0,8},{1,9},{2,10},{3,11},{4,12},{5,13},{6,14},{7,15},{8,0},{9,1},... | collective-permute-start | bytes 921608 | tf_op jit(solution)/shard_map/ppermute | solution.py:134
  7.2 89.5 %collective-permute-start.12 = (bf16[1,160,960]{2,1,0:T(8,128)(2,1)S(1)}, bf16[1,160,960]{2,1,0:T(8,128)(2,1)S(1)}, u32[]{:S(2)}, u32[]{:S(2)}) collective-permute-start(bf16[1,160,960]{2,1,0:T(8,128)(2,1)S(1)} %get-tuple-element.34), channel_id=1, source_target_pairs={{0,8},{1,9},{2,10},{3,11},{4,12},{5,13},{6,14},{7,15},{8,0},{9,1},... | collective-permute-start | bytes 921608 | tf_op jit(solution)/shard_map/ppermute | solution.py:134
  10.0 86.9 %collective-permute-start.8 = (bf16[1,160,960]{2,1,0:T(8,128)(2,1)S(1)}, bf16[1,160,960]{2,1,0:T(8,128)(2,1)S(1)}, u32[]{:S(2)}, u32[]{:S(2)}) collective-permute-start(bf16[1,160,960]{2,1,0:T(8,128)(2,1)S(1)} %get-tuple-element.29), channel_id=1, source_target_pairs={{0,8},{1,9},{2,10},{3,11},{4,12},{5,13},{6,14},{7,15},{8,0},{9,1},... | collective-permute-start | bytes 921608 | tf_op jit(solution)/shard_map/ppermute | solution.py:134
  42.5 17.0 %collective-permute-start.5 = (bf16[2,160,960]{2,1,0:T(8,128)(2,1)S(1)}, bf16[2,160,960]{2,1,0:T(8,128)(2,1)}, u32[]{:S(2)}, u32[]{:S(2)}) collective-permute-start(bf16[2,160,960]{2,1,0:T(8,128)(2,1)S(1)} %pad_maximum_fusion.13), channel_id=1, source_target_pairs={{0,2},{1,3},{2,0},{3,1},{4,6},{5,7},{6,4},{7,5},{8,10},{9,11},{10,... | collective-permute-start | bytes 1843208 | tf_op jit(solution)/shard_map/ppermute | solution.py:134
  44.5 13.2 %collective-permute-start.1 = (bf16[240]{0:T(256)(128)(2,1)S(1)}, bf16[240]{0:T(256)(128)(2,1)S(1)}, u32[]{:S(2)}, u32[]{:S(2)}) collective-permute-start(bf16[240]{0:T(256)(128)(2,1)S(1)} %pad_maximum_fusion.38), channel_id=1, source_target_pairs={{0,2},{1,3},{2,0},{3,1},{4,6},{5,7},{6,4},{7,5},{8,10},{9,11},{10,... | collective-permute-start | bytes 1448 | tf_op jit(solution)/shard_map/ppermute | solution.py:134
  57.9 4.6 %collective-permute-start.2 = (bf16[480]{0:T(512)(128)(2,1)S(1)}, bf16[480]{0:T(512)(128)(2,1)S(1)}, u32[]{:S(2)}, u32[]{:S(2)}) collective-permute-start(bf16[480]{0:T(512)(128)(2,1)S(1)} %pad_maximum_fusion.37), channel_id=1, source_target_pairs={{0,4},{1,5},{2,6},{3,7},{4,0},{5,1},{6,2},{7,3},{8,12},{9,13},{10,... | collective-permute-start | bytes 2888 | tf_op jit(solution)/shard_map/ppermute | solution.py:134
  62.0 37.0 %collective-permute-start.6 = (bf16[2,2,160,960]{3,2,0,1:T(8,128)(2,1)}, bf16[2,2,160,960]{3,2,0,1:T(8,128)(2,1)}, u32[]{:S(2)}, u32[]{:S(2)}) collective-permute-start(bf16[2,2,160,960]{3,2,0,1:T(8,128)(2,1)} %pad_maximum_fusion.5), channel_id=1, source_target_pairs={{0,4},{1,5},{2,6},{3,7},{4,0},{5,1},{6,2},{7,3},{8,12},{9,13},{10,... | collective-permute-start | bytes 3686408 | tf_op jit(solution)/shard_map/ppermute | solution.py:134
  63.2 26.4 %collective-permute-start.3 = (bf16[960]{0:T(1024)(128)(2,1)}, bf16[960]{0:T(1024)(128)(2,1)}, u32[]{:S(2)}, u32[]{:S(2)}) collective-permute-start(bf16[960]{0:T(1024)(128)(2,1)} %pad_maximum_fusion.36), channel_id=1, source_target_pairs={{0,8},{1,9},{2,10},{3,11},{4,12},{5,13},{6,14},{7,15},{8,0},{9,1},... | collective-permute-start | bytes 5768 | tf_op jit(solution)/shard_map/ppermute | solution.py:134
  90.5 21.8 %collective-permute-start.17 = (bf16[2,160,960]{2,1,0:T(8,128)(2,1)S(1)}, bf16[2,160,960]{2,1,0:T(8,128)(2,1)S(1)}, u32[]{:S(2)}, u32[]{:S(2)}) collective-permute-start(bf16[2,160,960]{2,1,0:T(8,128)(2,1)S(1)} %pad_maximum_fusion.16), channel_id=1, source_target_pairs={{0,4},{1,5},{2,6},{3,7},{4,0},{5,1},{6,2},{7,3},{8,12},{9,13},{10,... | collective-permute-start | bytes 1843208 | tf_op jit(solution)/shard_map/ppermute | solution.py:134
  96.8 29.6 %collective-permute-start.13 = (bf16[2,160,960]{2,1,0:T(8,128)(2,1)S(1)}, bf16[2,160,960]{2,1,0:T(8,128)(2,1)S(1)}, u32[]{:S(2)}, u32[]{:S(2)}) collective-permute-start(bf16[2,160,960]{2,1,0:T(8,128)(2,1)S(1)} %pad_maximum_fusion.15), channel_id=1, source_target_pairs={{0,4},{1,5},{2,6},{3,7},{4,0},{5,1},{6,2},{7,3},{8,12},{9,13},{10,... | collective-permute-start | bytes 1843208 | tf_op jit(solution)/shard_map/ppermute | solution.py:134
  96.9 39.7 %collective-permute-start.9 = (bf16[2,160,960]{2,1,0:T(8,128)(2,1)S(1)}, bf16[2,160,960]{2,1,0:T(8,128)(2,1)S(1)}, u32[]{:S(2)}, u32[]{:S(2)}) collective-permute-start(bf16[2,160,960]{2,1,0:T(8,128)(2,1)S(1)} %pad_maximum_fusion.14), channel_id=1, source_target_pairs={{0,4},{1,5},{2,6},{3,7},{4,0},{5,1},{6,2},{7,3},{8,12},{9,13},{10,... | collective-permute-start | bytes 1843208 | tf_op jit(solution)/shard_map/ppermute | solution.py:134
  99.0 40.0 %slice-start.4 = ((s8[5242880]{0:T(1024)(128)(4,1)}), s8[4194304]{0:T(1024)(128)(4,1)S(1)}, s32[]{:S(2)}) async-start(s8[5242880]{0:T(1024)(128)(4,1)} %bitcast.319), calls=%async_computation.4 | async-start | bytes 8388608
  100.7 38.3 %slice-start.5 = ((s8[5242880]{0:T(1024)(128)(4,1)}), s8[1048576]{0:T(1024)(128)(4,1)S(1)}, s32[]{:S(2)}) async-start(s8[5242880]{0:T(1024)(128)(4,1)} %bitcast.319), calls=%async_computation.5 | async-start | bytes 2097152
  100.7 38.4 %slice-start = ((s8[5242880]{0:T(1024)(128)(4,1)}), s8[4194304]{0:T(1024)(128)(4,1)S(1)}, s32[]{:S(2)}) async-start(s8[5242880]{0:T(1024)(128)(4,1)} %bitcast.311), calls=%async_computation | async-start | bytes 8388608
  100.9 38.1 %slice-start.1 = ((s8[5242880]{0:T(1024)(128)(4,1)}), s8[1048576]{0:T(1024)(128)(4,1)S(1)}, s32[]{:S(2)}) async-start(s8[5242880]{0:T(1024)(128)(4,1)} %bitcast.311), calls=%async_computation.1 | async-start | bytes 2097152
  100.9 94.0 %collective-permute-start.7 = (bf16[2,2,2,160,960]{4,3,0,2,1:T(8,128)(2,1)S(1)}, bf16[2,2,2,160,960]{4,3,0,2,1:T(8,128)(2,1)S(1)}, u32[]{:S(2)}, u32[]{:S(2)}) collective-permute-start(bf16[2,2,2,160,960]{4,3,0,2,1:T(8,128)(2,1)S(1)} %pad_maximum_fusion.1), channel_id=1, source_target_pairs={{0,1},{1,0},{2,3},{3,2},{4,5},{5,4},{6,7},{7,6},{8,9},{9,8},{10,11... | collective-permute-start | bytes 7372808 | tf_op jit(solution)/shard_map/ppermute | solution.py:134
  112.5 31.8 %collective-permute-start.18 = (bf16[4,160,960]{2,1,0:T(8,128)(2,1)S(1)}, bf16[4,160,960]{2,1,0:T(8,128)(2,1)S(1)}, u32[]{:S(2)}, u32[]{:S(2)}) collective-permute-start(bf16[4,160,960]{2,1,0:T(8,128)(2,1)S(1)} %pad_maximum_fusion.8), channel_id=1, source_target_pairs={{0,2},{1,3},{2,0},{3,1},{4,6},{5,7},{6,4},{7,5},{8,10},{9,11},{10,... | collective-permute-start | bytes 3686408 | tf_op jit(solution)/shard_map/ppermute | solution.py:134
  126.5 45.8 %collective-permute-start.14 = (bf16[4,160,960]{2,1,0:T(8,128)(2,1)S(1)}, bf16[4,160,960]{2,1,0:T(8,128)(2,1)S(1)}, u32[]{:S(2)}, u32[]{:S(2)}) collective-permute-start(bf16[4,160,960]{2,1,0:T(8,128)(2,1)S(1)} %pad_maximum_fusion.7), channel_id=1, source_target_pairs={{0,2},{1,3},{2,0},{3,1},{4,6},{5,7},{6,4},{7,5},{8,10},{9,11},{10,... | collective-permute-start | bytes 3686408 | tf_op jit(solution)/shard_map/ppermute | solution.py:134
  136.7 55.1 %collective-permute-start.10 = (bf16[4,160,960]{2,1,0:T(8,128)(2,1)S(1)}, bf16[4,160,960]{2,1,0:T(8,128)(2,1)S(1)}, u32[]{:S(2)}, u32[]{:S(2)}) collective-permute-start(bf16[4,160,960]{2,1,0:T(8,128)(2,1)S(1)} %pad_maximum_fusion.6), channel_id=1, source_target_pairs={{0,2},{1,3},{2,0},{3,1},{4,6},{5,7},{6,4},{7,5},{8,10},{9,11},{10,... | collective-permute-start | bytes 3686408 | tf_op jit(solution)/shard_map/ppermute | solution.py:134
  146.0 53.1 %collective-permute-start.19 = (bf16[8,160,960]{2,1,0:T(8,128)(2,1)}, bf16[8,160,960]{2,1,0:T(8,128)(2,1)}, u32[]{:S(2)}, u32[]{:S(2)}) collective-permute-start(bf16[8,160,960]{2,1,0:T(8,128)(2,1)} %pad_maximum_fusion.4), channel_id=1, source_target_pairs={{0,1},{1,0},{2,3},{3,2},{4,5},{5,4},{6,7},{7,6},{8,9},{9,8},{10,11... | collective-permute-start | bytes 7372808 | tf_op jit(solution)/shard_map/ppermute | solution.py:134
  174.0 27.3 %collective-permute-start.15 = (bf16[8,160,960]{2,1,0:T(8,128)(2,1)}, bf16[8,160,960]{2,1,0:T(8,128)(2,1)}, u32[]{:S(2)}, u32[]{:S(2)}) collective-permute-start(bf16[8,160,960]{2,1,0:T(8,128)(2,1)} %pad_maximum_fusion.3), channel_id=1, source_target_pairs={{0,1},{1,0},{2,3},{3,2},{4,5},{5,4},{6,7},{7,6},{8,9},{9,8},{10,11... | collective-permute-start | bytes 7372808 | tf_op jit(solution)/shard_map/ppermute | solution.py:134
  193.5 15.2 %collective-permute-start.11 = (bf16[8,160,960]{2,1,0:T(8,128)(2,1)}, bf16[8,160,960]{2,1,0:T(8,128)(2,1)S(1)}, u32[]{:S(2)}, u32[]{:S(2)}) collective-permute-start(bf16[8,160,960]{2,1,0:T(8,128)(2,1)} %pad_maximum_fusion.2), channel_id=1, source_target_pairs={{0,1},{1,0},{2,3},{3,2},{4,5},{5,4},{6,7},{7,6},{8,9},{9,8},{10,11... | collective-permute-start | bytes 7372808 | tf_op jit(solution)/shard_map/ppermute | solution.py:134
  218.1 9.3 %collective-permute-start.20 = (bf16[128,960]{0,1:T(8,128)(2,1)S(1)}, bf16[128,960]{0,1:T(8,128)(2,1)S(1)}, u32[]{:S(2)}, u32[]{:S(2)}) collective-permute-start(bf16[128,960]{0,1:T(8,128)(2,1)S(1)} %fusion.42), channel_id=1, source_target_pairs={{0,16},{1,17},{2,18},{3,19},{4,20},{5,21},{6,22},{7,23},{8,24},{9,... | collective-permute-start | bytes 737288 | tf_op jit(solution)/shard_map/ppermute | solution.py:285
  227.5 61.2 %copy-start.9 = (bf16[128,960]{0,1:T(8,128)(2,1)}, bf16[128,960]{0,1:T(8,128)(2,1)S(1)}, u32[]{:S(2)}) copy-start(bf16[128,960]{0,1:T(8,128)(2,1)S(1)} %get-tuple-element.13) | copy-start | bytes 737284
  227.5 24.9 %copy-start.51 = (f32[128]{0:T(128)}, f32[128]{0:T(128)S(1)}, u32[]{:S(2)}) copy-start(f32[128]{0:T(128)S(1)} %get-tuple-element.75) | copy-start | bytes 1540
  227.5 24.9 %copy-start.55 = (f32[128]{0:T(128)}, f32[128]{0:T(128)S(1)}, u32[]{:S(2)}) copy-start(f32[128]{0:T(128)S(1)} %get-tuple-element.74) | copy-start | bytes 1540
  231.9 17.9 %copy-start.16 = (bf16[128,5,3,32]{0,3,2,1:T(8,128)(2,1)}, bf16[128,5,3,32]{0,3,2,1:T(8,128)(2,1)S(1)}, u32[]{:S(2)}) copy-start(bf16[128,5,3,32]{0,3,2,1:T(8,128)(2,1)S(1)} %get-tuple-element.50) | copy-start | bytes 368644
  232.0 18.3 %copy-start.27 = (bf16[128,5,32]{0,2,1:T(8,128)(2,1)}, bf16[128,5,32]{0,2,1:T(8,128)(2,1)S(1)}, u32[]{:S(2)}) copy-start(bf16[128,5,32]{0,2,1:T(8,128)(2,1)S(1)} %get-tuple-element.57) | copy-start | bytes 122884
  232.0 18.3 %copy-start.29 = (bf16[128,5,32]{0,2,1:T(8,128)(2,1)}, bf16[128,5,32]{0,2,1:T(8,128)(2,1)S(1)}, u32[]{:S(2)}) copy-start(bf16[128,5,32]{0,2,1:T(8,128)(2,1)S(1)} %get-tuple-element.58) | copy-start | bytes 122884
  234.4 46.6 %copy-start.47 = (f32[128]{0:T(128)}, f32[128]{0:T(128)S(1)}, u32[]{:S(2)}) copy-start(f32[128]{0:T(128)S(1)} %get-tuple-element.77) | copy-start | bytes 1540
  234.4 46.6 %copy-start.53 = (f32[128]{0:T(128)}, f32[128]{0:T(128)S(1)}, u32[]{:S(2)}) copy-start(f32[128]{0:T(128)S(1)} %get-tuple-element.76) | copy-start | bytes 1540
  253.3 9.8 %collective-permute-start.21 = (bf16[128,960]{0,1:T(8,128)(2,1)}, bf16[128,960]{0,1:T(8,128)(2,1)S(1)}, u32[]{:S(2)}, u32[]{:S(2)}) collective-permute-start(bf16[128,960]{0,1:T(8,128)(2,1)} %fusion.98), channel_id=1, source_target_pairs={{16,0},{17,1},{18,2},{19,3},{20,4},{21,5},{22,6},{23,7},{24,8},{25... | collective-permute-start | bytes 737288 | tf_op jit(solution)/shard_map/ppermute | solution.py:289
  255.2 54.9 %collective-permute-start.24 = (bf16[128,960]{0,1:T(8,128)(2,1)}, bf16[128,960]{0,1:T(8,128)(2,1)}, u32[]{:S(2)}, u32[]{:S(2)}) collective-permute-start(bf16[128,960]{0,1:T(8,128)(2,1)} %fusion.107), channel_id=1, source_target_pairs={{0,2},{1,3},{2,0},{3,1},{4,6},{5,7},{6,4},{7,5},{8,10},{9,11},{10,... | collective-permute-start | bytes 737288 | tf_op jit(solution)/shard_map/ppermute | solution.py:134
  256.7 48.2 %collective-permute-start.32 = (bf16[128,960]{0,1:T(8,128)(2,1)S(1)}, bf16[128,960]{0,1:T(8,128)(2,1)}, u32[]{:S(2)}, u32[]{:S(2)}) collective-permute-start(bf16[128,960]{0,1:T(8,128)(2,1)S(1)} %multiply_convert_fusion.14), channel_id=1, source_target_pairs={{0,2},{1,3},{2,0},{3,1},{4,6},{5,7},{6,4},{7,5},{8,10},{9,11},{10,... | collective-permute-start | bytes 737288 | tf_op jit(solution)/shard_map/ppermute | solution.py:134
  287.0 37.3 %collective-permute-start.26 = (bf16[128,960]{0,1:T(8,128)(2,1)}, bf16[128,960]{0,1:T(8,128)(2,1)}, u32[]{:S(2)}, u32[]{:S(2)}) collective-permute-start(bf16[128,960]{0,1:T(8,128)(2,1)} %fusion.169), channel_id=1, source_target_pairs={{0,2},{1,3},{2,0},{3,1},{4,6},{5,7},{6,4},{7,5},{8,10},{9,11},{10,... | collective-permute-start | bytes 737288 | tf_op jit(solution)/shard_map/ppermute | solution.py:134
  291.0 34.4 %collective-permute-start.40 = (bf16[128,960]{0,1:T(8,128)(2,1)}, bf16[128,960]{0,1:T(8,128)(2,1)}, u32[]{:S(2)}, u32[]{:S(2)}) collective-permute-start(bf16[128,960]{0,1:T(8,128)(2,1)} %broadcast_select_fusion), channel_id=1, source_target_pairs={{0,2},{1,3},{2,0},{3,1},{4,6},{5,7},{6,4},{7,5},{8,10},{9,11},{10,... | collective-permute-start | bytes 737288 | tf_op jit(solution)/shard_map/ppermute | solution.py:134
  295.8 9.0 %collective-permute-start.44 = (f32[960]{0:T(1024)S(1)}, f32[960]{0:T(1024)S(1)}, u32[]{:S(2)}, u32[]{:S(2)}) collective-permute-start(f32[960]{0:T(1024)S(1)} %broadcast_select_fusion.2), channel_id=1, source_target_pairs={{0,8},{1,9},{2,10},{3,11},{4,12},{5,13},{6,14},{7,15},{8,0},{9,1},... | collective-permute-start | bytes 11528 | tf_op jit(solution)/shard_map/ppermute | solution.py:134
  304.8 4.4 collective-permute-start.45
  307.6 19.5 %collective-permute-start.22 = (bf16[2,2,2,160,128]{4,3,1,0,2:T(8,128)(2,1)S(1)}, bf16[2,2,2,160,128]{4,3,1,0,2:T(8,128)(2,1)S(1)}, u32[]{:S(2)}, u32[]{:S(2)}) collective-permute-start(bf16[2,2,2,160,128]{4,3,1,0,2:T(8,128)(2,1)S(1)} %bitcast.374), channel_id=1, source_target_pairs={{0,2},{1,3},{2,0},{3,1},{4,6},{5,7},{6,4},{7,5},{8,10},{9,11},{10,... | collective-permute-start | bytes 983048 | tf_op jit(solution)/shard_map/ppermute | solution.py:134
  309.2 18.2 %collective-permute-start.38 = (bf16[1,2,2,2,160,128]{5,4,3,2,1,0:T(8,128)(2,1)S(1)}, bf16[1,2,2,2,160,128]{5,4,3,2,1,0:T(8,128)(2,1)S(1)}, u32[]{:S(2)}, u32[]{:S(2)}) collective-permute-start(bf16[1,2,2,2,160,128]{5,4,3,2,1,0:T(8,128)(2,1)S(1)} %copy-done.31), channel_id=1, source_target_pairs={{0,2},{1,3},{2,0},{3,1},{4,6},{5,7},{6,4},{7,5},{8,10},{9,11},{10,... | collective-permute-start | bytes 983048 | tf_op jit(solution)/shard_map/ppermute | solution.py:134
  310.1 12.5 %collective-permute-start.46 = (f32[240]{0:T(256)S(1)}, f32[240]{0:T(256)S(1)}, u32[]{:S(2)}, u32[]{:S(2)}) collective-permute-start(f32[240]{0:T(256)S(1)} %broadcast_select_fusion.9), channel_id=1, source_target_pairs={{0,2},{1,3},{2,0},{3,1},{4,6},{5,7},{6,4},{7,5},{8,10},{9,11},{10,... | collective-permute-start | bytes 2888 | tf_op jit(solution)/shard_map/ppermute | solution.py:134
  322.6 14.0 %collective-permute-start.30 = (bf16[2,2,2,2,160,128]{5,4,3,2,1,0:T(8,128)(2,1)S(1)}, bf16[2,2,2,2,160,128]{5,4,3,2,1,0:T(8,128)(2,1)S(1)}, u32[]{:S(2)}, u32[]{:S(2)}) collective-permute-start(bf16[2,2,2,2,160,128]{5,4,3,2,1,0:T(8,128)(2,1)S(1)} %copy-done.20), channel_id=1, source_target_pairs={{0,2},{1,3},{2,0},{3,1},{4,6},{5,7},{6,4},{7,5},{8,10},{9,11},{10,... | collective-permute-start | bytes 1966088 | tf_op jit(solution)/shard_map/ppermute | solution.py:134
  324.3 3.7 collective-permute-start.47
  325.5 17.1 %collective-permute-start.27 = (bf16[256,960]{0,1:T(8,128)(2,1)S(1)}, bf16[256,960]{0,1:T(8,128)(2,1)S(1)}, u32[]{:S(2)}, u32[]{:S(2)}) collective-permute-start(bf16[256,960]{0,1:T(8,128)(2,1)S(1)} %pad_maximum_fusion.20), channel_id=1, source_target_pairs={{0,1},{1,0},{2,3},{3,2},{4,5},{5,4},{6,7},{7,6},{8,9},{9,8},{10,11... | collective-permute-start | bytes 1474568 | tf_op jit(solution)/shard_map/ppermute | solution.py:134
  327.1 11.0 %collective-permute-start.41 = (bf16[256,960]{0,1:T(8,128)(2,1)S(1)}, bf16[256,960]{0,1:T(8,128)(2,1)S(1)}, u32[]{:S(2)}, u32[]{:S(2)}) collective-permute-start(bf16[256,960]{0,1:T(8,128)(2,1)S(1)} %pad_maximum_fusion.22), channel_id=1, source_target_pairs={{0,1},{1,0},{2,3},{3,2},{4,5},{5,4},{6,7},{7,6},{8,9},{9,8},{10,11... | collective-permute-start | bytes 1474568 | tf_op jit(solution)/shard_map/ppermute | solution.py:134
  327.3 15.2 %collective-permute-start.23 = (bf16[2,2,160,256]{3,2,1,0:T(8,128)(2,1)S(1)}, bf16[2,2,160,256]{3,2,1,0:T(8,128)(2,1)S(1)}, u32[]{:S(2)}, u32[]{:S(2)}) collective-permute-start(bf16[2,2,160,256]{3,2,1,0:T(8,128)(2,1)S(1)} %get-tuple-element.40), channel_id=1, source_target_pairs={{0,1},{1,0},{2,3},{3,2},{4,5},{5,4},{6,7},{7,6},{8,9},{9,8},{10,11... | collective-permute-start | bytes 983048 | tf_op jit(solution)/shard_map/ppermute | solution.py:134
  328.0 9.7 %collective-permute-start.39 = (bf16[1,2,2,160,256]{4,3,2,1,0:T(8,128)(2,1)S(1)}, bf16[1,2,2,160,256]{4,3,2,1,0:T(8,128)(2,1)S(1)}, u32[]{:S(2)}, u32[]{:S(2)}) collective-permute-start(bf16[1,2,2,160,256]{4,3,2,1,0:T(8,128)(2,1)S(1)} %get-tuple-element.36), channel_id=1, source_target_pairs={{0,1},{1,0},{2,3},{3,2},{4,5},{5,4},{6,7},{7,6},{8,9},{9,8},{10,11... | collective-permute-start | bytes 983048 | tf_op jit(solution)/shard_map/ppermute | solution.py:134
  336.6 7.9 %collective-permute-start.25 = (bf16[256,960]{0,1:T(8,128)(2,1)S(1)}, bf16[256,960]{0,1:T(8,128)(2,1)S(1)}, u32[]{:S(2)}, u32[]{:S(2)}) collective-permute-start(bf16[256,960]{0,1:T(8,128)(2,1)S(1)} %pad_maximum_fusion.19), channel_id=1, source_target_pairs={{0,1},{1,0},{2,3},{3,2},{4,5},{5,4},{6,7},{7,6},{8,9},{9,8},{10,11... | collective-permute-start | bytes 1474568 | tf_op jit(solution)/shard_map/ppermute | solution.py:134
  337.6 18.1 %collective-permute-start.33 = (bf16[256,960]{0,1:T(8,128)(2,1)}, bf16[256,960]{0,1:T(8,128)(2,1)}, u32[]{:S(2)}, u32[]{:S(2)}) collective-permute-start(bf16[256,960]{0,1:T(8,128)(2,1)} %pad_maximum_fusion.21), channel_id=1, source_target_pairs={{0,1},{1,0},{2,3},{3,2},{4,5},{5,4},{6,7},{7,6},{8,9},{9,8},{10,11... | collective-permute-start | bytes 1474568 | tf_op jit(solution)/shard_map/ppermute | solution.py:134
  338.1 16.4 %collective-permute-start.31 = (bf16[2,2,2,160,256]{4,3,2,1,0:T(8,128)(2,1)}, bf16[2,2,2,160,256]{4,3,2,1,0:T(8,128)(2,1)}, u32[]{:S(2)}, u32[]{:S(2)}) collective-permute-start(bf16[2,2,2,160,256]{4,3,2,1,0:T(8,128)(2,1)} %get-tuple-element.24), channel_id=1, source_target_pairs={{0,1},{1,0},{2,3},{3,2},{4,5},{5,4},{6,7},{7,6},{8,9},{9,8},{10,11... | collective-permute-start | bytes 1966088 | tf_op jit(solution)/shard_map/ppermute | solution.py:134
  347.4 36.2 %collective-permute-start.28 = (bf16[2,160,960]{2,1,0:T(8,128)(2,1)}, bf16[2,160,960]{2,1,0:T(8,128)(2,1)}, u32[]{:S(2)}, u32[]{:S(2)}) collective-permute-start(bf16[2,160,960]{2,1,0:T(8,128)(2,1)} %fusion.72), channel_id=1, source_target_pairs={{0,4},{1,5},{2,6},{3,7},{4,0},{5,1},{6,2},{7,3},{8,12},{9,13},{10,... | collective-permute-start | bytes 1843208 | tf_op jit(solution)/shard_map/ppermute | solution.py:134
  354.2 25.1 %collective-permute-start.42 = (bf16[2,160,960]{2,1,0:T(8,128)(2,1)}, bf16[2,160,960]{2,1,0:T(8,128)(2,1)}, u32[]{:S(2)}, u32[]{:S(2)}) collective-permute-start(bf16[2,160,960]{2,1,0:T(8,128)(2,1)} %bitcast.364), channel_id=1, source_target_pairs={{0,4},{1,5},{2,6},{3,7},{4,0},{5,1},{6,2},{7,3},{8,12},{9,13},{10,... | collective-permute-start | bytes 1843208 | tf_op jit(solution)/shard_map/ppermute | solution.py:134
  368.9 44.7 %collective-permute-start.36 = (bf16[2,160,960]{2,1,0:T(8,128)(2,1)}, bf16[2,160,960]{2,1,0:T(8,128)(2,1)}, u32[]{:S(2)}, u32[]{:S(2)}) collective-permute-start(bf16[2,160,960]{2,1,0:T(8,128)(2,1)} %bitcast.365), channel_id=1, source_target_pairs={{0,4},{1,5},{2,6},{3,7},{4,0},{5,1},{6,2},{7,3},{8,12},{9,13},{10,... | collective-permute-start | bytes 1843208 | tf_op jit(solution)/shard_map/ppermute | solution.py:134
  374.6 46.4 %collective-permute-start.34 = (bf16[2,160,960]{2,1,0:T(8,128)(2,1)}, bf16[2,160,960]{2,1,0:T(8,128)(2,1)S(1)}, u32[]{:S(2)}, u32[]{:S(2)}) collective-permute-start(bf16[2,160,960]{2,1,0:T(8,128)(2,1)} %bitcast.363), channel_id=1, source_target_pairs={{0,4},{1,5},{2,6},{3,7},{4,0},{5,1},{6,2},{7,3},{8,12},{9,13},{10,... | collective-permute-start | bytes 1843208 | tf_op jit(solution)/shard_map/ppermute | solution.py:134
  381.0 32.5 %collective-permute-start.43 = (bf16[160,960]{1,0:T(8,128)(2,1)S(1)}, bf16[160,960]{1,0:T(8,128)(2,1)S(1)}, u32[]{:S(2)}, u32[]{:S(2)}) collective-permute-start(bf16[160,960]{1,0:T(8,128)(2,1)S(1)} %fusion.129), channel_id=1, source_target_pairs={{0,8},{1,9},{2,10},{3,11},{4,12},{5,13},{6,14},{7,15},{8,0},{9,1},... | collective-permute-start | bytes 921608 | tf_op jit(solution)/shard_map/ppermute | solution.py:134
  384.9 28.7 %copy-start.3 = (f32[320,960]{1,0:T(8,128)S(1)}, f32[320,960]{1,0:T(8,128)}, u32[]{:S(2)}) copy-start(f32[320,960]{1,0:T(8,128)} %copy.55) | copy-start | bytes 3686404
  385.0 37.1 %collective-permute-start.29 = (bf16[160,960]{1,0:T(8,128)(2,1)S(1)}, bf16[160,960]{1,0:T(8,128)(2,1)S(1)}, u32[]{:S(2)}, u32[]{:S(2)}) collective-permute-start(bf16[160,960]{1,0:T(8,128)(2,1)S(1)} %fusion.125), channel_id=1, source_target_pairs={{0,8},{1,9},{2,10},{3,11},{4,12},{5,13},{6,14},{7,15},{8,0},{9,1},... | collective-permute-start | bytes 921608 | tf_op jit(solution)/shard_map/ppermute | solution.py:134
  415.1 28.9 %collective-permute-start.37 = (bf16[160,960]{1,0:T(8,128)(2,1)S(1)}, bf16[160,960]{1,0:T(8,128)(2,1)S(1)}, u32[]{:S(2)}, u32[]{:S(2)}) collective-permute-start(bf16[160,960]{1,0:T(8,128)(2,1)S(1)} %fusion.128), channel_id=1, source_target_pairs={{0,8},{1,9},{2,10},{3,11},{4,12},{5,13},{6,14},{7,15},{8,0},{9,1},... | collective-permute-start | bytes 921608 | tf_op jit(solution)/shard_map/ppermute | solution.py:134
  421.3 29.7 %collective-permute-start.35 = (bf16[160,960]{1,0:T(8,128)(2,1)S(1)}, bf16[160,960]{1,0:T(8,128)(2,1)S(1)}, u32[]{:S(2)}, u32[]{:S(2)}) collective-permute-start(bf16[160,960]{1,0:T(8,128)(2,1)S(1)} %fusion.127), channel_id=1, source_target_pairs={{0,8},{1,9},{2,10},{3,11},{4,12},{5,13},{6,14},{7,15},{8,0},{9,1},... | collective-permute-start | bytes 921608 | tf_op jit(solution)/shard_map/ppermute | solution.py:134
  (55 other events, 217.8 us)

commit v3 on v2

--- a/solution.py
+++ b/solution.py
@@ -14,6 +14,7 @@
 epsilon = 1e-05
 theta_base = 100000.0
 Z2_BIT, Z1_BIT, Y_BIT, CORE_BIT = 8, 4, 2, 1
+EXTRA_ROWS = 8
 bf16 = jnp.bfloat16
 f32 = jnp.float32
 
@@ -81,10 +82,12 @@
     h1 = u + dot_nn(o, out_w)
     r2 = lax.rsqrt(jnp.mean(h1 * h1, axis=-1, keepdims=True) + epsilon)
     m = (h1 * r2 * gain_two).astype(bf16)
-    gate = dot_nt(m, gate_w)
-    up = dot_nt(m, up_w)
-    act = (jax.nn.silu(gate) * up).astype(bf16)
-    out = h1 + dot_nn(act, down_w)
+    gate = [dot_nt(m, w) for w in gate_w]
+    up = [dot_nt(m, w) for w in up_w]
+    act = [(jax.nn.silu(g) * p).astype(bf16) for g, p in zip(gate, up)]
+    out = h1
+    for a, w in zip(act, down_w):
+        out = out + dot_nn(a, w)
     return out, (u, r1, n, q, k, v, lse, o, h1, r2, m, gate, up, act)
 
 
@@ -101,11 +104,15 @@
     tokens = u.shape[0]
     eb = e.astype(bf16)
     e = e.astype(f32)
-    da = dot_nt(eb, down_w)
-    sig = jax.nn.sigmoid(gate)
-    dgate = (da * up * sig * (1.0 + gate * (1.0 - sig))).astype(bf16)
-    dup = (da * gate * sig).astype(bf16)
-    dm = dot_nn(dgate, gate_w) + dot_nn(dup, up_w)
+    dgate, dup = [], []
+    for g, p, w in zip(gate, up, down_w):
+        da = dot_nt(eb, w)
+        sig = jax.nn.sigmoid(g)
+        dgate.append((da * p * sig * (1.0 + g * (1.0 - sig))).astype(bf16))
+        dup.append((da * g * sig).astype(bf16))
+    dm = 0.0
+    for g, p, wg, wu in zip(dgate, dup, gate_w, up_w):
+        dm = dm + dot_nn(g, wg) + dot_nn(p, wu)
     part, gain_two_grad = norm_back(dm, h1, r2, gain_two)
     dh1 = e + part
     dz = dh1.astype(bf16)
@@ -162,6 +169,7 @@
 def grads_generic(pieces):
     n, dproj, o, dz, m, dgate, dup, eb, act = pieces
     attn = jnp.concatenate([dot_nn(dproj.T, n), dot_nn(o.T, dz)], axis=0)
+    dgate, dup, act = (jnp.concatenate(v, axis=1) for v in (dgate, dup, act))
     both = [
         lax.psum_scatter(g, "dp", scatter_dimension=0, tiled=True)
         for g in (attn, dot_nn(dgate.T, m), dot_nn(dup.T, m), dot_nn(act.T, eb))
@@ -169,37 +177,53 @@
     return both[0], jnp.stack(both[1:])
 
 
-def plane_rows(x):
-    x = jnp.concatenate([x, flip(x, Y_BIT)], axis=0)
-    return jnp.concatenate([x, flip(x, CORE_BIT)], axis=0)
-
-
-def doubled(block, bits):
-    block = block[None]
-    for bit in bits:
-        block = jnp.concatenate([block, flip(block, bit)], axis=0)
-    return block
-
-
-def doubled_in_order(block, bits, me):
-    rows, width = block.shape
+def z_pairs(x, pairs):
+    return lax.ppermute(x, "dp", [(4 * a + i, 4 * b + i) for a, b in pairs for i in range(4)])
+
+
+def inner_swap(x):
+    return z_pairs(x, [(1, 2), (2, 1)])
+
+
+def from_far(x, is_inner):
+    inner = inner_swap(x)
+    outer = z_pairs(inner, [(1, 0), (2, 3)])
+    return jnp.where(is_inner, inner, outer)
+
+
+def gather_ffn(block, is_inner):
+    near = jnp.stack([block, flip(block, Z1_BIT)])
+    far = from_far(near, is_inner)
+    half = jnp.concatenate([near, far, flip(near, Y_BIT), flip(far, Y_BIT)], axis=0)
+    half = half.reshape(-1, block.shape[1])
+    return [half, flip(half, CORE_BIT)]
+
+
+def gather_attn(block, me, is_inner):
     have = []
-    for bit in bits:
-        other = flip(block, bit)
+    for bit in (Z1_BIT, Y_BIT, Z2_BIT, CORE_BIT):
+        other = from_far(block, is_inner) if bit == Z2_BIT else flip(block, bit)
         high = (me & bit) != 0
         have = sorted(have + [bit], reverse=True)
         block = jnp.stack(
             [jnp.where(high, other, block), jnp.where(high, block, other)], axis=have.index(bit)
         )
-    return block.reshape(-1, width)
-
-
-def ffn_cols(*arrays):
-    tokens, cols = arrays[0].shape
-    share = cols // 16
-    x = jnp.stack([a.T.reshape(2, 2, 2, 2, share, tokens) for a in arrays])
-    x = jnp.concatenate([x[:, :, 0], flip(x[:, :, 1], Y_BIT)], axis=-1)
-    return jnp.concatenate([x[:, 0], flip(x[:, 1], CORE_BIT)], axis=-1)
+    return block.reshape(16, *block.shape[-2:])
+
+
+def plane_rows(x):
+    x = jnp.concatenate([x, flip(x, Y_BIT)], axis=0)
+    return jnp.concatenate([x, flip(x, CORE_BIT)], axis=0)
+
+
+def ffn_cols_y(own, other):
+    tokens, cols = own.shape
+    x = jnp.stack([own.T, other.T]).reshape(2, 2, 4, cols // 8, tokens)
+    return jnp.concatenate([x[:, 0], flip(x[:, 1], Y_BIT)], axis=-1)
+
+
+def ffn_cols_core(x):
+    return jnp.concatenate([x[0], flip(x[1], CORE_BIT)], axis=-1)
 
 
 def attn_cols(array, y, core):
@@ -211,46 +235,67 @@
     return jnp.concatenate([pick(x, core), flip(pick(x, 1 - core), CORE_BIT)], axis=-1)
 
 
-def halved(keep, send, bit):
-    return keep.astype(f32) + flip(send.astype(bf16), bit).astype(f32)
+def line_sum(near, far):
+    far = far + z_pairs(far.astype(bf16), [(0, 1), (3, 2)]).astype(f32)
+    return near + inner_swap(far.astype(bf16)).astype(f32)
+
+
+def pair_sum(keep, send):
+    return keep + flip(send.astype(bf16), Z1_BIT).astype(f32)
 
 
 def ffn_sum(parts):
-    x = halved(parts[0], parts[1], Z1_BIT)
-    return halved(x[0], x[1], Z2_BIT)
+    near = line_sum(parts[:2], parts[2:])
+    return pair_sum(near[0], near[1])
 
 
 def attn_sum(parts, z2, z1):
-    pick = lambda v, i, axis: lax.dynamic_index_in_dim(v, i, axis, keepdims=False)
-    x = halved(pick(parts, z1, 1), pick(parts, 1 - z1, 1), Z1_BIT)
-    return halved(pick(x, z2, 0), pick(x, 1 - z2, 0), Z2_BIT)
-
-
-def grads_planes(pieces, me):
+    pick = lambda v, i: lax.dynamic_index_in_dim(v, i, 0, keepdims=False)
+    near = line_sum(pick(parts, z2), pick(parts, 1 - z2))
+    return pair_sum(pick(near, z1), pick(near, 1 - z1))
+
+
+def early_exchange(state):
+    n, m, act = state[2], state[10], state[13]
+    return (
+        jnp.concatenate([m, flip(m, Y_BIT)], axis=0),
+        jnp.concatenate([n, flip(n, Y_BIT)], axis=0),
+        ffn_cols_y(*act),
+    )
+
+
+def grads_planes(pieces, early, gain_grad, me):
     n, dproj, o, dz, m, dgate, dup, eb, act = pieces
+    m_y, n_y, act_y = early
     z2, z1, y, core = (me >> 3) & 1, (me >> 2) & 1, (me >> 1) & 1, me & 1
-    tokens = n.shape[0]
-    share = act.shape[1] // 16
-    wide = 4 * tokens
-    m_all = plane_rows(m)
-    n_all = plane_rows(n)
-    act_c = ffn_cols(act)[0]
+    width = n.shape[1]
+    over_core = lambda v: jnp.concatenate([v, flip(v, CORE_BIT)], axis=0)
+    eb_all = plane_rows(eb)
+    act_c = ffn_cols_core(act_y)
+    share = act_c.shape[1]
+
+    def product(cols, rows):
+        return dot_nn(cols.reshape(4 * share, -1), rows).reshape(4, share, -1)
+
+    down = ffn_sum(product(act_c, eb_all))
+    m_all = over_core(m_y)
+    gate = ffn_sum(product(ffn_cols_core(ffn_cols_y(*dgate)), m_all))
+    up = ffn_sum(product(ffn_cols_core(ffn_cols_y(*dup)), m_all))
+    n_all = over_core(n_y)
+    dz_all = plane_rows(dz)
     o_c = attn_cols(jnp.concatenate([dproj, o], axis=1), y, core)
-    eb_all = plane_rows(eb)
-
-    def product(cols, rows):
-        return dot_nn(cols.reshape(4 * share, wide), rows).reshape(2, 2, share, -1)
-
-    down = ffn_sum(product(act_c, eb_all))
-    gu_c = ffn_cols(dgate, dup)
-    gate = ffn_sum(product(gu_c[0], m_all))
-    up = ffn_sum(product(gu_c[1], m_all))
-    dz_all = plane_rows(dz)
-    owners = (jnp.arange(4, dtype=jnp.int32) * 4 + y * 2 + core).reshape(2, 2, 1, 1)
+    owners = (jnp.arange(4, dtype=jnp.int32) * 4 + y * 2 + core).reshape(4, 1, 1)
     is_qkv = owners * share < QKV_COLS
     attn = jnp.where(is_qkv, product(o_c, n_all), product(o_c, dz_all))
-    attn = attn_sum(attn, z2, z1)
-    return attn, jnp.stack([gate, up, down])
+    gain_grad = gain_grad + flip(gain_grad, CORE_BIT)
+    gain_grad = gain_grad + flip(gain_grad, Y_BIT)
+    gain_rows = gain_grad.reshape(4, 4, -1)
+    gain_rows = lax.dynamic_index_in_dim(gain_rows, y * 2 + core, 1, keepdims=True)
+    gain_share = gain_rows.shape[-1]
+    gain_rows = jnp.pad(gain_rows, ((0, 0), (0, EXTRA_ROWS - 1), (0, width - gain_share)))
+    parts = jnp.concatenate([attn, gain_rows], axis=1)
+    attn = attn_sum(parts.reshape(2, 2, share + EXTRA_ROWS, width), z2, z1)
+    return attn[:share], jnp.stack([gate, up, down]), attn[share : share + 1, :gain_share]
 
 
 def local(edge_data, segment_ids, attn_weight, ffn_weight, gains):
@@ -264,14 +309,18 @@
     attn_own = attn_weight[0].T
     ffn_own = ffn_weight[0].swapaxes(1, 2)
     if planes:
-        attn_t = doubled_in_order(attn_own, (Z2_BIT, Y_BIT, Z1_BIT, CORE_BIT), me)
-        ffn_t = [
-            doubled(ffn_own[i], (Z2_BIT, Z1_BIT, Y_BIT, CORE_BIT)).reshape(-1, width) for i in range(3)
-        ]
+        z = me // 4
+        is_inner = (z == 1) | (z == 2)
+        share = attn_own.shape[0]
+        gain_rows = jnp.pad(gains, ((0, EXTRA_ROWS - 1), (0, width - gains.shape[1])))
+        attn_all = gather_attn(jnp.concatenate([attn_own, gain_rows], axis=0), me, is_inner)
+        gain_row = attn_all[:, share, : gains.shape[1]].reshape(-1).astype(f32)
+        attn_t = attn_all[:, :share].reshape(-1, width)
+        ffn_t = [gather_ffn(ffn_own[i], is_inner) for i in range(3)]
     else:
         attn_t = lax.all_gather(attn_own, "dp", axis=0, tiled=True)
-        ffn_t = lax.all_gather(ffn_own, "dp", axis=1, tiled=True)
-    gain_row = gather_small(gains[0]).astype(f32)
+        ffn_t = [[w] for w in lax.all_gather(ffn_own, "dp", axis=1, tiled=True)]
+        gain_row = gather_small(gains[0]).astype(f32)
     weights = (
         attn_t[:QKV_COLS],
         attn_t[QKV_COLS:],
@@ -286,20 +335,24 @@
     u = jnp.where(leading, x, received)
     out, state = forward(u, weights, tables)
     first_grad, _, _ = backward(x, state, weights, tables)
-    received = lax.ppermute(first_grad.astype(bf16), "section", [(1, 0)])
+    first_grad = first_grad.astype(bf16)
+    if planes:
+        early = early_exchange(state)
+        first_grad, early = lax.optimization_barrier((first_grad, early))
+    received = lax.ppermute(first_grad, "section", [(1, 0)])
     e = jnp.where(leading, received, x)
     du, pieces, gain_grad = backward(e, state, weights, tables)
     if planes:
-        attn_rows, ffn_rows = grads_planes(pieces, me)
+        attn_rows, ffn_rows, gain_shard = grads_planes(pieces, early, gain_grad, me)
     else:
         attn_rows, ffn_rows = grads_generic(pieces)
-    gain_shard = scatter_small(gain_grad)
+        gain_shard = scatter_small(gain_grad)[None]
     edge_out = jnp.where(leading, du, out).astype(bf16).reshape(micro, block, width)
     return (
         edge_out[None],
         attn_rows.T[None],
         ffn_rows.swapaxes(1, 2)[None],
-        gain_shard[None],
+        gain_shard,
     )
 
 

time: 458 us -> 496 us (1.083)
  waiting for transfers between devices: 230 us -> 180 us
  starting transfers between devices: 56.5 us -> 86.3 us
  local copies, waits for them, and re-layouts: 48.2 us -> 77.7 us
  matrix products: 76.8 us -> 94.2 us
  other arithmetic: 39.1 us -> 49.2 us
    ppermute x46 -> x37, waiting for transfers between devices: 223 us -> 88.6 us  [flip(): return lax.ppermute(x, 'dp', [(i, i ^ bit) for i in range(size)])]
    ppermute x1 -> x17, waiting for transfers between devices: 5.93 us -> 88.1 us  [the longest x16 83.9 us: z_pairs(): lax.ppermute(x, 'dp', [(4 * a + i, 4 * b + i) for a, b in pairs for i in...]
    ppermute x1 -> x17, starting transfers between devices: 1.28 us -> 26.5 us  [the longest x16 25.2 us: z_pairs(): lax.ppermute(x, 'dp', [(4 * a + i, 4 * b + i) for a, b in pairs for i in...]
    reshape x0 -> x4, local copies, waits for them, and re-layouts: none -> 11.5 us  [the longest x3 11.4 us: gather_ffn(): half = half.reshape(-1, block.shape[1])]
    dot_general x9 -> x14, matrix products: 26.3 us -> 37.2 us  [dot_nt(): lax.dot_general(a, b, (((1,), (1,)), ((), ())), preferred_element_type=f32)]
    another operation x19 -> x22, other arithmetic: 6.16 us -> 14.9 us  [the longest x8 8.81 us: gather_attn(): jnp.stack([jnp.where(high, other, block), jnp.where(high, block, other)],...]
    convert_element_type x8 -> x11, local copies, waits for them, and re-layouts: 4.26 us -> 12.5 us  [the longest x2 3.84 us: backward(): dup.append((da * g * sig).astype(bf16))]
    convert_element_type x2 -> x9, other arithmetic: 0.99 us -> 8.58 us  [the longest x4 4.22 us: line_sum(): return near + inner_swap(far.astype(bf16)).astype(f32)]
  transfers between devices with their start and end apart: 48 -> 55, of which waited for: 18 -> 23; matrix products, arithmetic and copies ran while one was open for 28% -> 35% of each run, Pallas kernels for 0% -> 0%
where the time goes in v3:
time: 496 us; the launch traced here: 490 us
  waiting for transfers between devices  180 us (36%)
  matrix products  94.2 us (19%)
  starting transfers between devices  86.3 us (17%)
  local copies, waits for them, and re-layouts  77.7 us (16%)
  other arithmetic  49.2 us (10%)
    ppermute x37, waiting for transfers between devices, flip(): return lax.ppermute(x, 'dp', [(i, i ^ bit) for i in range(size)])  88.6 us
    ppermute x16, waiting for transfers between devices, z_pairs(): lax.ppermute(x, 'dp', [(4 * a + i, 4 * b + i) for a, b in pairs for i in...  83.9 us
    ppermute x37, starting transfers between devices, flip(): return lax.ppermute(x, 'dp', [(i, i ^ bit) for i in range(size)])  55.7 us
    dot_general x21, matrix products, dot_nn(): lax.dot_general(a, b, (((1,), (0,)), ((), ())), preferred_element_type=f32)  53.1 us
    dot_general x14, matrix products, dot_nt(): lax.dot_general(a, b, (((1,), (1,)), ((), ())), preferred_element_type=f32)  37.2 us
    ppermute x16, starting transfers between devices, z_pairs(): lax.ppermute(x, 'dp', [(4 * a + i, 4 * b + i) for a, b in pairs for i in...  25.2 us
    slice x9, local copies, waits for them, and re-layouts, ffn_sum(): near = line_sum(parts[:2], parts[2:])  21.5 us
    unnamed x147, local copies, waits for them, and re-layouts  13.6 us
  transfers between devices with their start and end apart: 55, of which 23 were waited for; matrix products, arithmetic and copies ran while one was open for 35% of the time, Pallas kernels for 0%

profile of v3, /device:TPU:0, one launch (start us, length us, event | category | flops | bytes accessed | tf_op | source)
XLA Modules:
  0.0 490.0 jit_solution(16737479750445315216)
XLA Ops:
  1.7 3.1 collective-permute-start
  4.7 8.1 %collective-permute-done = bf16[168,960]{1,0:T(8,128)(2,1)S(1)} collective-permute-done((bf16[168,960]{1,0:T(8,128)(2,1)S(1)}, bf16[168,960]{1,0:T(8,128)(2,1)S(1)}, u32[]{:S(2)}, u32[]{:S(2)}) %collective-permute-start) | collective-permute-done | bytes 322592 | tf_op jit(solution)/shard_map/ppermute | solution.py:141
  15.8 14.9 %collective-permute-done.1 = bf16[2,168,960]{2,1,0:T(8,128)(2,1)S(1)} collective-permute-done((bf16[2,168,960]{2,1,0:T(8,128)(2,1)S(1)}, bf16[2,168,960]{2,1,0:T(8,128)(2,1)S(1)}, u32[]{:S(2)}, u32[]{:S(2)}) %collective-permute-start.1) | collective-permute-done | bytes 645152 | tf_op jit(solution)/shard_map/ppermute | solution.py:141
  35.7 3.2 collective-permute-start.15
  42.9 4.9 %collective-permute-done.15 = bf16[160,960]{1,0:T(8,128)(2,1)} collective-permute-done((bf16[160,960]{1,0:T(8,128)(2,1)}, bf16[160,960]{1,0:T(8,128)(2,1)}, u32[]{:S(2)}, u32[]{:S(2)}) %collective-permute-start.15) | collective-permute-done | bytes 307232 | tf_op jit(solution)/shard_map/ppermute | solution.py:141
  56.7 2.2 collective-permute-done.10
  62.0 36.7 %collective-permute-done.3 = bf16[2,2,168,960]{3,2,1,0:T(8,128)(2,1)} collective-permute-done((bf16[2,2,168,960]{3,2,1,0:T(8,128)(2,1)}, bf16[2,2,168,960]{3,2,1,0:T(8,128)(2,1)}, u32[]{:S(2)}, u32[]{:S(2)}) %collective-permute-start.3) | collective-permute-done | bytes 1290272 | tf_op jit(solution)/shard_map/ppermute | solution.py:181
  112.6 11.3 %collective-permute-done.7 = bf16[2,160,960]{2,1,0:T(8,128)(2,1)S(1)} collective-permute-done((bf16[2,160,960]{2,1,0:T(8,128)(2,1)S(1)}, bf16[2,160,960]{2,1,0:T(8,128)(2,1)S(1)}, u32[]{:S(2)}, u32[]{:S(2)}) %collective-permute-start.7) | collective-permute-done | bytes 614432 | tf_op jit(solution)/shard_map/ppermute | solution.py:181
  127.1 10.5 %collective-permute-done.12 = bf16[2,160,960]{2,1,0:T(8,128)(2,1)S(1)} collective-permute-done((bf16[2,160,960]{2,1,0:T(8,128)(2,1)S(1)}, bf16[2,160,960]{2,1,0:T(8,128)(2,1)S(1)}, u32[]{:S(2)}, u32[]{:S(2)}) %collective-permute-start.12) | collective-permute-done | bytes 614432 | tf_op jit(solution)/shard_map/ppermute | solution.py:181
  142.8 12.8 %collective-permute-done.19 = bf16[2,160,960]{2,1,0:T(8,128)(2,1)S(1)} collective-permute-done((bf16[2,160,960]{2,1,0:T(8,128)(2,1)S(1)}, bf16[2,160,960]{2,1,0:T(8,128)(2,1)S(1)}, u32[]{:S(2)}, u32[]{:S(2)}) %collective-permute-start.19) | collective-permute-done | bytes 614432 | tf_op jit(solution)/shard_map/ppermute | solution.py:141
  156.5 4.4 copy.114
  160.9 8.9 %collective-permute-done.9 = bf16[2,160,960]{2,1,0:T(8,128)(2,1)} collective-permute-done((bf16[2,160,960]{2,1,0:T(8,128)(2,1)}, bf16[2,160,960]{2,1,0:T(8,128)(2,1)}, u32[]{:S(2)}, u32[]{:S(2)}) %collective-permute-start.9) | collective-permute-done | bytes 614432 | tf_op jit(solution)/shard_map/ppermute | solution.py:141
  170.9 2.7 copy.112
  173.6 9.8 %collective-permute-done.14 = bf16[2,160,960]{2,1,0:T(8,128)(2,1)} collective-permute-done((bf16[2,160,960]{2,1,0:T(8,128)(2,1)}, bf16[2,160,960]{2,1,0:T(8,128)(2,1)}, u32[]{:S(2)}, u32[]{:S(2)}) %collective-permute-start.14) | collective-permute-done | bytes 614432 | tf_op jit(solution)/shard_map/ppermute | solution.py:141
  185.4 4.3 copy.113
  189.8 3.7 convolution_bitcast_fusion.1
  196.1 2.4 slice.274
  199.8 2.9 fusion.187
  203.8 3.1 slice.282
  210.1 3.3 fusion.189
  215.5 5.1 %fusion.106 = f32[128,960]{0,1:T(8,128)} fusion(bf16[1280,960]{0,1:T(8,128)(2,1)} %collective-permute-done.22, f32[128,1280]{1,0:T(8,128)} %fusion.189, bf16[1280,960]{0,1:T(8,128)(2,1)} %collective-permute-done.21, f32[128,960]{0,1:T(8,128)} %copy-done.29, f32[960]{0:T(1024)S(1)} %slice.221, f32[128]{0:T(128)S(1)} %add_rsqrt_fusion.3), kind=kOutput, calls=%fused_computation.247 | convolution fusion | flops 630497280 | bytes 6557952 | tf_op jit(solution)/shard_map/dot_general | solution.py:23
  220.6 5.6 %fusion.14 = bf16[128,960]{0,1:T(8,128)(2,1)} fusion(f32[128,960]{0,1:T(8,128)} %fusion.106, f32[128,960]{0,1:T(8,128)} %copy-done.29, bf16[1280,960]{1,0:T(8,128)(2,1)} %bitcast.38, f32[128,1280]{1,0:T(8,128)} %fusion.188, bf16[1280,960]{1,0:T(8,128)(2,1)} %bitcast.35, f32[960]{0:T(1024)S(1)} %slice.221, f32[128]{0:T(128)S(1)} %add_rsqrt_fusion.3), kind=kOutput, calls=%fused_computation.56 | convolution fusion | flops 630865920 | bytes 6803712 | tf_op jit(solution)/shard_map/dot_general | solution.py:23
  226.2 4.1 collective-permute-start.23
  230.3 2.2 convolution_bitcast_fusion
  232.5 3.5 collective-permute-done.23
  245.8 3.9 fusion.67
  249.7 3.1 fusion.107
  252.8 2.4 fusion.191
  255.2 3.4 fusion.62
  258.5 2.8 fusion.109
  261.4 2.6 fusion.108
  269.8 2.4 fusion.88
  279.3 3.7 fusion.113
  292.4 4.2 collective-permute-done.27
  296.6 3.9 fusion.59
  300.5 3.0 fusion.110
  303.5 3.3 fusion.54
  306.8 2.6 fusion.112
  309.3 2.6 fusion.111
  319.9 2.2 fusion.91
  329.9 2.1 fusion.116
  332.0 3.3 fusion.84
  347.2 3.4 collective-permute-done.44
  351.7 4.1 collective-permute-done.50
  356.7 6.2 %collective-permute-done.38 = bf16[2,4,160,128]{3,2,1,0:T(8,128)(2,1)S(1)} collective-permute-done((bf16[2,4,160,128]{3,2,1,0:T(8,128)(2,1)S(1)}, bf16[2,4,160,128]{3,2,1,0:T(8,128)(2,1)S(1)}, u32[]{:S(2)}, u32[]{:S(2)}) %collective-permute-start.38) | collective-permute-done | bytes 327712 | tf_op jit(solution)/shard_map/ppermute | solution.py:141
  362.9 5.2 %collective-permute-done.28 = bf16[2,2,2,160,128]{4,3,1,0,2:T(8,128)(2,1)S(1)} collective-permute-done((bf16[2,2,2,160,128]{4,3,1,0,2:T(8,128)(2,1)}, bf16[2,2,2,160,128]{4,3,1,0,2:T(8,128)(2,1)S(1)}, u32[]{:S(2)}, u32[]{:S(2)}) %collective-permute-start.28) | collective-permute-done | bytes 327712 | tf_op jit(solution)/shard_map/ppermute | solution.py:141
  372.0 2.4 fusion.41
  378.7 3.9 fusion.176
  382.6 3.0 copy.135
  388.3 6.2 %collective-permute-start.46 = (bf16[2,160,960]{2,1,0:T(8,128)(2,1)}, bf16[2,160,960]{2,1,0:T(8,128)(2,1)}, u32[]{:S(2)}, u32[]{:S(2)}) collective-permute-start(bf16[2,160,960]{2,1,0:T(8,128)(2,1)} %convert_element_type.310), channel_id=1, source_target_pairs={{0,4},{1,5},{2,6},{3,7},{12,8},{13,9},{14,10},{15,11},{16,20},{17,... | collective-permute-start | bytes 1843208 | tf_op jit(solution)/shard_map/ppermute | solution.py:181
  394.6 2.1 collective-permute-start.41
  396.7 2.2 fusion.28
  401.0 3.0 copy.143
  404.0 2.2 convert_element_type.316
  406.2 2.1 collective-permute-start.52
  408.4 2.1 fusion.23
  410.5 2.1 convolution_select_fusion
  416.8 2.9 copy.142
  425.2 11.9 %collective-permute-done.52 = bf16[2,160,960]{2,1,0:T(8,128)(2,1)} collective-permute-done((bf16[2,160,960]{2,1,0:T(8,128)(2,1)}, bf16[2,160,960]{2,1,0:T(8,128)(2,1)}, u32[]{:S(2)}, u32[]{:S(2)}) %collective-permute-start.52) | collective-permute-done | bytes 614432 | tf_op jit(solution)/shard_map/ppermute | solution.py:181
  439.2 12.3 %collective-permute-done.35 = bf16[2,168,960]{2,1,0:T(8,128)(2,1)S(1)} collective-permute-done((bf16[2,168,960]{2,1,0:T(8,128)(2,1)}, bf16[2,168,960]{2,1,0:T(8,128)(2,1)S(1)}, u32[]{:S(2)}, u32[]{:S(2)}) %collective-permute-start.35) | collective-permute-done | bytes 645152 | tf_op jit(solution)/shard_map/ppermute | solution.py:181
  452.9 5.2 %collective-permute-start.48 = (bf16[160,960]{1,0:T(8,128)(2,1)S(1)}, bf16[160,960]{1,0:T(8,128)(2,1)S(1)}, u32[]{:S(2)}, u32[]{:S(2)}) collective-permute-start(bf16[160,960]{1,0:T(8,128)(2,1)S(1)} %fusion.123), channel_id=1, source_target_pairs={{0,4},{1,5},{2,6},{3,7},{4,0},{5,1},{6,2},{7,3},{8,12},{9,13},{10,... | collective-permute-start | bytes 921608 | tf_op jit(solution)/shard_map/ppermute | solution.py:141
  458.6 7.3 %collective-permute-start.54 = (bf16[160,960]{1,0:T(8,128)(2,1)S(1)}, bf16[160,960]{1,0:T(8,128)(2,1)S(1)}, u32[]{:S(2)}, u32[]{:S(2)}) collective-permute-start(bf16[160,960]{1,0:T(8,128)(2,1)S(1)} %fusion.124), channel_id=1, source_target_pairs={{0,4},{1,5},{2,6},{3,7},{4,0},{5,1},{6,2},{7,3},{8,12},{9,13},{10,... | collective-permute-start | bytes 921608 | tf_op jit(solution)/shard_map/ppermute | solution.py:141
  466.2 14.1 %collective-permute-start.37 = (bf16[168,960]{1,0:T(8,128)(2,1)S(1)}, bf16[168,960]{1,0:T(8,128)(2,1)S(1)}, u32[]{:S(2)}, u32[]{:S(2)}) collective-permute-start(bf16[168,960]{1,0:T(8,128)(2,1)S(1)} %fusion.105), channel_id=1, source_target_pairs={{0,4},{1,5},{2,6},{3,7},{4,0},{5,1},{6,2},{7,3},{8,12},{9,13},{10,... | collective-permute-start | bytes 967688 | tf_op jit(solution)/shard_map/ppermute | solution.py:141
  482.2 6.1 %collective-permute-done.37 = bf16[168,960]{1,0:T(8,128)(2,1)S(1)} collective-permute-done((bf16[168,960]{1,0:T(8,128)(2,1)S(1)}, bf16[168,960]{1,0:T(8,128)(2,1)S(1)}, u32[]{:S(2)}, u32[]{:S(2)}) %collective-permute-start.37) | collective-permute-done | bytes 322592 | tf_op jit(solution)/shard_map/ppermute | solution.py:141
  (385 shorter events, 152.4 us)
Async XLA Ops:
  1.7 11.2 %collective-permute-start = (bf16[168,960]{1,0:T(8,128)(2,1)S(1)}, bf16[168,960]{1,0:T(8,128)(2,1)S(1)}, u32[]{:S(2)}, u32[]{:S(2)}) collective-permute-start(bf16[168,960]{1,0:T(8,128)(2,1)S(1)} %fusion.104), channel_id=1, source_target_pairs={{0,4},{1,5},{2,6},{3,7},{4,0},{5,1},{6,2},{7,3},{8,12},{9,13},{10,... | collective-permute-start | bytes 967688 | tf_op jit(solution)/shard_map/ppermute | solution.py:141
  14.0 16.7 %collective-permute-start.1 = (bf16[2,168,960]{2,1,0:T(8,128)(2,1)S(1)}, bf16[2,168,960]{2,1,0:T(8,128)(2,1)S(1)}, u32[]{:S(2)}, u32[]{:S(2)}) collective-permute-start(bf16[2,168,960]{2,1,0:T(8,128)(2,1)S(1)} %pad_maximum_fusion.3), channel_id=1, source_target_pairs={{0,2},{1,3},{2,0},{3,1},{4,6},{5,7},{6,4},{7,5},{8,10},{9,11},{10,... | collective-permute-start | bytes 1935368 | tf_op jit(solution)/shard_map/ppermute | solution.py:141
  32.2 9.2 %collective-permute-start.2 = (bf16[2,2,168,960]{3,2,1,0:T(8,128)(2,1)}, bf16[2,2,168,960]{3,2,1,0:T(8,128)(2,1)}, u32[]{:S(2)}, u32[]{:S(2)}) collective-permute-start(bf16[2,2,168,960]{3,2,1,0:T(8,128)(2,1)} %pad_maximum_fusion.2), channel_id=1, source_target_pairs={{4,8},{5,9},{6,10},{7,11},{8,4},{9,5},{10,6},{11,7},{20,24},{21,25... | collective-permute-start | bytes 3870728 | tf_op jit(solution)/shard_map/ppermute | solution.py:181
  35.7 12.1 %collective-permute-start.15 = (bf16[160,960]{1,0:T(8,128)(2,1)}, bf16[160,960]{1,0:T(8,128)(2,1)}, u32[]{:S(2)}, u32[]{:S(2)}) collective-permute-start(bf16[160,960]{1,0:T(8,128)(2,1)} %get-tuple-element.51), channel_id=1, source_target_pairs={{0,4},{1,5},{2,6},{3,7},{4,0},{5,1},{6,2},{7,3},{8,12},{9,13},{10,... | collective-permute-start | bytes 921608 | tf_op jit(solution)/shard_map/ppermute | solution.py:141
  38.9 16.0 %collective-permute-start.5 = (bf16[160,960]{1,0:T(8,128)(2,1)}, bf16[160,960]{1,0:T(8,128)(2,1)}, u32[]{:S(2)}, u32[]{:S(2)}) collective-permute-start(bf16[160,960]{1,0:T(8,128)(2,1)} %get-tuple-element.47), channel_id=1, source_target_pairs={{0,4},{1,5},{2,6},{3,7},{4,0},{5,1},{6,2},{7,3},{8,12},{9,13},{10,... | collective-permute-start | bytes 921608 | tf_op jit(solution)/shard_map/ppermute | solution.py:141
  38.9 20.0 %collective-permute-start.10 = (bf16[160,960]{1,0:T(8,128)(2,1)}, bf16[160,960]{1,0:T(8,128)(2,1)}, u32[]{:S(2)}, u32[]{:S(2)}) collective-permute-start(bf16[160,960]{1,0:T(8,128)(2,1)} %get-tuple-element.49), channel_id=1, source_target_pairs={{0,4},{1,5},{2,6},{3,7},{4,0},{5,1},{6,2},{7,3},{8,12},{9,13},{10,... | collective-permute-start | bytes 921608 | tf_op jit(solution)/shard_map/ppermute | solution.py:141
  41.4 57.3 %collective-permute-start.3 = (bf16[2,2,168,960]{3,2,1,0:T(8,128)(2,1)}, bf16[2,2,168,960]{3,2,1,0:T(8,128)(2,1)}, u32[]{:S(2)}, u32[]{:S(2)}) collective-permute-start(bf16[2,2,168,960]{3,2,1,0:T(8,128)(2,1)} %collective-permute-done.2), channel_id=1, source_target_pairs={{4,0},{5,1},{6,2},{7,3},{8,12},{9,13},{10,14},{11,15},{20,16},{21,... | collective-permute-start | bytes 3870728 | tf_op jit(solution)/shard_map/ppermute | solution.py:181
  49.8 10.9 %collective-permute-start.16 = (bf16[2,160,960]{2,1,0:T(8,128)(2,1)}, bf16[2,160,960]{2,1,0:T(8,128)(2,1)}, u32[]{:S(2)}, u32[]{:S(2)}) collective-permute-start(bf16[2,160,960]{2,1,0:T(8,128)(2,1)} %pad_maximum_fusion.6), channel_id=1, source_target_pairs={{4,8},{5,9},{6,10},{7,11},{8,4},{9,5},{10,6},{11,7},{20,24},{21,25... | collective-permute-start | bytes 1843208 | tf_op jit(solution)/shard_map/ppermute | solution.py:181
  52.0 46.8 %copy-start.19 = (bf16[2,1,168,960]{3,2,1,0:T(8,128)(2,1)S(1)}, bf16[2,1,168,960]{3,2,1,0:T(8,128)(2,1)}, u32[]{:S(2)}) copy-start(bf16[2,1,168,960]{3,2,1,0:T(8,128)(2,1)} %copy-done.18) | copy-start | bytes 1935364
  52.0 46.8 %copy-start.21 = (bf16[2,1,168,960]{3,2,1,0:T(8,128)(2,1)S(1)}, bf16[2,1,168,960]{3,2,1,0:T(8,128)(2,1)}, u32[]{:S(2)}) copy-start(bf16[2,1,168,960]{3,2,1,0:T(8,128)(2,1)} %copy-done.20) | copy-start | bytes 1935364
  52.6 74.0 %collective-permute-start.18 = (bf16[2,160,960]{2,1,0:T(8,128)(2,1)}, bf16[2,160,960]{2,1,0:T(8,128)(2,1)S(1)}, u32[]{:S(2)}, u32[]{:S(2)}) collective-permute-start(bf16[2,160,960]{2,1,0:T(8,128)(2,1)} %pad_maximum_fusion.6), channel_id=1, source_target_pairs={{0,2},{1,3},{2,0},{3,1},{4,6},{5,7},{6,4},{7,5},{8,10},{9,11},{10,... | collective-permute-start | bytes 1843208 | tf_op jit(solution)/shard_map/ppermute | solution.py:141
  56.0 48.5 %collective-permute-start.6 = (bf16[2,160,960]{2,1,0:T(8,128)(2,1)S(1)}, bf16[2,160,960]{2,1,0:T(8,128)(2,1)S(1)}, u32[]{:S(2)}, u32[]{:S(2)}) collective-permute-start(bf16[2,160,960]{2,1,0:T(8,128)(2,1)S(1)} %pad_maximum_fusion.4), channel_id=1, source_target_pairs={{4,8},{5,9},{6,10},{7,11},{8,4},{9,5},{10,6},{11,7},{20,24},{21,25... | collective-permute-start | bytes 1843208 | tf_op jit(solution)/shard_map/ppermute | solution.py:181
  60.0 46.8 %collective-permute-start.11 = (bf16[2,160,960]{2,1,0:T(8,128)(2,1)S(1)}, bf16[2,160,960]{2,1,0:T(8,128)(2,1)S(1)}, u32[]{:S(2)}, u32[]{:S(2)}) collective-permute-start(bf16[2,160,960]{2,1,0:T(8,128)(2,1)S(1)} %pad_maximum_fusion.5), channel_id=1, source_target_pairs={{4,8},{5,9},{6,10},{7,11},{8,4},{9,5},{10,6},{11,7},{20,24},{21,25... | collective-permute-start | bytes 1843208 | tf_op jit(solution)/shard_map/ppermute | solution.py:181
  60.7 49.3 %collective-permute-start.17 = (bf16[2,160,960]{2,1,0:T(8,128)(2,1)}, bf16[2,160,960]{2,1,0:T(8,128)(2,1)S(1)}, u32[]{:S(2)}, u32[]{:S(2)}) collective-permute-start(bf16[2,160,960]{2,1,0:T(8,128)(2,1)} %collective-permute-done.16), channel_id=1, source_target_pairs={{4,0},{5,1},{6,2},{7,3},{8,12},{9,13},{10,14},{11,15},{20,16},{21,... | collective-permute-start | bytes 1843208 | tf_op jit(solution)/shard_map/ppermute | solution.py:181
  102.8 90.7 %collective-permute-start.4 = (bf16[2,2,2,168,960]{4,3,2,1,0:T(8,128)(2,1)}, bf16[2,2,2,168,960]{4,3,2,1,0:T(8,128)(2,1)}, u32[]{:S(2)}, u32[]{:S(2)}) collective-permute-start(bf16[2,2,2,168,960]{4,3,2,1,0:T(8,128)(2,1)} %pad_maximum_fusion.1), channel_id=1, source_target_pairs={{0,1},{1,0},{2,3},{3,2},{4,5},{5,4},{6,7},{7,6},{8,9},{9,8},{10,11... | collective-permute-start | bytes 7741448 | tf_op jit(solution)/shard_map/ppermute | solution.py:141
  104.5 19.4 %collective-permute-start.7 = (bf16[2,160,960]{2,1,0:T(8,128)(2,1)S(1)}, bf16[2,160,960]{2,1,0:T(8,128)(2,1)S(1)}, u32[]{:S(2)}, u32[]{:S(2)}) collective-permute-start(bf16[2,160,960]{2,1,0:T(8,128)(2,1)S(1)} %collective-permute-done.6), channel_id=1, source_target_pairs={{4,0},{5,1},{6,2},{7,3},{8,12},{9,13},{10,14},{11,15},{20,16},{21,... | collective-permute-start | bytes 1843208 | tf_op jit(solution)/shard_map/ppermute | solution.py:181
  106.8 30.8 %collective-permute-start.12 = (bf16[2,160,960]{2,1,0:T(8,128)(2,1)S(1)}, bf16[2,160,960]{2,1,0:T(8,128)(2,1)S(1)}, u32[]{:S(2)}, u32[]{:S(2)}) collective-permute-start(bf16[2,160,960]{2,1,0:T(8,128)(2,1)S(1)} %collective-permute-done.11), channel_id=1, source_target_pairs={{4,0},{5,1},{6,2},{7,3},{8,12},{9,13},{10,14},{11,15},{20,16},{21,... | collective-permute-start | bytes 1843208 | tf_op jit(solution)/shard_map/ppermute | solution.py:181
  110.0 30.4 %collective-permute-start.8 = (bf16[2,160,960]{2,1,0:T(8,128)(2,1)S(1)}, bf16[2,160,960]{2,1,0:T(8,128)(2,1)S(1)}, u32[]{:S(2)}, u32[]{:S(2)}) collective-permute-start(bf16[2,160,960]{2,1,0:T(8,128)(2,1)S(1)} %pad_maximum_fusion.4), channel_id=1, source_target_pairs={{0,2},{1,3},{2,0},{3,1},{4,6},{5,7},{6,4},{7,5},{8,10},{9,11},{10,... | collective-permute-start | bytes 1843208 | tf_op jit(solution)/shard_map/ppermute | solution.py:141
  123.9 18.0 %collective-permute-start.13 = (bf16[2,160,960]{2,1,0:T(8,128)(2,1)S(1)}, bf16[2,160,960]{2,1,0:T(8,128)(2,1)S(1)}, u32[]{:S(2)}, u32[]{:S(2)}) collective-permute-start(bf16[2,160,960]{2,1,0:T(8,128)(2,1)S(1)} %pad_maximum_fusion.5), channel_id=1, source_target_pairs={{0,2},{1,3},{2,0},{3,1},{4,6},{5,7},{6,4},{7,5},{8,10},{9,11},{10,... | collective-permute-start | bytes 1843208 | tf_op jit(solution)/shard_map/ppermute | solution.py:141
  126.6 29.0 %collective-permute-start.19 = (bf16[2,160,960]{2,1,0:T(8,128)(2,1)S(1)}, bf16[2,160,960]{2,1,0:T(8,128)(2,1)S(1)}, u32[]{:S(2)}, u32[]{:S(2)}) collective-permute-start(bf16[2,160,960]{2,1,0:T(8,128)(2,1)S(1)} %get-tuple-element.29), channel_id=1, source_target_pairs={{0,2},{1,3},{2,0},{3,1},{4,6},{5,7},{6,4},{7,5},{8,10},{9,11},{10,... | collective-permute-start | bytes 1843208 | tf_op jit(solution)/shard_map/ppermute | solution.py:141
  137.6 32.2 %collective-permute-start.9 = (bf16[2,160,960]{2,1,0:T(8,128)(2,1)}, bf16[2,160,960]{2,1,0:T(8,128)(2,1)}, u32[]{:S(2)}, u32[]{:S(2)}) collective-permute-start(bf16[2,160,960]{2,1,0:T(8,128)(2,1)} %get-tuple-element.25), channel_id=1, source_target_pairs={{0,2},{1,3},{2,0},{3,1},{4,6},{5,7},{6,4},{7,5},{8,10},{9,11},{10,... | collective-permute-start | bytes 1843208 | tf_op jit(solution)/shard_map/ppermute | solution.py:141
  140.4 43.0 %collective-permute-start.14 = (bf16[2,160,960]{2,1,0:T(8,128)(2,1)}, bf16[2,160,960]{2,1,0:T(8,128)(2,1)}, u32[]{:S(2)}, u32[]{:S(2)}) collective-permute-start(bf16[2,160,960]{2,1,0:T(8,128)(2,1)} %get-tuple-element.27), channel_id=1, source_target_pairs={{0,2},{1,3},{2,0},{3,1},{4,6},{5,7},{6,4},{7,5},{8,10},{9,11},{10,... | collective-permute-start | bytes 1843208 | tf_op jit(solution)/shard_map/ppermute | solution.py:141
  160.9 54.6 %collective-permute-start.22 = (bf16[1280,960]{0,1:T(8,128)(2,1)}, bf16[1280,960]{0,1:T(8,128)(2,1)}, u32[]{:S(2)}, u32[]{:S(2)}) collective-permute-start(bf16[1280,960]{0,1:T(8,128)(2,1)} %copy.114), channel_id=1, source_target_pairs={{0,1},{1,0},{2,3},{3,2},{4,5},{5,4},{6,7},{7,6},{8,9},{9,8},{10,11... | collective-permute-start | bytes 7372808 | tf_op jit(solution)/shard_map/ppermute | solution.py:141
  173.6 36.5 %collective-permute-start.20 = (bf16[1280,960]{0,1:T(8,128)(2,1)}, bf16[1280,960]{0,1:T(8,128)(2,1)}, u32[]{:S(2)}, u32[]{:S(2)}) collective-permute-start(bf16[1280,960]{0,1:T(8,128)(2,1)} %copy.112), channel_id=1, source_target_pairs={{0,1},{1,0},{2,3},{3,2},{4,5},{5,4},{6,7},{7,6},{8,9},{9,8},{10,11... | collective-permute-start | bytes 7372808 | tf_op jit(solution)/shard_map/ppermute | solution.py:141
  189.7 25.7 %collective-permute-start.21 = (bf16[1280,960]{0,1:T(8,128)(2,1)}, bf16[1280,960]{0,1:T(8,128)(2,1)}, u32[]{:S(2)}, u32[]{:S(2)}) collective-permute-start(bf16[1280,960]{0,1:T(8,128)(2,1)} %copy.113), channel_id=1, source_target_pairs={{0,1},{1,0},{2,3},{3,2},{4,5},{5,4},{6,7},{7,6},{8,9},{9,8},{10,11... | collective-permute-start | bytes 7372808 | tf_op jit(solution)/shard_map/ppermute | solution.py:141
  226.2 9.8 %collective-permute-start.23 = (bf16[128,960]{0,1:T(8,128)(2,1)}, bf16[128,960]{0,1:T(8,128)(2,1)S(1)}, u32[]{:S(2)}, u32[]{:S(2)}) collective-permute-start(bf16[128,960]{0,1:T(8,128)(2,1)} %fusion.14), channel_id=1, source_target_pairs={{0,16},{1,17},{2,18},{3,19},{4,20},{5,21},{6,22},{7,23},{8,24},{9,... | collective-permute-start | bytes 737288 | tf_op jit(solution)/shard_map/ppermute | solution.py:334
  236.1 33.7 %copy-start.32 = (bf16[128,960]{0,1:T(8,128)(2,1)}, bf16[128,960]{0,1:T(8,128)(2,1)S(1)}, u32[]{:S(2)}) copy-start(bf16[128,960]{0,1:T(8,128)(2,1)S(1)} %get-tuple-element.23) | copy-start | bytes 737284
  239.7 27.2 %copy-start.48 = (bf16[128,5,3,32]{0,3,2,1:T(8,128)(2,1)}, bf16[128,5,3,32]{0,3,2,1:T(8,128)(2,1)S(1)}, u32[]{:S(2)}) copy-start(bf16[128,5,3,32]{0,3,2,1:T(8,128)(2,1)S(1)} %get-tuple-element.77) | copy-start | bytes 368644
  239.7 27.2 %copy-start.50 = (bf16[128,5,3,32]{0,3,2,1:T(8,128)(2,1)}, bf16[128,5,3,32]{0,3,2,1:T(8,128)(2,1)S(1)}, u32[]{:S(2)}) copy-start(bf16[128,5,3,32]{0,3,2,1:T(8,128)(2,1)S(1)} %get-tuple-element.78) | copy-start | bytes 368644
  239.8 27.5 %copy-start.56 = (bf16[128,5,32]{0,2,1:T(8,128)(2,1)}, bf16[128,5,32]{0,2,1:T(8,128)(2,1)S(1)}, u32[]{:S(2)}) copy-start(bf16[128,5,32]{0,2,1:T(8,128)(2,1)S(1)} %get-tuple-element.86) | copy-start | bytes 122884
  240.1 26.5 %copy-start.5 = (f32[5,3,128,128]{2,3,1,0:T(8,128)}, f32[5,3,128,128]{2,3,1,0:T(8,128)S(1)}, u32[]{:S(2)}) copy-start(f32[5,3,128,128]{2,3,1,0:T(8,128)S(1)} %get-tuple-element.101) | copy-start | bytes 2949124
  267.5 15.8 %collective-permute-start.24 = (bf16[128,960]{0,1:T(8,128)(2,1)}, bf16[128,960]{0,1:T(8,128)(2,1)}, u32[]{:S(2)}, u32[]{:S(2)}) collective-permute-start(bf16[128,960]{0,1:T(8,128)(2,1)} %multiply_convert_fusion.14), channel_id=1, source_target_pairs={{0,2},{1,3},{2,0},{3,1},{4,6},{5,7},{6,4},{7,5},{8,10},{9,11},{10,... | collective-permute-start | bytes 737288 | tf_op jit(solution)/shard_map/ppermute | solution.py:141
  269.1 16.1 %collective-permute-start.25 = (bf16[128,960]{0,1:T(8,128)(2,1)}, bf16[128,960]{0,1:T(8,128)(2,1)}, u32[]{:S(2)}, u32[]{:S(2)}) collective-permute-start(bf16[128,960]{0,1:T(8,128)(2,1)} %fusion.87), channel_id=1, source_target_pairs={{0,2},{1,3},{2,0},{3,1},{4,6},{5,7},{6,4},{7,5},{8,10},{9,11},{10,... | collective-permute-start | bytes 737288 | tf_op jit(solution)/shard_map/ppermute | solution.py:141
  277.8 9.8 %collective-permute-start.26 = (bf16[2,4,160,128]{3,2,1,0:T(8,128)(2,1)S(1)}, bf16[2,4,160,128]{3,2,1,0:T(8,128)(2,1)S(1)}, u32[]{:S(2)}, u32[]{:S(2)}) collective-permute-start(bf16[2,4,160,128]{3,2,1,0:T(8,128)(2,1)S(1)} %get-tuple-element.72), channel_id=1, source_target_pairs={{0,2},{1,3},{2,0},{3,1},{4,6},{5,7},{6,4},{7,5},{8,10},{9,11},{10,... | collective-permute-start | bytes 983048 | tf_op jit(solution)/shard_map/ppermute | solution.py:141
  287.7 8.9 %collective-permute-start.27 = (bf16[128,960]{0,1:T(8,128)(2,1)S(1)}, bf16[128,960]{0,1:T(8,128)(2,1)S(1)}, u32[]{:S(2)}, u32[]{:S(2)}) collective-permute-start(bf16[128,960]{0,1:T(8,128)(2,1)S(1)} %fusion.80), channel_id=1, source_target_pairs={{16,0},{17,1},{18,2},{19,3},{20,4},{21,5},{22,6},{23,7},{24,8},{25... | collective-permute-start | bytes 737288 | tf_op jit(solution)/shard_map/ppermute | solution.py:342
  289.0 121.5 %collective-permute-start.30 = (bf16[256,960]{0,1:T(8,128)(2,1)}, bf16[256,960]{0,1:T(8,128)(2,1)}, u32[]{:S(2)}, u32[]{:S(2)}) collective-permute-start(bf16[256,960]{0,1:T(8,128)(2,1)} %pad_maximum_fusion.11), channel_id=1, source_target_pairs={{0,1},{1,0},{2,3},{3,2},{4,5},{5,4},{6,7},{7,6},{8,9},{9,8},{10,11... | collective-permute-start | bytes 1474568 | tf_op jit(solution)/shard_map/ppermute | solution.py:141
  290.0 98.4 %collective-permute-start.49 = (bf16[4,160,256]{2,1,0:T(8,128)(2,1)}, bf16[4,160,256]{2,1,0:T(8,128)(2,1)}, u32[]{:S(2)}, u32[]{:S(2)}) collective-permute-start(bf16[4,160,256]{2,1,0:T(8,128)(2,1)} %get-tuple-element.66), channel_id=1, source_target_pairs={{0,1},{1,0},{2,3},{3,2},{4,5},{5,4},{6,7},{7,6},{8,9},{9,8},{10,11... | collective-permute-start | bytes 983048 | tf_op jit(solution)/shard_map/ppermute | solution.py:141
  290.5 50.6 %collective-permute-start.40 = (bf16[256,960]{0,1:T(8,128)(2,1)}, bf16[256,960]{0,1:T(8,128)(2,1)}, u32[]{:S(2)}, u32[]{:S(2)}) collective-permute-start(bf16[256,960]{0,1:T(8,128)(2,1)} %pad_maximum_fusion.10), channel_id=1, source_target_pairs={{0,1},{1,0},{2,3},{3,2},{4,5},{5,4},{6,7},{7,6},{8,9},{9,8},{10,11... | collective-permute-start | bytes 1474568 | tf_op jit(solution)/shard_map/ppermute | solution.py:141
  318.3 25.9 %collective-permute-start.31 = (bf16[128,960]{0,1:T(8,128)(2,1)}, bf16[128,960]{0,1:T(8,128)(2,1)}, u32[]{:S(2)}, u32[]{:S(2)}) collective-permute-start(bf16[128,960]{0,1:T(8,128)(2,1)} %fusion.147), channel_id=1, source_target_pairs={{0,2},{1,3},{2,0},{3,1},{4,6},{5,7},{6,4},{7,5},{8,10},{9,11},{10,... | collective-permute-start | bytes 737288 | tf_op jit(solution)/shard_map/ppermute | solution.py:141
  322.3 13.9 %collective-permute-start.33 = (f32[1920]{0:T(1024)S(1)}, f32[1920]{0:T(1024)S(1)}, u32[]{:S(2)}, u32[]{:S(2)}) collective-permute-start(f32[1920]{0:T(1024)S(1)} %pad_maximum_fusion.29), channel_id=1, source_target_pairs={{0,1},{1,0},{2,3},{3,2},{4,5},{5,4},{6,7},{7,6},{8,9},{9,8},{10,11... | collective-permute-start | bytes 23048 | tf_op jit(solution)/shard_map/ppermute | solution.py:141
  336.2 3.7 collective-permute-start.34
  339.9 10.7 %collective-permute-start.44 = (bf16[2,4,160,128]{3,2,1,0:T(8,128)(2,1)S(1)}, bf16[2,4,160,128]{3,2,1,0:T(8,128)(2,1)S(1)}, u32[]{:S(2)}, u32[]{:S(2)}) collective-permute-start(bf16[2,4,160,128]{3,2,1,0:T(8,128)(2,1)S(1)} %copy-done.58), channel_id=1, source_target_pairs={{0,2},{1,3},{2,0},{3,1},{4,6},{5,7},{6,4},{7,5},{8,10},{9,11},{10,... | collective-permute-start | bytes 983048 | tf_op jit(solution)/shard_map/ppermute | solution.py:141
  341.1 14.7 %collective-permute-start.50 = (bf16[128,960]{0,1:T(8,128)(2,1)S(1)}, bf16[128,960]{0,1:T(8,128)(2,1)S(1)}, u32[]{:S(2)}, u32[]{:S(2)}) collective-permute-start(bf16[128,960]{0,1:T(8,128)(2,1)S(1)} %copy-done.42), channel_id=1, source_target_pairs={{0,2},{1,3},{2,0},{3,1},{4,6},{5,7},{6,4},{7,5},{8,10},{9,11},{10,... | collective-permute-start | bytes 737288 | tf_op jit(solution)/shard_map/ppermute | solution.py:141
  344.2 18.6 %collective-permute-start.38 = (bf16[2,4,160,128]{3,2,1,0:T(8,128)(2,1)S(1)}, bf16[2,4,160,128]{3,2,1,0:T(8,128)(2,1)S(1)}, u32[]{:S(2)}, u32[]{:S(2)}) collective-permute-start(bf16[2,4,160,128]{3,2,1,0:T(8,128)(2,1)S(1)} %copy-done.59), channel_id=1, source_target_pairs={{0,2},{1,3},{2,0},{3,1},{4,6},{5,7},{6,4},{7,5},{8,10},{9,11},{10,... | collective-permute-start | bytes 983048 | tf_op jit(solution)/shard_map/ppermute | solution.py:141
  350.6 17.6 %collective-permute-start.28 = (bf16[2,2,2,160,128]{4,3,1,0,2:T(8,128)(2,1)}, bf16[2,2,2,160,128]{4,3,1,0,2:T(8,128)(2,1)S(1)}, u32[]{:S(2)}, u32[]{:S(2)}) collective-permute-start(bf16[2,2,2,160,128]{4,3,1,0,2:T(8,128)(2,1)} %bitcast.408), channel_id=1, source_target_pairs={{0,2},{1,3},{2,0},{3,1},{4,6},{5,7},{6,4},{7,5},{8,10},{9,11},{10,... | collective-permute-start | bytes 983048 | tf_op jit(solution)/shard_map/ppermute | solution.py:141
  355.8 13.1 %collective-permute-start.45 = (bf16[4,160,256]{2,1,0:T(8,128)(2,1)S(1)}, bf16[4,160,256]{2,1,0:T(8,128)(2,1)S(1)}, u32[]{:S(2)}, u32[]{:S(2)}) collective-permute-start(bf16[4,160,256]{2,1,0:T(8,128)(2,1)S(1)} %get-tuple-element.62), channel_id=1, source_target_pairs={{0,1},{1,0},{2,3},{3,2},{4,5},{5,4},{6,7},{7,6},{8,9},{9,8},{10,11... | collective-permute-start | bytes 983048 | tf_op jit(solution)/shard_map/ppermute | solution.py:141
  362.8 45.5 %collective-permute-start.32 = (bf16[256,960]{0,1:T(8,128)(2,1)}, bf16[256,960]{0,1:T(8,128)(2,1)}, u32[]{:S(2)}, u32[]{:S(2)}) collective-permute-start(bf16[256,960]{0,1:T(8,128)(2,1)} %pad_maximum_fusion.12), channel_id=1, source_target_pairs={{0,1},{1,0},{2,3},{3,2},{4,5},{5,4},{6,7},{7,6},{8,9},{9,8},{10,11... | collective-permute-start | bytes 1474568 | tf_op jit(solution)/shard_map/ppermute | solution.py:141
  368.1 26.5 %collective-permute-start.51 = (bf16[256,960]{0,1:T(8,128)(2,1)}, bf16[256,960]{0,1:T(8,128)(2,1)}, u32[]{:S(2)}, u32[]{:S(2)}) collective-permute-start(bf16[256,960]{0,1:T(8,128)(2,1)} %pad_maximum_fusion.13), channel_id=1, source_target_pairs={{0,1},{1,0},{2,3},{3,2},{4,5},{5,4},{6,7},{7,6},{8,9},{9,8},{10,11... | collective-permute-start | bytes 1474568 | tf_op jit(solution)/shard_map/ppermute | solution.py:141
  368.9 3.1 collective-permute-start.39
  372.0 34.3 %collective-permute-start.29 = (bf16[2,2,160,256]{3,2,1,0:T(8,128)(2,1)}, bf16[2,2,160,256]{3,2,1,0:T(8,128)(2,1)S(1)}, u32[]{:S(2)}, u32[]{:S(2)}) collective-permute-start(bf16[2,2,160,256]{3,2,1,0:T(8,128)(2,1)} %get-tuple-element.68), channel_id=1, source_target_pairs={{0,1},{1,0},{2,3},{3,2},{4,5},{5,4},{6,7},{7,6},{8,9},{9,8},{10,11... | collective-permute-start | bytes 983048 | tf_op jit(solution)/shard_map/ppermute | solution.py:141
  388.3 31.3 %collective-permute-start.46 = (bf16[2,160,960]{2,1,0:T(8,128)(2,1)}, bf16[2,160,960]{2,1,0:T(8,128)(2,1)}, u32[]{:S(2)}, u32[]{:S(2)}) collective-permute-start(bf16[2,160,960]{2,1,0:T(8,128)(2,1)} %convert_element_type.310), channel_id=1, source_target_pairs={{0,4},{1,5},{2,6},{3,7},{12,8},{13,9},{14,10},{15,11},{16,20},{17,... | collective-permute-start | bytes 1843208 | tf_op jit(solution)/shard_map/ppermute | solution.py:181
  394.6 28.5 %collective-permute-start.41 = (bf16[2,160,960]{2,1,0:T(8,128)(2,1)}, bf16[2,160,960]{2,1,0:T(8,128)(2,1)}, u32[]{:S(2)}, u32[]{:S(2)}) collective-permute-start(bf16[2,160,960]{2,1,0:T(8,128)(2,1)} %convert_element_type.302), channel_id=1, source_target_pairs={{0,4},{1,5},{2,6},{3,7},{12,8},{13,9},{14,10},{15,11},{16,20},{17,... | collective-permute-start | bytes 1843208 | tf_op jit(solution)/shard_map/ppermute | solution.py:181
  406.2 30.9 %collective-permute-start.52 = (bf16[2,160,960]{2,1,0:T(8,128)(2,1)}, bf16[2,160,960]{2,1,0:T(8,128)(2,1)}, u32[]{:S(2)}, u32[]{:S(2)}) collective-permute-start(bf16[2,160,960]{2,1,0:T(8,128)(2,1)} %convert_element_type.316), channel_id=1, source_target_pairs={{0,4},{1,5},{2,6},{3,7},{12,8},{13,9},{14,10},{15,11},{16,20},{17,... | collective-permute-start | bytes 1843208 | tf_op jit(solution)/shard_map/ppermute | solution.py:181
  415.4 36.1 %collective-permute-start.35 = (bf16[2,168,960]{2,1,0:T(8,128)(2,1)}, bf16[2,168,960]{2,1,0:T(8,128)(2,1)S(1)}, u32[]{:S(2)}, u32[]{:S(2)}) collective-permute-start(bf16[2,168,960]{2,1,0:T(8,128)(2,1)} %bitcast_convert_fusion), channel_id=1, source_target_pairs={{0,4},{1,5},{2,6},{3,7},{12,8},{13,9},{14,10},{15,11},{16,20},{17,... | collective-permute-start | bytes 1935368 | tf_op jit(solution)/shard_map/ppermute | solution.py:181
  421.0 30.4 %copy-start.9 = (f32[4,168,960]{2,1,0:T(8,128)S(1)}, f32[4,168,960]{2,1,0:T(8,128)}, u32[]{:S(2)}) copy-start(f32[4,168,960]{2,1,0:T(8,128)} %copy-done.8) | copy-start | bytes 7741444
  421.0 31.5 %collective-permute-start.47 = (bf16[2,160,960]{2,1,0:T(8,128)(2,1)S(1)}, bf16[2,160,960]{2,1,0:T(8,128)(2,1)S(1)}, u32[]{:S(2)}, u32[]{:S(2)}) collective-permute-start(bf16[2,160,960]{2,1,0:T(8,128)(2,1)S(1)} %add_convert_fusion.1), channel_id=1, source_target_pairs={{4,8},{5,9},{6,10},{7,11},{8,4},{9,5},{10,6},{11,7},{20,24},{21,25... | collective-permute-start | bytes 1843208 | tf_op jit(solution)/shard_map/ppermute | solution.py:181
  424.4 28.2 %copy-start.26 = (f32[320,960]{1,0:T(8,128)S(1)}, f32[320,960]{1,0:T(8,128)}, u32[]{:S(2)}) copy-start(f32[320,960]{1,0:T(8,128)} %copy.140) | copy-start | bytes 3686404
  424.4 33.7 %collective-permute-start.42 = (bf16[2,160,960]{2,1,0:T(8,128)(2,1)S(1)}, bf16[2,160,960]{2,1,0:T(8,128)(2,1)S(1)}, u32[]{:S(2)}, u32[]{:S(2)}) collective-permute-start(bf16[2,160,960]{2,1,0:T(8,128)(2,1)S(1)} %add_convert_fusion.2), channel_id=1, source_target_pairs={{4,8},{5,9},{6,10},{7,11},{8,4},{9,5},{10,6},{11,7},{20,24},{21,25... | collective-permute-start | bytes 1843208 | tf_op jit(solution)/shard_map/ppermute | solution.py:181
  438.4 20.0 %collective-permute-start.53 = (bf16[2,160,960]{2,1,0:T(8,128)(2,1)S(1)}, bf16[2,160,960]{2,1,0:T(8,128)(2,1)S(1)}, u32[]{:S(2)}, u32[]{:S(2)}) collective-permute-start(bf16[2,160,960]{2,1,0:T(8,128)(2,1)S(1)} %add_convert_fusion), channel_id=1, source_target_pairs={{4,8},{5,9},{6,10},{7,11},{8,4},{9,5},{10,6},{11,7},{20,24},{21,25... | collective-permute-start | bytes 1843208 | tf_op jit(solution)/shard_map/ppermute | solution.py:181
  451.7 14.2 %collective-permute-start.36 = (bf16[2,168,960]{2,1,0:T(8,128)(2,1)S(1)}, bf16[2,168,960]{2,1,0:T(8,128)(2,1)S(1)}, u32[]{:S(2)}, u32[]{:S(2)}) collective-permute-start(bf16[2,168,960]{2,1,0:T(8,128)(2,1)S(1)} %fusion), channel_id=1, source_target_pairs={{4,8},{5,9},{6,10},{7,11},{8,4},{9,5},{10,6},{11,7},{20,24},{21,25... | collective-permute-start | bytes 1935368 | tf_op jit(solution)/shard_map/ppermute | solution.py:181
  452.9 27.5 %collective-permute-start.48 = (bf16[160,960]{1,0:T(8,128)(2,1)S(1)}, bf16[160,960]{1,0:T(8,128)(2,1)S(1)}, u32[]{:S(2)}, u32[]{:S(2)}) collective-permute-start(bf16[160,960]{1,0:T(8,128)(2,1)S(1)} %fusion.123), channel_id=1, source_target_pairs={{0,4},{1,5},{2,6},{3,7},{4,0},{5,1},{6,2},{7,3},{8,12},{9,13},{10,... | collective-permute-start | bytes 921608 | tf_op jit(solution)/shard_map/ppermute | solution.py:141
  458.3 22.1 %collective-permute-start.43 = (bf16[160,960]{1,0:T(8,128)(2,1)S(1)}, bf16[160,960]{1,0:T(8,128)(2,1)S(1)}, u32[]{:S(2)}, u32[]{:S(2)}) collective-permute-start(bf16[160,960]{1,0:T(8,128)(2,1)S(1)} %fusion.122), channel_id=1, source_target_pairs={{0,4},{1,5},{2,6},{3,7},{4,0},{5,1},{6,2},{7,3},{8,12},{9,13},{10,... | collective-permute-start | bytes 921608 | tf_op jit(solution)/shard_map/ppermute | solution.py:141
  458.6 21.9 %collective-permute-start.54 = (bf16[160,960]{1,0:T(8,128)(2,1)S(1)}, bf16[160,960]{1,0:T(8,128)(2,1)S(1)}, u32[]{:S(2)}, u32[]{:S(2)}) collective-permute-start(bf16[160,960]{1,0:T(8,128)(2,1)S(1)} %fusion.124), channel_id=1, source_target_pairs={{0,4},{1,5},{2,6},{3,7},{4,0},{5,1},{6,2},{7,3},{8,12},{9,13},{10,... | collective-permute-start | bytes 921608 | tf_op jit(solution)/shard_map/ppermute | solution.py:141
  466.2 22.1 %collective-permute-start.37 = (bf16[168,960]{1,0:T(8,128)(2,1)S(1)}, bf16[168,960]{1,0:T(8,128)(2,1)S(1)}, u32[]{:S(2)}, u32[]{:S(2)}) collective-permute-start(bf16[168,960]{1,0:T(8,128)(2,1)S(1)} %fusion.105), channel_id=1, source_target_pairs={{0,4},{1,5},{2,6},{3,7},{4,0},{5,1},{6,2},{7,3},{8,12},{9,13},{10,... | collective-permute-start | bytes 967688 | tf_op jit(solution)/shard_map/ppermute | solution.py:141
  (62 other events, 416.8 us)

commit v4 on v2

v4 whole, which is shorter than its diff:
```python
import jax
import jax.numpy as jnp
from jax import lax
from jax.experimental import pallas as pl
from jax.experimental.pallas import tpu as pltpu
from jax.sharding import PartitionSpec as P

QUERY_HEADS = 15
KEY_VALUE_HEADS = 5
HEAD_SIZE = 64
GROUP = QUERY_HEADS // KEY_VALUE_HEADS
Q_COLS = QUERY_HEADS * HEAD_SIZE
KV_COLS = KEY_VALUE_HEADS * HEAD_SIZE
QKV_COLS = Q_COLS + 2 * KV_COLS

epsilon = 1e-05
theta_base = 100000.0
Z2_BIT, Z1_BIT, Y_BIT, CORE_BIT = 8, 4, 2, 1
EXTRA_ROWS = 8
bf16 = jnp.bfloat16
f32 = jnp.float32


def dot_nn(a, b):
    return lax.dot_general(a, b, (((1,), (0,)), ((), ())), preferred_element_type=f32)


def dot_nt(a, b):
    return lax.dot_general(a, b, (((1,), (1,)), ((), ())), preferred_element_type=f32)


def rope(rows, cosine, sine):
    half = rows.shape[-1] // 2
    a, b = rows[..., :half], rows[..., half:]
    return jnp.concatenate([a * cosine - b * sine, b * cosine + a * sine], axis=-1)


def block_tables(segments):
    micro, block_len = segments.shape
    offsets = jnp.arange(block_len, dtype=jnp.int32)
    same = segments[:, :, None] == segments[:, None, :]
    start = jnp.min(jnp.where(same, offsets, block_len), axis=-1)
    positions = (offsets - start).astype(f32).reshape(-1)
    half = HEAD_SIZE // 2
    frequency = theta_base ** (-(2.0 * jnp.arange(half, dtype=f32)) / HEAD_SIZE)
    angles = positions[:, None] * frequency
    allowed = same & (offsets[:, None] >= offsets[None, :])
    eye = jnp.eye(micro, dtype=bool)
    full = allowed[:, :, None, :] & eye[:, None, :, None]
    total = micro * block_len
    return jnp.cos(angles), jnp.sin(angles), full.reshape(total, total)


def scores_of(q, k, allowed):
    s = jnp.einsum("tgrd,ugd->grtu", q, k, preferred_element_type=f32) * HEAD_SIZE**-0.5
    return jnp.where(allowed, s, -1000000000.0)


def forward(u, weights, tables):
    qkv_w, out_w, ffn_w, gain_one, gain_two = weights
    cosine, sine, allowed = tables
    tokens = u.shape[0]
    u = u.astype(f32)
    r1 = lax.rsqrt(jnp.mean(u * u, axis=-1, keepdims=True) + epsilon)
    n = (u * r1 * gain_one).astype(bf16)
    proj = dot_nt(n, qkv_w)
    q = rope(
        proj[:, :Q_COLS].reshape(tokens, KEY_VALUE_HEADS, GROUP, HEAD_SIZE),
        cosine[:, None, None, :],
        sine[:, None, None, :],
    ).astype(bf16)
    k = rope(
        proj[:, Q_COLS : Q_COLS + KV_COLS].reshape(tokens, KEY_VALUE_HEADS, HEAD_SIZE),
        cosine[:, None, :],
        sine[:, None, :],
    ).astype(bf16)
    v = proj[:, Q_COLS + KV_COLS :].reshape(tokens, KEY_VALUE_HEADS, HEAD_SIZE).astype(bf16)
    masked = scores_of(q, k, allowed)
    peak = jnp.max(masked, axis=-1, keepdims=True)
    lse = peak + jnp.log(jnp.sum(jnp.exp(masked - peak), axis=-1, keepdims=True))
    prob = jnp.exp(masked - lse).astype(bf16)
    o = jnp.einsum("grtu,ugd->tgrd", prob, v, preferred_element_type=f32)
    o = o.reshape(tokens, Q_COLS).astype(bf16)
    h1 = u + dot_nn(o, out_w)
    r2 = lax.rsqrt(jnp.mean(h1 * h1, axis=-1, keepdims=True) + epsilon)
    m = (h1 * r2 * gain_two).astype(bf16)
    gate, up, act, out = ffn_forward(m, h1, ffn_w)
    return out, (u, r1, n, q, k, v, lse, o, h1, r2, m, gate, up, act)


def norm_back(grad, rows, r, gain):
    scaled = grad * gain
    part = r * scaled - rows * (r * r * r) * jnp.mean(scaled * rows, axis=-1, keepdims=True)
    return part, jnp.sum(grad * rows * r, axis=0)


def backward_ffn(eb, state, weights):
    gate, up = state[11], state[12]
    return ffn_backward(eb, gate, up, weights[2])


def backward_mid(e, dm, state, weights):
    out_w, gain_two = weights[1], weights[4]
    h1, r2 = state[8], state[9]
    part, gain_two_grad = norm_back(dm, h1, r2, gain_two)
    dh1 = e.astype(f32) + part
    dz = dh1.astype(bf16)
    return dh1, dz, dot_nt(dz, out_w).astype(bf16), gain_two_grad


def backward_attention(do, state, tables):
    cosine, sine, allowed = tables
    q, k, v, lse = state[3:7]
    tokens = do.shape[0]
    do = do.reshape(tokens, KEY_VALUE_HEADS, GROUP, HEAD_SIZE)
    prob = jnp.exp(scores_of(q, k, allowed) - lse)
    dv = jnp.einsum("grtu,tgrd->ugd", prob.astype(bf16), do, preferred_element_type=f32)
    dp = jnp.einsum("tgrd,ugd->grtu", do, v, preferred_element_type=f32)
    ds = (prob * (dp - jnp.sum(dp * prob, axis=-1, keepdims=True))).astype(bf16)
    dq = jnp.einsum("grtu,ugd->tgrd", ds, k, preferred_element_type=f32) * HEAD_SIZE**-0.5
    dk = jnp.einsum("grtu,tgrd->ugd", ds, q, preferred_element_type=f32) * HEAD_SIZE**-0.5
    dq = rope(dq, cosine[:, None, None, :], -sine[:, None, None, :])
    dk = rope(dk, cosine[:, None, :], -sine[:, None, :])
    return jnp.concatenate(
        [dq.reshape(tokens, Q_COLS), dk.reshape(tokens, KV_COLS), dv.reshape(tokens, KV_COLS)],
        axis=1,
    ).astype(bf16)


def backward_in(dproj, dh1, state, weights):
    qkv_w, gain_one = weights[0], weights[3]
    u, r1 = state[0], state[1]
    part, gain_one_grad = norm_back(dot_nn(dproj, qkv_w), u, r1, gain_one)
    return dh1 + part, gain_one_grad


def backward(e, state, weights, tables):
    dgate, dup, dm = backward_ffn(e.astype(bf16), state, weights)
    dh1, dz, do, gain_two_grad = backward_mid(e, dm, state, weights)
    dproj = backward_attention(do, state, tables)
    du, gain_one_grad = backward_in(dproj, dh1, state, weights)
    pieces = (state[2], dproj, state[7], dz, state[10], dgate, dup, e.astype(bf16), state[13])
    return du, pieces, jnp.concatenate([gain_one_grad, gain_two_grad])


def ffn_forward_kernel(m_ref, h1_ref, wg_ref, wu_ref, wd_ref, gate_ref, up_ref, act_ref, out_ref):
    flat = lambda ref: ref[...].reshape(-1, ref.shape[-1])
    m = m_ref[...]
    gate = dot_nt(m, flat(wg_ref))
    up = dot_nt(m, flat(wu_ref))
    act = (gate * jax.nn.sigmoid(gate) * up).astype(bf16)
    gate_ref[...] = gate
    up_ref[...] = up
    act_ref[...] = act
    add = dot_nn(act, flat(wd_ref))

    @pl.when(pl.program_id(0) == 0)
    def _():
        out_ref[...] = h1_ref[...] + add

    @pl.when(pl.program_id(0) > 0)
    def _():
        out_ref[...] += add


def ffn_backward_kernel(
    eb_ref, gate_ref, up_ref, wg_ref, wu_ref, wd_ref, dgate_ref, dup_ref, dm_ref
):
    flat = lambda ref: ref[...].reshape(-1, ref.shape[-1])
    da = dot_nt(eb_ref[...], flat(wd_ref))
    gate = gate_ref[...]
    sig = jax.nn.sigmoid(gate)
    dgate = (da * up_ref[...] * sig * (1.0 + gate * (1.0 - sig))).astype(bf16)
    dup = (da * gate * sig).astype(bf16)
    dgate_ref[...] = dgate
    dup_ref[...] = dup
    add = dot_nn(dgate, flat(wg_ref)) + dot_nn(dup, flat(wu_ref))

    @pl.when(pl.program_id(0) == 0)
    def _():
        dm_ref[...] = add

    @pl.when(pl.program_id(0) > 0)
    def _():
        dm_ref[...] += add


def weight_spec(w, matrix):
    lines, _, _, share, width = w.shape
    return pl.BlockSpec((lines, None, None, share, width), lambda i: (0, i, matrix, 0, 0))


def ffn_call(kernel, w, wholes, blocks, out_blocks):
    lines, steps, _, share, width = w.shape
    tokens, cols = wholes[0].shape[0], lines * share
    whole = pl.BlockSpec((tokens, width), lambda i: (0, 0))
    block = pl.BlockSpec((None, tokens, cols), lambda i: (i, 0, 0))
    return pl.pallas_call(
        kernel,
        grid=(steps,),
        in_specs=[whole] * len(wholes)
        + [block] * len(blocks)
        + [weight_spec(w, matrix) for matrix in (1, 2, 3)],
        out_specs=[block] * len(out_blocks) + [whole],
        out_shape=[jax.ShapeDtypeStruct((steps, tokens, cols), t) for t in out_blocks]
        + [jax.ShapeDtypeStruct((tokens, width), f32)],
        compiler_params=pltpu.CompilerParams(
            dimension_semantics=("arbitrary",), vmem_limit_bytes=40 * 1024 * 1024
        ),
        cost_estimate=pl.CostEstimate(
            flops=6 * tokens * steps * cols * width,
            bytes_accessed=6 * steps * cols * width,
            transcendentals=tokens * steps * cols,
        ),
    )(*wholes, *blocks, w, w, w)


def ffn_forward(m, h1, w):
    if w.ndim == 5:
        return ffn_call(ffn_forward_kernel, w, (m, h1), (), (f32, f32, bf16))
    gate, up = dot_nt(m, w[0]), dot_nt(m, w[1])
    act = (jax.nn.silu(gate) * up).astype(bf16)
    return gate, up, act, h1 + dot_nn(act, w[2])


def ffn_backward(eb, gate, up, w):
    if w.ndim == 5:
        return ffn_call(ffn_backward_kernel, w, (eb,), (gate, up), (bf16, bf16))
    da = dot_nt(eb, w[2])
    sig = jax.nn.sigmoid(gate)
    dgate = (da * up * sig * (1.0 + gate * (1.0 - sig))).astype(bf16)
    dup = (da * gate * sig).astype(bf16)
    return dgate, dup, dot_nn(dgate, w[0]) + dot_nn(dup, w[1])


def flip(x, bit):
    size = lax.axis_size("dp")
    return lax.ppermute(x, "dp", [(i, i ^ bit) for i in range(size)])


def gather_small(row):
    size = lax.axis_size("dp")
    me = lax.axis_index("dp")
    bit = 1
    while bit < size:
        other = flip(row, bit)
        high = (me & bit) != 0
        row = jnp.concatenate([jnp.where(high, other, row), jnp.where(high, row, other)])
        bit *= 2
    return row


def scatter_small(row):
    size = lax.axis_size("dp")
    me = lax.axis_index("dp")
    bit = size // 2
    while bit >= 1:
        half = row.shape[0] // 2
        low, top = row[:half], row[half:]
        high = (me & bit) != 0
        row = jnp.where(high, top, low) + flip(jnp.where(high, low, top), bit)
        bit //= 2
    return row


def grads_generic(pieces):
    n, dproj, o, dz, m, dgate, dup, eb, act = pieces
    attn = jnp.concatenate([dot_nn(dproj.T, n), dot_nn(o.T, dz)], axis=0)
    both = [
        lax.psum_scatter(g, "dp", scatter_dimension=0, tiled=True)
        for g in (attn, dot_nn(dgate.T, m), dot_nn(dup.T, m), dot_nn(act.T, eb))
    ]
    return both[0], jnp.stack(both[1:])


def z_pairs(x, pairs):
    return lax.ppermute(x, "dp", [(4 * a + i, 4 * b + i) for a, b in pairs for i in range(4)])


def inner_swap(x):
    return z_pairs(x, [(1, 2), (2, 1)])


def at(x, i):
    return lax.dynamic_index_in_dim(x, i, 0, keepdims=False)


def with_other(x, bit):
    return jnp.concatenate([x, flip(x, bit)], axis=0)


def cols_y(x, y):
    x = x.reshape(2, 2, *x.shape[1:])
    return jnp.concatenate([at(x, y), flip(at(x, 1 - y), Y_BIT)], axis=1)


def cols_core(x, core):
    return jnp.concatenate([at(x, core), flip(at(x, 1 - core), CORE_BIT)], axis=0)


def product(cols, rows):
    out = lax.dot_general(cols, rows, (((0,), (0,)), ((), ())), preferred_element_type=f32)
    return out.reshape(4, -1, rows.shape[1])


def direct_send(parts, z):
    size = 4
    received = []
    for k in (2, 1, 3):
        send = at(parts, (z + k) % size).astype(bf16)
        received.append(z_pairs(send, [(a, (a + k) % size) for a in range(size)]))
    return at(parts, z), received


def direct_total(own, received):
    return own + sum(r.astype(f32) for r in received)


def line_first(parts, z2):
    parts = parts.reshape(2, 2, *parts.shape[1:])
    far = at(parts, 1 - z2)
    return at(parts, z2), far + z_pairs(far.astype(bf16), [(0, 1), (3, 2)]).astype(f32)


def line_second(near, far):
    return near + inner_swap(far.astype(bf16)).astype(f32)


def line_third(near, z1):
    return at(near, z1) + flip(at(near, 1 - z1).astype(bf16), Z1_BIT).astype(f32)


tie = lax.optimization_barrier


def last_round(e, state, early, weights, tables, me):
    n, o, m, act = state[2], state[7], state[10], state[13]
    z, y, core = me // 4, (me >> 1) & 1, me & 1
    z2, z1 = z >> 1, z & 1
    m_all, n_all, act_c = early
    tokens, width = n.shape
    eb = e.astype(bf16)
    eb_y = with_other(eb, Y_BIT)
    dgate, dup, dm = backward_ffn(eb, state, weights)
    dgate, dup, dm, eb_y = tie((dgate, dup, dm, eb_y))
    gate_y = cols_y(dgate, y)
    up_y = cols_y(dup, y)
    eb_all = with_other(eb_y, CORE_BIT)
    dh1, dz, do, gain_two_grad = backward_mid(e, dm, state, weights)
    do, dz, eb_all, gate_y = tie((do, dz, eb_all, gate_y))
    down_near, down_far = line_first(product(act_c, eb_all), z2)
    gate_c = cols_core(gate_y, core)
    dz_y = with_other(dz, Y_BIT)
    dproj = backward_attention(do, state, tables)
    dproj, gate_c, dz_y, up_y, down_near, down_far = tie(
        (dproj, gate_c, dz_y, up_y, down_near, down_far)
    )
    gate_near, gate_far = line_first(product(gate_c, m_all), z2)
    down_near = line_second(down_near, down_far)
    up_c = cols_core(up_y, core)
    share = act_c.shape[1] // 4
    attn_cols = jnp.concatenate([dproj, o], axis=1).reshape(tokens, 4, 4, share)
    attn_cols = attn_cols.transpose(2, 0, 1, 3).reshape(4, tokens, 4 * share)
    attn_y = cols_y(attn_cols, y)
    dz_all = with_other(dz_y, CORE_BIT)
    du, gain_one_grad = backward_in(dproj, dh1, state, weights)
    gain_grad = jnp.concatenate([gain_one_grad, gain_two_grad])
    gain_grad, up_c, attn_y, dz_all, gate_near, gate_far = tie(
        (gain_grad, up_c, attn_y, dz_all, gate_near, gate_far)
    )
    up_own, up_received = direct_send(product(up_c, m_all), z)
    gate_near = line_second(gate_near, gate_far)
    attn_c = cols_core(attn_y, core)
    gain_grad = gain_grad + flip(gain_grad, CORE_BIT)
    gain_grad = gain_grad + flip(gain_grad, Y_BIT)
    owners = (jnp.arange(4, dtype=jnp.int32) * 4 + y * 2 + core).reshape(4, 1, 1)
    is_qkv = owners * share < QKV_COLS
    attn = jnp.where(is_qkv, product(attn_c, n_all), product(attn_c, dz_all))
    gain_rows = at(gain_grad.reshape(4, 4, -1).transpose(1, 0, 2), y * 2 + core)[:, None]
    gain_share = gain_rows.shape[-1]
    gain_rows = jnp.pad(gain_rows, ((0, 0), (0, EXTRA_ROWS - 1), (0, width - gain_share)))
    attn_own, attn_received = direct_send(jnp.concatenate([attn, gain_rows], axis=1), z)
    attn_received, up_received = tie((attn_received, up_received))
    down = line_third(down_near, z1)
    gate = line_third(gate_near, z1)
    up = direct_total(up_own, up_received)
    attn = direct_total(attn_own, attn_received)
    return (
        du,
        attn[:share],
        jnp.stack([gate, up, down]),
        attn[share : share + 1, :gain_share],
    )


def local(edge_data, segment_ids, attn_weight, ffn_weight, gains):
    micro = segment_ids.shape[0]
    leading = lax.axis_index("section") == 0
    tables = block_tables(segment_ids)
    block, width = edge_data.shape[2], edge_data.shape[3]
    x = edge_data[0].reshape(micro * block, width)
    planes = lax.axis_size("dp") == 16
    me = lax.axis_index("dp")
    attn_own = attn_weight[0].T
    ffn_own = ffn_weight[0].swapaxes(1, 2)
    share = attn_own.shape[0]
    if planes:
        own = jnp.concatenate([attn_own[None], ffn_own], axis=0).reshape(-1, width)
        everything = lax.all_gather(own, "dp", axis=0, tiled=True).reshape(4, 4, 4, share, width)
        attn_t = everything[:, :, 0].reshape(-1, width)
        ffn_t = everything
    else:
        attn_t = lax.all_gather(attn_own, "dp", axis=0, tiled=True)
        ffn_t = lax.all_gather(ffn_own, "dp", axis=1, tiled=True)
    gain_row = gather_small(gains[0]).astype(f32)
    weights = (
        attn_t[:QKV_COLS],
        attn_t[QKV_COLS:],
        ffn_t,
        gain_row[:width],
        gain_row[width:],
    )
    first, _ = forward(x, weights, tables)
    received = lax.ppermute(first.astype(bf16), "section", [(0, 1)])
    u = jnp.where(leading, x, received)
    out, state = forward(u, weights, tables)
    first_grad, _, _ = backward(x, state, weights, tables)
    first_grad = first_grad.astype(bf16)
    if planes:
        y, core = (me >> 1) & 1, me & 1
        n, m, act = state[2], state[10], state[13]
        early = (with_other(m, Y_BIT), with_other(n, Y_BIT), cols_y(act, y))
        first_grad, early = tie((first_grad, early))
        received = lax.ppermute(first_grad, "section", [(1, 0)])
        early = (
            with_other(early[0], CORE_BIT),
            with_other(early[1], CORE_BIT),
            cols_core(early[2], core),
        )
        received, early = tie((received, early))
        e = jnp.where(leading, received, x)
        du, attn_rows, ffn_rows, gain_shard = last_round(e, state, early, weights, tables, me)
    else:
        received = lax.ppermute(first_grad, "section", [(1, 0)])
        e = jnp.where(leading, received, x)
        du, pieces, gain_grad = backward(e, state, weights, tables)
        attn_rows, ffn_rows = grads_generic(pieces)
        gain_shard = scatter_small(gain_grad)[None]
    edge_out = jnp.where(leading, du, out).astype(bf16).reshape(micro, block, width)
    return (
        edge_out[None],
        attn_rows.T[None],
        ffn_rows.swapaxes(1, 2)[None],
        gain_shard,
    )


def solution(mesh):
    in_specs = (
        P("section", None, "dp", None),
        P(None, "dp"),
        P("section", None, "dp"),
        P("section", None, None, "dp"),
        P("section", "dp"),
    )
    out_specs = (
        P("section", None, "dp", None),
        P("section", None, "dp"),
        P("section", None, None, "dp"),
        P("section", "dp"),
    )
    return jax.shard_map(local, mesh=mesh, in_specs=in_specs, out_specs=out_specs, check_vma=False)
```

time: 458 us -> 382 us (0.83); the launches traced: 453 us -> 381 us
  matrix products: 76.8 us -> 16.2 us
  waiting for transfers between devices: 230 us -> 193 us
  Pallas kernels: 0 us -> 36.4 us
  local copies, waits for them, and re-layouts: 48.2 us -> 16.4 us
  starting transfers between devices: 56.5 us -> 80.3 us
  other arithmetic: 39.1 us -> 24.4 us
  between operations: 2.47 us -> 15.3 us
    ppermute x46 -> x24, waiting for transfers between devices: 223 us -> 43.9 us  [flip(): return lax.ppermute(x, 'dp', [(i, i ^ bit) for i in range(size)])]
    all_gather x0 -> x1, waiting for transfers between devices: none -> 97.4 us  [local(): lax.all_gather(own, 'dp', axis=0, tiled=True).reshape(4, 4, 4, share, width)]
    dot_general x15 -> x4, matrix products: 46.5 us -> 2.69 us  [dot_nn(): lax.dot_general(a, b, (((1,), (0,)), ((), ())), preferred_element_type=f32)]
    ppermute x1 -> x11, waiting for transfers between devices: 5.93 us -> 45.5 us  [the longest x10 41.2 us: z_pairs(): lax.ppermute(x, 'dp', [(4 * a + i, 4 * b + i) for a, b in pairs for i in...]
    pallas_call x0 -> x4, Pallas kernels: none -> 36.4 us  [ffn_call(): pl.pallas_call(kernel, grid=(steps,), in_specs=[whole] * len(wholes) + [b...]
    dot_general x9 -> x4, matrix products: 26.3 us -> 5.39 us  [dot_nt(): lax.dot_general(a, b, (((1,), (1,)), ((), ())), preferred_element_type=f32)]
    ppermute x1 -> x11, starting transfers between devices: 1.28 us -> 21.9 us  [the longest x10 20.4 us: z_pairs(): lax.ppermute(x, 'dp', [(4 * a + i, 4 * b + i) for a, b in pairs for i in...]
    slice x13 -> x2, local copies, waits for them, and re-layouts: 22.8 us -> 3.91 us  [the longest x1 3.4 us: local(): attn_t = everything[:, :, 0].reshape(-1, width)]
  transfers between devices with their start and end apart: 48 -> 37, of which waited for: 18 -> 22; matrix products, arithmetic and copies ran while one was open for 28% -> 8% of each run, Pallas kernels for 0% -> 2%
where the time goes in v4:
time: 382 us; the launch traced here: 381 us
  waiting for transfers between devices  193 us (51%)
  starting transfers between devices  80.3 us (21%)
  Pallas kernels  36.4 us (10%)
  other arithmetic  24.4 us (6%)
  local copies, waits for them, and re-layouts  16.4 us (4%)
  matrix products  16.2 us (4%)
  between operations  15.3 us (4%)
    all_gather x1, waiting for transfers between devices, local(): lax.all_gather(own, 'dp', axis=0, tiled=True).reshape(4, 4, 4, share, width)  97.4 us
    ppermute x24, starting transfers between devices, flip(): return lax.ppermute(x, 'dp', [(i, i ^ bit) for i in range(size)])  54.8 us
    ppermute x24, waiting for transfers between devices, flip(): return lax.ppermute(x, 'dp', [(i, i ^ bit) for i in range(size)])  43.9 us
    ppermute x10, waiting for transfers between devices, z_pairs(): lax.ppermute(x, 'dp', [(4 * a + i, 4 * b + i) for a, b in pairs for i in...  41.2 us
    pallas_call x4, Pallas kernels, ffn_call(): pl.pallas_call(kernel, grid=(steps,), in_specs=[whole] * len(wholes) + [b...  36.4 us
    ppermute x10, starting transfers between devices, z_pairs(): lax.ppermute(x, 'dp', [(4 * a + i, 4 * b + i) for a, b in pairs for i in...  20.4 us
  transfers between devices with their start and end apart: 37, of which 22 were waited for; matrix products, arithmetic and copies ran while one was open for 8% of the time, Pallas kernels for 2%

profile of v4, /device:TPU:0, one launch (start us, length us, event | category | flops | bytes accessed | tf_op | source)
XLA Modules:
  0.0 381.4 jit_solution(16955347777782214884)
XLA Ops:
  7.2 2.5 pad_maximum_fusion
  11.2 2.8 collective-permute-start.1
  14.2 1.4 collective-permute-done.1
  15.7 2.1 collective-permute-start.2
  17.9 1.4 collective-permute-done.2
  19.5 3.0 collective-permute-start.3
  22.8 1.3 collective-permute-done.3
  24.4 97.4 %all-gather.2.cloned.1.call-done = bf16[10240,960]{1,0:T(8,128)(2,1)} async-done(((bf16[640,960]{1,0:T(8,128)(2,1)}), bf16[10240,960]{1,0:T(8,128)(2,1)}) %all-gather.2.cloned.1.call-update) | async-done | bytes 19660816 | tf_op jit(solution)/shard_map/all_gather | solution.py:409
  121.8 3.4 slice.119
  125.2 1.1 fusion.6
  128.2 9.6 %shard_map.84 = (f32[4,128,640]{2,1,0:T(8,128)}, f32[4,128,640]{2,1,0:T(8,128)}, bf16[4,128,640]{2,1,0:T(8,128)(2,1)}, f32[128,960]{1,0:T(8,128)S(1)}) custom-call(bf16[128,960]{1,0:T(8,128)(2,1)S(1)} %multiply_convert_fusion.3.m_ref, f32[128,960]{1,0:T(8,128)S(1)} %get-tuple-element.156.h1_ref, bf16[4,4,4,160,960]{4,3,2,1,0:T(8,128)(2,1)} %bitcast.245, ...), custom_call_target="tpu_custom_call" | custom-call | flops 1887436800 | bytes 14745600 | tf_op jit(solution)/shard_map/pallas_call | solution.py:198
  137.8 3.6 collective-permute-start.4
  141.4 5.8 %collective-permute-done.4 = bf16[128,960]{1,0:T(8,128)(2,1)S(1)} collective-permute-done((bf16[128,960]{1,0:T(8,128)(2,1)S(1)}, bf16[128,960]{1,0:T(8,128)(2,1)S(1)}, u32[]{:S(2)}, u32[]{:S(2)}) %collective-permute-start.4) | collective-permute-done | bytes 245792 | tf_op jit(solution)/shard_map/ppermute | solution.py:424
  147.5 2.9 fusion.4
  151.7 2.1 copy-done.6
  154.5 8.3 %shard_map.85 = (f32[4,128,640]{2,1,0:T(8,128)S(1)}, f32[4,128,640]{2,1,0:T(8,128)S(1)}, bf16[4,128,640]{2,1,0:T(8,128)(2,1)S(1)}, f32[128,960]{1,0:T(8,128)S(1)}) custom-call(bf16[128,960]{1,0:T(8,128)(2,1)S(1)} %multiply_convert_fusion.2.m_ref, f32[128,960]{1,0:T(8,128)S(1)} %get-tuple-element.160.h1_ref, bf16[4,4,4,160,960]{4,3,2,1,0:T(8,128)(2,1)} %bitcast.248, ...), custom_call_target="tpu_custom_call" | custom-call | flops 1887436800 | bytes 14745600 | tf_op jit(solution)/shard_map/pallas_call | solution.py:198
  163.6 9.6 %shard_map.86 = (bf16[4,128,640]{2,1,0:T(8,128)(2,1)}, bf16[4,128,640]{2,1,0:T(8,128)(2,1)}, f32[128,960]{1,0:T(8,128)S(1)}) custom-call(bf16[128,960]{1,0:T(8,128)(2,1)S(1)} %bitcast.240, f32[4,128,640]{2,1,0:T(8,128)S(1)} %get-tuple-element.48.gate_ref, f32[4,128,640]{2,1,0:T(8,128)S(1)} %get-tuple-element.49.up_ref, ...), custom_call_target="tpu_custom_call" | custom-call | flops 1887436800 | bytes 14745600 | tf_op jit(solution)/shard_map/pallas_call | solution.py:198
  175.8 1.3 collective-permute-start.5
  178.9 1.3 collective-permute-start.7
  180.2 0.9 fusion.49
  181.1 4.0 %collective-permute-done.5 = bf16[128,960]{1,0:T(8,128)(2,1)S(1)} collective-permute-done((bf16[128,960]{1,0:T(8,128)(2,1)S(1)}, bf16[128,960]{1,0:T(8,128)(2,1)S(1)}, u32[]{:S(2)}, u32[]{:S(2)}) %collective-permute-start.5) | collective-permute-done | bytes 245792 | tf_op jit(solution)/shard_map/ppermute | solution.py:238
  186.0 4.7 %collective-permute-done.6 = bf16[128,960]{1,0:T(8,128)(2,1)S(1)} collective-permute-done((bf16[128,960]{1,0:T(8,128)(2,1)S(1)}, bf16[128,960]{1,0:T(8,128)(2,1)S(1)}, u32[]{:S(2)}, u32[]{:S(2)}) %collective-permute-start.6) | collective-permute-done | bytes 245792 | tf_op jit(solution)/shard_map/ppermute | solution.py:238
  191.6 4.6 %collective-permute-done.7 = bf16[2,128,640]{2,1,0:T(8,128)(2,1)S(1)} collective-permute-done((bf16[2,128,640]{2,1,0:T(8,128)(2,1)S(1)}, bf16[2,128,640]{2,1,0:T(8,128)(2,1)S(1)}, u32[]{:S(2)}, u32[]{:S(2)}) %collective-permute-start.7) | collective-permute-done | bytes 327712 | tf_op jit(solution)/shard_map/ppermute | solution.py:238
  196.3 1.0 dynamic-slice_bitcast_fusion.15
  197.8 1.5 collective-permute-start.8
  199.3 1.1 pad_maximum_fusion.6
  200.5 1.5 pad_maximum_fusion.1
  202.0 2.4 pad_maximum_fusion.2
  204.3 4.3 %collective-permute-done.8 = bf16[128,960]{1,0:T(8,128)(2,1)S(1)} collective-permute-done((bf16[128,960]{1,0:T(8,128)(2,1)}, bf16[128,960]{1,0:T(8,128)(2,1)S(1)}, u32[]{:S(2)}, u32[]{:S(2)}) %collective-permute-start.8) | collective-permute-done | bytes 245792 | tf_op jit(solution)/shard_map/ppermute | solution.py:434
  208.7 1.3 collective-permute-start.12
  210.6 8.8 %shard_map.87 = (bf16[4,128,640]{2,1,0:T(8,128)(2,1)S(1)}, bf16[4,128,640]{2,1,0:T(8,128)(2,1)S(1)}, f32[128,960]{1,0:T(8,128)S(1)}) custom-call(bf16[128,960]{1,0:T(8,128)(2,1)S(1)} %broadcast_select_fusion.1.eb_ref, f32[4,128,640]{2,1,0:T(8,128)S(1)} %get-tuple-element.48.gate_ref, f32[4,128,640]{2,1,0:T(8,128)S(1)} %get-tuple-element.49.up_ref, ...), custom_call_target="tpu_custom_call" | custom-call | flops 1887436800 | bytes 14745600 | tf_op jit(solution)/shard_map/pallas_call | solution.py:198
  221.4 1.3 collective-permute-start.17
  223.4 7.7 %collective-permute-done.14 = bf16[2,128,640]{2,1,0:T(8,128)(2,1)S(1)} collective-permute-done((bf16[2,128,640]{2,1,0:T(8,128)(2,1)S(1)}, bf16[2,128,640]{2,1,0:T(8,128)(2,1)S(1)}, u32[]{:S(2)}, u32[]{:S(2)}) %collective-permute-start.14) | collective-permute-done | bytes 327712 | tf_op jit(solution)/shard_map/ppermute | solution.py:238
  231.1 6.5 %collective-permute-done.17 = bf16[2,128,640]{2,1,0:T(8,128)(2,1)S(1)} collective-permute-done((bf16[2,128,640]{2,1,0:T(8,128)(2,1)S(1)}, bf16[2,128,640]{2,1,0:T(8,128)(2,1)S(1)}, u32[]{:S(2)}, u32[]{:S(2)}) %collective-permute-start.17) | collective-permute-done | bytes 327712 | tf_op jit(solution)/shard_map/ppermute | solution.py:238
  242.7 3.5 collective-permute-start.18
  246.3 3.2 collective-permute-done.16
  249.6 10.9 %collective-permute-done.18 = bf16[2,160,960]{2,1,0:T(8,128)(2,1)S(1)} collective-permute-done((bf16[2,160,960]{2,1,0:T(8,128)(2,1)S(1)}, bf16[2,160,960]{2,1,0:T(8,128)(2,1)S(1)}, u32[]{:S(2)}, u32[]{:S(2)}) %collective-permute-start.18) | collective-permute-done | bytes 614432 | tf_op jit(solution)/shard_map/ppermute | solution.py:277
  262.0 1.3 collective-permute-start.20
  263.5 0.9 fusion.105
  264.5 4.4 %collective-permute-start.22 = (bf16[2,160,960]{2,1,0:T(8,128)(2,1)S(1)}, bf16[2,160,960]{2,1,0:T(8,128)(2,1)S(1)}, u32[]{:S(2)}, u32[]{:S(2)}) collective-permute-start(bf16[2,160,960]{2,1,0:T(8,128)(2,1)S(1)} %bitcast_convert_fusion), channel_id=1, source_target_pairs={{0,4},{1,5},{2,6},{3,7},{12,8},{13,9},{14,10},{15,11},{16,20},{17,... | collective-permute-start | bytes 1843208 | tf_op jit(solution)/shard_map/ppermute | solution.py:277
  269.6 1.0 fusion.53
  270.7 1.2 dynamic-slice_bitcast_fusion
  272.2 1.1 pad_maximum_fusion.4
  273.3 10.0 %collective-permute-done.22 = bf16[2,160,960]{2,1,0:T(8,128)(2,1)S(1)} collective-permute-done((bf16[2,160,960]{2,1,0:T(8,128)(2,1)S(1)}, bf16[2,160,960]{2,1,0:T(8,128)(2,1)S(1)}, u32[]{:S(2)}, u32[]{:S(2)}) %collective-permute-start.22) | collective-permute-done | bytes 614432 | tf_op jit(solution)/shard_map/ppermute | solution.py:277
  283.3 1.0 bitcast_add_fusion
  286.7 2.5 collective-permute-start.35
  289.2 0.9 fusion.106
  290.9 1.0 fusion.77
  292.0 0.9 collective-permute-start.29
  292.8 2.0 collective-permute-start.30
  294.9 1.8 collective-permute-start.31
  296.8 5.5 %collective-permute-done.35 = bf16[160,960]{1,0:T(8,128)(2,1)} collective-permute-done((bf16[160,960]{1,0:T(8,128)(2,1)}, bf16[160,960]{1,0:T(8,128)(2,1)}, u32[]{:S(2)}, u32[]{:S(2)}) %collective-permute-start.35) | collective-permute-done | bytes 307232 | tf_op jit(solution)/shard_map/ppermute | solution.py:238
  302.3 1.0 collective-permute-start.32
  303.2 1.3 fusion.42
  307.8 2.3 collective-permute-start.26
  310.1 7.8 %collective-permute-done.29 = bf16[160,960]{1,0:T(8,128)(2,1)} collective-permute-done((bf16[160,960]{1,0:T(8,128)(2,1)}, bf16[160,960]{1,0:T(8,128)(2,1)}, u32[]{:S(2)}, u32[]{:S(2)}) %collective-permute-start.29) | collective-permute-done | bytes 307232 | tf_op jit(solution)/shard_map/ppermute | solution.py:277
  317.9 3.8 %collective-permute-start.28 = (bf16[168,960]{1,0:T(8,128)(2,1)S(1)}, bf16[168,960]{1,0:T(8,128)(2,1)S(1)}, u32[]{:S(2)}, u32[]{:S(2)}) collective-permute-start(bf16[168,960]{1,0:T(8,128)(2,1)S(1)} %get-tuple-element.98), channel_id=1, source_target_pairs={{0,12},{1,13},{2,14},{3,15},{4,0},{5,1},{6,2},{7,3},{8,4},{9,5},{1... | collective-permute-start | bytes 967688 | tf_op jit(solution)/shard_map/ppermute | solution.py:277
  322.0 32.5 %collective-permute-start.33 = (bf16[160,960]{1,0:T(8,128)(2,1)S(1)}, bf16[160,960]{1,0:T(8,128)(2,1)S(1)}, u32[]{:S(2)}, u32[]{:S(2)}) collective-permute-start(bf16[160,960]{1,0:T(8,128)(2,1)S(1)} %fusion.78), channel_id=1, source_target_pairs={{0,4},{1,5},{2,6},{3,7},{4,0},{5,1},{6,2},{7,3},{8,12},{9,13},{10,... | collective-permute-start | bytes 921608 | tf_op jit(solution)/shard_map/ppermute | solution.py:238
  354.5 6.5 %collective-permute-done.26 = bf16[168,960]{1,0:T(8,128)(2,1)S(1)} collective-permute-done((bf16[168,960]{1,0:T(8,128)(2,1)S(1)}, bf16[168,960]{1,0:T(8,128)(2,1)S(1)}, u32[]{:S(2)}, u32[]{:S(2)}) %collective-permute-start.26) | collective-permute-done | bytes 322592 | tf_op jit(solution)/shard_map/ppermute | solution.py:277
  361.0 5.9 %collective-permute-done.28 = bf16[168,960]{1,0:T(8,128)(2,1)S(1)} collective-permute-done((bf16[168,960]{1,0:T(8,128)(2,1)S(1)}, bf16[168,960]{1,0:T(8,128)(2,1)S(1)}, u32[]{:S(2)}, u32[]{:S(2)}) %collective-permute-start.28) | collective-permute-done | bytes 322592 | tf_op jit(solution)/shard_map/ppermute | solution.py:277
  367.2 0.9 slice_bitcast_fusion
  368.6 1.3 fusion.43
  369.9 3.1 collective-permute-done.33
  373.2 1.4 maximum_bitcast_fusion
  (227 shorter events, 32.7 us)
Async XLA Ops:
  7.2 114.6 %all-gather.2.cloned.1.call-start = ((), (), s32[]{:S(2)}) async-start(), calls=%async_computation | async-start | bytes 22282240 | tf_op jit(solution)/shard_map/all_gather | solution.py:409
  7.2 2.6 copy-start.29
  7.2 3.1 copy-start.25
  7.2 10.5 %copy-start = (bf16[1,2,64,960]{3,2,1,0:T(8,128)(2,1)S(1)}, bf16[1,2,64,960]{3,2,1,0:T(8,128)(2,1)}, u32[]{:S(2)}) copy-start(bf16[1,2,64,960]{3,2,1,0:T(8,128)(2,1)} %param.5) | copy-start | bytes 737284
  9.8 1.3 collective-permute-start
  11.2 4.3 %collective-permute-start.1 = (bf16[240]{0:T(256)(128)(2,1)S(1)}, bf16[240]{0:T(256)(128)(2,1)S(1)}, u32[]{:S(2)}, u32[]{:S(2)}) collective-permute-start(bf16[240]{0:T(256)(128)(2,1)S(1)} %pad_maximum_fusion.32), channel_id=1, source_target_pairs={{0,2},{1,3},{2,0},{3,1},{4,6},{5,7},{6,4},{7,5},{8,10},{9,11},{10,... | collective-permute-start | bytes 1448 | tf_op jit(solution)/shard_map/ppermute | solution.py:238
  15.7 3.6 collective-permute-start.2
  19.5 4.7 %collective-permute-start.3 = (bf16[960]{0:T(1024)(128)(2,1)S(1)}, bf16[960]{0:T(1024)(128)(2,1)S(1)}, u32[]{:S(2)}, u32[]{:S(2)}) collective-permute-start(bf16[960]{0:T(1024)(128)(2,1)S(1)} %pad_maximum_fusion.30), channel_id=1, source_target_pairs={{0,8},{1,9},{2,10},{3,11},{4,12},{5,13},{6,14},{7,15},{8,0},{9,1},... | collective-permute-start | bytes 5768 | tf_op jit(solution)/shard_map/ppermute | solution.py:238
  125.2 2.4 copy-start.5
  137.8 9.4 %collective-permute-start.4 = (bf16[128,960]{1,0:T(8,128)(2,1)S(1)}, bf16[128,960]{1,0:T(8,128)(2,1)S(1)}, u32[]{:S(2)}, u32[]{:S(2)}) collective-permute-start(bf16[128,960]{1,0:T(8,128)(2,1)S(1)} %convert_element_type.215), channel_id=1, source_target_pairs={{0,16},{1,17},{2,18},{3,19},{4,20},{5,21},{6,22},{7,23},{8,24},{9,... | collective-permute-start | bytes 737288 | tf_op jit(solution)/shard_map/ppermute | solution.py:424
  147.4 32.8 %copy-start.9 = (bf16[128,960]{1,0:T(8,128)(2,1)}, bf16[128,960]{1,0:T(8,128)(2,1)S(1)}, u32[]{:S(2)}) copy-start(bf16[128,960]{1,0:T(8,128)(2,1)S(1)} %get-tuple-element.97) | copy-start | bytes 737284
  150.6 3.2 copy-start.6
  150.7 24.5 %copy-start.17 = (bf16[128,5,3,32]{0,3,2,1:T(8,128)(2,1)}, bf16[128,5,3,32]{0,3,2,1:T(8,128)(2,1)S(1)}, u32[]{:S(2)}) copy-start(bf16[128,5,3,32]{0,3,2,1:T(8,128)(2,1)S(1)} %get-tuple-element.124) | copy-start | bytes 368644
  150.7 24.5 %copy-start.19 = (bf16[128,5,3,32]{0,3,2,1:T(8,128)(2,1)}, bf16[128,5,3,32]{0,3,2,1:T(8,128)(2,1)S(1)}, u32[]{:S(2)}) copy-start(bf16[128,5,3,32]{0,3,2,1:T(8,128)(2,1)S(1)} %get-tuple-element.125) | copy-start | bytes 368644
  150.7 24.8 %copy-start.21 = (bf16[128,5,32]{0,2,1:T(8,128)(2,1)}, bf16[128,5,32]{0,2,1:T(8,128)(2,1)S(1)}, u32[]{:S(2)}) copy-start(bf16[128,5,32]{0,2,1:T(8,128)(2,1)S(1)} %get-tuple-element.132) | copy-start | bytes 122884
  150.7 24.8 %copy-start.23 = (bf16[128,5,32]{0,2,1:T(8,128)(2,1)}, bf16[128,5,32]{0,2,1:T(8,128)(2,1)S(1)}, u32[]{:S(2)}) copy-start(bf16[128,5,32]{0,2,1:T(8,128)(2,1)S(1)} %get-tuple-element.133) | copy-start | bytes 122884
  151.1 23.9 %copy-start.3 = (f32[5,3,128,128]{2,3,1,0:T(8,128)}, f32[5,3,128,128]{2,3,1,0:T(8,128)S(1)}, u32[]{:S(2)}) copy-start(f32[5,3,128,128]{2,3,1,0:T(8,128)S(1)} %get-tuple-element.158) | copy-start | bytes 2949124
  151.4 22.8 %copy-start.7 = (bf16[5,3,128,128]{2,3,1,0:T(8,128)(2,1)}, bf16[5,3,128,128]{2,3,1,0:T(8,128)(2,1)S(1)}, u32[]{:S(2)}) copy-start(bf16[5,3,128,128]{2,3,1,0:T(8,128)(2,1)S(1)} %fusion.63) | copy-start | bytes 1474564
  151.7 2.7 copy-start.15
  154.3 19.0 %copy-start.26 = (f32[128]{0:T(128)}, f32[128]{0:T(128)S(1)}, u32[]{:S(2)}) copy-start(f32[128]{0:T(128)S(1)} %get-tuple-element.151) | copy-start | bytes 1540
  175.8 9.3 %collective-permute-start.5 = (bf16[128,960]{1,0:T(8,128)(2,1)S(1)}, bf16[128,960]{1,0:T(8,128)(2,1)S(1)}, u32[]{:S(2)}, u32[]{:S(2)}) collective-permute-start(bf16[128,960]{1,0:T(8,128)(2,1)S(1)} %multiply_convert_fusion.2.m_ref), channel_id=1, source_target_pairs={{0,2},{1,3},{2,0},{3,1},{4,6},{5,7},{6,4},{7,5},{8,10},{9,11},{10,... | collective-permute-start | bytes 737288 | tf_op jit(solution)/shard_map/ppermute | solution.py:238
  177.1 13.6 %collective-permute-start.6 = (bf16[128,960]{1,0:T(8,128)(2,1)S(1)}, bf16[128,960]{1,0:T(8,128)(2,1)S(1)}, u32[]{:S(2)}, u32[]{:S(2)}) collective-permute-start(bf16[128,960]{1,0:T(8,128)(2,1)S(1)} %fusion.58), channel_id=1, source_target_pairs={{0,2},{1,3},{2,0},{3,1},{4,6},{5,7},{6,4},{7,5},{8,10},{9,11},{10,... | collective-permute-start | bytes 737288 | tf_op jit(solution)/shard_map/ppermute | solution.py:238
  178.9 17.3 %collective-permute-start.7 = (bf16[2,128,640]{2,1,0:T(8,128)(2,1)S(1)}, bf16[2,128,640]{2,1,0:T(8,128)(2,1)S(1)}, u32[]{:S(2)}, u32[]{:S(2)}) collective-permute-start(bf16[2,128,640]{2,1,0:T(8,128)(2,1)S(1)} %get-tuple-element.119), channel_id=1, source_target_pairs={{0,2},{1,3},{2,0},{3,1},{4,6},{5,7},{6,4},{7,5},{8,10},{9,11},{10,... | collective-permute-start | bytes 983048 | tf_op jit(solution)/shard_map/ppermute | solution.py:238
  196.2 4.3 %collective-permute-start.9 = (bf16[256,960]{1,0:T(8,128)(2,1)}, bf16[256,960]{1,0:T(8,128)(2,1)}, u32[]{:S(2)}, u32[]{:S(2)}) collective-permute-start(bf16[256,960]{1,0:T(8,128)(2,1)} %pad_maximum_fusion.14), channel_id=1, source_target_pairs={{0,1},{1,0},{2,3},{3,2},{4,5},{5,4},{6,7},{7,6},{8,9},{9,8},{10,11... | collective-permute-start | bytes 1474568 | tf_op jit(solution)/shard_map/ppermute | solution.py:238
  197.3 2.1 collective-permute-start.11
  197.7 4.2 %collective-permute-start.10 = (bf16[256,960]{1,0:T(8,128)(2,1)}, bf16[256,960]{1,0:T(8,128)(2,1)}, u32[]{:S(2)}, u32[]{:S(2)}) collective-permute-start(bf16[256,960]{1,0:T(8,128)(2,1)} %pad_maximum_fusion.15), channel_id=1, source_target_pairs={{0,1},{1,0},{2,3},{3,2},{4,5},{5,4},{6,7},{7,6},{8,9},{9,8},{10,11... | collective-permute-start | bytes 1474568 | tf_op jit(solution)/shard_map/ppermute | solution.py:238
  197.8 10.9 %collective-permute-start.8 = (bf16[128,960]{1,0:T(8,128)(2,1)}, bf16[128,960]{1,0:T(8,128)(2,1)S(1)}, u32[]{:S(2)}, u32[]{:S(2)}) collective-permute-start(bf16[128,960]{1,0:T(8,128)(2,1)} %fusion.49), channel_id=1, source_target_pairs={{16,0},{17,1},{18,2},{19,3},{20,4},{21,5},{22,6},{23,7},{24,8},{25... | collective-permute-start | bytes 737288 | tf_op jit(solution)/shard_map/ppermute | solution.py:434
  200.5 22.2 %slice-start = ((s8[5242880]{0:T(1024)(128)(4,1)}), s8[4194304]{0:T(1024)(128)(4,1)S(1)}, s32[]{:S(2)}) async-start(s8[5242880]{0:T(1024)(128)(4,1)} %bitcast.269), calls=%async_computation.1 | async-start | bytes 8388608
  208.7 10.7 %collective-permute-start.12 = (bf16[128,960]{1,0:T(8,128)(2,1)S(1)}, bf16[128,960]{1,0:T(8,128)(2,1)S(1)}, u32[]{:S(2)}, u32[]{:S(2)}) collective-permute-start(bf16[128,960]{1,0:T(8,128)(2,1)S(1)} %broadcast_select_fusion.1.eb_ref), channel_id=1, source_target_pairs={{0,2},{1,3},{2,0},{3,1},{4,6},{5,7},{6,4},{7,5},{8,10},{9,11},{10,... | collective-permute-start | bytes 737288 | tf_op jit(solution)/shard_map/ppermute | solution.py:238
  210.6 12.1 %slice-start.1 = ((s8[5242880]{0:T(1024)(128)(4,1)}), s8[1048576]{0:T(1024)(128)(4,1)S(1)}, s32[]{:S(2)}) async-start(s8[5242880]{0:T(1024)(128)(4,1)} %bitcast.269), calls=%async_computation.2 | async-start | bytes 2097152
  220.3 17.4 %collective-permute-start.13 = (bf16[256,960]{1,0:T(8,128)(2,1)S(1)}, bf16[256,960]{1,0:T(8,128)(2,1)S(1)}, u32[]{:S(2)}, u32[]{:S(2)}) collective-permute-start(bf16[256,960]{1,0:T(8,128)(2,1)S(1)} %pad_maximum_fusion.16), channel_id=1, source_target_pairs={{0,1},{1,0},{2,3},{3,2},{4,5},{5,4},{6,7},{7,6},{8,9},{9,8},{10,11... | collective-permute-start | bytes 1474568 | tf_op jit(solution)/shard_map/ppermute | solution.py:238
  220.5 10.6 %collective-permute-start.14 = (bf16[2,128,640]{2,1,0:T(8,128)(2,1)S(1)}, bf16[2,128,640]{2,1,0:T(8,128)(2,1)S(1)}, u32[]{:S(2)}, u32[]{:S(2)}) collective-permute-start(bf16[2,128,640]{2,1,0:T(8,128)(2,1)S(1)} %get-tuple-element.115), channel_id=1, source_target_pairs={{0,2},{1,3},{2,0},{3,1},{4,6},{5,7},{6,4},{7,5},{8,10},{9,11},{10,... | collective-permute-start | bytes 983048 | tf_op jit(solution)/shard_map/ppermute | solution.py:238
  221.4 16.3 %collective-permute-start.17 = (bf16[2,128,640]{2,1,0:T(8,128)(2,1)S(1)}, bf16[2,128,640]{2,1,0:T(8,128)(2,1)S(1)}, u32[]{:S(2)}, u32[]{:S(2)}) collective-permute-start(bf16[2,128,640]{2,1,0:T(8,128)(2,1)S(1)} %get-tuple-element.111), channel_id=1, source_target_pairs={{0,2},{1,3},{2,0},{3,1},{4,6},{5,7},{6,4},{7,5},{8,10},{9,11},{10,... | collective-permute-start | bytes 983048 | tf_op jit(solution)/shard_map/ppermute | solution.py:238
  231.1 6.7 %copy-start.8 = (bf16[5,3,128,128]{2,3,1,0:T(8,128)(2,1)S(1)}, bf16[5,3,128,128]{2,3,1,0:T(8,128)(2,1)}, u32[]{:S(2)}) copy-start(bf16[5,3,128,128]{2,3,1,0:T(8,128)(2,1)} %copy-done.7) | copy-start | bytes 1474564
  237.7 1.2 copy-start.4
  238.9 1.0 copy-start.20
  239.2 0.9 copy-start.24
  240.6 8.9 %collective-permute-start.15 = (bf16[256,640]{1,0:T(8,128)(2,1)S(1)}, bf16[256,640]{1,0:T(8,128)(2,1)S(1)}, u32[]{:S(2)}, u32[]{:S(2)}) collective-permute-start(bf16[256,640]{1,0:T(8,128)(2,1)S(1)} %get-tuple-element.113), channel_id=1, source_target_pairs={{0,1},{1,0},{2,3},{3,2},{4,5},{5,4},{6,7},{7,6},{8,9},{9,8},{10,11... | collective-permute-start | bytes 983048 | tf_op jit(solution)/shard_map/ppermute | solution.py:238
  240.7 8.7 %collective-permute-start.16 = (bf16[128,960]{1,0:T(8,128)(2,1)S(1)}, bf16[128,960]{1,0:T(8,128)(2,1)S(1)}, u32[]{:S(2)}, u32[]{:S(2)}) collective-permute-start(bf16[128,960]{1,0:T(8,128)(2,1)S(1)} %get-tuple-element.65), channel_id=1, source_target_pairs={{0,2},{1,3},{2,0},{3,1},{4,6},{5,7},{6,4},{7,5},{8,10},{9,11},{10,... | collective-permute-start | bytes 737288 | tf_op jit(solution)/shard_map/ppermute | solution.py:238
  242.7 17.7 %collective-permute-start.18 = (bf16[2,160,960]{2,1,0:T(8,128)(2,1)S(1)}, bf16[2,160,960]{2,1,0:T(8,128)(2,1)S(1)}, u32[]{:S(2)}, u32[]{:S(2)}) collective-permute-start(bf16[2,160,960]{2,1,0:T(8,128)(2,1)S(1)} %bitcast_convert_fusion.1), channel_id=1, source_target_pairs={{0,4},{1,5},{2,6},{3,7},{12,8},{13,9},{14,10},{15,11},{16,20},{17,... | collective-permute-start | bytes 1843208 | tf_op jit(solution)/shard_map/ppermute | solution.py:277
  249.5 11.2 %copy-start.10 = (bf16[128,960]{1,0:T(8,128)(2,1)S(1)}, bf16[128,960]{1,0:T(8,128)(2,1)}, u32[]{:S(2)}) copy-start(bf16[128,960]{1,0:T(8,128)(2,1)} %copy-done.9) | copy-start | bytes 737284
  260.7 0.9 copy-start.16
  261.8 10.2 %collective-permute-start.19 = (bf16[256,640]{1,0:T(8,128)(2,1)S(1)}, bf16[256,640]{1,0:T(8,128)(2,1)S(1)}, u32[]{:S(2)}, u32[]{:S(2)}) collective-permute-start(bf16[256,640]{1,0:T(8,128)(2,1)S(1)} %get-tuple-element.109), channel_id=1, source_target_pairs={{0,1},{1,0},{2,3},{3,2},{4,5},{5,4},{6,7},{7,6},{8,9},{9,8},{10,11... | collective-permute-start | bytes 983048 | tf_op jit(solution)/shard_map/ppermute | solution.py:238
  261.9 7.7 %copy-start.2 = (f32[128,960]{1,0:T(8,128)S(1)}, f32[128,960]{1,0:T(8,128)}, u32[]{:S(2)}) copy-start(f32[128,960]{1,0:T(8,128)} %copy-done.1) | copy-start | bytes 1474564
  262.0 10.2 %collective-permute-start.20 = (bf16[2,128,640]{1,2,0:T(8,128)(2,1)S(1)}, bf16[2,128,640]{1,2,0:T(8,128)(2,1)S(1)}, u32[]{:S(2)}, u32[]{:S(2)}) collective-permute-start(bf16[2,128,640]{1,2,0:T(8,128)(2,1)S(1)} %get-tuple-element.107), channel_id=1, source_target_pairs={{0,2},{1,3},{2,0},{3,1},{4,6},{5,7},{6,4},{7,5},{8,10},{9,11},{10,... | collective-permute-start | bytes 983048 | tf_op jit(solution)/shard_map/ppermute | solution.py:238
  263.3 9.0 %collective-permute-start.21 = (bf16[256,960]{1,0:T(8,128)(2,1)S(1)}, bf16[256,960]{1,0:T(8,128)(2,1)S(1)}, u32[]{:S(2)}, u32[]{:S(2)}) collective-permute-start(bf16[256,960]{1,0:T(8,128)(2,1)S(1)} %pad_maximum_fusion.17), channel_id=1, source_target_pairs={{0,1},{1,0},{2,3},{3,2},{4,5},{5,4},{6,7},{7,6},{8,9},{9,8},{10,11... | collective-permute-start | bytes 1474568 | tf_op jit(solution)/shard_map/ppermute | solution.py:238
  264.5 18.8 %collective-permute-start.22 = (bf16[2,160,960]{2,1,0:T(8,128)(2,1)S(1)}, bf16[2,160,960]{2,1,0:T(8,128)(2,1)S(1)}, u32[]{:S(2)}, u32[]{:S(2)}) collective-permute-start(bf16[2,160,960]{2,1,0:T(8,128)(2,1)S(1)} %bitcast_convert_fusion), channel_id=1, source_target_pairs={{0,4},{1,5},{2,6},{3,7},{12,8},{13,9},{14,10},{15,11},{16,20},{17,... | collective-permute-start | bytes 1843208 | tf_op jit(solution)/shard_map/ppermute | solution.py:277
  268.9 16.7 %collective-permute-start.34 = (bf16[2,160,960]{2,1,0:T(8,128)(2,1)S(1)}, bf16[2,160,960]{2,1,0:T(8,128)(2,1)S(1)}, u32[]{:S(2)}, u32[]{:S(2)}) collective-permute-start(bf16[2,160,960]{2,1,0:T(8,128)(2,1)S(1)} %bitcast_add_fusion.1), channel_id=1, source_target_pairs={{4,8},{5,9},{6,10},{7,11},{8,4},{9,5},{10,6},{11,7},{20,24},{21,25... | collective-permute-start | bytes 1843208 | tf_op jit(solution)/shard_map/ppermute | solution.py:277
  284.3 5.7 %collective-permute-start.24 = (f32[1920]{0:T(1024)S(1)}, f32[1920]{0:T(1024)S(1)}, u32[]{:S(2)}, u32[]{:S(2)}) collective-permute-start(f32[1920]{0:T(1024)S(1)} %pad_maximum_fusion.29), channel_id=1, source_target_pairs={{0,1},{1,0},{2,3},{3,2},{4,5},{5,4},{6,7},{7,6},{8,9},{9,8},{10,11... | collective-permute-start | bytes 23048 | tf_op jit(solution)/shard_map/ppermute | solution.py:238
  285.1 19.4 %collective-permute-start.23 = (bf16[256,640]{0,1:T(8,128)(2,1)}, bf16[256,640]{0,1:T(8,128)(2,1)S(1)}, u32[]{:S(2)}, u32[]{:S(2)}) collective-permute-start(bf16[256,640]{0,1:T(8,128)(2,1)} %get-tuple-element.105), channel_id=1, source_target_pairs={{0,1},{1,0},{2,3},{3,2},{4,5},{5,4},{6,7},{7,6},{8,9},{9,8},{10,11... | collective-permute-start | bytes 983048 | tf_op jit(solution)/shard_map/ppermute | solution.py:238
  285.8 4.3 %copy-start.14 = (f32[2,160,960]{2,1,0:T(8,128)}, f32[2,160,960]{2,1,0:T(8,128)S(1)}, u32[]{:S(2)}) copy-start(f32[2,160,960]{2,1,0:T(8,128)S(1)} %convert_add_fusion) | copy-start | bytes 3686404
  286.7 15.6 %collective-permute-start.35 = (bf16[160,960]{1,0:T(8,128)(2,1)}, bf16[160,960]{1,0:T(8,128)(2,1)}, u32[]{:S(2)}, u32[]{:S(2)}) collective-permute-start(bf16[160,960]{1,0:T(8,128)(2,1)} %fusion.79), channel_id=1, source_target_pairs={{0,4},{1,5},{2,6},{3,7},{4,0},{5,1},{6,2},{7,3},{8,12},{9,13},{10,... | collective-permute-start | bytes 921608 | tf_op jit(solution)/shard_map/ppermute | solution.py:238
  290.1 4.8 %collective-permute-start.25 = (f32[1920]{0:T(1024)S(1)}, f32[1920]{0:T(1024)S(1)}, u32[]{:S(2)}, u32[]{:S(2)}) collective-permute-start(f32[1920]{0:T(1024)S(1)} %add.292), channel_id=1, source_target_pairs={{0,2},{1,3},{2,0},{3,1},{4,6},{5,7},{6,4},{7,5},{8,10},{9,11},{10,... | collective-permute-start | bytes 23048 | tf_op jit(solution)/shard_map/ppermute | solution.py:238
  292.0 26.0 %collective-permute-start.29 = (bf16[160,960]{1,0:T(8,128)(2,1)}, bf16[160,960]{1,0:T(8,128)(2,1)}, u32[]{:S(2)}, u32[]{:S(2)}) collective-permute-start(bf16[160,960]{1,0:T(8,128)(2,1)} %get-tuple-element.103), channel_id=1, source_target_pairs={{0,8},{1,9},{2,10},{3,11},{4,12},{5,13},{6,14},{7,15},{8,0},{9,1},... | collective-permute-start | bytes 921608 | tf_op jit(solution)/shard_map/ppermute | solution.py:277
  292.8 29.1 %collective-permute-start.30 = (bf16[160,960]{1,0:T(8,128)(2,1)}, bf16[160,960]{1,0:T(8,128)(2,1)}, u32[]{:S(2)}, u32[]{:S(2)}) collective-permute-start(bf16[160,960]{1,0:T(8,128)(2,1)} %get-tuple-element.102), channel_id=1, source_target_pairs={{0,4},{1,5},{2,6},{3,7},{4,8},{5,9},{6,10},{7,11},{8,12},{9,13},{1... | collective-permute-start | bytes 921608 | tf_op jit(solution)/shard_map/ppermute | solution.py:277
  294.9 59.6 %collective-permute-start.31 = (bf16[160,960]{1,0:T(8,128)(2,1)}, bf16[160,960]{1,0:T(8,128)(2,1)}, u32[]{:S(2)}, u32[]{:S(2)}) collective-permute-start(bf16[160,960]{1,0:T(8,128)(2,1)} %get-tuple-element.101), channel_id=1, source_target_pairs={{0,12},{1,13},{2,14},{3,15},{4,0},{5,1},{6,2},{7,3},{8,4},{9,5},{1... | collective-permute-start | bytes 921608 | tf_op jit(solution)/shard_map/ppermute | solution.py:277
  296.8 7.8 %copy-start.12 = (bf16[512,960]{1,0:T(8,128)(2,1)S(1)}, bf16[512,960]{1,0:T(8,128)(2,1)}, u32[]{:S(2)}) copy-start(bf16[512,960]{1,0:T(8,128)(2,1)} %pad_maximum_fusion.2) | copy-start | bytes 2949124
  302.3 15.7 %collective-permute-start.32 = (bf16[2,160,960]{2,1,0:T(8,128)(2,1)}, bf16[2,160,960]{2,1,0:T(8,128)(2,1)S(1)}, u32[]{:S(2)}, u32[]{:S(2)}) collective-permute-start(bf16[2,160,960]{2,1,0:T(8,128)(2,1)} %bitcast_add_fusion), channel_id=1, source_target_pairs={{4,8},{5,9},{6,10},{7,11},{8,4},{9,5},{10,6},{11,7},{20,24},{21,25... | collective-permute-start | bytes 1843208 | tf_op jit(solution)/shard_map/ppermute | solution.py:277
  304.5 1.2 copy-start.13
  307.6 14.1 %copy-start.11 = (f32[2,160,960]{2,1,0:T(8,128)S(1)}, f32[2,160,960]{2,1,0:T(8,128)}, u32[]{:S(2)}) copy-start(f32[2,160,960]{2,1,0:T(8,128)} %dynamic-slice_bitcast_fusion) | copy-start | bytes 3686404
  307.8 53.2 %collective-permute-start.26 = (bf16[168,960]{1,0:T(8,128)(2,1)S(1)}, bf16[168,960]{1,0:T(8,128)(2,1)S(1)}, u32[]{:S(2)}, u32[]{:S(2)}) collective-permute-start(bf16[168,960]{1,0:T(8,128)(2,1)S(1)} %get-tuple-element.100), channel_id=1, source_target_pairs={{0,8},{1,9},{2,10},{3,11},{4,12},{5,13},{6,14},{7,15},{8,0},{9,1},... | collective-permute-start | bytes 967688 | tf_op jit(solution)/shard_map/ppermute | solution.py:277
  317.9 43.1 %collective-permute-start.27 = (bf16[168,960]{1,0:T(8,128)(2,1)S(1)}, bf16[168,960]{1,0:T(8,128)(2,1)S(1)}, u32[]{:S(2)}, u32[]{:S(2)}) collective-permute-start(bf16[168,960]{1,0:T(8,128)(2,1)S(1)} %get-tuple-element.99), channel_id=1, source_target_pairs={{0,4},{1,5},{2,6},{3,7},{4,8},{5,9},{6,10},{7,11},{8,12},{9,13},{1... | collective-permute-start | bytes 967688 | tf_op jit(solution)/shard_map/ppermute | solution.py:277
  317.9 49.1 %collective-permute-start.28 = (bf16[168,960]{1,0:T(8,128)(2,1)S(1)}, bf16[168,960]{1,0:T(8,128)(2,1)S(1)}, u32[]{:S(2)}, u32[]{:S(2)}) collective-permute-start(bf16[168,960]{1,0:T(8,128)(2,1)S(1)} %get-tuple-element.98), channel_id=1, source_target_pairs={{0,12},{1,13},{2,14},{3,15},{4,0},{5,1},{6,2},{7,3},{8,4},{9,5},{1... | collective-permute-start | bytes 967688 | tf_op jit(solution)/shard_map/ppermute | solution.py:277
  322.0 51.1 %collective-permute-start.33 = (bf16[160,960]{1,0:T(8,128)(2,1)S(1)}, bf16[160,960]{1,0:T(8,128)(2,1)S(1)}, u32[]{:S(2)}, u32[]{:S(2)}) collective-permute-start(bf16[160,960]{1,0:T(8,128)(2,1)S(1)} %fusion.78), channel_id=1, source_target_pairs={{0,4},{1,5},{2,6},{3,7},{4,0},{5,1},{6,2},{7,3},{8,12},{9,13},{10,... | collective-permute-start | bytes 921608 | tf_op jit(solution)/shard_map/ppermute | solution.py:238
  (5 other events, 4.1 us)
Sparse Core Ops, SparseCore 0:
  10.2 111.5 all-gather.1

commit v5 on v4

--- a/solution.py
+++ b/solution.py
@@ -56,7 +56,7 @@
     return jnp.where(allowed, s, -1000000000.0)
 
 
-def forward(u, weights, tables):
+def forward_attention(u, weights, tables):
     qkv_w, out_w, ffn_w, gain_one, gain_two = weights
     cosine, sine, allowed = tables
     tokens = u.shape[0]
@@ -84,8 +84,13 @@
     h1 = u + dot_nn(o, out_w)
     r2 = lax.rsqrt(jnp.mean(h1 * h1, axis=-1, keepdims=True) + epsilon)
     m = (h1 * r2 * gain_two).astype(bf16)
-    gate, up, act, out = ffn_forward(m, h1, ffn_w)
-    return out, (u, r1, n, q, k, v, lse, o, h1, r2, m, gate, up, act)
+    return u, r1, n, q, k, v, lse, o, h1, r2, m
+
+
+def forward(u, weights, tables):
+    state = forward_attention(u, weights, tables)
+    gate, up, act, out = ffn_forward(state[10], state[8], weights[2])
+    return out, (*state, gate, up, act)
 
 
 def norm_back(grad, rows, r, gain):
@@ -303,13 +308,18 @@
     return out.reshape(4, -1, rows.shape[1])
 
 
-def direct_send(parts, z):
-    size = 4
-    received = []
-    for k in (2, 1, 3):
-        send = at(parts, (z + k) % size).astype(bf16)
-        received.append(z_pairs(send, [(a, (a + k) % size) for a in range(size)]))
-    return at(parts, z), received
+LINE = 4
+
+
+def direct_parts(parts, z):
+    return at(parts, z), [at(parts, (z + k) % LINE).astype(bf16) for k in (2, 1, 3)]
+
+
+def direct_send(sends):
+    return [
+        z_pairs(send, [(a, (a + k) % LINE) for a in range(LINE)])
+        for k, send in zip((2, 1, 3), sends)
+    ]
 
 
 def direct_total(own, received):
@@ -333,58 +343,82 @@
 tie = lax.optimization_barrier
 
 
+def middle_rounds(u, x, weights, tables, me):
+    y, core = (me >> 1) & 1, me & 1
+    state = forward_attention(u, weights, tables)
+    n, m = state[2], state[10]
+    gate, up, act, out = ffn_forward(m, state[8], weights[2])
+    m_y, n_y = with_other(m, Y_BIT), with_other(n, Y_BIT)
+    gate, up, act, out, m_y, n_y = tie((gate, up, act, out, m_y, n_y))
+    state = (*state, gate, up, act)
+    act_y = cols_y(act, y)
+    m_all, n_all = with_other(m_y, CORE_BIT), with_other(n_y, CORE_BIT)
+    _, _, dm = backward_ffn(x, state, weights)
+    dm, act_y, m_all, n_all = tie((dm, act_y, m_all, n_all))
+    act_c = cols_core(act_y, core)
+    dh1, _, do, _ = backward_mid(x, dm, state, weights)
+    dproj = backward_attention(do, state, tables)
+    first_grad, _ = backward_in(dproj, dh1, state, weights)
+    first_grad, act_c = tie((first_grad.astype(bf16), act_c))
+    return out, state, first_grad, (m_all, n_all, act_c)
+
+
 def last_round(e, state, early, weights, tables, me):
-    n, o, m, act = state[2], state[7], state[10], state[13]
+    o = state[7]
     z, y, core = me // 4, (me >> 1) & 1, me & 1
     z2, z1 = z >> 1, z & 1
     m_all, n_all, act_c = early
-    tokens, width = n.shape
+    tokens, width = o.shape[0], e.shape[1]
+    share = act_c.shape[1] // 4
     eb = e.astype(bf16)
     eb_y = with_other(eb, Y_BIT)
     dgate, dup, dm = backward_ffn(eb, state, weights)
     dgate, dup, dm, eb_y = tie((dgate, dup, dm, eb_y))
     gate_y = cols_y(dgate, y)
-    up_y = cols_y(dup, y)
     eb_all = with_other(eb_y, CORE_BIT)
     dh1, dz, do, gain_two_grad = backward_mid(e, dm, state, weights)
-    do, dz, eb_all, gate_y = tie((do, dz, eb_all, gate_y))
-    down_near, down_far = line_first(product(act_c, eb_all), z2)
+    do, dz, eb_all, dup = tie((do, dz, eb_all, dup))
+    down_own, down_sends = direct_parts(product(act_c, eb_all), z)
+    do, down_sends = tie((do, down_sends))
+    down_two, down_one, down_three = direct_send(down_sends)
     gate_c = cols_core(gate_y, core)
-    dz_y = with_other(dz, Y_BIT)
+    up_y = cols_y(dup, y)
     dproj = backward_attention(do, state, tables)
-    dproj, gate_c, dz_y, up_y, down_near, down_far = tie(
-        (dproj, gate_c, dz_y, up_y, down_near, down_far)
-    )
+    dproj, gate_c, up_y, down_two = tie((dproj, gate_c, up_y, down_two))
     gate_near, gate_far = line_first(product(gate_c, m_all), z2)
-    down_near = line_second(down_near, down_far)
     up_c = cols_core(up_y, core)
-    share = act_c.shape[1] // 4
     attn_cols = jnp.concatenate([dproj, o], axis=1).reshape(tokens, 4, 4, share)
     attn_cols = attn_cols.transpose(2, 0, 1, 3).reshape(4, tokens, 4 * share)
     attn_y = cols_y(attn_cols, y)
+    dz_y = with_other(dz, Y_BIT)
+    gate_near, gate_far, up_c, attn_y, dz_y, down_one = tie(
+        (gate_near, gate_far, up_c, attn_y, dz_y, down_one)
+    )
+    up_near, up_far = line_first(product(up_c, m_all), z2)
+    gate_near = line_second(gate_near, gate_far)
+    attn_c = cols_core(attn_y, core)
     dz_all = with_other(dz_y, CORE_BIT)
     du, gain_one_grad = backward_in(dproj, dh1, state, weights)
     gain_grad = jnp.concatenate([gain_one_grad, gain_two_grad])
-    gain_grad, up_c, attn_y, dz_all, gate_near, gate_far = tie(
-        (gain_grad, up_c, attn_y, dz_all, gate_near, gate_far)
-    )
-    up_own, up_received = direct_send(product(up_c, m_all), z)
-    gate_near = line_second(gate_near, gate_far)
-    attn_c = cols_core(attn_y, core)
     gain_grad = gain_grad + flip(gain_grad, CORE_BIT)
     gain_grad = gain_grad + flip(gain_grad, Y_BIT)
+    attn_c, dz_all, gain_grad, up_near, up_far, gate_near, down_three = tie(
+        (attn_c, dz_all, gain_grad, up_near, up_far, gate_near, down_three)
+    )
     owners = (jnp.arange(4, dtype=jnp.int32) * 4 + y * 2 + core).reshape(4, 1, 1)
     is_qkv = owners * share < QKV_COLS
     attn = jnp.where(is_qkv, product(attn_c, n_all), product(attn_c, dz_all))
     gain_rows = at(gain_grad.reshape(4, 4, -1).transpose(1, 0, 2), y * 2 + core)[:, None]
     gain_share = gain_rows.shape[-1]
     gain_rows = jnp.pad(gain_rows, ((0, 0), (0, EXTRA_ROWS - 1), (0, width - gain_share)))
-    attn_own, attn_received = direct_send(jnp.concatenate([attn, gain_rows], axis=1), z)
-    attn_received, up_received = tie((attn_received, up_received))
-    down = line_third(down_near, z1)
+    attn_near, attn_far = line_first(jnp.concatenate([attn, gain_rows], axis=1), z2)
+    up_near = line_second(up_near, up_far)
     gate = line_third(gate_near, z1)
-    up = direct_total(up_own, up_received)
-    attn = direct_total(attn_own, attn_received)
+    down = direct_total(down_own, (down_two, down_one, down_three))
+    attn_near, attn_far, up_near, gate, down = tie((attn_near, attn_far, up_near, gate, down))
+    attn_near = line_second(attn_near, attn_far)
+    up = line_third(up_near, z1)
+    attn = line_third(attn_near, z1)
     return (
         du,
         attn[:share],
@@ -423,25 +457,15 @@
     first, _ = forward(x, weights, tables)
     received = lax.ppermute(first.astype(bf16), "section", [(0, 1)])
     u = jnp.where(leading, x, received)
-    out, state = forward(u, weights, tables)
-    first_grad, _, _ = backward(x, state, weights, tables)
-    first_grad = first_grad.astype(bf16)
     if planes:
-        y, core = (me >> 1) & 1, me & 1
-        n, m, act = state[2], state[10], state[13]
-        early = (with_other(m, Y_BIT), with_other(n, Y_BIT), cols_y(act, y))
-        first_grad, early = tie((first_grad, early))
+        out, state, first_grad, early = middle_rounds(u, x, weights, tables, me)
         received = lax.ppermute(first_grad, "section", [(1, 0)])
-        early = (
-            with_other(early[0], CORE_BIT),
-            with_other(early[1], CORE_BIT),
-            cols_core(early[2], core),
-        )
-        received, early = tie((received, early))
         e = jnp.where(leading, received, x)
         du, attn_rows, ffn_rows, gain_shard = last_round(e, state, early, weights, tables, me)
     else:
-        received = lax.ppermute(first_grad, "section", [(1, 0)])
+        out, state = forward(u, weights, tables)
+        first_grad, _, _ = backward(x, state, weights, tables)
+        received = lax.ppermute(first_grad.astype(bf16), "section", [(1, 0)])
         e = jnp.where(leading, received, x)
         du, pieces, gain_grad = backward(e, state, weights, tables)
         attn_rows, ffn_rows = grads_generic(pieces)

time: 382 us -> 378 us (0.990)
  other arithmetic: 24.4 us -> 38.5 us
  waiting for transfers between devices: 193 us -> 180 us
  starting transfers between devices: 80.3 us -> 68.3 us
  matrix products: 16.2 us -> 22.2 us
    ppermute x10 -> x9, waiting for transfers between devices: 41.2 us -> 20.5 us  [z_pairs(): lax.ppermute(x, 'dp', [(4 * a + i, 4 * b + i) for a, b in pairs for i in...]
    ppermute x24 -> x25, starting transfers between devices: 54.8 us -> 40.1 us  [flip(): return lax.ppermute(x, 'dp', [(i, i ^ bit) for i in range(size)])]
    concatenate x8, other arithmetic: 6.82 us -> 13 us  [with_other(): return jnp.concatenate([x, flip(x, bit)], axis=0)]
    ppermute x1, waiting for transfers between devices: 4.34 us -> 8.99 us  [local(): received = lax.ppermute(first_grad, 'section', [(1, 0)])]
    ppermute x24 -> x25, waiting for transfers between devices: 43.9 us -> 47.5 us  [flip(): return lax.ppermute(x, 'dp', [(i, i ^ bit) for i in range(size)])]
    ppermute x10 -> x9, starting transfers between devices: 20.4 us -> 23.1 us  [z_pairs(): lax.ppermute(x, 'dp', [(4 * a + i, 4 * b + i) for a, b in pairs for i in...]
  transfers between devices with their start and end apart: 37 -> 37, of which waited for: 22 -> 19; matrix products, arithmetic and copies ran while one was open for 8% -> 11% of each run, Pallas kernels for 2% -> 7%
where the time goes in v5:
time: 378 us; the launch traced here: 377 us
  waiting for transfers between devices  180 us (48%)
  starting transfers between devices  68.3 us (18%)
  other arithmetic  38.5 us (10%)
  Pallas kernels  36.3 us (10%)
  matrix products  22.2 us (6%)
  local copies, waits for them, and re-layouts  16.1 us (4%)
  between operations  15.4 us (4%)
    all_gather x1, waiting for transfers between devices, local(): lax.all_gather(own, 'dp', axis=0, tiled=True).reshape(4, 4, 4, share, width)  97.4 us
    ppermute x25, waiting for transfers between devices, flip(): return lax.ppermute(x, 'dp', [(i, i ^ bit) for i in range(size)])  47.5 us
    ppermute x25, starting transfers between devices, flip(): return lax.ppermute(x, 'dp', [(i, i ^ bit) for i in range(size)])  40.1 us
    pallas_call x4, Pallas kernels, ffn_call(): pl.pallas_call(kernel, grid=(steps,), in_specs=[whole] * len(wholes) + [b...  36.3 us
    ppermute x9, starting transfers between devices, z_pairs(): lax.ppermute(x, 'dp', [(4 * a + i, 4 * b + i) for a, b in pairs for i in...  23.1 us
    ppermute x9, waiting for transfers between devices, z_pairs(): lax.ppermute(x, 'dp', [(4 * a + i, 4 * b + i) for a, b in pairs for i in...  20.5 us
    concatenate x8, other arithmetic, with_other(): return jnp.concatenate([x, flip(x, bit)], axis=0)  13 us
    ppermute x1, waiting for transfers between devices, local(): received = lax.ppermute(first_grad, 'section', [(1, 0)])  8.99 us
  transfers between devices with their start and end apart: 37, of which 19 were waited for; matrix products, arithmetic and copies ran while one was open for 11% of the time, Pallas kernels for 7%

profile of v5, /device:TPU:0, one launch (start us, length us, event | category | flops | bytes accessed | tf_op | source)
XLA Modules:
  0.0 377.0 jit_solution(1855534798928521112)
XLA Ops:
  7.2 2.5 pad_maximum_fusion
  11.2 2.8 collective-permute-start.1
  14.2 1.4 collective-permute-done.1
  15.7 2.1 collective-permute-start.2
  17.9 1.4 collective-permute-done.2
  19.5 3.0 collective-permute-start.3
  22.8 1.3 collective-permute-done.3
  24.4 97.4 %all-gather.2.cloned.1.call-done = bf16[10240,960]{1,0:T(8,128)(2,1)} async-done(((bf16[640,960]{1,0:T(8,128)(2,1)}), bf16[10240,960]{1,0:T(8,128)(2,1)}) %all-gather.2.cloned.1.call-update) | async-done | bytes 19660816 | tf_op jit(solution)/shard_map/all_gather | solution.py:443
  121.8 3.3 slice.119
  125.0 1.1 fusion.6
  128.1 9.6 %shard_map.84 = (f32[4,128,640]{2,1,0:T(8,128)}, f32[4,128,640]{2,1,0:T(8,128)}, bf16[4,128,640]{2,1,0:T(8,128)(2,1)}, f32[128,960]{1,0:T(8,128)S(1)}) custom-call(bf16[128,960]{1,0:T(8,128)(2,1)S(1)} %multiply_convert_fusion.3.m_ref, f32[128,960]{1,0:T(8,128)S(1)} %get-tuple-element.177.h1_ref, bf16[4,4,4,160,960]{4,3,2,1,0:T(8,128)(2,1)} %bitcast.243, ...), custom_call_target="tpu_custom_call" | custom-call | flops 1887436800 | bytes 14745600 | tf_op jit(solution)/shard_map/pallas_call | solution.py:203
  137.7 3.6 collective-permute-start.4
  141.3 5.8 %collective-permute-done.4 = bf16[128,960]{1,0:T(8,128)(2,1)S(1)} collective-permute-done((bf16[128,960]{1,0:T(8,128)(2,1)S(1)}, bf16[128,960]{1,0:T(8,128)(2,1)S(1)}, u32[]{:S(2)}, u32[]{:S(2)}) %collective-permute-start.4) | collective-permute-done | bytes 245792 | tf_op jit(solution)/shard_map/ppermute | solution.py:458
  148.1 3.0 fusion.4
  153.0 2.2 multiply_reduce_fusion.5
  156.6 1.2 collective-permute-start.5
  158.6 8.3 %shard_map.85 = (f32[4,128,640]{2,1,0:T(8,128)S(1)}, f32[4,128,640]{2,1,0:T(8,128)S(1)}, bf16[4,128,640]{2,1,0:T(8,128)(2,1)S(1)}, f32[128,960]{1,0:T(8,128)S(1)}) custom-call(bf16[128,960]{1,0:T(8,128)(2,1)} %multiply_convert_fusion.2.m_ref, f32[128,960]{1,0:T(8,128)S(1)} %get-tuple-element.181.h1_ref, bf16[4,4,4,160,960]{4,3,2,1,0:T(8,128)(2,1)} %bitcast.246, ...), custom_call_target="tpu_custom_call" | custom-call | flops 1887436800 | bytes 14745600 | tf_op jit(solution)/shard_map/pallas_call | solution.py:203
  166.9 2.1 pad_maximum_fusion.13
  168.9 1.1 collective-permute-done.6
  170.0 1.8 pad_maximum_fusion.14
  172.7 1.2 collective-permute-start.7
  174.2 9.7 %shard_map.86 = (bf16[4,128,640]{2,1,0:T(8,128)(2,1)}, bf16[4,128,640]{2,1,0:T(8,128)(2,1)}, f32[128,960]{1,0:T(8,128)S(1)}) custom-call(bf16[128,960]{1,0:T(8,128)(2,1)S(1)} %bitcast.238, f32[4,128,640]{2,1,0:T(8,128)S(1)} %get-tuple-element.64.gate_ref, f32[4,128,640]{2,1,0:T(8,128)S(1)} %get-tuple-element.65.up_ref, ...), custom_call_target="tpu_custom_call" | custom-call | flops 1887436800 | bytes 14745600 | tf_op jit(solution)/shard_map/pallas_call | solution.py:203
  183.9 1.0 pad_maximum_fusion.5
  184.9 2.4 pad_maximum_fusion.1
  187.4 2.3 pad_maximum_fusion.2
  190.0 2.3 fusion.30
  197.1 1.5 collective-permute-start.11
  198.6 9.0 %collective-permute-done.11 = bf16[128,960]{1,0:T(8,128)(2,1)S(1)} collective-permute-done((bf16[128,960]{1,0:T(8,128)(2,1)S(1)}, bf16[128,960]{1,0:T(8,128)(2,1)S(1)}, u32[]{:S(2)}, u32[]{:S(2)}) %collective-permute-start.11) | collective-permute-done | bytes 245792 | tf_op jit(solution)/shard_map/ppermute | solution.py:462
  209.1 8.8 %shard_map.87 = (bf16[4,128,640]{2,1,0:T(8,128)(2,1)S(1)}, bf16[4,128,640]{2,1,0:T(8,128)(2,1)S(1)}, f32[128,960]{1,0:T(8,128)S(1)}) custom-call(bf16[128,960]{1,0:T(8,128)(2,1)} %broadcast_select_fusion.1.eb_ref, f32[4,128,640]{2,1,0:T(8,128)S(1)} %get-tuple-element.64.gate_ref, f32[4,128,640]{2,1,0:T(8,128)S(1)} %get-tuple-element.65.up_ref, ...), custom_call_target="tpu_custom_call" | custom-call | flops 1887436800 | bytes 14745600 | tf_op jit(solution)/shard_map/pallas_call | solution.py:203
  217.9 1.0 pad_maximum_fusion.15
  219.2 1.3 collective-permute-start.14
  220.6 1.9 fusion.97
  222.5 2.2 fusion.33
  224.7 4.7 %collective-permute-done.14 = bf16[2,128,640]{2,1,0:T(8,128)(2,1)S(1)} collective-permute-done((bf16[2,128,640]{2,1,0:T(8,128)(2,1)S(1)}, bf16[2,128,640]{2,1,0:T(8,128)(2,1)S(1)}, u32[]{:S(2)}, u32[]{:S(2)}) %collective-permute-start.14) | collective-permute-done | bytes 327712 | tf_op jit(solution)/shard_map/ppermute | solution.py:243
  231.5 1.6 copy-done.11
  235.2 1.3 collective-permute-start.16
  236.5 2.4 collective-permute-start.17
  239.7 1.4 collective-permute-start.22
  241.3 9.7 %collective-permute-done.21 = bf16[128,960]{1,0:T(8,128)(2,1)S(1)} collective-permute-done((bf16[128,960]{1,0:T(8,128)(2,1)S(1)}, bf16[128,960]{1,0:T(8,128)(2,1)S(1)}, u32[]{:S(2)}, u32[]{:S(2)}) %collective-permute-start.21) | collective-permute-done | bytes 245792 | tf_op jit(solution)/shard_map/ppermute | solution.py:243
  251.9 9.3 %collective-permute-done.17 = bf16[160,960]{1,0:T(8,128)(2,1)S(1)} collective-permute-done((bf16[160,960]{1,0:T(8,128)(2,1)S(1)}, bf16[160,960]{1,0:T(8,128)(2,1)S(1)}, u32[]{:S(2)}, u32[]{:S(2)}) %collective-permute-start.17) | collective-permute-done | bytes 307232 | tf_op jit(solution)/shard_map/ppermute | solution.py:282
  261.3 2.0 fusion.60
  264.3 1.3 collective-permute-start.18
  267.0 1.2 dynamic-slice_bitcast_fusion.2
  268.3 7.8 %collective-permute-done.20 = bf16[2,128,640]{1,2,0:T(8,128)(2,1)S(1)} collective-permute-done((bf16[2,128,640]{1,2,0:T(8,128)(2,1)S(1)}, bf16[2,128,640]{1,2,0:T(8,128)(2,1)S(1)}, u32[]{:S(2)}, u32[]{:S(2)}) %collective-permute-start.20) | collective-permute-done | bytes 327712 | tf_op jit(solution)/shard_map/ppermute | solution.py:243
  276.1 3.2 collective-permute-done.18
  279.4 1.1 bitcast_add_fusion.2
  283.8 5.2 %collective-permute-start.27 = (bf16[2,160,960]{2,1,0:T(8,128)(2,1)}, bf16[2,160,960]{2,1,0:T(8,128)(2,1)}, u32[]{:S(2)}, u32[]{:S(2)}) collective-permute-start(bf16[2,160,960]{2,1,0:T(8,128)(2,1)} %bitcast_convert_fusion.1), channel_id=1, source_target_pairs={{0,4},{1,5},{2,6},{3,7},{12,8},{13,9},{14,10},{15,11},{16,20},{17,... | collective-permute-start | bytes 1843208 | tf_op jit(solution)/shard_map/ppermute | solution.py:282
  290.4 1.3 collective-permute-start.29
  291.7 1.0 collective-permute-done.26
  293.7 1.2 dynamic-slice_bitcast_fusion.1
  294.8 1.1 pad_maximum_fusion.12
  296.0 2.4 pad_maximum_fusion.4
  298.4 5.2 %collective-permute-done.27 = bf16[2,160,960]{2,1,0:T(8,128)(2,1)} collective-permute-done((bf16[2,160,960]{2,1,0:T(8,128)(2,1)}, bf16[2,160,960]{2,1,0:T(8,128)(2,1)}, u32[]{:S(2)}, u32[]{:S(2)}) %collective-permute-start.27) | collective-permute-done | bytes 614432 | tf_op jit(solution)/shard_map/ppermute | solution.py:282
  303.6 2.1 bitcast_add_fusion.1
  305.7 1.2 convert_add_fusion.2
  306.9 2.7 collective-permute-done.29
  313.1 8.9 %collective-permute-start.30 = (bf16[2,168,960]{2,1,0:T(8,128)(2,1)S(1)}, bf16[2,168,960]{2,1,0:T(8,128)(2,1)S(1)}, u32[]{:S(2)}, u32[]{:S(2)}) collective-permute-start(bf16[2,168,960]{2,1,0:T(8,128)(2,1)S(1)} %bitcast_convert_fusion), channel_id=1, source_target_pairs={{0,4},{1,5},{2,6},{3,7},{12,8},{13,9},{14,10},{15,11},{16,20},{17,... | collective-permute-start | bytes 1935368 | tf_op jit(solution)/shard_map/ppermute | solution.py:282
  322.8 3.0 collective-permute-start.32
  325.8 1.4 bitcast_add_fusion.5
  327.3 15.0 %collective-permute-done.32 = bf16[160,960]{1,0:T(8,128)(2,1)S(1)} collective-permute-done((bf16[160,960]{1,0:T(8,128)(2,1)S(1)}, bf16[160,960]{1,0:T(8,128)(2,1)S(1)}, u32[]{:S(2)}, u32[]{:S(2)}) %collective-permute-start.32) | collective-permute-done | bytes 307232 | tf_op jit(solution)/shard_map/ppermute | solution.py:243
  345.1 6.0 %collective-permute-start.35 = (bf16[160,960]{1,0:T(8,128)(2,1)S(1)}, bf16[160,960]{1,0:T(8,128)(2,1)S(1)}, u32[]{:S(2)}, u32[]{:S(2)}) collective-permute-start(bf16[160,960]{1,0:T(8,128)(2,1)S(1)} %fusion.73), channel_id=1, source_target_pairs={{0,4},{1,5},{2,6},{3,7},{4,0},{5,1},{6,2},{7,3},{8,12},{9,13},{10,... | collective-permute-start | bytes 921608 | tf_op jit(solution)/shard_map/ppermute | solution.py:243
  351.4 12.1 %collective-permute-start.34 = (bf16[168,960]{1,0:T(8,128)(2,1)S(1)}, bf16[168,960]{1,0:T(8,128)(2,1)S(1)}, u32[]{:S(2)}, u32[]{:S(2)}) collective-permute-start(bf16[168,960]{1,0:T(8,128)(2,1)S(1)} %fusion.68), channel_id=1, source_target_pairs={{0,4},{1,5},{2,6},{3,7},{4,0},{5,1},{6,2},{7,3},{8,12},{9,13},{10,... | collective-permute-start | bytes 967688 | tf_op jit(solution)/shard_map/ppermute | solution.py:243
  363.6 1.4 maximum_bitcast_fusion
  365.0 3.7 collective-permute-done.34
  (278 shorter events, 40.1 us)
Async XLA Ops:
  7.2 114.6 %all-gather.2.cloned.1.call-start = ((), (), s32[]{:S(2)}) async-start(), calls=%async_computation | async-start | bytes 22282240 | tf_op jit(solution)/shard_map/all_gather | solution.py:443
  7.2 2.6 copy-start.49
  7.2 3.1 copy-start.43
  7.2 10.5 %copy-start = (bf16[1,2,64,960]{3,2,1,0:T(8,128)(2,1)S(1)}, bf16[1,2,64,960]{3,2,1,0:T(8,128)(2,1)}, u32[]{:S(2)}) copy-start(bf16[1,2,64,960]{3,2,1,0:T(8,128)(2,1)} %param.5) | copy-start | bytes 737284
  9.8 1.3 collective-permute-start
  11.2 4.3 %collective-permute-start.1 = (bf16[240]{0:T(256)(128)(2,1)S(1)}, bf16[240]{0:T(256)(128)(2,1)S(1)}, u32[]{:S(2)}, u32[]{:S(2)}) collective-permute-start(bf16[240]{0:T(256)(128)(2,1)S(1)} %pad_maximum_fusion.29), channel_id=1, source_target_pairs={{0,2},{1,3},{2,0},{3,1},{4,6},{5,7},{6,4},{7,5},{8,10},{9,11},{10,... | collective-permute-start | bytes 1448 | tf_op jit(solution)/shard_map/ppermute | solution.py:243
  15.7 3.6 collective-permute-start.2
  19.5 4.7 %collective-permute-start.3 = (bf16[960]{0:T(1024)(128)(2,1)S(1)}, bf16[960]{0:T(1024)(128)(2,1)S(1)}, u32[]{:S(2)}, u32[]{:S(2)}) collective-permute-start(bf16[960]{0:T(1024)(128)(2,1)S(1)} %pad_maximum_fusion.27), channel_id=1, source_target_pairs={{0,8},{1,9},{2,10},{3,11},{4,12},{5,13},{6,14},{7,15},{8,0},{9,1},... | collective-permute-start | bytes 5768 | tf_op jit(solution)/shard_map/ppermute | solution.py:243
  137.7 9.3 %collective-permute-start.4 = (bf16[128,960]{1,0:T(8,128)(2,1)S(1)}, bf16[128,960]{1,0:T(8,128)(2,1)S(1)}, u32[]{:S(2)}, u32[]{:S(2)}) collective-permute-start(bf16[128,960]{1,0:T(8,128)(2,1)S(1)} %convert_element_type.209), channel_id=1, source_target_pairs={{0,16},{1,17},{2,18},{3,19},{4,20},{5,21},{6,22},{7,23},{8,24},{9,... | collective-permute-start | bytes 737288 | tf_op jit(solution)/shard_map/ppermute | solution.py:458
  147.3 5.7 %copy-start.12 = (bf16[128,960]{1,0:T(8,128)(2,1)}, bf16[128,960]{1,0:T(8,128)(2,1)S(1)}, u32[]{:S(2)}) copy-start(bf16[128,960]{1,0:T(8,128)(2,1)S(1)} %get-tuple-element.121) | copy-start | bytes 737284
  147.3 48.4 %copy-start.44 = (f32[128]{0:T(128)}, f32[128]{0:T(128)S(1)}, u32[]{:S(2)}) copy-start(f32[128]{0:T(128)S(1)} %get-tuple-element.170) | copy-start | bytes 1540
  156.6 10.3 %collective-permute-start.5 = (bf16[128,960]{1,0:T(8,128)(2,1)}, bf16[128,960]{1,0:T(8,128)(2,1)}, u32[]{:S(2)}, u32[]{:S(2)}) collective-permute-start(bf16[128,960]{1,0:T(8,128)(2,1)} %multiply_convert_fusion.2.m_ref), channel_id=1, source_target_pairs={{0,2},{1,3},{2,0},{3,1},{4,6},{5,7},{6,4},{7,5},{8,10},{9,11},{10,... | collective-permute-start | bytes 737288 | tf_op jit(solution)/shard_map/ppermute | solution.py:243
  157.8 12.2 %collective-permute-start.6 = (bf16[128,960]{1,0:T(8,128)(2,1)}, bf16[128,960]{1,0:T(8,128)(2,1)S(1)}, u32[]{:S(2)}, u32[]{:S(2)}) collective-permute-start(bf16[128,960]{1,0:T(8,128)(2,1)} %fusion.56), channel_id=1, source_target_pairs={{0,2},{1,3},{2,0},{3,1},{4,6},{5,7},{6,4},{7,5},{8,10},{9,11},{10,... | collective-permute-start | bytes 737288 | tf_op jit(solution)/shard_map/ppermute | solution.py:243
  166.9 5.9 %copy-start.1 = (f32[128,960]{1,0:T(8,128)}, f32[128,960]{1,0:T(8,128)S(1)}, u32[]{:S(2)}) copy-start(f32[128,960]{1,0:T(8,128)S(1)} %get-tuple-element.87) | copy-start | bytes 1474564
  171.8 13.1 %collective-permute-start.8 = (bf16[256,960]{1,0:T(8,128)(2,1)}, bf16[256,960]{1,0:T(8,128)(2,1)}, u32[]{:S(2)}, u32[]{:S(2)}) collective-permute-start(bf16[256,960]{1,0:T(8,128)(2,1)} %pad_maximum_fusion.13), channel_id=1, source_target_pairs={{0,1},{1,0},{2,3},{3,2},{4,5},{5,4},{6,7},{7,6},{8,9},{9,8},{10,11... | collective-permute-start | bytes 1474568 | tf_op jit(solution)/shard_map/ppermute | solution.py:243
  172.7 11.1 %collective-permute-start.7 = (bf16[2,128,640]{2,1,0:T(8,128)(2,1)}, bf16[2,128,640]{2,1,0:T(8,128)(2,1)}, u32[]{:S(2)}, u32[]{:S(2)}) collective-permute-start(bf16[2,128,640]{2,1,0:T(8,128)(2,1)} %get-tuple-element.140), channel_id=1, source_target_pairs={{0,2},{1,3},{2,0},{3,1},{4,6},{5,7},{6,4},{7,5},{8,10},{9,11},{10,... | collective-permute-start | bytes 983048 | tf_op jit(solution)/shard_map/ppermute | solution.py:243
  174.0 13.4 %collective-permute-start.9 = (bf16[256,960]{1,0:T(8,128)(2,1)}, bf16[256,960]{1,0:T(8,128)(2,1)}, u32[]{:S(2)}, u32[]{:S(2)}) collective-permute-start(bf16[256,960]{1,0:T(8,128)(2,1)} %pad_maximum_fusion.14), channel_id=1, source_target_pairs={{0,1},{1,0},{2,3},{3,2},{4,5},{5,4},{6,7},{7,6},{8,9},{9,8},{10,11... | collective-permute-start | bytes 1474568 | tf_op jit(solution)/shard_map/ppermute | solution.py:243
  174.2 9.7 %copy-start.24 = (bf16[2,128,640]{2,1,0:T(8,128)(2,1)S(1)}, bf16[2,128,640]{2,1,0:T(8,128)(2,1)}, u32[]{:S(2)}) copy-start(bf16[2,128,640]{2,1,0:T(8,128)(2,1)} %get-tuple-element.139) | copy-start | bytes 983044
  184.9 9.9 %slice-start = ((s8[5242880]{0:T(1024)(128)(4,1)}), s8[4194304]{0:T(1024)(128)(4,1)S(1)}, s32[]{:S(2)}) async-start(s8[5242880]{0:T(1024)(128)(4,1)} %bitcast.269), calls=%async_computation.1 | async-start | bytes 8388608
  189.8 2.5 copy-start.10
  190.0 2.7 copy-start.4
  192.3 2.5 slice-start.1
  194.5 1.7 collective-permute-start.10
  197.1 10.5 %collective-permute-start.11 = (bf16[128,960]{1,0:T(8,128)(2,1)S(1)}, bf16[128,960]{1,0:T(8,128)(2,1)S(1)}, u32[]{:S(2)}, u32[]{:S(2)}) collective-permute-start(bf16[128,960]{1,0:T(8,128)(2,1)S(1)} %fusion.47), channel_id=1, source_target_pairs={{16,0},{17,1},{18,2},{19,3},{20,4},{21,5},{22,6},{23,7},{24,8},{25... | collective-permute-start | bytes 737288 | tf_op jit(solution)/shard_map/ppermute | solution.py:462
  208.3 9.6 %collective-permute-start.12 = (bf16[128,960]{1,0:T(8,128)(2,1)}, bf16[128,960]{1,0:T(8,128)(2,1)S(1)}, u32[]{:S(2)}, u32[]{:S(2)}) collective-permute-start(bf16[128,960]{1,0:T(8,128)(2,1)} %broadcast_select_fusion.1.eb_ref), channel_id=1, source_target_pairs={{0,2},{1,3},{2,0},{3,1},{4,6},{5,7},{6,4},{7,5},{8,10},{9,11},{10,... | collective-permute-start | bytes 737288 | tf_op jit(solution)/shard_map/ppermute | solution.py:243
  217.9 2.7 copy-start.47
  219.1 10.5 %collective-permute-start.13 = (bf16[256,960]{1,0:T(8,128)(2,1)S(1)}, bf16[256,960]{1,0:T(8,128)(2,1)S(1)}, u32[]{:S(2)}, u32[]{:S(2)}) collective-permute-start(bf16[256,960]{1,0:T(8,128)(2,1)S(1)} %pad_maximum_fusion.15), channel_id=1, source_target_pairs={{0,1},{1,0},{2,3},{3,2},{4,5},{5,4},{6,7},{7,6},{8,9},{9,8},{10,11... | collective-permute-start | bytes 1474568 | tf_op jit(solution)/shard_map/ppermute | solution.py:243
  219.2 10.2 %collective-permute-start.14 = (bf16[2,128,640]{2,1,0:T(8,128)(2,1)S(1)}, bf16[2,128,640]{2,1,0:T(8,128)(2,1)S(1)}, u32[]{:S(2)}, u32[]{:S(2)}) collective-permute-start(bf16[2,128,640]{2,1,0:T(8,128)(2,1)S(1)} %get-tuple-element.135), channel_id=1, source_target_pairs={{0,2},{1,3},{2,0},{3,1},{4,6},{5,7},{6,4},{7,5},{8,10},{9,11},{10,... | collective-permute-start | bytes 983048 | tf_op jit(solution)/shard_map/ppermute | solution.py:243
  224.7 5.0 %copy-start.17 = (bf16[512,640]{1,0:T(8,128)(2,1)S(1)}, bf16[512,640]{1,0:T(8,128)(2,1)}, u32[]{:S(2)}) copy-start(bf16[512,640]{1,0:T(8,128)(2,1)} %pad_maximum_fusion.6) | copy-start | bytes 1966084
  229.5 11.7 %collective-permute-start.15 = (bf16[256,640]{1,0:T(8,128)(2,1)S(1)}, bf16[256,640]{1,0:T(8,128)(2,1)S(1)}, u32[]{:S(2)}, u32[]{:S(2)}) collective-permute-start(bf16[256,640]{1,0:T(8,128)(2,1)S(1)} %get-tuple-element.134), channel_id=1, source_target_pairs={{0,1},{1,0},{2,3},{3,2},{4,5},{5,4},{6,7},{7,6},{8,9},{9,8},{10,11... | collective-permute-start | bytes 983048 | tf_op jit(solution)/shard_map/ppermute | solution.py:243
  229.7 31.5 %slice-start.2 = ((s8[5242880]{0:T(1024)(128)(4,1)}), s8[4194304]{0:T(1024)(128)(4,1)S(1)}, s32[]{:S(2)}) async-start(s8[5242880]{0:T(1024)(128)(4,1)} %bitcast.272), calls=%async_computation.3 | async-start | bytes 8388608
  230.6 3.2 copy-start.7
  230.6 2.8 copy-start.5
  233.8 27.4 %slice-start.3 = ((s8[5242880]{0:T(1024)(128)(4,1)}), s8[1048576]{0:T(1024)(128)(4,1)S(1)}, s32[]{:S(2)}) async-start(s8[5242880]{0:T(1024)(128)(4,1)} %bitcast.272), calls=%async_computation.4 | async-start | bytes 2097152
  235.2 16.7 %collective-permute-start.16 = (bf16[2,128,640]{2,1,0:T(8,128)(2,1)S(1)}, bf16[2,128,640]{2,1,0:T(8,128)(2,1)S(1)}, u32[]{:S(2)}, u32[]{:S(2)}) collective-permute-start(bf16[2,128,640]{2,1,0:T(8,128)(2,1)S(1)} %get-tuple-element.132), channel_id=1, source_target_pairs={{0,2},{1,3},{2,0},{3,1},{4,6},{5,7},{6,4},{7,5},{8,10},{9,11},{10,... | collective-permute-start | bytes 983048 | tf_op jit(solution)/shard_map/ppermute | solution.py:243
  236.5 24.8 %collective-permute-start.17 = (bf16[160,960]{1,0:T(8,128)(2,1)S(1)}, bf16[160,960]{1,0:T(8,128)(2,1)S(1)}, u32[]{:S(2)}, u32[]{:S(2)}) collective-permute-start(bf16[160,960]{1,0:T(8,128)(2,1)S(1)} %get-tuple-element.85), channel_id=1, source_target_pairs={{0,8},{1,9},{2,10},{3,11},{4,12},{5,13},{6,14},{7,15},{8,0},{9,1},... | collective-permute-start | bytes 921608 | tf_op jit(solution)/shard_map/ppermute | solution.py:282
  238.9 12.1 %collective-permute-start.21 = (bf16[128,960]{1,0:T(8,128)(2,1)S(1)}, bf16[128,960]{1,0:T(8,128)(2,1)S(1)}, u32[]{:S(2)}, u32[]{:S(2)}) collective-permute-start(bf16[128,960]{1,0:T(8,128)(2,1)S(1)} %get-tuple-element.91), channel_id=1, source_target_pairs={{0,2},{1,3},{2,0},{3,1},{4,6},{5,7},{6,4},{7,5},{8,10},{9,11},{10,... | collective-permute-start | bytes 737288 | tf_op jit(solution)/shard_map/ppermute | solution.py:243
  239.7 40.8 %collective-permute-start.22 = (bf16[160,960]{1,0:T(8,128)(2,1)S(1)}, bf16[160,960]{1,0:T(8,128)(2,1)S(1)}, u32[]{:S(2)}, u32[]{:S(2)}) collective-permute-start(bf16[160,960]{1,0:T(8,128)(2,1)S(1)} %get-tuple-element.92), channel_id=1, source_target_pairs={{0,4},{1,5},{2,6},{3,7},{4,8},{5,9},{6,10},{7,11},{8,12},{9,13},{1... | collective-permute-start | bytes 921608 | tf_op jit(solution)/shard_map/ppermute | solution.py:282
  241.2 20.1 %copy-start.14 = (bf16[128,960]{1,0:T(8,128)(2,1)S(1)}, bf16[128,960]{1,0:T(8,128)(2,1)}, u32[]{:S(2)}) copy-start(bf16[128,960]{1,0:T(8,128)(2,1)} %copy-done.12) | copy-start | bytes 737284
  251.9 11.4 %copy-start.22 = (bf16[5,64,3,128]{3,1,2,0:T(8,128)(2,1)S(1)}, bf16[5,64,3,128]{3,1,2,0:T(8,128)(2,1)}, u32[]{:S(2)}) copy-start(bf16[5,64,3,128]{3,1,2,0:T(8,128)(2,1)} %copy-done.21) | copy-start | bytes 737284
  251.9 11.4 %copy-start.8 = (bf16[512,960]{1,0:T(8,128)(2,1)S(1)}, bf16[512,960]{1,0:T(8,128)(2,1)}, u32[]{:S(2)}) copy-start(bf16[512,960]{1,0:T(8,128)(2,1)} %pad_maximum_fusion.1) | copy-start | bytes 2949124
  264.3 15.1 %collective-permute-start.18 = (bf16[2,160,960]{2,1,0:T(8,128)(2,1)S(1)}, bf16[2,160,960]{2,1,0:T(8,128)(2,1)S(1)}, u32[]{:S(2)}, u32[]{:S(2)}) collective-permute-start(bf16[2,160,960]{2,1,0:T(8,128)(2,1)S(1)} %bitcast_convert_fusion.2), channel_id=1, source_target_pairs={{0,4},{1,5},{2,6},{3,7},{12,8},{13,9},{14,10},{15,11},{16,20},{17,... | collective-permute-start | bytes 1843208 | tf_op jit(solution)/shard_map/ppermute | solution.py:282
  265.7 2.5 collective-permute-start.19
  265.9 10.2 %collective-permute-start.20 = (bf16[2,128,640]{1,2,0:T(8,128)(2,1)S(1)}, bf16[2,128,640]{1,2,0:T(8,128)(2,1)S(1)}, u32[]{:S(2)}, u32[]{:S(2)}) collective-permute-start(bf16[2,128,640]{1,2,0:T(8,128)(2,1)S(1)} %get-tuple-element.128), channel_id=1, source_target_pairs={{0,2},{1,3},{2,0},{3,1},{4,6},{5,7},{6,4},{7,5},{8,10},{9,11},{10,... | collective-permute-start | bytes 983048 | tf_op jit(solution)/shard_map/ppermute | solution.py:243
  266.8 22.2 %collective-permute-start.25 = (f32[1920]{0:T(1024)S(1)}, f32[1920]{0:T(1024)S(1)}, u32[]{:S(2)}, u32[]{:S(2)}) collective-permute-start(f32[1920]{0:T(1024)S(1)} %pad_maximum_fusion.26), channel_id=1, source_target_pairs={{0,1},{1,0},{2,3},{3,2},{4,5},{5,4},{6,7},{7,6},{8,9},{9,8},{10,11... | collective-permute-start | bytes 23048 | tf_op jit(solution)/shard_map/ppermute | solution.py:243
  281.4 13.4 %collective-permute-start.23 = (bf16[256,640]{0,1:T(8,128)(2,1)}, bf16[256,640]{0,1:T(8,128)(2,1)}, u32[]{:S(2)}, u32[]{:S(2)}) collective-permute-start(bf16[256,640]{0,1:T(8,128)(2,1)} %get-tuple-element.126), channel_id=1, source_target_pairs={{0,1},{1,0},{2,3},{3,2},{4,5},{5,4},{6,7},{7,6},{8,9},{9,8},{10,11... | collective-permute-start | bytes 983048 | tf_op jit(solution)/shard_map/ppermute | solution.py:243
  281.4 14.5 %collective-permute-start.24 = (bf16[256,960]{1,0:T(8,128)(2,1)}, bf16[256,960]{1,0:T(8,128)(2,1)}, u32[]{:S(2)}, u32[]{:S(2)}) collective-permute-start(bf16[256,960]{1,0:T(8,128)(2,1)} %pad_maximum_fusion.16), channel_id=1, source_target_pairs={{0,1},{1,0},{2,3},{3,2},{4,5},{5,4},{6,7},{7,6},{8,9},{9,8},{10,11... | collective-permute-start | bytes 1474568 | tf_op jit(solution)/shard_map/ppermute | solution.py:243
  283.8 19.8 %collective-permute-start.27 = (bf16[2,160,960]{2,1,0:T(8,128)(2,1)}, bf16[2,160,960]{2,1,0:T(8,128)(2,1)}, u32[]{:S(2)}, u32[]{:S(2)}) collective-permute-start(bf16[2,160,960]{2,1,0:T(8,128)(2,1)} %bitcast_convert_fusion.1), channel_id=1, source_target_pairs={{0,4},{1,5},{2,6},{3,7},{12,8},{13,9},{14,10},{15,11},{16,20},{17,... | collective-permute-start | bytes 1843208 | tf_op jit(solution)/shard_map/ppermute | solution.py:282
  289.0 3.7 collective-permute-start.26
  290.4 19.3 %collective-permute-start.29 = (bf16[160,960]{1,0:T(8,128)(2,1)}, bf16[160,960]{1,0:T(8,128)(2,1)}, u32[]{:S(2)}, u32[]{:S(2)}) collective-permute-start(bf16[160,960]{1,0:T(8,128)(2,1)} %get-tuple-element.98), channel_id=1, source_target_pairs={{0,12},{1,13},{2,14},{3,15},{4,0},{5,1},{6,2},{7,3},{8,4},{9,5},{1... | collective-permute-start | bytes 921608 | tf_op jit(solution)/shard_map/ppermute | solution.py:282
  292.7 13.0 %collective-permute-start.28 = (bf16[2,160,960]{2,1,0:T(8,128)(2,1)}, bf16[2,160,960]{2,1,0:T(8,128)(2,1)S(1)}, u32[]{:S(2)}, u32[]{:S(2)}) collective-permute-start(bf16[2,160,960]{2,1,0:T(8,128)(2,1)} %bitcast_add_fusion.2), channel_id=1, source_target_pairs={{4,8},{5,9},{6,10},{7,11},{8,4},{9,5},{10,6},{11,7},{20,24},{21,25... | collective-permute-start | bytes 1843208 | tf_op jit(solution)/shard_map/ppermute | solution.py:282
  295.9 9.7 %copy-start.15 = (f32[2,160,960]{2,1,0:T(8,128)S(1)}, f32[2,160,960]{2,1,0:T(8,128)}, u32[]{:S(2)}) copy-start(f32[2,160,960]{2,1,0:T(8,128)} %dynamic-slice_bitcast_fusion.2) | copy-start | bytes 3686404
  305.7 4.1 %copy-start.18 = (bf16[512,960]{1,0:T(8,128)(2,1)S(1)}, bf16[512,960]{1,0:T(8,128)(2,1)}, u32[]{:S(2)}) copy-start(bf16[512,960]{1,0:T(8,128)(2,1)} %pad_maximum_fusion.2) | copy-start | bytes 2949124
  312.7 9.3 %copy-start.31 = (bf16[2,160,960]{2,1,0:T(8,128)(2,1)S(1)}, bf16[2,160,960]{2,1,0:T(8,128)(2,1)}, u32[]{:S(2)}) copy-start(bf16[2,160,960]{2,1,0:T(8,128)(2,1)} %bitcast_add_fusion.1) | copy-start | bytes 1843204
  312.7 10.0 %copy-start.20 = (f32[2,160,960]{2,1,0:T(8,128)S(1)}, f32[2,160,960]{2,1,0:T(8,128)}, u32[]{:S(2)}) copy-start(f32[2,160,960]{2,1,0:T(8,128)} %convert_add_fusion.2) | copy-start | bytes 3686404
  312.9 12.8 %copy-start.40 = (bf16[160,960]{1,0:T(8,128)(2,1)S(1)}, bf16[160,960]{1,0:T(8,128)(2,1)}, u32[]{:S(2)}) copy-start(bf16[160,960]{1,0:T(8,128)(2,1)} %copy-done.39) | copy-start | bytes 921604
  312.9 12.8 %copy-start.42 = (bf16[160,960]{1,0:T(8,128)(2,1)S(1)}, bf16[160,960]{1,0:T(8,128)(2,1)}, u32[]{:S(2)}) copy-start(bf16[160,960]{1,0:T(8,128)(2,1)} %copy-done.41) | copy-start | bytes 921604
  313.1 29.7 %collective-permute-start.30 = (bf16[2,168,960]{2,1,0:T(8,128)(2,1)S(1)}, bf16[2,168,960]{2,1,0:T(8,128)(2,1)S(1)}, u32[]{:S(2)}, u32[]{:S(2)}) collective-permute-start(bf16[2,168,960]{2,1,0:T(8,128)(2,1)S(1)} %bitcast_convert_fusion), channel_id=1, source_target_pairs={{0,4},{1,5},{2,6},{3,7},{12,8},{13,9},{14,10},{15,11},{16,20},{17,... | collective-permute-start | bytes 1935368 | tf_op jit(solution)/shard_map/ppermute | solution.py:282
  322.0 20.4 %collective-permute-start.31 = (bf16[2,160,960]{2,1,0:T(8,128)(2,1)S(1)}, bf16[2,160,960]{2,1,0:T(8,128)(2,1)S(1)}, u32[]{:S(2)}, u32[]{:S(2)}) collective-permute-start(bf16[2,160,960]{2,1,0:T(8,128)(2,1)S(1)} %copy-done.31), channel_id=1, source_target_pairs={{4,8},{5,9},{6,10},{7,11},{8,4},{9,5},{10,6},{11,7},{20,24},{21,25... | collective-permute-start | bytes 1843208 | tf_op jit(solution)/shard_map/ppermute | solution.py:282
  322.8 19.6 %collective-permute-start.32 = (bf16[160,960]{1,0:T(8,128)(2,1)S(1)}, bf16[160,960]{1,0:T(8,128)(2,1)S(1)}, u32[]{:S(2)}, u32[]{:S(2)}) collective-permute-start(bf16[160,960]{1,0:T(8,128)(2,1)S(1)} %fusion.72), channel_id=1, source_target_pairs={{0,4},{1,5},{2,6},{3,7},{4,0},{5,1},{6,2},{7,3},{8,12},{9,13},{10,... | collective-permute-start | bytes 921608 | tf_op jit(solution)/shard_map/ppermute | solution.py:243
  327.1 15.3 %copy-start.16 = (f32[2,160,960]{2,1,0:T(8,128)S(1)}, f32[2,160,960]{2,1,0:T(8,128)}, u32[]{:S(2)}) copy-start(f32[2,160,960]{2,1,0:T(8,128)} %dynamic-slice_bitcast_fusion.1) | copy-start | bytes 3686404
  343.0 8.1 %collective-permute-start.33 = (bf16[2,168,960]{2,1,0:T(8,128)(2,1)S(1)}, bf16[2,168,960]{2,1,0:T(8,128)(2,1)S(1)}, u32[]{:S(2)}, u32[]{:S(2)}) collective-permute-start(bf16[2,168,960]{2,1,0:T(8,128)(2,1)S(1)} %bitcast_add_fusion), channel_id=1, source_target_pairs={{4,8},{5,9},{6,10},{7,11},{8,4},{9,5},{10,6},{11,7},{20,24},{21,25... | collective-permute-start | bytes 1935368 | tf_op jit(solution)/shard_map/ppermute | solution.py:282
  345.1 18.3 %collective-permute-start.35 = (bf16[160,960]{1,0:T(8,128)(2,1)S(1)}, bf16[160,960]{1,0:T(8,128)(2,1)S(1)}, u32[]{:S(2)}, u32[]{:S(2)}) collective-permute-start(bf16[160,960]{1,0:T(8,128)(2,1)S(1)} %fusion.73), channel_id=1, source_target_pairs={{0,4},{1,5},{2,6},{3,7},{4,0},{5,1},{6,2},{7,3},{8,12},{9,13},{10,... | collective-permute-start | bytes 921608 | tf_op jit(solution)/shard_map/ppermute | solution.py:243
  351.4 17.3 %collective-permute-start.34 = (bf16[168,960]{1,0:T(8,128)(2,1)S(1)}, bf16[168,960]{1,0:T(8,128)(2,1)S(1)}, u32[]{:S(2)}, u32[]{:S(2)}) collective-permute-start(bf16[168,960]{1,0:T(8,128)(2,1)S(1)} %fusion.68), channel_id=1, source_target_pairs={{0,4},{1,5},{2,6},{3,7},{4,0},{5,1},{6,2},{7,3},{8,12},{9,13},{10,... | collective-permute-start | bytes 967688 | tf_op jit(solution)/shard_map/ppermute | solution.py:243
  (28 other events, 33.5 us)
Sparse Core Ops, SparseCore 0:
  10.2 111.5 all-gather.1

commit v6 on v5

--- a/solution.py
+++ b/solution.py
@@ -300,25 +300,37 @@
 
 
 def cols_core(x, core):
-    return jnp.concatenate([at(x, core), flip(at(x, 1 - core), CORE_BIT)], axis=0)
+    return at(x, core), flip(at(x, 1 - core), CORE_BIT)
+
+
+def rows_core(x):
+    return x, flip(x, CORE_BIT)
 
 
 def product(cols, rows):
-    out = lax.dot_general(cols, rows, (((0,), (0,)), ((), ())), preferred_element_type=f32)
-    return out.reshape(4, -1, rows.shape[1])
+    out = sum(
+        lax.dot_general(c, r, (((0,), (0,)), ((), ())), preferred_element_type=f32)
+        for c, r in zip(cols, rows)
+    )
+    return out
+
+
+def by_owner(parts):
+    return parts.reshape(LINE, -1, parts.shape[-1])
 
 
 LINE = 4
+ORDER = (1, 2, 3)
 
 
 def direct_parts(parts, z):
-    return at(parts, z), [at(parts, (z + k) % LINE).astype(bf16) for k in (2, 1, 3)]
+    return at(parts, z), [at(parts, (z + k) % LINE).astype(bf16) for k in ORDER]
 
 
 def direct_send(sends):
     return [
         z_pairs(send, [(a, (a + k) % LINE) for a in range(LINE)])
-        for k, send in zip((2, 1, 3), sends)
+        for k, send in zip(ORDER, sends)
     ]
 
 
@@ -326,18 +338,14 @@
     return own + sum(r.astype(f32) for r in received)
 
 
-def line_first(parts, z2):
-    parts = parts.reshape(2, 2, *parts.shape[1:])
-    far = at(parts, 1 - z2)
-    return at(parts, z2), far + z_pairs(far.astype(bf16), [(0, 1), (3, 2)]).astype(f32)
-
-
-def line_second(near, far):
-    return near + inner_swap(far.astype(bf16)).astype(f32)
-
-
-def line_third(near, z1):
-    return at(near, z1) + flip(at(near, 1 - z1).astype(bf16), Z1_BIT).astype(f32)
+def pair_first(parts, z1):
+    parts = parts.reshape(2, 2, *parts.shape[1:]).swapaxes(0, 1)
+    return at(parts, z1), flip(at(parts, 1 - z1).astype(bf16), Z1_BIT)
+
+
+def pair_second(own, received, z2):
+    total = own + received.astype(f32)
+    return at(total, z2) + flip(at(total, 1 - z2).astype(bf16), Z2_BIT).astype(f32)
 
 
 tie = lax.optimization_barrier
@@ -352,7 +360,7 @@
     gate, up, act, out, m_y, n_y = tie((gate, up, act, out, m_y, n_y))
     state = (*state, gate, up, act)
     act_y = cols_y(act, y)
-    m_all, n_all = with_other(m_y, CORE_BIT), with_other(n_y, CORE_BIT)
+    m_all, n_all = rows_core(m_y), rows_core(n_y)
     _, _, dm = backward_ffn(x, state, weights)
     dm, act_y, m_all, n_all = tie((dm, act_y, m_all, n_all))
     act_c = cols_core(act_y, core)
@@ -369,56 +377,57 @@
     z2, z1 = z >> 1, z & 1
     m_all, n_all, act_c = early
     tokens, width = o.shape[0], e.shape[1]
-    share = act_c.shape[1] // 4
+    share = act_c[0].shape[1] // LINE
     eb = e.astype(bf16)
     eb_y = with_other(eb, Y_BIT)
     dgate, dup, dm = backward_ffn(eb, state, weights)
     dgate, dup, dm, eb_y = tie((dgate, dup, dm, eb_y))
+    eb_all = rows_core(eb_y)
     gate_y = cols_y(dgate, y)
-    eb_all = with_other(eb_y, CORE_BIT)
     dh1, dz, do, gain_two_grad = backward_mid(e, dm, state, weights)
     do, dz, eb_all, dup = tie((do, dz, eb_all, dup))
-    down_own, down_sends = direct_parts(product(act_c, eb_all), z)
-    do, down_sends = tie((do, down_sends))
-    down_two, down_one, down_three = direct_send(down_sends)
+    down_own, down_sends = direct_parts(by_owner(product(act_c, eb_all)), z)
+    do, gate_y, down_sends = tie((do, gate_y, down_sends))
+    down_one, down_two, down_three = direct_send(down_sends)
     gate_c = cols_core(gate_y, core)
     up_y = cols_y(dup, y)
     dproj = backward_attention(do, state, tables)
-    dproj, gate_c, up_y, down_two = tie((dproj, gate_c, up_y, down_two))
-    gate_near, gate_far = line_first(product(gate_c, m_all), z2)
+    dproj, gate_c, up_y, down_one = tie((dproj, gate_c, up_y, down_one))
+    gate_own, gate_received = pair_first(by_owner(product(gate_c, m_all)), z1)
     up_c = cols_core(up_y, core)
+    dz_y = with_other(dz, Y_BIT)
     attn_cols = jnp.concatenate([dproj, o], axis=1).reshape(tokens, 4, 4, share)
     attn_cols = attn_cols.transpose(2, 0, 1, 3).reshape(4, tokens, 4 * share)
     attn_y = cols_y(attn_cols, y)
-    dz_y = with_other(dz, Y_BIT)
-    gate_near, gate_far, up_c, attn_y, dz_y, down_one = tie(
-        (gate_near, gate_far, up_c, attn_y, dz_y, down_one)
-    )
-    up_near, up_far = line_first(product(up_c, m_all), z2)
-    gate_near = line_second(gate_near, gate_far)
+    dproj, up_c, dz_y, attn_y, down_three = tie((dproj, up_c, dz_y, attn_y, down_three))
+    up_own, up_received = pair_first(by_owner(product(up_c, m_all)), z1)
     attn_c = cols_core(attn_y, core)
-    dz_all = with_other(dz_y, CORE_BIT)
+    dz_all = rows_core(dz_y)
     du, gain_one_grad = backward_in(dproj, dh1, state, weights)
     gain_grad = jnp.concatenate([gain_one_grad, gain_two_grad])
     gain_grad = gain_grad + flip(gain_grad, CORE_BIT)
     gain_grad = gain_grad + flip(gain_grad, Y_BIT)
-    attn_c, dz_all, gain_grad, up_near, up_far, gate_near, down_three = tie(
-        (attn_c, dz_all, gain_grad, up_near, up_far, gate_near, down_three)
-    )
-    owners = (jnp.arange(4, dtype=jnp.int32) * 4 + y * 2 + core).reshape(4, 1, 1)
-    is_qkv = owners * share < QKV_COLS
-    attn = jnp.where(is_qkv, product(attn_c, n_all), product(attn_c, dz_all))
+    gain_grad, attn_c, dz_all, gate_own, gate_received, down_two = tie(
+        (gain_grad, attn_c, dz_all, gate_own, gate_received, down_two)
+    )
+    qkv_owners = QKV_COLS // share
+    from_n = product([c[:, : -(-qkv_owners // 4) * share] for c in attn_c], n_all)
+    from_dz = product([c[:, qkv_owners // 4 * share :] for c in attn_c], dz_all)
+    shared = qkv_owners // 4 * share
+    mixed = -(-qkv_owners // 4) * share - shared
+    is_qkv = qkv_owners // 4 * 4 + y * 2 + core < qkv_owners
+    both = jnp.where(is_qkv, from_n[shared:], from_dz[:mixed])
+    attn = by_owner(jnp.concatenate([from_n[:shared], both, from_dz[mixed:]], axis=0))
     gain_rows = at(gain_grad.reshape(4, 4, -1).transpose(1, 0, 2), y * 2 + core)[:, None]
     gain_share = gain_rows.shape[-1]
     gain_rows = jnp.pad(gain_rows, ((0, 0), (0, EXTRA_ROWS - 1), (0, width - gain_share)))
-    attn_near, attn_far = line_first(jnp.concatenate([attn, gain_rows], axis=1), z2)
-    up_near = line_second(up_near, up_far)
-    gate = line_third(gate_near, z1)
-    down = direct_total(down_own, (down_two, down_one, down_three))
-    attn_near, attn_far, up_near, gate, down = tie((attn_near, attn_far, up_near, gate, down))
-    attn_near = line_second(attn_near, attn_far)
-    up = line_third(up_near, z1)
-    attn = line_third(attn_near, z1)
+    attn_own, attn_sends = direct_parts(jnp.concatenate([attn, gain_rows], axis=1), z)
+    attn_received = direct_send(attn_sends)
+    down_received = (down_one, down_two, down_three)
+    gate = pair_second(gate_own, gate_received, z2)
+    up = pair_second(up_own, up_received, z2)
+    down = direct_total(down_own, down_received)
+    attn = direct_total(attn_own, attn_received)
     return (
         du,
         attn[:share],

time: 378 us -> 363 us (0.960)
  starting transfers between devices: 68.3 us -> 44.6 us
  matrix products: 22.2 us -> 35.2 us
  other arithmetic: 38.5 us -> 25.9 us
  local copies, waits for them, and re-layouts: 16.1 us -> 28.1 us
  waiting for transfers between devices: 180 us -> 176 us
    ppermute x9 -> x6, waiting for transfers between devices: 20.5 us -> 0.02 us  [z_pairs(): lax.ppermute(x, 'dp', [(4 * a + i, 4 * b + i) for a, b in pairs for i in...]
    ppermute x25 -> x26, waiting for transfers between devices: 47.5 us -> 63.6 us  [flip(): return lax.ppermute(x, 'dp', [(i, i ^ bit) for i in range(size)])]
    ppermute x9 -> x6, starting transfers between devices: 23.1 us -> 8.83 us  [z_pairs(): lax.ppermute(x, 'dp', [(4 * a + i, 4 * b + i) for a, b in pairs for i in...]
    ppermute x25 -> x26, starting transfers between devices: 40.1 us -> 30.7 us  [flip(): return lax.ppermute(x, 'dp', [(i, i ^ bit) for i in range(size)])]
    dot_general x5 -> x10, matrix products: 4.3 us -> 12.8 us  [product(): lax.dot_general(c, r, (((0,), (0,)), ((), ())), preferred_element_type=f32)]
    concatenate x8 -> x4, other arithmetic: 13 us -> 5.14 us  [with_other(): return jnp.concatenate([x, flip(x, bit)], axis=0)]
    add x0 -> x3, local copies, waits for them, and re-layouts: none -> 6.64 us  [product(): sum((lax.dot_general(c, r, (((0,), (0,)), ((), ())), preferred_element_ty...]
  transfers between devices with their start and end apart: 37 -> 35, of which waited for: 19 -> 14; matrix products, arithmetic and copies ran while one was open for 11% -> 14% of each run, Pallas kernels for 7% -> 7%
where the time goes in v6:
time: 363 us; the launch traced here: 362 us
  waiting for transfers between devices  176 us (48%)
  starting transfers between devices  44.6 us (12%)
  Pallas kernels  36.4 us (10%)
  matrix products  35.2 us (10%)
  local copies, waits for them, and re-layouts  28.1 us (8%)
  other arithmetic  25.9 us (7%)
  between operations  15.5 us (4%)
    all_gather x1, waiting for transfers between devices, local(): lax.all_gather(own, 'dp', axis=0, tiled=True).reshape(4, 4, 4, share, width)  97.4 us
    ppermute x26, waiting for transfers between devices, flip(): return lax.ppermute(x, 'dp', [(i, i ^ bit) for i in range(size)])  63.6 us
    pallas_call x4, Pallas kernels, ffn_call(): pl.pallas_call(kernel, grid=(steps,), in_specs=[whole] * len(wholes) + [b...  36.4 us
    ppermute x26, starting transfers between devices, flip(): return lax.ppermute(x, 'dp', [(i, i ^ bit) for i in range(size)])  30.7 us
    dot_general x10, matrix products, product(): lax.dot_general(c, r, (((0,), (0,)), ((), ())), preferred_element_type=f32)  12.8 us
    dot_general x4, matrix products, dot_nt(): lax.dot_general(a, b, (((1,), (1,)), ((), ())), preferred_element_type=f32)  9.47 us
    ppermute x1, waiting for transfers between devices, local(): received = lax.ppermute(first_grad, 'section', [(1, 0)])  9.21 us
    ppermute x6, starting transfers between devices, z_pairs(): lax.ppermute(x, 'dp', [(4 * a + i, 4 * b + i) for a, b in pairs for i in...  8.83 us
  transfers between devices with their start and end apart: 35, of which 14 were waited for; matrix products, arithmetic and copies ran while one was open for 14% of the time, Pallas kernels for 7%

profile of v6, /device:TPU:0, one launch (start us, length us, event | category | flops | bytes accessed | tf_op | source)
XLA Modules:
  0.0 361.7 jit_solution(5295792881538244749)
XLA Ops:
  7.2 2.5 pad_maximum_fusion.1
  11.2 2.8 collective-permute-start.1
  14.2 1.4 collective-permute-done.1
  15.7 2.1 collective-permute-start.2
  17.9 1.4 collective-permute-done.2
  19.5 3.0 collective-permute-start.3
  22.8 1.3 collective-permute-done.3
  24.4 97.4 %all-gather.2.cloned.1.call-done = bf16[10240,960]{1,0:T(8,128)(2,1)} async-done(((bf16[640,960]{1,0:T(8,128)(2,1)}), bf16[10240,960]{1,0:T(8,128)(2,1)}) %all-gather.2.cloned.1.call-update) | async-done | bytes 19660816 | tf_op jit(solution)/shard_map/all_gather | solution.py:452
  121.8 3.4 slice.151
  125.2 1.1 fusion.6
  128.3 9.6 %shard_map.84 = (f32[4,128,640]{2,1,0:T(8,128)}, f32[4,128,640]{2,1,0:T(8,128)}, bf16[4,128,640]{2,1,0:T(8,128)(2,1)}, f32[128,960]{1,0:T(8,128)S(1)}) custom-call(bf16[128,960]{1,0:T(8,128)(2,1)S(1)} %multiply_convert_fusion.3.m_ref, f32[128,960]{1,0:T(8,128)S(1)} %get-tuple-element.186.h1_ref, bf16[4,4,4,160,960]{4,3,2,1,0:T(8,128)(2,1)} %bitcast.258, ...), custom_call_target="tpu_custom_call" | custom-call | flops 1887436800 | bytes 14745600 | tf_op jit(solution)/shard_map/pallas_call | solution.py:203
  137.9 3.6 collective-permute-start.4
  141.5 5.8 %collective-permute-done.4 = bf16[128,960]{1,0:T(8,128)(2,1)S(1)} collective-permute-done((bf16[128,960]{1,0:T(8,128)(2,1)S(1)}, bf16[128,960]{1,0:T(8,128)(2,1)S(1)}, u32[]{:S(2)}, u32[]{:S(2)}) %collective-permute-start.4) | collective-permute-done | bytes 245792 | tf_op jit(solution)/shard_map/ppermute | solution.py:467
  148.9 3.0 fusion.4
  153.8 2.2 multiply_reduce_fusion.5
  156.8 1.2 collective-permute-start.5
  158.8 8.3 %shard_map.85 = (f32[4,128,640]{2,1,0:T(8,128)S(1)}, f32[4,128,640]{2,1,0:T(8,128)S(1)}, bf16[4,128,640]{2,1,0:T(8,128)(2,1)S(1)}, f32[128,960]{1,0:T(8,128)S(1)}) custom-call(bf16[128,960]{1,0:T(8,128)(2,1)} %multiply_convert_fusion.2.m_ref, f32[128,960]{1,0:T(8,128)S(1)} %get-tuple-element.190.h1_ref, bf16[4,4,4,160,960]{4,3,2,1,0:T(8,128)(2,1)} %bitcast.261, ...), custom_call_target="tpu_custom_call" | custom-call | flops 1887436800 | bytes 14745600 | tf_op jit(solution)/shard_map/pallas_call | solution.py:203
  167.2 2.1 pad_maximum_fusion.7
  170.3 1.8 pad_maximum_fusion.8
  173.5 1.2 collective-permute-start.7
  174.8 9.7 %shard_map.86 = (bf16[4,128,640]{2,1,0:T(8,128)(2,1)}, bf16[4,128,640]{2,1,0:T(8,128)(2,1)}, f32[128,960]{1,0:T(8,128)S(1)}) custom-call(bf16[128,960]{1,0:T(8,128)(2,1)S(1)} %bitcast.253, f32[4,128,640]{2,1,0:T(8,128)S(1)} %get-tuple-element.66.gate_ref, f32[4,128,640]{2,1,0:T(8,128)S(1)} %get-tuple-element.67.up_ref, ...), custom_call_target="tpu_custom_call" | custom-call | flops 1887436800 | bytes 14745600 | tf_op jit(solution)/shard_map/pallas_call | solution.py:203
  185.9 2.3 fusion.30
  191.1 2.7 fusion.61
  194.1 1.5 collective-permute-start.11
  195.6 9.2 %collective-permute-done.11 = bf16[128,960]{1,0:T(8,128)(2,1)S(1)} collective-permute-done((bf16[128,960]{1,0:T(8,128)(2,1)S(1)}, bf16[128,960]{1,0:T(8,128)(2,1)S(1)}, u32[]{:S(2)}, u32[]{:S(2)}) %collective-permute-start.11) | collective-permute-done | bytes 245792 | tf_op jit(solution)/shard_map/ppermute | solution.py:471
  206.4 8.8 %shard_map.87 = (bf16[4,128,640]{2,1,0:T(8,128)(2,1)S(1)}, bf16[4,128,640]{2,1,0:T(8,128)(2,1)S(1)}, f32[128,960]{1,0:T(8,128)S(1)}) custom-call(bf16[128,960]{1,0:T(8,128)(2,1)} %broadcast_select_fusion.eb_ref, f32[4,128,640]{2,1,0:T(8,128)S(1)} %get-tuple-element.66.gate_ref, f32[4,128,640]{2,1,0:T(8,128)S(1)} %get-tuple-element.67.up_ref, ...), custom_call_target="tpu_custom_call" | custom-call | flops 1887436800 | bytes 14745600 | tf_op jit(solution)/shard_map/pallas_call | solution.py:203
  215.2 1.2 pad_maximum_fusion.9
  217.2 1.3 collective-permute-start.14
  218.5 1.1 fusion.105
  219.7 3.0 fusion.33
  222.7 4.7 %collective-permute-done.14 = bf16[2,128,640]{2,1,0:T(8,128)(2,1)S(1)} collective-permute-done((bf16[2,128,640]{2,1,0:T(8,128)(2,1)S(1)}, bf16[2,128,640]{2,1,0:T(8,128)(2,1)S(1)}, u32[]{:S(2)}, u32[]{:S(2)}) %collective-permute-start.14) | collective-permute-done | bytes 327712 | tf_op jit(solution)/shard_map/ppermute | solution.py:243
  229.6 2.2 copy.59
  231.8 2.6 fusion.77
  234.4 1.3 fusion.41
  237.9 1.3 collective-permute-start.16
  239.1 1.5 collective-permute-start.17
  241.4 2.3 collective-permute-start.21
  243.9 9.5 %collective-permute-done.19 = bf16[128,960]{1,0:T(8,128)(2,1)S(1)} collective-permute-done((bf16[128,960]{1,0:T(8,128)(2,1)S(1)}, bf16[128,960]{1,0:T(8,128)(2,1)S(1)}, u32[]{:S(2)}, u32[]{:S(2)}) %collective-permute-start.19) | collective-permute-done | bytes 245792 | tf_op jit(solution)/shard_map/ppermute | solution.py:243
  253.4 2.4 collective-permute-start.27
  258.0 1.2 collective-permute-start.20
  259.2 1.6 fusion.110
  260.9 1.7 convolution_add_fusion.1
  262.6 2.2 copy.66
  264.8 2.3 fusion.42
  267.9 2.5 dynamic-slice_bitcast_fusion
  271.6 2.8 fusion.64
  275.9 1.7 fusion.111
  277.7 1.7 convolution_add_fusion
  280.4 2.2 copy.68
  282.7 1.4 collective-permute-start.23
  284.2 1.4 fusion.43
  286.4 1.2 collective-permute-start.32
  287.8 1.5 fusion.90
  289.2 1.6 fusion.87
  290.8 1.5 convolution_add_fusion.3
  293.7 1.5 collective-permute-start.30
  296.2 1.4 convert_add_fusion
  297.7 2.6 collective-permute-start.31
  300.3 1.5 fusion.44
  301.8 8.7 %collective-permute-done.32 = bf16[2,160,960]{2,1,0:T(8,128)(2,1)S(1)} collective-permute-done((bf16[2,160,960]{2,1,0:T(8,128)(2,1)S(1)}, bf16[2,160,960]{2,1,0:T(8,128)(2,1)S(1)}, u32[]{:S(2)}, u32[]{:S(2)}) %collective-permute-start.32) | collective-permute-done | bytes 614432 | tf_op jit(solution)/shard_map/ppermute | solution.py:243
  310.8 6.4 %collective-permute-start.33 = (bf16[160,960]{1,0:T(8,128)(2,1)S(1)}, bf16[160,960]{1,0:T(8,128)(2,1)S(1)}, u32[]{:S(2)}, u32[]{:S(2)}) collective-permute-start(bf16[160,960]{1,0:T(8,128)(2,1)S(1)} %fusion.79), channel_id=1, source_target_pairs={{0,8},{1,9},{2,10},{3,11},{4,12},{5,13},{6,14},{7,15},{8,0},{9,1},... | collective-permute-start | bytes 921608 | tf_op jit(solution)/shard_map/ppermute | solution.py:243
  317.2 30.9 %collective-permute-done.31 = bf16[160,960]{1,0:T(8,128)(2,1)S(1)} collective-permute-done((bf16[160,960]{1,0:T(8,128)(2,1)S(1)}, bf16[160,960]{1,0:T(8,128)(2,1)S(1)}, u32[]{:S(2)}, u32[]{:S(2)}) %collective-permute-start.31) | collective-permute-done | bytes 307232 | tf_op jit(solution)/shard_map/ppermute | solution.py:243
  349.9 3.5 collective-permute-done.33
  353.5 1.4 maximum_bitcast_fusion
  (281 shorter events, 35.5 us)
Async XLA Ops:
  7.2 10.6 %copy-start = (bf16[1,2,64,960]{3,2,1,0:T(8,128)(2,1)S(1)}, bf16[1,2,64,960]{3,2,1,0:T(8,128)(2,1)}, u32[]{:S(2)}) copy-start(bf16[1,2,64,960]{3,2,1,0:T(8,128)(2,1)} %param.5) | copy-start | bytes 737284
  7.2 114.6 %all-gather.2.cloned.1.call-start = ((), (), s32[]{:S(2)}) async-start(), calls=%async_computation | async-start | bytes 22282240 | tf_op jit(solution)/shard_map/all_gather | solution.py:452
  9.8 1.3 collective-permute-start
  11.2 4.3 %collective-permute-start.1 = (bf16[240]{0:T(256)(128)(2,1)S(1)}, bf16[240]{0:T(256)(128)(2,1)S(1)}, u32[]{:S(2)}, u32[]{:S(2)}) collective-permute-start(bf16[240]{0:T(256)(128)(2,1)S(1)} %pad_maximum_fusion.23), channel_id=1, source_target_pairs={{0,2},{1,3},{2,0},{3,1},{4,6},{5,7},{6,4},{7,5},{8,10},{9,11},{10,... | collective-permute-start | bytes 1448 | tf_op jit(solution)/shard_map/ppermute | solution.py:243
  15.7 3.6 %collective-permute-start.2 = (bf16[480]{0:T(512)(128)(2,1)S(1)}, bf16[480]{0:T(512)(128)(2,1)S(1)}, u32[]{:S(2)}, u32[]{:S(2)}) collective-permute-start(bf16[480]{0:T(512)(128)(2,1)S(1)} %pad_maximum_fusion.22), channel_id=1, source_target_pairs={{0,4},{1,5},{2,6},{3,7},{4,0},{5,1},{6,2},{7,3},{8,12},{9,13},{10,... | collective-permute-start | bytes 2888 | tf_op jit(solution)/shard_map/ppermute | solution.py:243
  19.5 4.7 %collective-permute-start.3 = (bf16[960]{0:T(1024)(128)(2,1)S(1)}, bf16[960]{0:T(1024)(128)(2,1)S(1)}, u32[]{:S(2)}, u32[]{:S(2)}) collective-permute-start(bf16[960]{0:T(1024)(128)(2,1)S(1)} %pad_maximum_fusion.21), channel_id=1, source_target_pairs={{0,8},{1,9},{2,10},{3,11},{4,12},{5,13},{6,14},{7,15},{8,0},{9,1},... | collective-permute-start | bytes 5768 | tf_op jit(solution)/shard_map/ppermute | solution.py:243
  24.4 123.6 %copy-start.48 = (f32[960]{0:T(1024)}, f32[960]{0:T(1024)S(1)}, u32[]{:S(2)}) copy-start(f32[960]{0:T(1024)S(1)} %get-tuple-element.167) | copy-start | bytes 11524
  137.9 9.4 %collective-permute-start.4 = (bf16[128,960]{1,0:T(8,128)(2,1)S(1)}, bf16[128,960]{1,0:T(8,128)(2,1)S(1)}, u32[]{:S(2)}, u32[]{:S(2)}) collective-permute-start(bf16[128,960]{1,0:T(8,128)(2,1)S(1)} %convert_element_type.209), channel_id=1, source_target_pairs={{0,16},{1,17},{2,18},{3,19},{4,20},{5,21},{6,22},{7,23},{8,24},{9,... | collective-permute-start | bytes 737288 | tf_op jit(solution)/shard_map/ppermute | solution.py:467
  147.5 6.3 %copy-start.13 = (bf16[128,960]{1,0:T(8,128)(2,1)}, bf16[128,960]{1,0:T(8,128)(2,1)S(1)}, u32[]{:S(2)}) copy-start(bf16[128,960]{1,0:T(8,128)(2,1)S(1)} %get-tuple-element.125) | copy-start | bytes 737284
  148.0 3.9 %copy-start.54 = (f32[128]{0:T(128)}, f32[128]{0:T(128)S(1)}, u32[]{:S(2)}) copy-start(f32[128]{0:T(128)S(1)} %get-tuple-element.180) | copy-start | bytes 1540
  151.9 36.6 %copy-start.23 = (bf16[128,320]{0,1:T(8,128)(2,1)}, bf16[128,320]{0,1:T(8,128)(2,1)S(1)}, u32[]{:S(2)}) copy-start(bf16[128,320]{0,1:T(8,128)(2,1)S(1)} %slice.254) | copy-start | bytes 245764
  156.0 29.7 %copy-start.59 = (f32[128]{0:T(128)}, f32[128]{0:T(128)S(1)}, u32[]{:S(2)}) copy-start(f32[128]{0:T(128)S(1)} %get-tuple-element.181) | copy-start | bytes 1540
  156.0 60.5 %copy-start.53 = (f32[128]{0:T(128)}, f32[128]{0:T(128)S(1)}, u32[]{:S(2)}) copy-start(f32[128]{0:T(128)S(1)} %get-tuple-element.182) | copy-start | bytes 1540
  156.8 10.3 %collective-permute-start.5 = (bf16[128,960]{1,0:T(8,128)(2,1)}, bf16[128,960]{1,0:T(8,128)(2,1)}, u32[]{:S(2)}, u32[]{:S(2)}) collective-permute-start(bf16[128,960]{1,0:T(8,128)(2,1)} %multiply_convert_fusion.2.m_ref), channel_id=1, source_target_pairs={{0,2},{1,3},{2,0},{3,1},{4,6},{5,7},{6,4},{7,5},{8,10},{9,11},{10,... | collective-permute-start | bytes 737288 | tf_op jit(solution)/shard_map/ppermute | solution.py:243
  158.1 12.3 %collective-permute-start.6 = (bf16[128,960]{1,0:T(8,128)(2,1)}, bf16[128,960]{1,0:T(8,128)(2,1)S(1)}, u32[]{:S(2)}, u32[]{:S(2)}) collective-permute-start(bf16[128,960]{1,0:T(8,128)(2,1)} %fusion.60), channel_id=1, source_target_pairs={{0,2},{1,3},{2,0},{3,1},{4,6},{5,7},{6,4},{7,5},{8,10},{9,11},{10,... | collective-permute-start | bytes 737288 | tf_op jit(solution)/shard_map/ppermute | solution.py:243
  167.1 6.4 %copy-start.3 = (f32[128,960]{1,0:T(8,128)}, f32[128,960]{1,0:T(8,128)S(1)}, u32[]{:S(2)}) copy-start(f32[128,960]{1,0:T(8,128)S(1)} %get-tuple-element.96) | copy-start | bytes 1474564
  172.1 13.4 %collective-permute-start.8 = (bf16[256,960]{1,0:T(8,128)(2,1)}, bf16[256,960]{1,0:T(8,128)(2,1)}, u32[]{:S(2)}, u32[]{:S(2)}) collective-permute-start(bf16[256,960]{1,0:T(8,128)(2,1)} %pad_maximum_fusion.7), channel_id=1, source_target_pairs={{0,1},{1,0},{2,3},{3,2},{4,5},{5,4},{6,7},{7,6},{8,9},{9,8},{10,11... | collective-permute-start | bytes 1474568 | tf_op jit(solution)/shard_map/ppermute | solution.py:243
  172.1 13.4 %collective-permute-start.9 = (bf16[256,960]{1,0:T(8,128)(2,1)}, bf16[256,960]{1,0:T(8,128)(2,1)}, u32[]{:S(2)}, u32[]{:S(2)}) collective-permute-start(bf16[256,960]{1,0:T(8,128)(2,1)} %pad_maximum_fusion.8), channel_id=1, source_target_pairs={{0,1},{1,0},{2,3},{3,2},{4,5},{5,4},{6,7},{7,6},{8,9},{9,8},{10,11... | collective-permute-start | bytes 1474568 | tf_op jit(solution)/shard_map/ppermute | solution.py:243
  173.5 10.9 %collective-permute-start.7 = (bf16[2,128,640]{2,1,0:T(8,128)(2,1)}, bf16[2,128,640]{2,1,0:T(8,128)(2,1)}, u32[]{:S(2)}, u32[]{:S(2)}) collective-permute-start(bf16[2,128,640]{2,1,0:T(8,128)(2,1)} %get-tuple-element.149), channel_id=1, source_target_pairs={{0,2},{1,3},{2,0},{3,1},{4,6},{5,7},{6,4},{7,5},{8,10},{9,11},{10,... | collective-permute-start | bytes 983048 | tf_op jit(solution)/shard_map/ppermute | solution.py:243
  174.8 9.7 %copy-start.27 = (bf16[2,128,640]{2,1,0:T(8,128)(2,1)S(1)}, bf16[2,128,640]{2,1,0:T(8,128)(2,1)}, u32[]{:S(2)}) copy-start(bf16[2,128,640]{2,1,0:T(8,128)(2,1)} %get-tuple-element.148) | copy-start | bytes 983044
  191.1 3.0 collective-permute-start.10
  194.1 11.5 %copy-start.44 = (bf16[256,640]{1,0:T(8,128)(2,1)}, bf16[256,640]{1,0:T(8,128)(2,1)S(1)}, u32[]{:S(2)}) copy-start(bf16[256,640]{1,0:T(8,128)(2,1)S(1)} %collective-permute-done.10) | copy-start | bytes 983044
  194.1 10.7 %collective-permute-start.11 = (bf16[128,960]{1,0:T(8,128)(2,1)S(1)}, bf16[128,960]{1,0:T(8,128)(2,1)S(1)}, u32[]{:S(2)}, u32[]{:S(2)}) collective-permute-start(bf16[128,960]{1,0:T(8,128)(2,1)S(1)} %fusion.51), channel_id=1, source_target_pairs={{16,0},{17,1},{18,2},{19,3},{20,4},{21,5},{22,6},{23,7},{24,8},{25... | collective-permute-start | bytes 737288 | tf_op jit(solution)/shard_map/ppermute | solution.py:471
  205.6 9.6 %collective-permute-start.12 = (bf16[128,960]{1,0:T(8,128)(2,1)}, bf16[128,960]{1,0:T(8,128)(2,1)S(1)}, u32[]{:S(2)}, u32[]{:S(2)}) collective-permute-start(bf16[128,960]{1,0:T(8,128)(2,1)} %broadcast_select_fusion.eb_ref), channel_id=1, source_target_pairs={{0,2},{1,3},{2,0},{3,1},{4,6},{5,7},{6,4},{7,5},{8,10},{9,11},{10,... | collective-permute-start | bytes 737288 | tf_op jit(solution)/shard_map/ppermute | solution.py:243
  215.2 4.5 %copy-start.1 = (bf16[4,128,640]{2,1,0:T(8,128)(2,1)}, bf16[4,128,640]{2,1,0:T(8,128)(2,1)S(1)}, u32[]{:S(2)}) copy-start(bf16[4,128,640]{2,1,0:T(8,128)(2,1)S(1)} %get-tuple-element.89) | copy-start | bytes 1966084
  217.2 11.1 %collective-permute-start.13 = (bf16[256,960]{1,0:T(8,128)(2,1)S(1)}, bf16[256,960]{1,0:T(8,128)(2,1)S(1)}, u32[]{:S(2)}, u32[]{:S(2)}) collective-permute-start(bf16[256,960]{1,0:T(8,128)(2,1)S(1)} %pad_maximum_fusion.9), channel_id=1, source_target_pairs={{0,1},{1,0},{2,3},{3,2},{4,5},{5,4},{6,7},{7,6},{8,9},{9,8},{10,11... | collective-permute-start | bytes 1474568 | tf_op jit(solution)/shard_map/ppermute | solution.py:243
  217.2 10.2 %collective-permute-start.14 = (bf16[2,128,640]{2,1,0:T(8,128)(2,1)S(1)}, bf16[2,128,640]{2,1,0:T(8,128)(2,1)S(1)}, u32[]{:S(2)}, u32[]{:S(2)}) collective-permute-start(bf16[2,128,640]{2,1,0:T(8,128)(2,1)S(1)} %get-tuple-element.145), channel_id=1, source_target_pairs={{0,2},{1,3},{2,0},{3,1},{4,6},{5,7},{6,4},{7,5},{8,10},{9,11},{10,... | collective-permute-start | bytes 983048 | tf_op jit(solution)/shard_map/ppermute | solution.py:243
  219.7 9.2 %copy-start.35 = (bf16[128,960]{1,0:T(8,128)(2,1)}, bf16[128,960]{1,0:T(8,128)(2,1)S(1)}, u32[]{:S(2)}) copy-start(bf16[128,960]{1,0:T(8,128)(2,1)S(1)} %get-tuple-element.93) | copy-start | bytes 737284
  219.7 8.6 %copy-start.45 = (bf16[256,640]{1,0:T(8,128)(2,1)S(1)}, bf16[256,640]{1,0:T(8,128)(2,1)}, u32[]{:S(2)}) copy-start(bf16[256,640]{1,0:T(8,128)(2,1)} %copy-done.44) | copy-start | bytes 983044
  222.7 6.2 %copy-start.25 = (bf16[256,640]{1,0:T(8,128)(2,1)S(1)}, bf16[256,640]{1,0:T(8,128)(2,1)}, u32[]{:S(2)}) copy-start(bf16[256,640]{1,0:T(8,128)(2,1)} %get-tuple-element.83) | copy-start | bytes 983044
  229.5 4.8 %copy-start.12 = (bf16[5,3,128,128]{2,3,1,0:T(8,128)(2,1)S(1)}, bf16[5,3,128,128]{2,3,1,0:T(8,128)(2,1)}, u32[]{:S(2)}) copy-start(bf16[5,3,128,128]{2,3,1,0:T(8,128)(2,1)} %copy-done.10) | copy-start | bytes 1474564
  231.7 3.9 %copy-start.7 = (f32[5,3,128,128]{2,3,1,0:T(8,128)S(1)}, f32[5,3,128,128]{2,3,1,0:T(8,128)}, u32[]{:S(2)}) copy-start(f32[5,3,128,128]{2,3,1,0:T(8,128)} %copy-done.5) | copy-start | bytes 2949124
  231.8 3.9 %copy-start.24 = (bf16[128,320]{0,1:T(8,128)(2,1)S(1)}, bf16[128,320]{0,1:T(8,128)(2,1)}, u32[]{:S(2)}) copy-start(bf16[128,320]{0,1:T(8,128)(2,1)} %copy-done.23) | copy-start | bytes 245764
  231.8 3.9 %copy-start.37 = (bf16[128,960]{0,1:T(8,128)(2,1)S(1)}, bf16[128,960]{0,1:T(8,128)(2,1)}, u32[]{:S(2)}) copy-start(bf16[128,960]{0,1:T(8,128)(2,1)} %fusion.33) | copy-start | bytes 737284
  237.0 3.7 %copy-start.36 = (bf16[128,960]{1,0:T(8,128)(2,1)S(1)}, bf16[128,960]{1,0:T(8,128)(2,1)}, u32[]{:S(2)}) copy-start(bf16[128,960]{1,0:T(8,128)(2,1)} %copy-done.35) | copy-start | bytes 737284
  237.5 18.5 %collective-permute-start.15 = (bf16[256,640]{1,0:T(8,128)(2,1)S(1)}, bf16[256,640]{1,0:T(8,128)(2,1)S(1)}, u32[]{:S(2)}, u32[]{:S(2)}) collective-permute-start(bf16[256,640]{1,0:T(8,128)(2,1)S(1)} %get-tuple-element.142), channel_id=1, source_target_pairs={{0,1},{1,0},{2,3},{3,2},{4,5},{5,4},{6,7},{7,6},{8,9},{9,8},{10,11... | collective-permute-start | bytes 983048 | tf_op jit(solution)/shard_map/ppermute | solution.py:243
  237.9 18.0 %collective-permute-start.16 = (bf16[2,128,640]{2,1,0:T(8,128)(2,1)S(1)}, bf16[2,128,640]{2,1,0:T(8,128)(2,1)S(1)}, u32[]{:S(2)}, u32[]{:S(2)}) collective-permute-start(bf16[2,128,640]{2,1,0:T(8,128)(2,1)S(1)} %get-tuple-element.141), channel_id=1, source_target_pairs={{0,2},{1,3},{2,0},{3,1},{4,6},{5,7},{6,4},{7,5},{8,10},{9,11},{10,... | collective-permute-start | bytes 983048 | tf_op jit(solution)/shard_map/ppermute | solution.py:243
  239.1 16.8 %collective-permute-start.17 = (bf16[160,960]{1,0:T(8,128)(2,1)S(1)}, bf16[160,960]{1,0:T(8,128)(2,1)S(1)}, u32[]{:S(2)}, u32[]{:S(2)}) collective-permute-start(bf16[160,960]{1,0:T(8,128)(2,1)S(1)} %get-tuple-element.90), channel_id=1, source_target_pairs={{0,4},{1,5},{2,6},{3,7},{4,8},{5,9},{6,10},{7,11},{8,12},{9,13},{1... | collective-permute-start | bytes 921608 | tf_op jit(solution)/shard_map/ppermute | solution.py:282
  240.7 12.7 %collective-permute-start.19 = (bf16[128,960]{1,0:T(8,128)(2,1)S(1)}, bf16[128,960]{1,0:T(8,128)(2,1)S(1)}, u32[]{:S(2)}, u32[]{:S(2)}) collective-permute-start(bf16[128,960]{1,0:T(8,128)(2,1)S(1)} %copy-done.36), channel_id=1, source_target_pairs={{0,2},{1,3},{2,0},{3,1},{4,6},{5,7},{6,4},{7,5},{8,10},{9,11},{10,... | collective-permute-start | bytes 737288 | tf_op jit(solution)/shard_map/ppermute | solution.py:243
  241.4 30.1 %collective-permute-start.21 = (bf16[160,960]{1,0:T(8,128)(2,1)}, bf16[160,960]{1,0:T(8,128)(2,1)}, u32[]{:S(2)}, u32[]{:S(2)}) collective-permute-start(bf16[160,960]{1,0:T(8,128)(2,1)} %get-tuple-element.94), channel_id=1, source_target_pairs={{0,12},{1,13},{2,14},{3,15},{4,0},{5,1},{6,2},{7,3},{8,4},{9,5},{1... | collective-permute-start | bytes 921608 | tf_op jit(solution)/shard_map/ppermute | solution.py:282
  243.8 13.2 %copy-start.19 = (bf16[5,64,3,128]{3,1,2,0:T(8,128)(2,1)S(1)}, bf16[5,64,3,128]{3,1,2,0:T(8,128)(2,1)}, u32[]{:S(2)}) copy-start(bf16[5,64,3,128]{3,1,2,0:T(8,128)(2,1)} %copy-done.18) | copy-start | bytes 737284
  243.9 13.2 %copy-start.21 = (bf16[128,1600]{0,1:T(8,128)(2,1)}, bf16[128,1600]{0,1:T(8,128)(2,1)S(1)}, u32[]{:S(2)}) copy-start(bf16[128,1600]{0,1:T(8,128)(2,1)S(1)} %pad_maximum_fusion.11) | copy-start | bytes 1228804
  253.4 34.2 %collective-permute-start.27 = (bf16[160,960]{1,0:T(8,128)(2,1)}, bf16[160,960]{1,0:T(8,128)(2,1)}, u32[]{:S(2)}, u32[]{:S(2)}) collective-permute-start(bf16[160,960]{1,0:T(8,128)(2,1)} %get-tuple-element.103), channel_id=1, source_target_pairs={{0,8},{1,9},{2,10},{3,11},{4,12},{5,13},{6,14},{7,15},{8,0},{9,1},... | collective-permute-start | bytes 921608 | tf_op jit(solution)/shard_map/ppermute | solution.py:282
  257.0 14.6 %collective-permute-start.18 = (bf16[256,640]{1,0:T(8,128)(2,1)}, bf16[256,640]{1,0:T(8,128)(2,1)}, u32[]{:S(2)}, u32[]{:S(2)}) collective-permute-start(bf16[256,640]{1,0:T(8,128)(2,1)} %get-tuple-element.138), channel_id=1, source_target_pairs={{0,1},{1,0},{2,3},{3,2},{4,5},{5,4},{6,7},{7,6},{8,9},{9,8},{10,11... | collective-permute-start | bytes 983048 | tf_op jit(solution)/shard_map/ppermute | solution.py:243
  258.0 12.5 %collective-permute-start.20 = (bf16[2,128,640]{1,2,0:T(8,128)(2,1)}, bf16[2,128,640]{1,2,0:T(8,128)(2,1)}, u32[]{:S(2)}, u32[]{:S(2)}) collective-permute-start(bf16[2,128,640]{1,2,0:T(8,128)(2,1)} %get-tuple-element.137), channel_id=1, source_target_pairs={{0,2},{1,3},{2,0},{3,1},{4,6},{5,7},{6,4},{7,5},{8,10},{9,11},{10,... | collective-permute-start | bytes 983048 | tf_op jit(solution)/shard_map/ppermute | solution.py:243
  264.8 5.7 %copy-start.28 = (bf16[2,128,640]{1,2,0:T(8,128)(2,1)S(1)}, bf16[2,128,640]{1,2,0:T(8,128)(2,1)}, u32[]{:S(2)}) copy-start(bf16[2,128,640]{1,2,0:T(8,128)(2,1)} %get-tuple-element.136) | copy-start | bytes 983044
  264.8 6.8 %copy-start.15 = (bf16[128,960]{1,0:T(8,128)(2,1)S(1)}, bf16[128,960]{1,0:T(8,128)(2,1)}, u32[]{:S(2)}) copy-start(bf16[128,960]{1,0:T(8,128)(2,1)} %copy-done.13) | copy-start | bytes 737284
  264.8 6.8 %copy-start.22 = (bf16[128,1600]{0,1:T(8,128)(2,1)S(1)}, bf16[128,1600]{0,1:T(8,128)(2,1)}, u32[]{:S(2)}) copy-start(bf16[128,1600]{0,1:T(8,128)(2,1)} %copy-done.21) | copy-start | bytes 1228804
  264.8 6.8 %copy-start.50 = (f32[960]{0:T(1024)S(1)}, f32[960]{0:T(1024)}, u32[]{:S(2)}) copy-start(f32[960]{0:T(1024)} %copy-done.48) | copy-start | bytes 11524
  264.8 6.8 %copy-start.56 = (f32[128]{0:T(128)S(1)}, f32[128]{0:T(128)}, u32[]{:S(2)}) copy-start(f32[128]{0:T(128)} %copy-done.54) | copy-start | bytes 1540
  267.2 20.5 %collective-permute-start.26 = (bf16[2,160,960]{2,1,0:T(8,128)(2,1)}, bf16[2,160,960]{2,1,0:T(8,128)(2,1)}, u32[]{:S(2)}, u32[]{:S(2)}) collective-permute-start(bf16[2,160,960]{2,1,0:T(8,128)(2,1)} %fusion.42), channel_id=1, source_target_pairs={{0,4},{1,5},{2,6},{3,7},{4,0},{5,1},{6,2},{7,3},{8,12},{9,13},{10,... | collective-permute-start | bytes 1843208 | tf_op jit(solution)/shard_map/ppermute | solution.py:243
  274.5 8.2 %collective-permute-start.22 = (f32[1920]{0:T(1024)S(1)}, f32[1920]{0:T(1024)S(1)}, u32[]{:S(2)}, u32[]{:S(2)}) collective-permute-start(f32[1920]{0:T(1024)S(1)} %pad_maximum_fusion.20), channel_id=1, source_target_pairs={{0,1},{1,0},{2,3},{3,2},{4,5},{5,4},{6,7},{7,6},{8,9},{9,8},{10,11... | collective-permute-start | bytes 23048 | tf_op jit(solution)/shard_map/ppermute | solution.py:243
  275.4 12.2 %collective-permute-start.24 = (bf16[256,640]{0,1:T(8,128)(2,1)}, bf16[256,640]{0,1:T(8,128)(2,1)}, u32[]{:S(2)}, u32[]{:S(2)}) collective-permute-start(bf16[256,640]{0,1:T(8,128)(2,1)} %get-tuple-element.134), channel_id=1, source_target_pairs={{0,1},{1,0},{2,3},{3,2},{4,5},{5,4},{6,7},{7,6},{8,9},{9,8},{10,11... | collective-permute-start | bytes 983048 | tf_op jit(solution)/shard_map/ppermute | solution.py:243
  275.9 11.8 %collective-permute-start.25 = (bf16[256,960]{1,0:T(8,128)(2,1)S(1)}, bf16[256,960]{1,0:T(8,128)(2,1)}, u32[]{:S(2)}, u32[]{:S(2)}) collective-permute-start(bf16[256,960]{1,0:T(8,128)(2,1)S(1)} %pad_maximum_fusion.10), channel_id=1, source_target_pairs={{0,1},{1,0},{2,3},{3,2},{4,5},{5,4},{6,7},{7,6},{8,9},{9,8},{10,11... | collective-permute-start | bytes 1474568 | tf_op jit(solution)/shard_map/ppermute | solution.py:243
  282.7 3.7 %collective-permute-start.23 = (f32[1920]{0:T(1024)S(1)}, f32[1920]{0:T(1024)S(1)}, u32[]{:S(2)}, u32[]{:S(2)}) collective-permute-start(f32[1920]{0:T(1024)S(1)} %fusion.104), channel_id=1, source_target_pairs={{0,2},{1,3},{2,0},{3,1},{4,6},{5,7},{6,4},{7,5},{8,10},{9,11},{10,... | collective-permute-start | bytes 23048 | tf_op jit(solution)/shard_map/ppermute | solution.py:243
  285.6 5.2 %copy-start.20 = (bf16[256,640]{0,1:T(8,128)(2,1)S(1)}, bf16[256,640]{0,1:T(8,128)(2,1)}, u32[]{:S(2)}) copy-start(bf16[256,640]{0,1:T(8,128)(2,1)} %get-tuple-element.104) | copy-start | bytes 983044
  286.4 24.1 %collective-permute-start.32 = (bf16[2,160,960]{2,1,0:T(8,128)(2,1)S(1)}, bf16[2,160,960]{2,1,0:T(8,128)(2,1)S(1)}, u32[]{:S(2)}, u32[]{:S(2)}) collective-permute-start(bf16[2,160,960]{2,1,0:T(8,128)(2,1)S(1)} %fusion.43), channel_id=1, source_target_pairs={{0,4},{1,5},{2,6},{3,7},{4,0},{5,1},{6,2},{7,3},{8,12},{9,13},{10,... | collective-permute-start | bytes 1843208 | tf_op jit(solution)/shard_map/ppermute | solution.py:243
  293.6 6.7 %copy-start.47 = (bf16[160,960]{1,0:T(8,128)(2,1)S(1)}, bf16[160,960]{1,0:T(8,128)(2,1)}, u32[]{:S(2)}) copy-start(bf16[160,960]{1,0:T(8,128)(2,1)} %copy-done.46) | copy-start | bytes 921604
  293.7 54.6 %collective-permute-start.30 = (bf16[168,960]{1,0:T(8,128)(2,1)S(1)}, bf16[168,960]{1,0:T(8,128)(2,1)S(1)}, u32[]{:S(2)}, u32[]{:S(2)}) collective-permute-start(bf16[168,960]{1,0:T(8,128)(2,1)S(1)} %get-tuple-element.127), channel_id=1, source_target_pairs={{0,12},{1,13},{2,14},{3,15},{4,0},{5,1},{6,2},{7,3},{8,4},{9,5},{1... | collective-permute-start | bytes 967688 | tf_op jit(solution)/shard_map/ppermute | solution.py:282
  295.2 53.1 %collective-permute-start.29 = (bf16[168,960]{1,0:T(8,128)(2,1)S(1)}, bf16[168,960]{1,0:T(8,128)(2,1)S(1)}, u32[]{:S(2)}, u32[]{:S(2)}) collective-permute-start(bf16[168,960]{1,0:T(8,128)(2,1)S(1)} %get-tuple-element.128), channel_id=1, source_target_pairs={{0,8},{1,9},{2,10},{3,11},{4,12},{5,13},{6,14},{7,15},{8,0},{9,1},... | collective-permute-start | bytes 967688 | tf_op jit(solution)/shard_map/ppermute | solution.py:282
  296.0 14.6 %copy-start.9 = (f32[640,960]{1,0:T(8,128)S(1)}, f32[640,960]{1,0:T(8,128)}, u32[]{:S(2)}) copy-start(f32[640,960]{1,0:T(8,128)} %copy.68) | copy-start | bytes 7372804
  296.0 52.3 %collective-permute-start.28 = (bf16[168,960]{1,0:T(8,128)(2,1)S(1)}, bf16[168,960]{1,0:T(8,128)(2,1)S(1)}, u32[]{:S(2)}, u32[]{:S(2)}) collective-permute-start(bf16[168,960]{1,0:T(8,128)(2,1)S(1)} %get-tuple-element.126), channel_id=1, source_target_pairs={{0,4},{1,5},{2,6},{3,7},{4,8},{5,9},{6,10},{7,11},{8,12},{9,13},{1... | collective-permute-start | bytes 967688 | tf_op jit(solution)/shard_map/ppermute | solution.py:282
  297.7 50.4 %collective-permute-start.31 = (bf16[160,960]{1,0:T(8,128)(2,1)S(1)}, bf16[160,960]{1,0:T(8,128)(2,1)S(1)}, u32[]{:S(2)}, u32[]{:S(2)}) collective-permute-start(bf16[160,960]{1,0:T(8,128)(2,1)S(1)} %fusion.78), channel_id=1, source_target_pairs={{0,8},{1,9},{2,10},{3,11},{4,12},{5,13},{6,14},{7,15},{8,0},{9,1},... | collective-permute-start | bytes 921608 | tf_op jit(solution)/shard_map/ppermute | solution.py:243
  310.8 42.6 %collective-permute-start.33 = (bf16[160,960]{1,0:T(8,128)(2,1)S(1)}, bf16[160,960]{1,0:T(8,128)(2,1)S(1)}, u32[]{:S(2)}, u32[]{:S(2)}) collective-permute-start(bf16[160,960]{1,0:T(8,128)(2,1)S(1)} %fusion.79), channel_id=1, source_target_pairs={{0,8},{1,9},{2,10},{3,11},{4,12},{5,13},{6,14},{7,15},{8,0},{9,1},... | collective-permute-start | bytes 921608 | tf_op jit(solution)/shard_map/ppermute | solution.py:243
  (33 other events, 58.1 us)
Sparse Core Ops, SparseCore 0:
  10.2 111.5 all-gather.1

commit v7 on v6

--- a/solution.py
+++ b/solution.py
@@ -290,57 +290,108 @@
     return lax.dynamic_index_in_dim(x, i, 0, keepdims=False)
 
 
-def with_other(x, bit):
-    return jnp.concatenate([x, flip(x, bit)], axis=0)
+def rows_of_plane(x):
+    x_y = flip(x, Y_BIT)
+    return x, x_y, flip(x, CORE_BIT), flip(x_y, CORE_BIT)
 
 
 def cols_y(x, y):
     x = x.reshape(2, 2, *x.shape[1:])
-    return jnp.concatenate([at(x, y), flip(at(x, 1 - y), Y_BIT)], axis=1)
-
-
-def cols_core(x, core):
-    return at(x, core), flip(at(x, 1 - core), CORE_BIT)
-
-
-def rows_core(x):
-    return x, flip(x, CORE_BIT)
-
-
-def product(cols, rows):
-    out = sum(
-        lax.dot_general(c, r, (((0,), (0,)), ((), ())), preferred_element_type=f32)
-        for c, r in zip(cols, rows)
-    )
-    return out
-
-
-def by_owner(parts):
-    return parts.reshape(LINE, -1, parts.shape[-1])
+    return flip(at(x, 1 - y), Y_BIT)
+
+
+def cols_core(x, x_y, y, core):
+    other = 1 - core
+    return flip(jnp.stack([at(x, 2 * y + other), at(x_y, other)]), CORE_BIT)
+
+
+def plane_kernel(n_rows, split, n_own, picks_ref, *refs):
+    cols_ref, y_ref, core_ref = refs[:3]
+    rows = [
+        jnp.concatenate([r[...] for r in refs[3 + 4 * i : 7 + 4 * i]], axis=0) for i in range(n_rows)
+    ]
+    rest = refs[3 + 4 * n_rows :]
+    extra_ref = rest[0] if n_rows == 2 else None
+    outs, total = rest[n_rows - 1 : -1], rest[-1]
+    cols = jnp.concatenate(
+        [cols_ref[picks_ref[0]], y_ref[picks_ref[1]], core_ref[0], core_ref[1]], axis=0
+    )
+    share = total.shape[0] // LINE
+
+    def dot(c, r):
+        return lax.dot_general(c, r, (((0,), (0,)), ((), ())), preferred_element_type=f32)
+
+    if n_rows == 1:
+        total[...] = dot(cols, rows[0])
+    else:
+        low, top = split
+        total[...] = dot(cols, rows[1])
+        first = dot(cols, rows[0])
+        total[: low * share] = first[: low * share]
+        if top > low:
+
+            @pl.when(picks_ref[2] > 0)
+            def _():
+                total[low * share : top * share] = first[low * share : top * share]
+
+    slot = 3
+    for number, ref in enumerate(outs):
+        for i in range(ref.shape[0]):
+            pick = picks_ref[slot]
+            slot += 1
+            block = total[pl.ds(pl.multiple_of(pick * share, 8), share)]
+            ref[i, :share] = block.astype(ref.dtype)
+            if extra_ref is not None:
+                ref[i, share:] = extra_ref[pick].astype(ref.dtype)
+
+
+def plane_product(cols, x_y, x_core, rows, picks, out_counts, split=None, extra=None):
+    blocks, tokens, width_cols = cols.shape
+    share, width = width_cols // LINE, rows[0][0].shape[1]
+    tall = share + (0 if extra is None else extra.shape[1])
+    operands = [cols, x_y, x_core, *[r for chunk in rows for r in chunk]]
+    if extra is not None:
+        operands.append(extra)
+    whole = lambda v: pl.BlockSpec(v.shape, lambda i, picks, n=v.ndim: (0,) * n)
+    shapes = [
+        jax.ShapeDtypeStruct((count, tall, width), f32 if i == 0 else bf16)
+        for i, count in enumerate(out_counts)
+    ]
+    kernel = lambda *refs: plane_kernel(len(rows), split, out_counts[0], *refs)
+    return pl.pallas_call(
+        kernel,
+        grid_spec=pltpu.PrefetchScalarGridSpec(
+            num_scalar_prefetch=1,
+            grid=(1,),
+            in_specs=[whole(v) for v in operands],
+            out_specs=[whole(v) for v in shapes],
+            scratch_shapes=[pltpu.VMEM((LINE * share, width), f32)],
+        ),
+        out_shape=shapes,
+        compiler_params=pltpu.CompilerParams(
+            dimension_semantics=("arbitrary",), vmem_limit_bytes=32 * 1024 * 1024
+        ),
+        cost_estimate=pl.CostEstimate(
+            flops=8 * tokens * width_cols * width * len(rows),
+            bytes_accessed=8 * tokens * (width_cols + width) + 8 * width_cols * width,
+            transcendentals=0,
+        ),
+    )(jnp.stack([jnp.asarray(p, jnp.int32) for p in picks]), *operands)
 
 
 LINE = 4
 ORDER = (1, 2, 3)
 
 
-def direct_parts(parts, z):
-    return at(parts, z), [at(parts, (z + k) % LINE).astype(bf16) for k in ORDER]
-
-
 def direct_send(sends):
     return [
-        z_pairs(send, [(a, (a + k) % LINE) for a in range(LINE)])
+        z_pairs(send[0], [(a, (a + k) % LINE) for a in range(LINE)])
         for k, send in zip(ORDER, sends)
     ]
 
 
 def direct_total(own, received):
     return own + sum(r.astype(f32) for r in received)
-
-
-def pair_first(parts, z1):
-    parts = parts.reshape(2, 2, *parts.shape[1:]).swapaxes(0, 1)
-    return at(parts, z1), flip(at(parts, 1 - z1).astype(bf16), Z1_BIT)
 
 
 def pair_second(own, received, z2):
@@ -356,14 +407,15 @@
     state = forward_attention(u, weights, tables)
     n, m = state[2], state[10]
     gate, up, act, out = ffn_forward(m, state[8], weights[2])
-    m_y, n_y = with_other(m, Y_BIT), with_other(n, Y_BIT)
+    m_y, n_y = flip(m, Y_BIT), flip(n, Y_BIT)
     gate, up, act, out, m_y, n_y = tie((gate, up, act, out, m_y, n_y))
     state = (*state, gate, up, act)
     act_y = cols_y(act, y)
-    m_all, n_all = rows_core(m_y), rows_core(n_y)
+    m_all = (m, m_y, flip(m, CORE_BIT), flip(m_y, CORE_BIT))
+    n_all = (n, n_y, flip(n, CORE_BIT), flip(n_y, CORE_BIT))
     _, _, dm = backward_ffn(x, state, weights)
     dm, act_y, m_all, n_all = tie((dm, act_y, m_all, n_all))
-    act_c = cols_core(act_y, core)
+    act_c = (act, act_y, cols_core(act, act_y, y, core))
     dh1, _, do, _ = backward_mid(x, dm, state, weights)
     dproj = backward_attention(do, state, tables)
     first_grad, _ = backward_in(dproj, dh1, state, weights)
@@ -377,57 +429,68 @@
     z2, z1 = z >> 1, z & 1
     m_all, n_all, act_c = early
     tokens, width = o.shape[0], e.shape[1]
-    share = act_c[0].shape[1] // LINE
+    share = act_c[0].shape[2] // LINE
+    here = (2 * y + core, core)
+    others = [(z + k) % LINE for k in ORDER]
+    pairs = (z1, 2 + z1, 1 - z1, 3 - z1)
     eb = e.astype(bf16)
-    eb_y = with_other(eb, Y_BIT)
+    eb_y, eb_c = flip(eb, Y_BIT), flip(eb, CORE_BIT)
     dgate, dup, dm = backward_ffn(eb, state, weights)
-    dgate, dup, dm, eb_y = tie((dgate, dup, dm, eb_y))
-    eb_all = rows_core(eb_y)
+    dgate, dup, dm, eb_y, eb_c = tie((dgate, dup, dm, eb_y, eb_c))
+    eb_all = (eb, eb_y, eb_c, flip(eb_y, CORE_BIT))
     gate_y = cols_y(dgate, y)
     dh1, dz, do, gain_two_grad = backward_mid(e, dm, state, weights)
     do, dz, eb_all, dup = tie((do, dz, eb_all, dup))
-    down_own, down_sends = direct_parts(by_owner(product(act_c, eb_all)), z)
-    do, gate_y, down_sends = tie((do, gate_y, down_sends))
+    down_own, *down_sends = plane_product(*act_c, [eb_all], (*here, 0, z, *others), (1, 1, 1, 1))
+    do, dup, gate_y, down_sends = tie((do, dup, gate_y, down_sends))
     down_one, down_two, down_three = direct_send(down_sends)
-    gate_c = cols_core(gate_y, core)
+    gate_c = cols_core(dgate, gate_y, y, core)
     up_y = cols_y(dup, y)
+    gate_c, down_one = tie((gate_c, down_one))
+    gate_own, gate_send = plane_product(dgate, gate_y, gate_c, [m_all], (*here, 0, *pairs), (2, 2))
+    gate_own, gate_send, up_y = tie((gate_own, gate_send, up_y))
+    gate_received = flip(gate_send, Z1_BIT)
+    up_c = cols_core(dup, up_y, y, core)
+    up_own, up_send = plane_product(dup, up_y, up_c, [m_all], (*here, 0, *pairs), (2, 2))
+    do, dz, up_own, up_send, down_three = tie((do, dz, up_own, up_send, down_three))
+    up_received = flip(up_send, Z1_BIT)
     dproj = backward_attention(do, state, tables)
-    dproj, gate_c, up_y, down_one = tie((dproj, gate_c, up_y, down_one))
-    gate_own, gate_received = pair_first(by_owner(product(gate_c, m_all)), z1)
-    up_c = cols_core(up_y, core)
-    dz_y = with_other(dz, Y_BIT)
+    dz_y, dz_c = flip(dz, Y_BIT), flip(dz, CORE_BIT)
     attn_cols = jnp.concatenate([dproj, o], axis=1).reshape(tokens, 4, 4, share)
     attn_cols = attn_cols.transpose(2, 0, 1, 3).reshape(4, tokens, 4 * share)
     attn_y = cols_y(attn_cols, y)
-    dproj, up_c, dz_y, attn_y, down_three = tie((dproj, up_c, dz_y, attn_y, down_three))
-    up_own, up_received = pair_first(by_owner(product(up_c, m_all)), z1)
-    attn_c = cols_core(attn_y, core)
-    dz_all = rows_core(dz_y)
+    dproj, attn_y, dz_y, dz_c, gate_own, gate_received, down_two = tie(
+        (dproj, attn_y, dz_y, dz_c, gate_own, gate_received, down_two)
+    )
+    dz_all = (dz, dz_y, dz_c, flip(dz_y, CORE_BIT))
+    attn_c = cols_core(attn_cols, attn_y, y, core)
     du, gain_one_grad = backward_in(dproj, dh1, state, weights)
     gain_grad = jnp.concatenate([gain_one_grad, gain_two_grad])
-    gain_grad = gain_grad + flip(gain_grad, CORE_BIT)
-    gain_grad = gain_grad + flip(gain_grad, Y_BIT)
-    gain_grad, attn_c, dz_all, gate_own, gate_received, down_two = tie(
-        (gain_grad, attn_c, dz_all, gate_own, gate_received, down_two)
-    )
-    qkv_owners = QKV_COLS // share
-    from_n = product([c[:, : -(-qkv_owners // 4) * share] for c in attn_c], n_all)
-    from_dz = product([c[:, qkv_owners // 4 * share :] for c in attn_c], dz_all)
-    shared = qkv_owners // 4 * share
-    mixed = -(-qkv_owners // 4) * share - shared
-    is_qkv = qkv_owners // 4 * 4 + y * 2 + core < qkv_owners
-    both = jnp.where(is_qkv, from_n[shared:], from_dz[:mixed])
-    attn = by_owner(jnp.concatenate([from_n[:shared], both, from_dz[mixed:]], axis=0))
+    gain_grad = gain_grad + sum(
+        flip(gain_grad, bit) for bit in (CORE_BIT, Y_BIT, CORE_BIT | Y_BIT)
+    )
     gain_rows = at(gain_grad.reshape(4, 4, -1).transpose(1, 0, 2), y * 2 + core)[:, None]
     gain_share = gain_rows.shape[-1]
     gain_rows = jnp.pad(gain_rows, ((0, 0), (0, EXTRA_ROWS - 1), (0, width - gain_share)))
-    attn_own, attn_sends = direct_parts(jnp.concatenate([attn, gain_rows], axis=1), z)
+    qkv_owners = QKV_COLS // share
+    is_qkv = (qkv_owners // 4 * 4 + y * 2 + core < qkv_owners).astype(jnp.int32)
+    attn_own, *attn_sends = plane_product(
+        attn_cols,
+        attn_y,
+        attn_c,
+        [n_all, dz_all],
+        (*here, is_qkv, z, *others),
+        (1, 1, 1, 1),
+        (qkv_owners // 4, -(-qkv_owners // 4)),
+        gain_rows,
+    )
+    up_own, attn_own = tie((up_own, attn_own))
     attn_received = direct_send(attn_sends)
     down_received = (down_one, down_two, down_three)
     gate = pair_second(gate_own, gate_received, z2)
     up = pair_second(up_own, up_received, z2)
-    down = direct_total(down_own, down_received)
-    attn = direct_total(attn_own, attn_received)
+    down = direct_total(down_own[0], down_received)
+    attn = direct_total(attn_own[0], attn_received)
     return (
         du,
         attn[:share],

time: 363 us -> 358 us (0.986)
  waiting for transfers between devices: 176 us -> 193 us
  matrix products: 35.2 us -> 18.4 us
  Pallas kernels: 36.4 us -> 48.6 us
  starting transfers between devices: 44.6 us -> 36.3 us
  local copies, waits for them, and re-layouts: 28.1 us -> 23.4 us
    ppermute x6, waiting for transfers between devices: 0.02 us -> 44.4 us  [z_pairs(): lax.ppermute(x, 'dp', [(4 * a + i, 4 * b + i) for a, b in pairs for i in...]
    ppermute x26 -> x31, waiting for transfers between devices: 63.6 us -> 36.3 us  [flip(): return lax.ppermute(x, 'dp', [(i, i ^ bit) for i in range(size)])]
    dot_general x10 -> x0, matrix products: 12.8 us -> none  [product(): lax.dot_general(c, r, (((0,), (0,)), ((), ())), preferred_element_type=f32)]
    pallas_call x0 -> x4, Pallas kernels: none -> 12.1 us  [plane_product(): pl.pallas_call(kernel, grid_spec=pltpu.PrefetchScalarGridSpec(num_scalar_...]
    unnamed x124 -> x162, local copies, waits for them, and re-layouts: 1.99 us -> 10.7 us
    concatenate x10 -> x0, other arithmetic: 8.71 us -> none  [the longest x4 5.14 us: with_other(): return jnp.concatenate([x, flip(x, bit)], axis=0)]
    add x3 -> x0, local copies, waits for them, and re-layouts: 6.64 us -> none  [product(): sum((lax.dot_general(c, r, (((0,), (0,)), ((), ())), preferred_element_ty...]
    convert_element_type x4 -> x0, local copies, waits for them, and re-layouts: 6.51 us -> none  [the longest x2 3.75 us: pair_first(): return (at(parts, z1), flip(at(parts, 1 - z1).astype(bf16), Z1_BIT))]
  transfers between devices with their start and end apart: 35 -> 40, of which waited for: 14 -> 19; matrix products, arithmetic and copies ran while one was open for 14% -> 7% of each run, Pallas kernels for 7% -> 11%
where the time goes in v7:
time: 358 us; the launch traced here: 357 us
  waiting for transfers between devices  193 us (54%)
  Pallas kernels  48.6 us (14%)
  starting transfers between devices  36.3 us (10%)
  local copies, waits for them, and re-layouts  23.4 us (7%)
  other arithmetic  22.5 us (6%)
  matrix products  18.4 us (5%)
  between operations  15.4 us (4%)
    all_gather x1, waiting for transfers between devices, local(): lax.all_gather(own, 'dp', axis=0, tiled=True).reshape(4, 4, 4, share, width)  97.4 us
    ppermute x6, waiting for transfers between devices, z_pairs(): lax.ppermute(x, 'dp', [(4 * a + i, 4 * b + i) for a, b in pairs for i in...  44.4 us
    pallas_call x4, Pallas kernels, ffn_call(): pl.pallas_call(kernel, grid=(steps,), in_specs=[whole] * len(wholes) + [b...  36.6 us
    ppermute x31, waiting for transfers between devices, flip(): return lax.ppermute(x, 'dp', [(i, i ^ bit) for i in range(size)])  36.3 us
    ppermute x31, starting transfers between devices, flip(): return lax.ppermute(x, 'dp', [(i, i ^ bit) for i in range(size)])  26 us
    pallas_call x4, Pallas kernels, plane_product(): pl.pallas_call(kernel, grid_spec=pltpu.PrefetchScalarGridSpec(num_scalar_...  12.1 us
    unnamed x162, local copies, waits for them, and re-layouts  10.7 us
    ppermute x1, waiting for transfers between devices, local(): received = lax.ppermute(first_grad, 'section', [(1, 0)])  8.84 us
  transfers between devices with their start and end apart: 40, of which 19 were waited for; matrix products, arithmetic and copies ran while one was open for 7% of the time, Pallas kernels for 11%

profile of v7, /device:TPU:0, one launch (start us, length us, event | category | flops | bytes accessed | tf_op | source)
XLA Modules:
  0.0 357.3 jit_solution(14091368045113448234)
XLA Ops:
  7.2 2.5 pad_maximum_fusion
  11.2 2.8 collective-permute-start.1
  14.2 1.4 collective-permute-done.1
  15.7 2.1 collective-permute-start.2
  17.9 1.4 collective-permute-done.2
  19.5 3.0 collective-permute-start.3
  22.8 1.3 collective-permute-done.3
  24.4 97.4 %all-gather.2.cloned.1.call-done = bf16[10240,960]{1,0:T(8,128)(2,1)} async-done(((bf16[640,960]{1,0:T(8,128)(2,1)}), bf16[10240,960]{1,0:T(8,128)(2,1)}) %all-gather.2.cloned.1.call-update) | async-done | bytes 19660816 | tf_op jit(solution)/shard_map/all_gather | solution.py:515
  121.8 3.3 slice.119
  125.0 1.1 fusion.6
  128.1 9.6 %shard_map.84 = (f32[4,128,640]{2,1,0:T(8,128)}, f32[4,128,640]{2,1,0:T(8,128)}, bf16[4,128,640]{2,1,0:T(8,128)(2,1)}, f32[128,960]{1,0:T(8,128)S(1)}) custom-call(bf16[128,960]{1,0:T(8,128)(2,1)S(1)} %multiply_convert_fusion.3.m_ref, f32[128,960]{1,0:T(8,128)S(1)} %get-tuple-element.204.h1_ref, bf16[4,4,4,160,960]{4,3,2,1,0:T(8,128)(2,1)} %bitcast.207, ...), custom_call_target="tpu_custom_call" | custom-call | flops 1887436800 | bytes 14745600 | tf_op jit(solution)/shard_map/pallas_call | solution.py:203
  137.7 3.6 collective-permute-start.4
  141.3 5.8 %collective-permute-done.4 = bf16[128,960]{1,0:T(8,128)(2,1)S(1)} collective-permute-done((bf16[128,960]{1,0:T(8,128)(2,1)S(1)}, bf16[128,960]{1,0:T(8,128)(2,1)S(1)}, u32[]{:S(2)}, u32[]{:S(2)}) %collective-permute-start.4) | collective-permute-done | bytes 245792 | tf_op jit(solution)/shard_map/ppermute | solution.py:530
  148.1 3.0 fusion.4
  153.0 2.2 multiply_reduce_fusion.5
  156.1 1.2 collective-permute-start.5
  158.1 8.3 %shard_map.85 = (f32[4,128,640]{2,1,0:T(8,128)S(1)}, f32[4,128,640]{2,1,0:T(8,128)S(1)}, bf16[4,128,640]{2,1,0:T(8,128)(2,1)S(1)}, f32[128,960]{1,0:T(8,128)S(1)}) custom-call(bf16[128,960]{1,0:T(8,128)(2,1)} %multiply_convert_fusion.2.m_ref.refs_4_, f32[128,960]{1,0:T(8,128)S(1)} %get-tuple-element.208.h1_ref, bf16[4,4,4,160,960]{4,3,2,1,0:T(8,128)(2,1)} %bitcast.210, ...), custom_call_target="tpu_custom_call" | custom-call | flops 1887436800 | bytes 14745600 | tf_op jit(solution)/shard_map/pallas_call | solution.py:203
  166.5 3.2 collective-permute-done.6.refs_5_
  170.4 1.2 collective-permute-start.7
  172.7 1.1 constant_dynamic-slice_fusion.9
  173.8 9.9 %shard_map.86 = (bf16[4,128,640]{2,1,0:T(8,128)(2,1)}, bf16[4,128,640]{2,1,0:T(8,128)(2,1)}, f32[128,960]{1,0:T(8,128)S(1)}) custom-call(bf16[128,960]{1,0:T(8,128)(2,1)S(1)} %bitcast.198, f32[4,128,640]{2,1,0:T(8,128)S(1)} %get-tuple-element.87.gate_ref, f32[4,128,640]{2,1,0:T(8,128)S(1)} %get-tuple-element.88.up_ref, ...), custom_call_target="tpu_custom_call" | custom-call | flops 1887436800 | bytes 14745600 | tf_op jit(solution)/shard_map/pallas_call | solution.py:203
  187.1 0.9 constant_dynamic-slice_fusion.8
  189.8 1.5 collective-permute-start.13
  191.3 8.8 %collective-permute-done.13 = bf16[128,960]{1,0:T(8,128)(2,1)S(1)} collective-permute-done((bf16[128,960]{1,0:T(8,128)(2,1)S(1)}, bf16[128,960]{1,0:T(8,128)(2,1)S(1)}, u32[]{:S(2)}, u32[]{:S(2)}) %collective-permute-start.13) | collective-permute-done | bytes 245792 | tf_op jit(solution)/shard_map/ppermute | solution.py:534
  201.8 8.8 %shard_map.87 = (bf16[4,128,640]{2,1,0:T(8,128)(2,1)S(1)}, bf16[4,128,640]{2,1,0:T(8,128)(2,1)S(1)}, f32[128,960]{1,0:T(8,128)S(1)}) custom-call(bf16[128,960]{1,0:T(8,128)(2,1)} %broadcast_select_fusion.eb_ref.refs_4_, f32[4,128,640]{2,1,0:T(8,128)S(1)} %get-tuple-element.87.gate_ref, f32[4,128,640]{2,1,0:T(8,128)S(1)} %get-tuple-element.88.up_ref, ...), custom_call_target="tpu_custom_call" | custom-call | flops 1887436800 | bytes 14745600 | tf_op jit(solution)/shard_map/pallas_call | solution.py:203
  210.8 2.1 fusion.90
  213.6 1.3 collective-permute-start.17
  214.9 2.9 fusion.33
  217.8 3.5 shard_map.88
  221.3 2.0 collective-permute-done.17.refs_2_
  224.1 1.5 collective-permute-start.19
  226.4 1.2 collective-permute-start.20
  227.7 0.9 constant_dynamic-slice_fusion.5
  228.7 7.6 %collective-permute-done.19 = bf16[160,960]{1,0:T(8,128)(2,1)S(1)} collective-permute-done((bf16[160,960]{1,0:T(8,128)(2,1)}, bf16[160,960]{1,0:T(8,128)(2,1)S(1)}, u32[]{:S(2)}, u32[]{:S(2)}) %collective-permute-start.19) | collective-permute-done | bytes 307232 | tf_op jit(solution)/shard_map/ppermute | solution.py:282
  237.7 1.0 copy-done.14
  238.7 1.0 copy-done.22
  239.7 2.6 shard_map.89
  243.9 1.5 collective-permute-start.22
  245.6 1.1 collective-permute-start.26
  246.7 2.6 shard_map.90
  249.4 6.4 %collective-permute-done.22 = bf16[160,960]{1,0:T(8,128)(2,1)} collective-permute-done((bf16[160,960]{1,0:T(8,128)(2,1)}, bf16[160,960]{1,0:T(8,128)(2,1)}, u32[]{:S(2)}, u32[]{:S(2)}) %collective-permute-start.22) | collective-permute-done | bytes 307232 | tf_op jit(solution)/shard_map/ppermute | solution.py:282
  257.7 1.3 collective-permute-start.24
  261.7 1.4 copy.41.refs_1_
  263.1 1.1 pad_maximum_fusion.2
  264.2 3.5 collective-permute-done.27
  268.5 7.3 %collective-permute-done.26 = bf16[2,160,960]{2,1,0:T(8,128)(2,1)} collective-permute-done((bf16[2,160,960]{2,1,0:T(8,128)(2,1)}, bf16[2,160,960]{2,1,0:T(8,128)(2,1)}, u32[]{:S(2)}, u32[]{:S(2)}) %collective-permute-start.26) | collective-permute-done | bytes 614432 | tf_op jit(solution)/shard_map/ppermute | solution.py:243
  275.8 3.4 fusion.62
  279.5 1.2 collective-permute-start.30
  282.8 2.1 fusion.42
  284.9 1.2 convert_add_fusion.1
  286.2 1.0 copy-done.46
  289.1 0.9 copy-done.30
  290.0 0.9 copy-done.32
  291.0 0.9 copy-done.34
  291.9 3.4 shard_map.91
  295.4 1.4 convert_add_fusion
  296.8 2.0 collective-permute-start.38
  298.8 1.0 fusion.53
  299.8 13.4 %collective-permute-done.36 = bf16[160,960]{1,0:T(8,128)(2,1)S(1)} collective-permute-done((bf16[160,960]{1,0:T(8,128)(2,1)S(1)}, bf16[160,960]{1,0:T(8,128)(2,1)S(1)}, u32[]{:S(2)}, u32[]{:S(2)}) %collective-permute-start.36) | collective-permute-done | bytes 307232 | tf_op jit(solution)/shard_map/ppermute | solution.py:243
  314.1 1.3 collective-permute-start.33
  315.4 4.9 %collective-permute-done.38 = bf16[160,960]{1,0:T(8,128)(2,1)S(1)} collective-permute-done((bf16[160,960]{1,0:T(8,128)(2,1)S(1)}, bf16[160,960]{1,0:T(8,128)(2,1)S(1)}, u32[]{:S(2)}, u32[]{:S(2)}) %collective-permute-start.38) | collective-permute-done | bytes 307232 | tf_op jit(solution)/shard_map/ppermute | solution.py:243
  320.4 1.5 maximum_bitcast_fusion
  321.9 4.8 %collective-permute-done.35 = bf16[168,960]{1,0:T(8,128)(2,1)S(1)} collective-permute-done((bf16[168,960]{1,0:T(8,128)(2,1)S(1)}, bf16[168,960]{1,0:T(8,128)(2,1)S(1)}, u32[]{:S(2)}, u32[]{:S(2)}) %collective-permute-start.35) | collective-permute-done | bytes 322592 | tf_op jit(solution)/shard_map/ppermute | solution.py:282
  326.7 22.2 %collective-permute-done.34 = bf16[168,960]{1,0:T(8,128)(2,1)S(1)} collective-permute-done((bf16[168,960]{1,0:T(8,128)(2,1)S(1)}, bf16[168,960]{1,0:T(8,128)(2,1)S(1)}, u32[]{:S(2)}, u32[]{:S(2)}) %collective-permute-start.34) | collective-permute-done | bytes 322592 | tf_op jit(solution)/shard_map/ppermute | solution.py:282
  (317 shorter events, 35.2 us)
Async XLA Ops:
  7.2 114.6 %all-gather.2.cloned.1.call-start = ((), (), s32[]{:S(2)}) async-start(), calls=%async_computation | async-start | bytes 22282240 | tf_op jit(solution)/shard_map/all_gather | solution.py:515
  7.2 10.5 %copy-start = (bf16[1,2,64,960]{3,2,1,0:T(8,128)(2,1)S(1)}, bf16[1,2,64,960]{3,2,1,0:T(8,128)(2,1)}, u32[]{:S(2)}) copy-start(bf16[1,2,64,960]{3,2,1,0:T(8,128)(2,1)} %param.5) | copy-start | bytes 737284
  9.8 1.3 collective-permute-start
  11.2 4.3 %collective-permute-start.1 = (bf16[240]{0:T(256)(128)(2,1)S(1)}, bf16[240]{0:T(256)(128)(2,1)S(1)}, u32[]{:S(2)}, u32[]{:S(2)}) collective-permute-start(bf16[240]{0:T(256)(128)(2,1)S(1)} %pad_maximum_fusion.18), channel_id=1, source_target_pairs={{0,2},{1,3},{2,0},{3,1},{4,6},{5,7},{6,4},{7,5},{8,10},{9,11},{10,... | collective-permute-start | bytes 1448 | tf_op jit(solution)/shard_map/ppermute | solution.py:243
  15.7 3.6 %collective-permute-start.2 = (bf16[480]{0:T(512)(128)(2,1)S(1)}, bf16[480]{0:T(512)(128)(2,1)S(1)}, u32[]{:S(2)}, u32[]{:S(2)}) collective-permute-start(bf16[480]{0:T(512)(128)(2,1)S(1)} %pad_maximum_fusion.17), channel_id=1, source_target_pairs={{0,4},{1,5},{2,6},{3,7},{4,0},{5,1},{6,2},{7,3},{8,12},{9,13},{10,... | collective-permute-start | bytes 2888 | tf_op jit(solution)/shard_map/ppermute | solution.py:243
  19.5 4.7 %collective-permute-start.3 = (bf16[960]{0:T(1024)(128)(2,1)S(1)}, bf16[960]{0:T(1024)(128)(2,1)S(1)}, u32[]{:S(2)}, u32[]{:S(2)}) collective-permute-start(bf16[960]{0:T(1024)(128)(2,1)S(1)} %pad_maximum_fusion.16), channel_id=1, source_target_pairs={{0,8},{1,9},{2,10},{3,11},{4,12},{5,13},{6,14},{7,15},{8,0},{9,1},... | collective-permute-start | bytes 5768 | tf_op jit(solution)/shard_map/ppermute | solution.py:243
  137.7 9.4 %collective-permute-start.4 = (bf16[128,960]{1,0:T(8,128)(2,1)S(1)}, bf16[128,960]{1,0:T(8,128)(2,1)S(1)}, u32[]{:S(2)}, u32[]{:S(2)}) collective-permute-start(bf16[128,960]{1,0:T(8,128)(2,1)S(1)} %convert_element_type.162), channel_id=1, source_target_pairs={{0,16},{1,17},{2,18},{3,19},{4,20},{5,21},{6,22},{7,23},{8,24},{9,... | collective-permute-start | bytes 737288 | tf_op jit(solution)/shard_map/ppermute | solution.py:530
  147.3 41.7 %copy-start.75 = (f32[128]{0:T(128)}, f32[128]{0:T(128)S(1)}, u32[]{:S(2)}) copy-start(f32[128]{0:T(128)S(1)} %get-tuple-element.197) | copy-start | bytes 1540
  151.4 35.3 %copy-start.67 = (bf16[128,5,32]{0,2,1:T(8,128)(2,1)}, bf16[128,5,32]{0,2,1:T(8,128)(2,1)S(1)}, u32[]{:S(2)}) copy-start(bf16[128,5,32]{0,2,1:T(8,128)(2,1)S(1)} %get-tuple-element.180) | copy-start | bytes 122884
  156.1 10.4 %collective-permute-start.5 = (bf16[128,960]{1,0:T(8,128)(2,1)}, bf16[128,960]{1,0:T(8,128)(2,1)}, u32[]{:S(2)}, u32[]{:S(2)}) collective-permute-start(bf16[128,960]{1,0:T(8,128)(2,1)} %multiply_convert_fusion.2.m_ref.refs_4_), channel_id=1, source_target_pairs={{0,2},{1,3},{2,0},{3,1},{4,6},{5,7},{6,4},{7,5},{8,10},{9,11},{10,... | collective-permute-start | bytes 737288 | tf_op jit(solution)/shard_map/ppermute | solution.py:243
  157.3 12.4 %collective-permute-start.6 = (bf16[128,960]{1,0:T(8,128)(2,1)}, bf16[128,960]{1,0:T(8,128)(2,1)}, u32[]{:S(2)}, u32[]{:S(2)}) collective-permute-start(bf16[128,960]{1,0:T(8,128)(2,1)} %fusion.58.refs_4_), channel_id=1, source_target_pairs={{0,2},{1,3},{2,0},{3,1},{4,6},{5,7},{6,4},{7,5},{8,10},{9,11},{10,... | collective-permute-start | bytes 737288 | tf_op jit(solution)/shard_map/ppermute | solution.py:243
  170.4 13.3 %collective-permute-start.7 = (bf16[2,128,640]{2,1,0:T(8,128)(2,1)}, bf16[2,128,640]{2,1,0:T(8,128)(2,1)}, u32[]{:S(2)}, u32[]{:S(2)}) collective-permute-start(bf16[2,128,640]{2,1,0:T(8,128)(2,1)} %dynamic-slice_bitcast_fusion.2), channel_id=1, source_target_pairs={{0,2},{1,3},{2,0},{3,1},{4,6},{5,7},{6,4},{7,5},{8,10},{9,11},{10,... | collective-permute-start | bytes 983048 | tf_op jit(solution)/shard_map/ppermute | solution.py:243
  171.6 12.0 %collective-permute-start.8 = (bf16[128,960]{1,0:T(8,128)(2,1)}, bf16[128,960]{1,0:T(8,128)(2,1)S(1)}, u32[]{:S(2)}, u32[]{:S(2)}) collective-permute-start(bf16[128,960]{1,0:T(8,128)(2,1)} %multiply_convert_fusion.2.m_ref.refs_4_), channel_id=1, source_target_pairs={{0,1},{1,0},{2,3},{3,2},{4,5},{5,4},{6,7},{7,6},{8,9},{9,8},{10,11... | collective-permute-start | bytes 737288 | tf_op jit(solution)/shard_map/ppermute | solution.py:243
  171.6 12.0 %collective-permute-start.10 = (bf16[128,960]{1,0:T(8,128)(2,1)}, bf16[128,960]{1,0:T(8,128)(2,1)S(1)}, u32[]{:S(2)}, u32[]{:S(2)}) collective-permute-start(bf16[128,960]{1,0:T(8,128)(2,1)} %fusion.58.refs_4_), channel_id=1, source_target_pairs={{0,1},{1,0},{2,3},{3,2},{4,5},{5,4},{6,7},{7,6},{8,9},{9,8},{10,11... | collective-permute-start | bytes 737288 | tf_op jit(solution)/shard_map/ppermute | solution.py:243
  172.2 11.5 %collective-permute-start.9 = (bf16[128,960]{1,0:T(8,128)(2,1)}, bf16[128,960]{1,0:T(8,128)(2,1)S(1)}, u32[]{:S(2)}, u32[]{:S(2)}) collective-permute-start(bf16[128,960]{1,0:T(8,128)(2,1)} %collective-permute-done.5.refs_5_), channel_id=1, source_target_pairs={{0,1},{1,0},{2,3},{3,2},{4,5},{5,4},{6,7},{7,6},{8,9},{9,8},{10,11... | collective-permute-start | bytes 737288 | tf_op jit(solution)/shard_map/ppermute | solution.py:243
  172.2 11.6 %collective-permute-start.11 = (bf16[128,960]{1,0:T(8,128)(2,1)}, bf16[128,960]{1,0:T(8,128)(2,1)S(1)}, u32[]{:S(2)}, u32[]{:S(2)}) collective-permute-start(bf16[128,960]{1,0:T(8,128)(2,1)} %collective-permute-done.6.refs_5_), channel_id=1, source_target_pairs={{0,1},{1,0},{2,3},{3,2},{4,5},{5,4},{6,7},{7,6},{8,9},{9,8},{10,11... | collective-permute-start | bytes 737288 | tf_op jit(solution)/shard_map/ppermute | solution.py:243
  172.7 11.4 %slice-start = ((s8[5242880]{0:T(1024)(128)(4,1)}), s8[4194304]{0:T(1024)(128)(4,1)S(1)}, s32[]{:S(2)}) async-start(s8[5242880]{0:T(1024)(128)(4,1)} %bitcast.225), calls=%async_computation.1 | async-start | bytes 8388608
  173.7 10.3 %slice-start.1 = ((s8[5242880]{0:T(1024)(128)(4,1)}), s8[1048576]{0:T(1024)(128)(4,1)S(1)}, s32[]{:S(2)}) async-start(s8[5242880]{0:T(1024)(128)(4,1)} %bitcast.225), calls=%async_computation.2 | async-start | bytes 2097152
  188.1 1.7 collective-permute-start.12
  189.8 11.1 %copy-start.19 = (bf16[2,128,640]{2,1,0:T(8,128)(2,1)}, bf16[2,128,640]{2,1,0:T(8,128)(2,1)S(1)}, u32[]{:S(2)}) copy-start(bf16[2,128,640]{2,1,0:T(8,128)(2,1)S(1)} %collective-permute-done.12.refs_3_) | copy-start | bytes 983044
  189.8 10.4 %collective-permute-start.13 = (bf16[128,960]{1,0:T(8,128)(2,1)S(1)}, bf16[128,960]{1,0:T(8,128)(2,1)S(1)}, u32[]{:S(2)}, u32[]{:S(2)}) collective-permute-start(bf16[128,960]{1,0:T(8,128)(2,1)S(1)} %fusion.49), channel_id=1, source_target_pairs={{16,0},{17,1},{18,2},{19,3},{20,4},{21,5},{22,6},{23,7},{24,8},{25... | collective-permute-start | bytes 737288 | tf_op jit(solution)/shard_map/ppermute | solution.py:534
  200.9 9.7 %collective-permute-start.14 = (bf16[128,960]{1,0:T(8,128)(2,1)}, bf16[128,960]{1,0:T(8,128)(2,1)S(1)}, u32[]{:S(2)}, u32[]{:S(2)}) collective-permute-start(bf16[128,960]{1,0:T(8,128)(2,1)} %broadcast_select_fusion.eb_ref.refs_4_), channel_id=1, source_target_pairs={{0,2},{1,3},{2,0},{3,1},{4,6},{5,7},{6,4},{7,5},{8,10},{9,11},{10,... | collective-permute-start | bytes 737288 | tf_op jit(solution)/shard_map/ppermute | solution.py:243
  201.7 8.9 %collective-permute-start.15 = (bf16[128,960]{1,0:T(8,128)(2,1)}, bf16[128,960]{1,0:T(8,128)(2,1)}, u32[]{:S(2)}, u32[]{:S(2)}) collective-permute-start(bf16[128,960]{1,0:T(8,128)(2,1)} %broadcast_select_fusion.eb_ref.refs_4_), channel_id=1, source_target_pairs={{0,1},{1,0},{2,3},{3,2},{4,5},{5,4},{6,7},{7,6},{8,9},{9,8},{10,11... | collective-permute-start | bytes 737288 | tf_op jit(solution)/shard_map/ppermute | solution.py:243
  210.6 15.0 %copy-start.3 = (bf16[4,128,640]{2,1,0:T(8,128)(2,1)}, bf16[4,128,640]{2,1,0:T(8,128)(2,1)S(1)}, u32[]{:S(2)}) copy-start(bf16[4,128,640]{2,1,0:T(8,128)(2,1)S(1)} %get-tuple-element.118.refs_1_) | copy-start | bytes 1966084
  213.0 4.8 %collective-permute-start.16 = (bf16[128,960]{1,0:T(8,128)(2,1)S(1)}, bf16[128,960]{1,0:T(8,128)(2,1)S(1)}, u32[]{:S(2)}, u32[]{:S(2)}) collective-permute-start(bf16[128,960]{1,0:T(8,128)(2,1)S(1)} %collective-permute-done.14.refs_5_), channel_id=1, source_target_pairs={{0,1},{1,0},{2,3},{3,2},{4,5},{5,4},{6,7},{7,6},{8,9},{9,8},{10,11... | collective-permute-start | bytes 737288 | tf_op jit(solution)/shard_map/ppermute | solution.py:243
  213.6 9.7 %collective-permute-start.17 = (bf16[2,128,640]{2,1,0:T(8,128)(2,1)S(1)}, bf16[2,128,640]{2,1,0:T(8,128)(2,1)S(1)}, u32[]{:S(2)}, u32[]{:S(2)}) collective-permute-start(bf16[2,128,640]{2,1,0:T(8,128)(2,1)S(1)} %dynamic-slice_bitcast_fusion.1), channel_id=1, source_target_pairs={{0,2},{1,3},{2,0},{3,1},{4,6},{5,7},{6,4},{7,5},{8,10},{9,11},{10,... | collective-permute-start | bytes 983048 | tf_op jit(solution)/shard_map/ppermute | solution.py:243
  217.8 20.0 %copy-start.6 = (bf16[4,128,640]{2,1,0:T(8,128)(2,1)S(1)}, bf16[4,128,640]{2,1,0:T(8,128)(2,1)}, u32[]{:S(2)}) copy-start(bf16[4,128,640]{2,1,0:T(8,128)(2,1)} %copy-done.5) | copy-start | bytes 1966084
  217.8 20.0 %copy-start.10 = (bf16[128,960]{1,0:T(8,128)(2,1)S(1)}, bf16[128,960]{1,0:T(8,128)(2,1)}, u32[]{:S(2)}) copy-start(bf16[128,960]{1,0:T(8,128)(2,1)} %copy-done.9) | copy-start | bytes 737284
  217.8 20.0 %copy-start.12 = (bf16[128,960]{1,0:T(8,128)(2,1)S(1)}, bf16[128,960]{1,0:T(8,128)(2,1)}, u32[]{:S(2)}) copy-start(bf16[128,960]{1,0:T(8,128)(2,1)} %copy-done.11) | copy-start | bytes 737284
  223.3 13.0 %copy-start.13 = (bf16[2,128,640]{2,1,0:T(8,128)(2,1)}, bf16[2,128,640]{2,1,0:T(8,128)(2,1)S(1)}, u32[]{:S(2)}) copy-start(bf16[2,128,640]{2,1,0:T(8,128)(2,1)S(1)} %collective-permute-done.17.refs_2_) | copy-start | bytes 983044
  224.1 12.9 %collective-permute-start.18 = (bf16[2,128,640]{2,1,0:T(8,128)(2,1)}, bf16[2,128,640]{2,1,0:T(8,128)(2,1)S(1)}, u32[]{:S(2)}, u32[]{:S(2)}) collective-permute-start(bf16[2,128,640]{2,1,0:T(8,128)(2,1)} %pad_maximum_fusion.4), channel_id=1, source_target_pairs={{0,1},{1,0},{2,3},{3,2},{4,5},{5,4},{6,7},{7,6},{8,9},{9,8},{10,11... | collective-permute-start | bytes 983048 | tf_op jit(solution)/shard_map/ppermute | solution.py:243
  224.1 12.1 %collective-permute-start.19 = (bf16[160,960]{1,0:T(8,128)(2,1)}, bf16[160,960]{1,0:T(8,128)(2,1)S(1)}, u32[]{:S(2)}, u32[]{:S(2)}) collective-permute-start(bf16[160,960]{1,0:T(8,128)(2,1)} %bitcast.59), channel_id=1, source_target_pairs={{0,4},{1,5},{2,6},{3,7},{4,8},{5,9},{6,10},{7,11},{8,12},{9,13},{1... | collective-permute-start | bytes 921608 | tf_op jit(solution)/shard_map/ppermute | solution.py:282
  226.4 20.3 %copy-start.4 = (bf16[4,128,640]{2,1,0:T(8,128)(2,1)S(1)}, bf16[4,128,640]{2,1,0:T(8,128)(2,1)}, u32[]{:S(2)}) copy-start(bf16[4,128,640]{2,1,0:T(8,128)(2,1)} %copy-done.3) | copy-start | bytes 1966084
  226.4 16.7 %collective-permute-start.20 = (bf16[2,128,640]{2,1,0:T(8,128)(2,1)}, bf16[2,128,640]{2,1,0:T(8,128)(2,1)S(1)}, u32[]{:S(2)}, u32[]{:S(2)}) collective-permute-start(bf16[2,128,640]{2,1,0:T(8,128)(2,1)} %dynamic-slice_bitcast_fusion), channel_id=1, source_target_pairs={{0,2},{1,3},{2,0},{3,1},{4,6},{5,7},{6,4},{7,5},{8,10},{9,11},{10,... | collective-permute-start | bytes 983048 | tf_op jit(solution)/shard_map/ppermute | solution.py:243
  243.1 12.6 %copy-start.62 = (bf16[128,960]{0,1:T(8,128)(2,1)S(1)}, bf16[128,960]{0,1:T(8,128)(2,1)}, u32[]{:S(2)}) copy-start(bf16[128,960]{0,1:T(8,128)(2,1)} %fusion.33) | copy-start | bytes 737284
  243.2 12.9 %copy-start.55 = (bf16[128,320]{0,1:T(8,128)(2,1)S(1)}, bf16[128,320]{0,1:T(8,128)(2,1)}, u32[]{:S(2)}) copy-start(bf16[128,320]{0,1:T(8,128)(2,1)} %copy-done.53) | copy-start | bytes 245764
  243.9 2.8 collective-permute-start.21
  243.9 11.8 %collective-permute-start.22 = (bf16[160,960]{1,0:T(8,128)(2,1)}, bf16[160,960]{1,0:T(8,128)(2,1)}, u32[]{:S(2)}, u32[]{:S(2)}) collective-permute-start(bf16[160,960]{1,0:T(8,128)(2,1)} %bitcast.62), channel_id=1, source_target_pairs={{0,12},{1,13},{2,14},{3,15},{4,0},{5,1},{6,2},{7,3},{8,4},{9,5},{1... | collective-permute-start | bytes 921608 | tf_op jit(solution)/shard_map/ppermute | solution.py:282
  245.5 10.2 %copy-start.41 = (bf16[5,3,128,128]{2,3,1,0:T(8,128)(2,1)S(1)}, bf16[5,3,128,128]{2,3,1,0:T(8,128)(2,1)}, u32[]{:S(2)}) copy-start(bf16[5,3,128,128]{2,3,1,0:T(8,128)(2,1)} %copy-done.39) | copy-start | bytes 1474564
  245.5 10.6 %copy-start.37 = (f32[5,3,128,128]{2,3,1,0:T(8,128)S(1)}, f32[5,3,128,128]{2,3,1,0:T(8,128)}, u32[]{:S(2)}) copy-start(f32[5,3,128,128]{2,3,1,0:T(8,128)} %copy-done.35) | copy-start | bytes 2949124
  245.5 10.6 %copy-start.63 = (bf16[128,960]{0,1:T(8,128)(2,1)S(1)}, bf16[128,960]{0,1:T(8,128)(2,1)}, u32[]{:S(2)}) copy-start(bf16[128,960]{0,1:T(8,128)(2,1)} %fusion.33) | copy-start | bytes 737284
  245.5 22.2 %collective-permute-start.27 = (bf16[160,960]{1,0:T(8,128)(2,1)}, bf16[160,960]{1,0:T(8,128)(2,1)}, u32[]{:S(2)}, u32[]{:S(2)}) collective-permute-start(bf16[160,960]{1,0:T(8,128)(2,1)} %bitcast.205), channel_id=1, source_target_pairs={{0,8},{1,9},{2,10},{3,11},{4,12},{5,13},{6,14},{7,15},{8,0},{9,1},... | collective-permute-start | bytes 921608 | tf_op jit(solution)/shard_map/ppermute | solution.py:282
  245.6 30.2 %collective-permute-start.26 = (bf16[2,160,960]{2,1,0:T(8,128)(2,1)}, bf16[2,160,960]{2,1,0:T(8,128)(2,1)}, u32[]{:S(2)}, u32[]{:S(2)}) collective-permute-start(bf16[2,160,960]{2,1,0:T(8,128)(2,1)} %copy-done.27), channel_id=1, source_target_pairs={{0,4},{1,5},{2,6},{3,7},{4,0},{5,1},{6,2},{7,3},{8,12},{9,13},{10,... | collective-permute-start | bytes 1843208 | tf_op jit(solution)/shard_map/ppermute | solution.py:243
  249.3 7.4 %copy-start.7 = (f32[2,160,960]{2,1,0:T(8,128)}, f32[2,160,960]{2,1,0:T(8,128)S(1)}, u32[]{:S(2)}) copy-start(f32[2,160,960]{2,1,0:T(8,128)S(1)} %get-tuple-element.154) | copy-start | bytes 3686404
  257.7 10.8 %collective-permute-start.24 = (bf16[128,960]{1,0:T(8,128)(2,1)S(1)}, bf16[128,960]{1,0:T(8,128)(2,1)}, u32[]{:S(2)}, u32[]{:S(2)}) collective-permute-start(bf16[128,960]{1,0:T(8,128)(2,1)S(1)} %copy-done.24), channel_id=1, source_target_pairs={{0,2},{1,3},{2,0},{3,1},{4,6},{5,7},{6,4},{7,5},{8,10},{9,11},{10,... | collective-permute-start | bytes 737288 | tf_op jit(solution)/shard_map/ppermute | solution.py:243
  259.0 9.5 %collective-permute-start.25 = (bf16[128,960]{1,0:T(8,128)(2,1)S(1)}, bf16[128,960]{1,0:T(8,128)(2,1)S(1)}, u32[]{:S(2)}, u32[]{:S(2)}) collective-permute-start(bf16[128,960]{1,0:T(8,128)(2,1)S(1)} %copy-done.24), channel_id=1, source_target_pairs={{0,1},{1,0},{2,3},{3,2},{4,5},{5,4},{6,7},{7,6},{8,9},{9,8},{10,11... | collective-permute-start | bytes 737288 | tf_op jit(solution)/shard_map/ppermute | solution.py:243
  259.9 7.8 %copy-start.26 = (bf16[2,160,960]{2,1,0:T(8,128)(2,1)S(1)}, bf16[2,160,960]{2,1,0:T(8,128)(2,1)}, u32[]{:S(2)}) copy-start(bf16[2,160,960]{2,1,0:T(8,128)(2,1)} %copy-done.25) | copy-start | bytes 1843204
  260.9 14.9 %collective-permute-start.23 = (bf16[2,128,640]{2,1,0:T(8,128)(2,1)}, bf16[2,128,640]{2,1,0:T(8,128)(2,1)S(1)}, u32[]{:S(2)}, u32[]{:S(2)}) collective-permute-start(bf16[2,128,640]{2,1,0:T(8,128)(2,1)} %bitcast.256), channel_id=1, source_target_pairs={{0,2},{1,3},{2,0},{3,1},{4,6},{5,7},{6,4},{7,5},{8,10},{9,11},{10,... | collective-permute-start | bytes 983048 | tf_op jit(solution)/shard_map/ppermute | solution.py:243
  264.2 18.6 %copy-start.16 = (f32[1,160,960]{2,1,0:T(8,128)S(1)}, f32[1,160,960]{2,1,0:T(8,128)}, u32[]{:S(2)}) copy-start(f32[1,160,960]{2,1,0:T(8,128)} %copy-done.15) | copy-start | bytes 1843204
  264.2 18.6 %copy-start.73 = (bf16[160,960]{1,0:T(8,128)(2,1)S(1)}, bf16[160,960]{1,0:T(8,128)(2,1)}, u32[]{:S(2)}) copy-start(bf16[160,960]{1,0:T(8,128)(2,1)} %copy-done.72) | copy-start | bytes 921604
  267.7 27.7 %collective-permute-start.37 = (bf16[2,160,960]{2,1,0:T(8,128)(2,1)S(1)}, bf16[2,160,960]{2,1,0:T(8,128)(2,1)}, u32[]{:S(2)}, u32[]{:S(2)}) collective-permute-start(bf16[2,160,960]{2,1,0:T(8,128)(2,1)S(1)} %copy-done.26), channel_id=1, source_target_pairs={{0,4},{1,5},{2,6},{3,7},{4,0},{5,1},{6,2},{7,3},{8,12},{9,13},{10,... | collective-permute-start | bytes 1843208 | tf_op jit(solution)/shard_map/ppermute | solution.py:243
  268.5 10.7 %copy-start.33 = (bf16[128,960]{1,0:T(8,128)(2,1)}, bf16[128,960]{1,0:T(8,128)(2,1)S(1)}, u32[]{:S(2)}) copy-start(bf16[128,960]{1,0:T(8,128)(2,1)S(1)} %collective-permute-done.25.refs_10_) | copy-start | bytes 737284
  279.3 7.9 %collective-permute-start.32 = (f32[1920]{0:T(1024)S(1)}, f32[1920]{0:T(1024)S(1)}, u32[]{:S(2)}, u32[]{:S(2)}) collective-permute-start(f32[1920]{0:T(1024)S(1)} %pad_maximum_fusion.15), channel_id=1, source_target_pairs={{0,3},{1,2},{2,1},{3,0},{4,7},{5,6},{6,5},{7,4},{8,11},{9,10},{10,... | collective-permute-start | bytes 23048 | tf_op jit(solution)/shard_map/ppermute | solution.py:243
  279.5 8.2 %collective-permute-start.30 = (f32[1920]{0:T(1024)S(1)}, f32[1920]{0:T(1024)S(1)}, u32[]{:S(2)}, u32[]{:S(2)}) collective-permute-start(f32[1920]{0:T(1024)S(1)} %pad_maximum_fusion.15), channel_id=1, source_target_pairs={{0,1},{1,0},{2,3},{3,2},{4,5},{5,4},{6,7},{7,6},{8,9},{9,8},{10,11... | collective-permute-start | bytes 23048 | tf_op jit(solution)/shard_map/ppermute | solution.py:243
  280.7 7.7 %collective-permute-start.31 = (f32[1920]{0:T(1024)S(1)}, f32[1920]{0:T(1024)S(1)}, u32[]{:S(2)}, u32[]{:S(2)}) collective-permute-start(f32[1920]{0:T(1024)S(1)} %pad_maximum_fusion.15), channel_id=1, source_target_pairs={{0,2},{1,3},{2,0},{3,1},{4,6},{5,7},{6,4},{7,5},{8,10},{9,11},{10,... | collective-permute-start | bytes 23048 | tf_op jit(solution)/shard_map/ppermute | solution.py:243
  282.8 6.3 %collective-permute-start.28 = (bf16[2,128,640]{2,1,0:T(8,128)(2,1)}, bf16[2,128,640]{2,1,0:T(8,128)(2,1)S(1)}, u32[]{:S(2)}, u32[]{:S(2)}) collective-permute-start(bf16[2,128,640]{2,1,0:T(8,128)(2,1)} %pad_maximum_fusion.6), channel_id=1, source_target_pairs={{0,1},{1,0},{2,3},{3,2},{4,5},{5,4},{6,7},{7,6},{8,9},{9,8},{10,11... | collective-permute-start | bytes 983048 | tf_op jit(solution)/shard_map/ppermute | solution.py:243
  287.2 1.9 collective-permute-start.29
  287.7 25.5 %collective-permute-start.36 = (bf16[160,960]{1,0:T(8,128)(2,1)S(1)}, bf16[160,960]{1,0:T(8,128)(2,1)S(1)}, u32[]{:S(2)}, u32[]{:S(2)}) collective-permute-start(bf16[160,960]{1,0:T(8,128)(2,1)S(1)} %fusion.70), channel_id=1, source_target_pairs={{0,8},{1,9},{2,10},{3,11},{4,12},{5,13},{6,14},{7,15},{8,0},{9,1},... | collective-permute-start | bytes 921608 | tf_op jit(solution)/shard_map/ppermute | solution.py:243
  296.8 16.5 %copy-start.47 = (f32[2,160,960]{2,1,0:T(8,128)S(1)}, f32[2,160,960]{2,1,0:T(8,128)}, u32[]{:S(2)}) copy-start(f32[2,160,960]{2,1,0:T(8,128)} %copy-done.46) | copy-start | bytes 3686404
  296.8 23.5 %collective-permute-start.38 = (bf16[160,960]{1,0:T(8,128)(2,1)S(1)}, bf16[160,960]{1,0:T(8,128)(2,1)S(1)}, u32[]{:S(2)}, u32[]{:S(2)}) collective-permute-start(bf16[160,960]{1,0:T(8,128)(2,1)S(1)} %fusion.71), channel_id=1, source_target_pairs={{0,8},{1,9},{2,10},{3,11},{4,12},{5,13},{6,14},{7,15},{8,0},{9,1},... | collective-permute-start | bytes 921608 | tf_op jit(solution)/shard_map/ppermute | solution.py:243
  299.8 20.6 %copy-start.48 = (f32[1,160,960]{2,1,0:T(8,128)S(1)}, f32[1,160,960]{2,1,0:T(8,128)}, u32[]{:S(2)}) copy-start(f32[1,160,960]{2,1,0:T(8,128)} %fusion.42) | copy-start | bytes 1843204
  313.3 13.4 %collective-permute-start.35 = (bf16[168,960]{1,0:T(8,128)(2,1)S(1)}, bf16[168,960]{1,0:T(8,128)(2,1)S(1)}, u32[]{:S(2)}, u32[]{:S(2)}) collective-permute-start(bf16[168,960]{1,0:T(8,128)(2,1)S(1)} %bitcast.204), channel_id=1, source_target_pairs={{0,12},{1,13},{2,14},{3,15},{4,0},{5,1},{6,2},{7,3},{8,4},{9,5},{1... | collective-permute-start | bytes 967688 | tf_op jit(solution)/shard_map/ppermute | solution.py:282
  314.1 34.8 %collective-permute-start.34 = (bf16[168,960]{1,0:T(8,128)(2,1)S(1)}, bf16[168,960]{1,0:T(8,128)(2,1)S(1)}, u32[]{:S(2)}, u32[]{:S(2)}) collective-permute-start(bf16[168,960]{1,0:T(8,128)(2,1)S(1)} %bitcast.203), channel_id=1, source_target_pairs={{0,8},{1,9},{2,10},{3,11},{4,12},{5,13},{6,14},{7,15},{8,0},{9,1},... | collective-permute-start | bytes 967688 | tf_op jit(solution)/shard_map/ppermute | solution.py:282
  314.1 34.8 %collective-permute-start.33 = (bf16[168,960]{1,0:T(8,128)(2,1)S(1)}, bf16[168,960]{1,0:T(8,128)(2,1)S(1)}, u32[]{:S(2)}, u32[]{:S(2)}) collective-permute-start(bf16[168,960]{1,0:T(8,128)(2,1)S(1)} %bitcast.202), channel_id=1, source_target_pairs={{0,4},{1,5},{2,6},{3,7},{4,8},{5,9},{6,10},{7,11},{8,12},{9,13},{1... | collective-permute-start | bytes 967688 | tf_op jit(solution)/shard_map/ppermute | solution.py:282
  (57 other events, 121.8 us)
Sparse Core Ops, SparseCore 0:
  10.2 111.5 all-gather.1

commit v8 on v7

--- a/solution.py
+++ b/solution.py
@@ -169,7 +169,7 @@
 
 
 def ffn_backward_kernel(
-    eb_ref, gate_ref, up_ref, wg_ref, wu_ref, wd_ref, dgate_ref, dup_ref, dm_ref
+    eb_ref, gate_ref, up_ref, wg_ref, wu_ref, wd_ref, both_ref, dm_ref
 ):
     flat = lambda ref: ref[...].reshape(-1, ref.shape[-1])
     da = dot_nt(eb_ref[...], flat(wd_ref))
@@ -177,8 +177,8 @@
     sig = jax.nn.sigmoid(gate)
     dgate = (da * up_ref[...] * sig * (1.0 + gate * (1.0 - sig))).astype(bf16)
     dup = (da * gate * sig).astype(bf16)
-    dgate_ref[...] = dgate
-    dup_ref[...] = dup
+    both_ref[0] = dgate
+    both_ref[1] = dup
     add = dot_nn(dgate, flat(wg_ref)) + dot_nn(dup, flat(wu_ref))
 
     @pl.when(pl.program_id(0) == 0)
@@ -200,14 +200,17 @@
     tokens, cols = wholes[0].shape[0], lines * share
     whole = pl.BlockSpec((tokens, width), lambda i: (0, 0))
     block = pl.BlockSpec((None, tokens, cols), lambda i: (i, 0, 0))
+    out_specs = [
+        pl.BlockSpec((None, *shape), lambda i, n=len(shape): (i,) + (0,) * n) for shape, _ in out_blocks
+    ]
     return pl.pallas_call(
         kernel,
         grid=(steps,),
         in_specs=[whole] * len(wholes)
         + [block] * len(blocks)
         + [weight_spec(w, matrix) for matrix in (1, 2, 3)],
-        out_specs=[block] * len(out_blocks) + [whole],
-        out_shape=[jax.ShapeDtypeStruct((steps, tokens, cols), t) for t in out_blocks]
+        out_specs=out_specs + [whole],
+        out_shape=[jax.ShapeDtypeStruct((steps, *shape), t) for shape, t in out_blocks]
         + [jax.ShapeDtypeStruct((tokens, width), f32)],
         compiler_params=pltpu.CompilerParams(
             dimension_semantics=("arbitrary",), vmem_limit_bytes=40 * 1024 * 1024
@@ -222,7 +225,8 @@
 
 def ffn_forward(m, h1, w):
     if w.ndim == 5:
-        return ffn_call(ffn_forward_kernel, w, (m, h1), (), (f32, f32, bf16))
+        shape = (m.shape[0], w.shape[0] * w.shape[3])
+        return ffn_call(ffn_forward_kernel, w, (m, h1), (), [(shape, t) for t in (f32, f32, bf16)])
     gate, up = dot_nt(m, w[0]), dot_nt(m, w[1])
     act = (jax.nn.silu(gate) * up).astype(bf16)
     return gate, up, act, h1 + dot_nn(act, w[2])
@@ -230,7 +234,9 @@
 
 def ffn_backward(eb, gate, up, w):
     if w.ndim == 5:
-        return ffn_call(ffn_backward_kernel, w, (eb,), (gate, up), (bf16, bf16))
+        shape = (2, eb.shape[0], w.shape[0] * w.shape[3])
+        both, dm = ffn_call(ffn_backward_kernel, w, (eb,), (gate, up), [(shape, bf16)])
+        return both, both, dm
     da = dot_nt(eb, w[2])
     sig = jax.nn.sigmoid(gate)
     dgate = (da * up * sig * (1.0 + gate * (1.0 - sig))).astype(bf16)
@@ -313,18 +319,24 @@
     rest = refs[3 + 4 * n_rows :]
     extra_ref = rest[0] if n_rows == 2 else None
     outs, total = rest[n_rows - 1 : -1], rest[-1]
-    cols = jnp.concatenate(
-        [cols_ref[picks_ref[0]], y_ref[picks_ref[1]], core_ref[0], core_ref[1]], axis=0
-    )
-    share = total.shape[0] // LINE
+    kinds = cols_ref.shape[1]
+    height = total.shape[0] // kinds
+    share = height // LINE
+
+    def cols_of(j):
+        return jnp.concatenate(
+            [cols_ref[picks_ref[0], j], y_ref[picks_ref[1], j], core_ref[0, j], core_ref[1, j]], axis=0
+        )
 
     def dot(c, r):
         return lax.dot_general(c, r, (((0,), (0,)), ((), ())), preferred_element_type=f32)
 
     if n_rows == 1:
-        total[...] = dot(cols, rows[0])
+        for j in range(kinds):
+            total[j * height : (j + 1) * height] = dot(cols_of(j), rows[0])
     else:
         low, top = split
+        cols = cols_of(0)
         total[...] = dot(cols, rows[1])
         first = dot(cols, rows[0])
         total[: low * share] = first[: low * share]
@@ -339,16 +351,17 @@
         for i in range(ref.shape[0]):
             pick = picks_ref[slot]
             slot += 1
-            block = total[pl.ds(pl.multiple_of(pick * share, 8), share)]
-            ref[i, :share] = block.astype(ref.dtype)
+            for j in range(kinds):
+                block = total[pl.ds(pl.multiple_of(j * height + pick * share, 8), share)]
+                ref[i, j * share : (j + 1) * share] = block.astype(ref.dtype)
             if extra_ref is not None:
                 ref[i, share:] = extra_ref[pick].astype(ref.dtype)
 
 
 def plane_product(cols, x_y, x_core, rows, picks, out_counts, split=None, extra=None):
-    blocks, tokens, width_cols = cols.shape
+    _, kinds, tokens, width_cols = cols.shape
     share, width = width_cols // LINE, rows[0][0].shape[1]
-    tall = share + (0 if extra is None else extra.shape[1])
+    tall = kinds * share + (0 if extra is None else extra.shape[1])
     operands = [cols, x_y, x_core, *[r for chunk in rows for r in chunk]]
     if extra is not None:
         operands.append(extra)
@@ -365,15 +378,15 @@
             grid=(1,),
             in_specs=[whole(v) for v in operands],
             out_specs=[whole(v) for v in shapes],
-            scratch_shapes=[pltpu.VMEM((LINE * share, width), f32)],
+            scratch_shapes=[pltpu.VMEM((kinds * LINE * share, width), f32)],
         ),
         out_shape=shapes,
         compiler_params=pltpu.CompilerParams(
             dimension_semantics=("arbitrary",), vmem_limit_bytes=32 * 1024 * 1024
         ),
         cost_estimate=pl.CostEstimate(
-            flops=8 * tokens * width_cols * width * len(rows),
-            bytes_accessed=8 * tokens * (width_cols + width) + 8 * width_cols * width,
+            flops=8 * tokens * kinds * width_cols * width * len(rows),
+            bytes_accessed=8 * tokens * (kinds * width_cols + width) + 4 * kinds * width_cols * width,
             transcendentals=0,
         ),
     )(jnp.stack([jnp.asarray(p, jnp.int32) for p in picks]), *operands)
@@ -410,6 +423,7 @@
     m_y, n_y = flip(m, Y_BIT), flip(n, Y_BIT)
     gate, up, act, out, m_y, n_y = tie((gate, up, act, out, m_y, n_y))
     state = (*state, gate, up, act)
+    act = act[:, None]
     act_y = cols_y(act, y)
     m_all = (m, m_y, flip(m, CORE_BIT), flip(m_y, CORE_BIT))
     n_all = (n, n_y, flip(n, CORE_BIT), flip(n_y, CORE_BIT))
@@ -429,72 +443,65 @@
     z2, z1 = z >> 1, z & 1
     m_all, n_all, act_c = early
     tokens, width = o.shape[0], e.shape[1]
-    share = act_c[0].shape[2] // LINE
+    share = act_c[0].shape[3] // LINE
     here = (2 * y + core, core)
     others = [(z + k) % LINE for k in ORDER]
-    pairs = (z1, 2 + z1, 1 - z1, 3 - z1)
     eb = e.astype(bf16)
     eb_y, eb_c = flip(eb, Y_BIT), flip(eb, CORE_BIT)
-    dgate, dup, dm = backward_ffn(eb, state, weights)
-    dgate, dup, dm, eb_y, eb_c = tie((dgate, dup, dm, eb_y, eb_c))
-    eb_all = (eb, eb_y, eb_c, flip(eb_y, CORE_BIT))
-    gate_y = cols_y(dgate, y)
+    both, _, dm = backward_ffn(eb, state, weights)
+    both, dm, eb_y, eb_c = tie((both, dm, eb_y, eb_c))
+    both_y = cols_y(both, y)
+    eb_yc = flip(eb_y, CORE_BIT)
+    dm, eb_yc = tie((dm, eb_yc))
+    direct = (*here, 0, z, *others)
+    ones = (1, 1, 1, 1)
+    down_own, *down_sends = plane_product(*act_c, [(eb, eb_y, eb_c, eb_yc)], direct, ones)
+    dm, down_sends = tie((dm, down_sends))
+    down_one, down_two, down_three = direct_send(down_sends)
     dh1, dz, do, gain_two_grad = backward_mid(e, dm, state, weights)
-    do, dz, eb_all, dup = tie((do, dz, eb_all, dup))
-    down_own, *down_sends = plane_product(*act_c, [eb_all], (*here, 0, z, *others), (1, 1, 1, 1))
-    do, dup, gate_y, down_sends = tie((do, dup, gate_y, down_sends))
-    down_one, down_two, down_three = direct_send(down_sends)
-    gate_c = cols_core(dgate, gate_y, y, core)
-    up_y = cols_y(dup, y)
-    gate_c, down_one = tie((gate_c, down_one))
-    gate_own, gate_send = plane_product(dgate, gate_y, gate_c, [m_all], (*here, 0, *pairs), (2, 2))
-    gate_own, gate_send, up_y = tie((gate_own, gate_send, up_y))
-    gate_received = flip(gate_send, Z1_BIT)
-    up_c = cols_core(dup, up_y, y, core)
-    up_own, up_send = plane_product(dup, up_y, up_c, [m_all], (*here, 0, *pairs), (2, 2))
-    do, dz, up_own, up_send, down_three = tie((do, dz, up_own, up_send, down_three))
-    up_received = flip(up_send, Z1_BIT)
+    do, dz, both_y, down_one = tie((do, dz, both_y, down_one))
+    both_c = cols_core(both, both_y, y, core)
+    both_own, *both_sends = plane_product(both, both_y, both_c, [m_all], direct, ones)
+    do, dz, both_sends = tie((do, dz, both_sends))
+    both_one, both_two, both_three = direct_send(both_sends)
     dproj = backward_attention(do, state, tables)
+    dproj, down_two, down_three = tie((dproj, down_two, down_three))
+    attn_cols = jnp.concatenate([dproj, o], axis=1).reshape(tokens, 4, 4, share)
+    attn_cols = attn_cols.transpose(2, 0, 1, 3).reshape(4, 1, tokens, 4 * share)
+    attn_y = cols_y(attn_cols, y)
     dz_y, dz_c = flip(dz, Y_BIT), flip(dz, CORE_BIT)
-    attn_cols = jnp.concatenate([dproj, o], axis=1).reshape(tokens, 4, 4, share)
-    attn_cols = attn_cols.transpose(2, 0, 1, 3).reshape(4, tokens, 4 * share)
-    attn_y = cols_y(attn_cols, y)
-    dproj, attn_y, dz_y, dz_c, gate_own, gate_received, down_two = tie(
-        (dproj, attn_y, dz_y, dz_c, gate_own, gate_received, down_two)
-    )
+    du, gain_one_grad = backward_in(dproj, dh1, state, weights)
+    gain_grad = jnp.concatenate([gain_one_grad, gain_two_grad])
+    gain_grad, attn_y, dz_y, dz_c, both_one = tie((gain_grad, attn_y, dz_y, dz_c, both_one))
+    gain_grad = gain_grad + flip(gain_grad, CORE_BIT)
+    gain_grad = gain_grad + flip(gain_grad, Y_BIT)
     dz_all = (dz, dz_y, dz_c, flip(dz_y, CORE_BIT))
     attn_c = cols_core(attn_cols, attn_y, y, core)
-    du, gain_one_grad = backward_in(dproj, dh1, state, weights)
-    gain_grad = jnp.concatenate([gain_one_grad, gain_two_grad])
-    gain_grad = gain_grad + sum(
-        flip(gain_grad, bit) for bit in (CORE_BIT, Y_BIT, CORE_BIT | Y_BIT)
-    )
+    gain_grad, dz_all, attn_c, both_two = tie((gain_grad, dz_all, attn_c, both_two))
     gain_rows = at(gain_grad.reshape(4, 4, -1).transpose(1, 0, 2), y * 2 + core)[:, None]
     gain_share = gain_rows.shape[-1]
     gain_rows = jnp.pad(gain_rows, ((0, 0), (0, EXTRA_ROWS - 1), (0, width - gain_share)))
     qkv_owners = QKV_COLS // share
     is_qkv = (qkv_owners // 4 * 4 + y * 2 + core < qkv_owners).astype(jnp.int32)
-    attn_own, *attn_sends = plane_product(
+    attn_own, attn_send = plane_product(
         attn_cols,
         attn_y,
         attn_c,
         [n_all, dz_all],
-        (*here, is_qkv, z, *others),
-        (1, 1, 1, 1),
+        (*here, is_qkv, z1, 2 + z1, 1 - z1, 3 - z1),
+        (2, 2),
         (qkv_owners // 4, -(-qkv_owners // 4)),
         gain_rows,
     )
-    up_own, attn_own = tie((up_own, attn_own))
-    attn_received = direct_send(attn_sends)
-    down_received = (down_one, down_two, down_three)
-    gate = pair_second(gate_own, gate_received, z2)
-    up = pair_second(up_own, up_received, z2)
-    down = direct_total(down_own[0], down_received)
-    attn = direct_total(attn_own[0], attn_received)
+    attn_received = flip(attn_send, Z1_BIT)
+    attn_own, attn_received, both_three = tie((attn_own, attn_received, both_three))
+    attn = pair_second(attn_own, attn_received, z2)
+    down = direct_total(down_own[0], (down_one, down_two, down_three))
+    both = direct_total(both_own[0], (both_one, both_two, both_three))
     return (
         du,
         attn[:share],
-        jnp.stack([gate, up, down]),
+        jnp.concatenate([both, down]).reshape(3, share, width),
         attn[share : share + 1, :gain_share],
     )
 

time: 358 us -> 359 us (level)
  starting transfers between devices: 36.3 us -> 55.7 us
  local copies, waits for them, and re-layouts: 23.4 us -> 14.9 us
  other arithmetic: 22.5 us -> 16.8 us
    ppermute x6, starting transfers between devices: 5.17 us -> 17.4 us  [z_pairs(): lax.ppermute(x, 'dp', [(4 * a + i, 4 * b + i) for a, b in pairs for i in...]
    ppermute x31 -> x26, starting transfers between devices: 26 us -> 33.4 us  [flip(): return lax.ppermute(x, 'dp', [(i, i ^ bit) for i in range(size)])]
    unnamed x162 -> x122, local copies, waits for them, and re-layouts: 10.7 us -> 3.98 us
    pallas_call x4 -> x3, Pallas kernels: 12.1 us -> 10.6 us  [plane_product(): pl.pallas_call(kernel, grid_spec=pltpu.PrefetchScalarGridSpec(num_scalar_...]
    ppermute x31 -> x26, waiting for transfers between devices: 36.3 us -> 36.9 us  [flip(): return lax.ppermute(x, 'dp', [(i, i ^ bit) for i in range(size)])]
  transfers between devices with their start and end apart: 40 -> 35, of which waited for: 19 -> 19; matrix products, arithmetic and copies ran while one was open for 7% -> 6% of each run, Pallas kernels for 11% -> 10%
where the time goes in v8:
time: 359 us; the launch traced here: 358 us
  waiting for transfers between devices  191 us (53%)
  starting transfers between devices  55.7 us (16%)
  Pallas kernels  47.2 us (13%)
  matrix products  17.8 us (5%)
  other arithmetic  16.8 us (5%)
  between operations  15.3 us (4%)
  local copies, waits for them, and re-layouts  14.9 us (4%)
    all_gather x1, waiting for transfers between devices, local(): lax.all_gather(own, 'dp', axis=0, tiled=True).reshape(4, 4, 4, share, width)  97.4 us
    ppermute x6, waiting for transfers between devices, z_pairs(): lax.ppermute(x, 'dp', [(4 * a + i, 4 * b + i) for a, b in pairs for i in...  41.8 us
    ppermute x26, waiting for transfers between devices, flip(): return lax.ppermute(x, 'dp', [(i, i ^ bit) for i in range(size)])  36.9 us
    pallas_call x4, Pallas kernels, ffn_call(): pl.pallas_call(kernel, grid=(steps,), in_specs=[whole] * len(wholes) + [b...  36.6 us
    ppermute x26, starting transfers between devices, flip(): return lax.ppermute(x, 'dp', [(i, i ^ bit) for i in range(size)])  33.4 us
    ppermute x6, starting transfers between devices, z_pairs(): lax.ppermute(x, 'dp', [(4 * a + i, 4 * b + i) for a, b in pairs for i in...  17.4 us
    pallas_call x3, Pallas kernels, plane_product(): pl.pallas_call(kernel, grid_spec=pltpu.PrefetchScalarGridSpec(num_scalar_...  10.6 us
    ppermute x1, waiting for transfers between devices, local(): received = lax.ppermute(first_grad, 'section', [(1, 0)])  9.06 us
  transfers between devices with their start and end apart: 35, of which 19 were waited for; matrix products, arithmetic and copies ran while one was open for 6% of the time, Pallas kernels for 10%

profile of v8, /device:TPU:0, one launch (start us, length us, event | category | flops | bytes accessed | tf_op | source)
XLA Modules:
  0.0 358.4 jit_solution(12944745408032165312)
XLA Ops:
  7.2 2.5 pad_maximum_fusion.1
  11.2 2.8 collective-permute-start.1
  14.2 1.4 collective-permute-done.1
  15.7 2.1 collective-permute-start.2
  17.9 1.4 collective-permute-done.2
  19.5 3.0 collective-permute-start.3
  22.8 1.3 collective-permute-done.3
  24.4 97.4 %all-gather.2.cloned.1.call-done = bf16[10240,960]{1,0:T(8,128)(2,1)} async-done(((bf16[640,960]{1,0:T(8,128)(2,1)}), bf16[10240,960]{1,0:T(8,128)(2,1)}) %all-gather.2.cloned.1.call-update) | async-done | bytes 19660816 | tf_op jit(solution)/shard_map/all_gather | solution.py:522
  121.8 3.3 slice.119
  125.0 1.1 fusion.6
  128.1 9.6 %shard_map.84 = (f32[4,128,640]{2,1,0:T(8,128)}, f32[4,128,640]{2,1,0:T(8,128)}, bf16[4,128,640]{2,1,0:T(8,128)(2,1)}, f32[128,960]{1,0:T(8,128)S(1)}) custom-call(bf16[128,960]{1,0:T(8,128)(2,1)S(1)} %multiply_convert_fusion.3.m_ref, f32[128,960]{1,0:T(8,128)S(1)} %get-tuple-element.198.h1_ref, bf16[4,4,4,160,960]{4,3,2,1,0:T(8,128)(2,1)} %bitcast.195, ...), custom_call_target="tpu_custom_call" | custom-call | flops 1887436800 | bytes 14745600 | tf_op jit(solution)/shard_map/pallas_call | solution.py:206
  137.7 3.6 collective-permute-start.4
  141.3 5.8 %collective-permute-done.4 = bf16[128,960]{1,0:T(8,128)(2,1)S(1)} collective-permute-done((bf16[128,960]{1,0:T(8,128)(2,1)S(1)}, bf16[128,960]{1,0:T(8,128)(2,1)S(1)}, u32[]{:S(2)}, u32[]{:S(2)}) %collective-permute-start.4) | collective-permute-done | bytes 245792 | tf_op jit(solution)/shard_map/ppermute | solution.py:537
  147.3 0.8 fusion.55.refs_4_
  148.1 3.0 fusion.4
  153.0 2.2 multiply_reduce_fusion.5
  155.7 0.8 multiply_convert_fusion.2.m_ref.refs_4_
  156.6 1.2 collective-permute-start.5
  157.8 0.8 collective-permute-start.6
  158.6 8.3 %shard_map.85 = (f32[4,128,640]{2,1,0:T(8,128)S(1)}, f32[4,128,640]{2,1,0:T(8,128)S(1)}, bf16[4,128,640]{2,1,0:T(8,128)(2,1)S(1)}, f32[128,960]{1,0:T(8,128)S(1)}) custom-call(bf16[128,960]{1,0:T(8,128)(2,1)} %multiply_convert_fusion.2.m_ref.refs_4_, f32[128,960]{1,0:T(8,128)S(1)} %get-tuple-element.202.h1_ref, bf16[4,4,4,160,960]{4,3,2,1,0:T(8,128)(2,1)} %bitcast.198, ...), custom_call_target="tpu_custom_call" | custom-call | flops 1887436800 | bytes 14745600 | tf_op jit(solution)/shard_map/pallas_call | solution.py:206
  166.9 3.2 collective-permute-done.6.refs_5_
  170.1 0.8 dynamic-slice_bitcast_fusion.1
  170.9 1.2 collective-permute-start.7
  173.2 1.1 dynamic-slice_bitcast_fusion.2
  174.3 9.9 %shard_map.86 = (bf16[4,2,128,640]{3,2,1,0:T(8,128)(2,1)}, f32[128,960]{1,0:T(8,128)S(1)}) custom-call(bf16[128,960]{1,0:T(8,128)(2,1)S(1)} %bitcast.185, f32[4,128,640]{2,1,0:T(8,128)S(1)} %get-tuple-element.84.gate_ref, f32[4,128,640]{2,1,0:T(8,128)S(1)} %get-tuple-element.85.up_ref, bf16[4,4,4,160,960]{4,3,2,1,0:T(8,128)(2,1)} %bitcast.201, ...), custom_call_target="tpu_custom_call" | custom-call | flops 1887436800 | bytes 14745600 | tf_op jit(solution)/shard_map/pallas_call | solution.py:206
  187.6 0.9 constant_dynamic-slice_fusion.6
  190.3 1.3 collective-permute-start.13
  191.6 9.1 %collective-permute-done.13 = bf16[128,960]{1,0:T(8,128)(2,1)S(1)} collective-permute-done((bf16[128,960]{1,0:T(8,128)(2,1)S(1)}, bf16[128,960]{1,0:T(8,128)(2,1)S(1)}, u32[]{:S(2)}, u32[]{:S(2)}) %collective-permute-start.13) | collective-permute-done | bytes 245792 | tf_op jit(solution)/shard_map/ppermute | solution.py:541
  200.7 0.8 broadcast_select_fusion.eb_ref.refs_4_
  201.5 0.8 collective-permute-start.14
  202.3 8.8 %shard_map.87 = (bf16[4,2,128,640]{3,2,1,0:T(8,128)(2,1)S(1)}, f32[128,960]{1,0:T(8,128)S(1)}) custom-call(bf16[128,960]{1,0:T(8,128)(2,1)} %broadcast_select_fusion.eb_ref.refs_4_, f32[4,128,640]{2,1,0:T(8,128)S(1)} %get-tuple-element.84.gate_ref, f32[4,128,640]{2,1,0:T(8,128)S(1)} %get-tuple-element.85.up_ref, bf16[4,4,4,160,960]{4,3,2,1,0:T(8,128)(2,1)} %bitcast.204, ...), custom_call_target="tpu_custom_call" | custom-call | flops 1887436800 | bytes 14745600 | tf_op jit(solution)/shard_map/pallas_call | solution.py:206
  211.8 1.3 collective-permute-start.17
  213.2 2.7 shard_map.88
  216.1 1.8 collective-permute-start.18
  217.9 1.9 fusion.86
  219.8 2.3 fusion.33
  222.1 5.7 %collective-permute-done.18 = bf16[160,960]{1,0:T(8,128)(2,1)S(1)} collective-permute-done((bf16[160,960]{1,0:T(8,128)(2,1)S(1)}, bf16[160,960]{1,0:T(8,128)(2,1)S(1)}, u32[]{:S(2)}, u32[]{:S(2)}) %collective-permute-start.18) | collective-permute-done | bytes 307232 | tf_op jit(solution)/shard_map/ppermute | solution.py:288
  228.8 2.5 collective-permute-start.20
  231.2 1.5 collective-permute-start.21
  232.7 4.3 %shard_map.89 = (f32[1,320,960]{2,1,0:T(8,128)S(1)}, bf16[1,320,960]{2,1,0:T(8,128)(2,1)}, bf16[1,320,960]{2,1,0:T(8,128)(2,1)S(1)}, bf16[1,320,960]{2,1,0:T(8,128)(2,1)S(1)}) custom-call(s32[7]{0:T(128)S(1)} %stack.73.refs_0_, bf16[4,2,128,640]{3,2,1,0:T(8,128)(2,1)S(1)} %get-tuple-element.107.refs_1_, ...), custom_call_target="tpu_custom_call" | custom-call | flops 1258291200 | bytes 7208960 | tf_op jit(solution)/shard_map/pallas_call | solution.py:374
  239.1 1.3 collective-permute-start.23
  240.6 6.7 %collective-permute-done.20 = bf16[160,960]{1,0:T(8,128)(2,1)S(1)} collective-permute-done((bf16[160,960]{1,0:T(8,128)(2,1)S(1)}, bf16[160,960]{1,0:T(8,128)(2,1)S(1)}, u32[]{:S(2)}, u32[]{:S(2)}) %collective-permute-start.20) | collective-permute-done | bytes 307232 | tf_op jit(solution)/shard_map/ppermute | solution.py:288
  247.4 7.2 %collective-permute-start.25 = (bf16[320,960]{1,0:T(8,128)(2,1)}, bf16[320,960]{1,0:T(8,128)(2,1)}, u32[]{:S(2)}, u32[]{:S(2)}) collective-permute-start(bf16[320,960]{1,0:T(8,128)(2,1)} %bitcast.86), channel_id=1, source_target_pairs={{0,4},{1,5},{2,6},{3,7},{4,8},{5,9},{6,10},{7,11},{8,12},{9,13},{1... | collective-permute-start | bytes 1843208 | tf_op jit(solution)/shard_map/ppermute | solution.py:288
  254.6 0.9 copy.41
  255.6 1.2 collective-permute-start.22
  256.8 3.4 fusion.59
  260.2 1.4 copy.43.refs_1_
  261.6 2.7 collective-permute-start.30
  265.0 8.3 %collective-permute-done.25 = bf16[320,960]{1,0:T(8,128)(2,1)} collective-permute-done((bf16[320,960]{1,0:T(8,128)(2,1)}, bf16[320,960]{1,0:T(8,128)(2,1)}, u32[]{:S(2)}, u32[]{:S(2)}) %collective-permute-start.25) | collective-permute-done | bytes 614432 | tf_op jit(solution)/shard_map/ppermute | solution.py:288
  274.6 1.5 collective-permute-done.26
  276.8 1.8 collective-permute-start.32
  278.6 1.1 collective-permute-done.27
  279.7 21.0 %collective-permute-done.30 = bf16[320,960]{1,0:T(8,128)(2,1)} collective-permute-done((bf16[320,960]{1,0:T(8,128)(2,1)}, bf16[320,960]{1,0:T(8,128)(2,1)}, u32[]{:S(2)}, u32[]{:S(2)}) %collective-permute-start.30) | collective-permute-done | bytes 614432 | tf_op jit(solution)/shard_map/ppermute | solution.py:288
  300.9 0.9 copy-done.10
  301.8 0.9 copy-done.12
  302.8 3.6 %shard_map.90 = (f32[2,168,960]{2,1,0:T(8,128)S(1)}, bf16[2,168,960]{2,1,0:T(8,128)(2,1)S(1)}) custom-call(s32[7]{0:T(128)S(1)} %stack.81.refs_0_, bf16[4,1,128,640]{3,2,1,0:T(8,128)(2,1)S(1)} %copy.43.refs_1_, bf16[2,1,128,640]{3,2,1,0:T(8,128)(2,1)S(1)} %collective-permute-done.22.refs_2_, bf16[2,1,128,640]{3,2,1,0:T(8,128)(2,1)} %collective-permute-done.29.refs_3_, ...), custom_call_target="tpu_custom_call" | custom-call | flops 1258291200 | bytes 4096000 | tf_op jit(solution)/shard_map/pallas_call | solution.py:374
  306.5 10.7 %collective-permute-start.31 = (bf16[2,168,960]{2,1,0:T(8,128)(2,1)S(1)}, bf16[2,168,960]{2,1,0:T(8,128)(2,1)S(1)}, u32[]{:S(2)}, u32[]{:S(2)}) collective-permute-start(bf16[2,168,960]{2,1,0:T(8,128)(2,1)S(1)} %get-tuple-element.142), channel_id=1, source_target_pairs={{0,4},{1,5},{2,6},{3,7},{4,0},{5,1},{6,2},{7,3},{8,12},{9,13},{10,... | collective-permute-start | bytes 1935368 | tf_op jit(solution)/shard_map/ppermute | solution.py:249
  317.2 1.0 fusion.50
  318.4 13.7 %collective-permute-done.31 = bf16[2,168,960]{2,1,0:T(8,128)(2,1)S(1)} collective-permute-done((bf16[2,168,960]{2,1,0:T(8,128)(2,1)S(1)}, bf16[2,168,960]{2,1,0:T(8,128)(2,1)S(1)}, u32[]{:S(2)}, u32[]{:S(2)}) %collective-permute-start.31) | collective-permute-done | bytes 645152 | tf_op jit(solution)/shard_map/ppermute | solution.py:249
  332.3 3.4 collective-permute-start.33
  335.8 1.9 bitcast_add_fusion
  337.7 1.4 pad_maximum_fusion
  339.1 11.0 %collective-permute-done.33 = bf16[168,960]{1,0:T(8,128)(2,1)S(1)} collective-permute-done((bf16[168,960]{1,0:T(8,128)(2,1)S(1)}, bf16[168,960]{1,0:T(8,128)(2,1)S(1)}, u32[]{:S(2)}, u32[]{:S(2)}) %collective-permute-start.33) | collective-permute-done | bytes 322592 | tf_op jit(solution)/shard_map/ppermute | solution.py:249
  350.2 0.9 slice_bitcast_fusion
  (259 shorter events, 20.8 us)
Async XLA Ops:
  7.2 114.6 %all-gather.2.cloned.1.call-start = ((), (), s32[]{:S(2)}) async-start(), calls=%async_computation | async-start | bytes 22282240 | tf_op jit(solution)/shard_map/all_gather | solution.py:522
  7.2 10.5 %copy-start = (bf16[1,2,64,960]{3,2,1,0:T(8,128)(2,1)S(1)}, bf16[1,2,64,960]{3,2,1,0:T(8,128)(2,1)}, u32[]{:S(2)}) copy-start(bf16[1,2,64,960]{3,2,1,0:T(8,128)(2,1)} %param.5) | copy-start | bytes 737284
  9.8 1.3 collective-permute-start
  11.2 4.3 %collective-permute-start.1 = (bf16[240]{0:T(256)(128)(2,1)S(1)}, bf16[240]{0:T(256)(128)(2,1)S(1)}, u32[]{:S(2)}, u32[]{:S(2)}) collective-permute-start(bf16[240]{0:T(256)(128)(2,1)S(1)} %pad_maximum_fusion.18), channel_id=1, source_target_pairs={{0,2},{1,3},{2,0},{3,1},{4,6},{5,7},{6,4},{7,5},{8,10},{9,11},{10,... | collective-permute-start | bytes 1448 | tf_op jit(solution)/shard_map/ppermute | solution.py:249
  15.7 3.6 %collective-permute-start.2 = (bf16[480]{0:T(512)(128)(2,1)S(1)}, bf16[480]{0:T(512)(128)(2,1)S(1)}, u32[]{:S(2)}, u32[]{:S(2)}) collective-permute-start(bf16[480]{0:T(512)(128)(2,1)S(1)} %pad_maximum_fusion.17), channel_id=1, source_target_pairs={{0,4},{1,5},{2,6},{3,7},{4,0},{5,1},{6,2},{7,3},{8,12},{9,13},{10,... | collective-permute-start | bytes 2888 | tf_op jit(solution)/shard_map/ppermute | solution.py:249
  19.5 4.7 %collective-permute-start.3 = (bf16[960]{0:T(1024)(128)(2,1)S(1)}, bf16[960]{0:T(1024)(128)(2,1)S(1)}, u32[]{:S(2)}, u32[]{:S(2)}) collective-permute-start(bf16[960]{0:T(1024)(128)(2,1)S(1)} %pad_maximum_fusion.16), channel_id=1, source_target_pairs={{0,8},{1,9},{2,10},{3,11},{4,12},{5,13},{6,14},{7,15},{8,0},{9,1},... | collective-permute-start | bytes 5768 | tf_op jit(solution)/shard_map/ppermute | solution.py:249
  137.7 9.3 %collective-permute-start.4 = (bf16[128,960]{1,0:T(8,128)(2,1)S(1)}, bf16[128,960]{1,0:T(8,128)(2,1)S(1)}, u32[]{:S(2)}, u32[]{:S(2)}) collective-permute-start(bf16[128,960]{1,0:T(8,128)(2,1)S(1)} %convert_element_type.150), channel_id=1, source_target_pairs={{0,16},{1,17},{2,18},{3,19},{4,20},{5,21},{6,22},{7,23},{8,24},{9,... | collective-permute-start | bytes 737288 | tf_op jit(solution)/shard_map/ppermute | solution.py:537
  147.3 5.8 %copy-start.24 = (bf16[128,960]{1,0:T(8,128)(2,1)}, bf16[128,960]{1,0:T(8,128)(2,1)S(1)}, u32[]{:S(2)}) copy-start(bf16[128,960]{1,0:T(8,128)(2,1)S(1)} %get-tuple-element.161) | copy-start | bytes 737284
  147.3 42.2 %copy-start.52 = (f32[128]{0:T(128)}, f32[128]{0:T(128)S(1)}, u32[]{:S(2)}) copy-start(f32[128]{0:T(128)S(1)} %get-tuple-element.192) | copy-start | bytes 1540
  147.3 42.2 %copy-start.54 = (f32[128]{0:T(128)}, f32[128]{0:T(128)S(1)}, u32[]{:S(2)}) copy-start(f32[128]{0:T(128)S(1)} %get-tuple-element.191) | copy-start | bytes 1540
  156.6 10.3 %collective-permute-start.5 = (bf16[128,960]{1,0:T(8,128)(2,1)}, bf16[128,960]{1,0:T(8,128)(2,1)}, u32[]{:S(2)}, u32[]{:S(2)}) collective-permute-start(bf16[128,960]{1,0:T(8,128)(2,1)} %multiply_convert_fusion.2.m_ref.refs_4_), channel_id=1, source_target_pairs={{0,2},{1,3},{2,0},{3,1},{4,6},{5,7},{6,4},{7,5},{8,10},{9,11},{10,... | collective-permute-start | bytes 737288 | tf_op jit(solution)/shard_map/ppermute | solution.py:249
  157.8 12.3 %collective-permute-start.6 = (bf16[128,960]{1,0:T(8,128)(2,1)}, bf16[128,960]{1,0:T(8,128)(2,1)}, u32[]{:S(2)}, u32[]{:S(2)}) collective-permute-start(bf16[128,960]{1,0:T(8,128)(2,1)} %fusion.55.refs_4_), channel_id=1, source_target_pairs={{0,2},{1,3},{2,0},{3,1},{4,6},{5,7},{6,4},{7,5},{8,10},{9,11},{10,... | collective-permute-start | bytes 737288 | tf_op jit(solution)/shard_map/ppermute | solution.py:249
  166.9 4.1 %copy-start.3 = (f32[128,960]{1,0:T(8,128)}, f32[128,960]{1,0:T(8,128)S(1)}, u32[]{:S(2)}) copy-start(f32[128,960]{1,0:T(8,128)S(1)} %get-tuple-element.123) | copy-start | bytes 1474564
  170.9 13.3 %collective-permute-start.7 = (bf16[2,1,128,640]{3,2,1,0:T(8,128)(2,1)}, bf16[2,1,128,640]{3,2,1,0:T(8,128)(2,1)}, u32[]{:S(2)}, u32[]{:S(2)}) collective-permute-start(bf16[2,1,128,640]{3,2,1,0:T(8,128)(2,1)} %dynamic-slice_bitcast_fusion.1), channel_id=1, source_target_pairs={{0,2},{1,3},{2,0},{3,1},{4,6},{5,7},{6,4},{7,5},{8,10},{9,11},{10,... | collective-permute-start | bytes 983048 | tf_op jit(solution)/shard_map/ppermute | solution.py:249
  172.2 12.0 %collective-permute-start.8 = (bf16[128,960]{1,0:T(8,128)(2,1)}, bf16[128,960]{1,0:T(8,128)(2,1)S(1)}, u32[]{:S(2)}, u32[]{:S(2)}) collective-permute-start(bf16[128,960]{1,0:T(8,128)(2,1)} %multiply_convert_fusion.2.m_ref.refs_4_), channel_id=1, source_target_pairs={{0,1},{1,0},{2,3},{3,2},{4,5},{5,4},{6,7},{7,6},{8,9},{9,8},{10,11... | collective-permute-start | bytes 737288 | tf_op jit(solution)/shard_map/ppermute | solution.py:249
  172.2 12.0 %collective-permute-start.10 = (bf16[128,960]{1,0:T(8,128)(2,1)}, bf16[128,960]{1,0:T(8,128)(2,1)S(1)}, u32[]{:S(2)}, u32[]{:S(2)}) collective-permute-start(bf16[128,960]{1,0:T(8,128)(2,1)} %fusion.55.refs_4_), channel_id=1, source_target_pairs={{0,1},{1,0},{2,3},{3,2},{4,5},{5,4},{6,7},{7,6},{8,9},{9,8},{10,11... | collective-permute-start | bytes 737288 | tf_op jit(solution)/shard_map/ppermute | solution.py:249
  172.7 11.5 %collective-permute-start.9 = (bf16[128,960]{1,0:T(8,128)(2,1)}, bf16[128,960]{1,0:T(8,128)(2,1)S(1)}, u32[]{:S(2)}, u32[]{:S(2)}) collective-permute-start(bf16[128,960]{1,0:T(8,128)(2,1)} %collective-permute-done.5.refs_5_), channel_id=1, source_target_pairs={{0,1},{1,0},{2,3},{3,2},{4,5},{5,4},{6,7},{7,6},{8,9},{9,8},{10,11... | collective-permute-start | bytes 737288 | tf_op jit(solution)/shard_map/ppermute | solution.py:249
  172.7 11.5 %collective-permute-start.11 = (bf16[128,960]{1,0:T(8,128)(2,1)}, bf16[128,960]{1,0:T(8,128)(2,1)S(1)}, u32[]{:S(2)}, u32[]{:S(2)}) collective-permute-start(bf16[128,960]{1,0:T(8,128)(2,1)} %collective-permute-done.6.refs_5_), channel_id=1, source_target_pairs={{0,1},{1,0},{2,3},{3,2},{4,5},{5,4},{6,7},{7,6},{8,9},{9,8},{10,11... | collective-permute-start | bytes 737288 | tf_op jit(solution)/shard_map/ppermute | solution.py:249
  173.2 11.4 %slice-start = ((s8[5242880]{0:T(1024)(128)(4,1)}), s8[4194304]{0:T(1024)(128)(4,1)S(1)}, s32[]{:S(2)}) async-start(s8[5242880]{0:T(1024)(128)(4,1)} %bitcast.213), calls=%async_computation.1 | async-start | bytes 8388608
  174.3 10.1 %copy-start.56 = (f32[128]{0:T(128)S(1)}, f32[128]{0:T(128)}, u32[]{:S(2)}) copy-start(f32[128]{0:T(128)} %get-tuple-element.193) | copy-start | bytes 1540
  174.3 10.3 %slice-start.1 = ((s8[5242880]{0:T(1024)(128)(4,1)}), s8[1048576]{0:T(1024)(128)(4,1)S(1)}, s32[]{:S(2)}) async-start(s8[5242880]{0:T(1024)(128)(4,1)} %bitcast.213), calls=%async_computation.2 | async-start | bytes 2097152
  188.6 1.7 collective-permute-start.12
  190.3 11.1 %copy-start.5 = (bf16[2,1,128,640]{3,2,1,0:T(8,128)(2,1)}, bf16[2,1,128,640]{3,2,1,0:T(8,128)(2,1)S(1)}, u32[]{:S(2)}) copy-start(bf16[2,1,128,640]{3,2,1,0:T(8,128)(2,1)S(1)} %collective-permute-done.12.refs_3_) | copy-start | bytes 983044
  190.3 10.4 %collective-permute-start.13 = (bf16[128,960]{1,0:T(8,128)(2,1)S(1)}, bf16[128,960]{1,0:T(8,128)(2,1)S(1)}, u32[]{:S(2)}, u32[]{:S(2)}) collective-permute-start(bf16[128,960]{1,0:T(8,128)(2,1)S(1)} %fusion.46), channel_id=1, source_target_pairs={{16,0},{17,1},{18,2},{19,3},{20,4},{21,5},{22,6},{23,7},{24,8},{25... | collective-permute-start | bytes 737288 | tf_op jit(solution)/shard_map/ppermute | solution.py:541
  201.5 9.7 %collective-permute-start.14 = (bf16[128,960]{1,0:T(8,128)(2,1)}, bf16[128,960]{1,0:T(8,128)(2,1)S(1)}, u32[]{:S(2)}, u32[]{:S(2)}) collective-permute-start(bf16[128,960]{1,0:T(8,128)(2,1)} %broadcast_select_fusion.eb_ref.refs_4_), channel_id=1, source_target_pairs={{0,2},{1,3},{2,0},{3,1},{4,6},{5,7},{6,4},{7,5},{8,10},{9,11},{10,... | collective-permute-start | bytes 737288 | tf_op jit(solution)/shard_map/ppermute | solution.py:249
  202.2 8.9 %collective-permute-start.15 = (bf16[128,960]{1,0:T(8,128)(2,1)}, bf16[128,960]{1,0:T(8,128)(2,1)}, u32[]{:S(2)}, u32[]{:S(2)}) collective-permute-start(bf16[128,960]{1,0:T(8,128)(2,1)} %broadcast_select_fusion.eb_ref.refs_4_), channel_id=1, source_target_pairs={{0,1},{1,0},{2,3},{3,2},{4,5},{5,4},{6,7},{7,6},{8,9},{9,8},{10,11... | collective-permute-start | bytes 737288 | tf_op jit(solution)/shard_map/ppermute | solution.py:249
  211.2 2.0 collective-permute-start.16
  211.8 6.1 %copy-start.57 = (f32[128]{0:T(128)S(1)}, f32[128]{0:T(128)}, u32[]{:S(2)}) copy-start(f32[128]{0:T(128)} %get-tuple-element.193) | copy-start | bytes 1540
  211.8 16.7 %collective-permute-start.17 = (bf16[2,2,128,640]{3,2,1,0:T(8,128)(2,1)S(1)}, bf16[2,2,128,640]{3,2,1,0:T(8,128)(2,1)S(1)}, u32[]{:S(2)}, u32[]{:S(2)}) collective-permute-start(bf16[2,2,128,640]{3,2,1,0:T(8,128)(2,1)S(1)} %dynamic-slice_bitcast_fusion), channel_id=1, source_target_pairs={{0,2},{1,3},{2,0},{3,1},{4,6},{5,7},{6,4},{7,5},{8,10},{9,11},{10,... | collective-permute-start | bytes 1966088 | tf_op jit(solution)/shard_map/ppermute | solution.py:249
  216.1 11.8 %collective-permute-start.18 = (bf16[160,960]{1,0:T(8,128)(2,1)S(1)}, bf16[160,960]{1,0:T(8,128)(2,1)S(1)}, u32[]{:S(2)}, u32[]{:S(2)}) collective-permute-start(bf16[160,960]{1,0:T(8,128)(2,1)S(1)} %bitcast.193), channel_id=1, source_target_pairs={{0,4},{1,5},{2,6},{3,7},{4,8},{5,9},{6,10},{7,11},{8,12},{9,13},{1... | collective-permute-start | bytes 921608 | tf_op jit(solution)/shard_map/ppermute | solution.py:288
  219.8 12.9 %copy-start.14 = (bf16[128,960]{1,0:T(8,128)(2,1)S(1)}, bf16[128,960]{1,0:T(8,128)(2,1)}, u32[]{:S(2)}) copy-start(bf16[128,960]{1,0:T(8,128)(2,1)} %copy-done.13) | copy-start | bytes 737284
  219.8 12.9 %copy-start.16 = (bf16[128,960]{1,0:T(8,128)(2,1)S(1)}, bf16[128,960]{1,0:T(8,128)(2,1)}, u32[]{:S(2)}) copy-start(bf16[128,960]{1,0:T(8,128)(2,1)} %copy-done.15) | copy-start | bytes 737284
  227.9 4.9 %copy-start.45 = (bf16[160,960]{1,0:T(8,128)(2,1)}, bf16[160,960]{1,0:T(8,128)(2,1)S(1)}, u32[]{:S(2)}) copy-start(bf16[160,960]{1,0:T(8,128)(2,1)S(1)} %collective-permute-done.18) | copy-start | bytes 921604
  228.7 4.0 %collective-permute-start.19 = (bf16[2,2,128,640]{3,2,1,0:T(8,128)(2,1)S(1)}, bf16[2,2,128,640]{3,2,1,0:T(8,128)(2,1)S(1)}, u32[]{:S(2)}, u32[]{:S(2)}) collective-permute-start(bf16[2,2,128,640]{3,2,1,0:T(8,128)(2,1)S(1)} %pad_maximum_fusion.2), channel_id=1, source_target_pairs={{0,1},{1,0},{2,3},{3,2},{4,5},{5,4},{6,7},{7,6},{8,9},{9,8},{10,11... | collective-permute-start | bytes 1966088 | tf_op jit(solution)/shard_map/ppermute | solution.py:249
  228.8 18.5 %collective-permute-start.20 = (bf16[160,960]{1,0:T(8,128)(2,1)S(1)}, bf16[160,960]{1,0:T(8,128)(2,1)S(1)}, u32[]{:S(2)}, u32[]{:S(2)}) collective-permute-start(bf16[160,960]{1,0:T(8,128)(2,1)S(1)} %bitcast.192), channel_id=1, source_target_pairs={{0,8},{1,9},{2,10},{3,11},{4,12},{5,13},{6,14},{7,15},{8,0},{9,1},... | collective-permute-start | bytes 921608 | tf_op jit(solution)/shard_map/ppermute | solution.py:288
  231.2 5.8 %copy-start.23 = (bf16[5,3,128,128]{2,3,1,0:T(8,128)(2,1)S(1)}, bf16[5,3,128,128]{2,3,1,0:T(8,128)(2,1)}, u32[]{:S(2)}) copy-start(bf16[5,3,128,128]{2,3,1,0:T(8,128)(2,1)} %copy-done.21) | copy-start | bytes 1474564
  231.2 6.1 %copy-start.19 = (f32[5,3,128,128]{2,3,1,0:T(8,128)S(1)}, f32[5,3,128,128]{2,3,1,0:T(8,128)}, u32[]{:S(2)}) copy-start(f32[5,3,128,128]{2,3,1,0:T(8,128)} %copy-done.17) | copy-start | bytes 2949124
  231.2 16.1 %collective-permute-start.21 = (bf16[160,960]{1,0:T(8,128)(2,1)S(1)}, bf16[160,960]{1,0:T(8,128)(2,1)S(1)}, u32[]{:S(2)}, u32[]{:S(2)}) collective-permute-start(bf16[160,960]{1,0:T(8,128)(2,1)S(1)} %bitcast.191), channel_id=1, source_target_pairs={{0,12},{1,13},{2,14},{3,15},{4,0},{5,1},{6,2},{7,3},{8,4},{9,5},{1... | collective-permute-start | bytes 921608 | tf_op jit(solution)/shard_map/ppermute | solution.py:288
  238.8 8.5 %copy-start.30 = (bf16[5,64,3,128]{3,1,2,0:T(8,128)(2,1)S(1)}, bf16[5,64,3,128]{3,1,2,0:T(8,128)(2,1)}, u32[]{:S(2)}) copy-start(bf16[5,64,3,128]{3,1,2,0:T(8,128)(2,1)} %copy-done.29) | copy-start | bytes 737284
  239.1 25.3 %collective-permute-start.23 = (bf16[128,960]{1,0:T(8,128)(2,1)S(1)}, bf16[128,960]{1,0:T(8,128)(2,1)}, u32[]{:S(2)}, u32[]{:S(2)}) collective-permute-start(bf16[128,960]{1,0:T(8,128)(2,1)S(1)} %get-tuple-element.136.refs_8_), channel_id=1, source_target_pairs={{0,2},{1,3},{2,0},{3,1},{4,6},{5,7},{6,4},{7,5},{8,10},{9,11},{10,... | collective-permute-start | bytes 737288 | tf_op jit(solution)/shard_map/ppermute | solution.py:249
  240.4 24.0 %collective-permute-start.24 = (bf16[128,960]{1,0:T(8,128)(2,1)S(1)}, bf16[128,960]{1,0:T(8,128)(2,1)}, u32[]{:S(2)}, u32[]{:S(2)}) collective-permute-start(bf16[128,960]{1,0:T(8,128)(2,1)S(1)} %get-tuple-element.136.refs_8_), channel_id=1, source_target_pairs={{0,1},{1,0},{2,3},{3,2},{4,5},{5,4},{6,7},{7,6},{8,9},{9,8},{10,11... | collective-permute-start | bytes 737288 | tf_op jit(solution)/shard_map/ppermute | solution.py:249
  240.6 16.2 %copy-start.26 = (bf16[128,960]{1,0:T(8,128)(2,1)S(1)}, bf16[128,960]{1,0:T(8,128)(2,1)}, u32[]{:S(2)}) copy-start(bf16[128,960]{1,0:T(8,128)(2,1)} %copy-done.24) | copy-start | bytes 737284
  240.6 16.2 %copy-start.53 = (f32[128]{0:T(128)S(1)}, f32[128]{0:T(128)}, u32[]{:S(2)}) copy-start(f32[128]{0:T(128)} %copy-done.52) | copy-start | bytes 1540
  247.3 7.3 %copy-start.47 = (bf16[160,960]{1,0:T(8,128)(2,1)}, bf16[160,960]{1,0:T(8,128)(2,1)S(1)}, u32[]{:S(2)}) copy-start(bf16[160,960]{1,0:T(8,128)(2,1)S(1)} %collective-permute-done.20) | copy-start | bytes 921604
  247.3 7.3 %copy-start.49 = (bf16[160,960]{1,0:T(8,128)(2,1)}, bf16[160,960]{1,0:T(8,128)(2,1)S(1)}, u32[]{:S(2)}) copy-start(bf16[160,960]{1,0:T(8,128)(2,1)S(1)} %collective-permute-done.21) | copy-start | bytes 921604
  247.4 7.2 %copy-start.28 = (bf16[4,128,4,160]{1,3,2,0:T(8,128)(2,1)}, bf16[4,128,4,160]{1,3,2,0:T(8,128)(2,1)S(1)}, u32[]{:S(2)}) copy-start(bf16[4,128,4,160]{1,3,2,0:T(8,128)(2,1)S(1)} %copy.38) | copy-start | bytes 1966084
  247.4 25.8 %collective-permute-start.25 = (bf16[320,960]{1,0:T(8,128)(2,1)}, bf16[320,960]{1,0:T(8,128)(2,1)}, u32[]{:S(2)}, u32[]{:S(2)}) collective-permute-start(bf16[320,960]{1,0:T(8,128)(2,1)} %bitcast.86), channel_id=1, source_target_pairs={{0,4},{1,5},{2,6},{3,7},{4,8},{5,9},{6,10},{7,11},{8,12},{9,13},{1... | collective-permute-start | bytes 1843208 | tf_op jit(solution)/shard_map/ppermute | solution.py:288
  255.6 9.4 %collective-permute-start.22 = (bf16[2,1,128,640]{3,2,1,0:T(8,128)(2,1)}, bf16[2,1,128,640]{3,2,1,0:T(8,128)(2,1)S(1)}, u32[]{:S(2)}, u32[]{:S(2)}) collective-permute-start(bf16[2,1,128,640]{3,2,1,0:T(8,128)(2,1)} %bitcast.242), channel_id=1, source_target_pairs={{0,2},{1,3},{2,0},{3,1},{4,6},{5,7},{6,4},{7,5},{8,10},{9,11},{10,... | collective-permute-start | bytes 983048 | tf_op jit(solution)/shard_map/ppermute | solution.py:249
  261.6 39.2 %collective-permute-start.30 = (bf16[320,960]{1,0:T(8,128)(2,1)}, bf16[320,960]{1,0:T(8,128)(2,1)}, u32[]{:S(2)}, u32[]{:S(2)}) collective-permute-start(bf16[320,960]{1,0:T(8,128)(2,1)} %bitcast.190), channel_id=1, source_target_pairs={{0,8},{1,9},{2,10},{3,11},{4,12},{5,13},{6,14},{7,15},{8,0},{9,1},... | collective-permute-start | bytes 1843208 | tf_op jit(solution)/shard_map/ppermute | solution.py:288
  274.1 26.7 %collective-permute-start.29 = (bf16[2,1,128,640]{3,2,1,0:T(8,128)(2,1)}, bf16[2,1,128,640]{3,2,1,0:T(8,128)(2,1)}, u32[]{:S(2)}, u32[]{:S(2)}) collective-permute-start(bf16[2,1,128,640]{3,2,1,0:T(8,128)(2,1)} %pad_maximum_fusion.6), channel_id=1, source_target_pairs={{0,1},{1,0},{2,3},{3,2},{4,5},{5,4},{6,7},{7,6},{8,9},{9,8},{10,11... | collective-permute-start | bytes 983048 | tf_op jit(solution)/shard_map/ppermute | solution.py:249
  274.1 26.7 %collective-permute-start.28 = (bf16[128,960]{1,0:T(8,128)(2,1)}, bf16[128,960]{1,0:T(8,128)(2,1)}, u32[]{:S(2)}, u32[]{:S(2)}) collective-permute-start(bf16[128,960]{1,0:T(8,128)(2,1)} %collective-permute-done.23.refs_9_), channel_id=1, source_target_pairs={{0,1},{1,0},{2,3},{3,2},{4,5},{5,4},{6,7},{7,6},{8,9},{9,8},{10,11... | collective-permute-start | bytes 737288 | tf_op jit(solution)/shard_map/ppermute | solution.py:249
  274.6 1.5 collective-permute-start.26
  276.1 3.7 %collective-permute-start.27 = (f32[1920]{0:T(1024)S(1)}, f32[1920]{0:T(1024)S(1)}, u32[]{:S(2)}, u32[]{:S(2)}) collective-permute-start(f32[1920]{0:T(1024)S(1)} %add.236), channel_id=1, source_target_pairs={{0,2},{1,3},{2,0},{3,1},{4,6},{5,7},{6,4},{7,5},{8,10},{9,11},{10,... | collective-permute-start | bytes 23048 | tf_op jit(solution)/shard_map/ppermute | solution.py:249
  276.8 41.6 %collective-permute-start.32 = (bf16[320,960]{1,0:T(8,128)(2,1)}, bf16[320,960]{1,0:T(8,128)(2,1)}, u32[]{:S(2)}, u32[]{:S(2)}) collective-permute-start(bf16[320,960]{1,0:T(8,128)(2,1)} %bitcast.189), channel_id=1, source_target_pairs={{0,12},{1,13},{2,14},{3,15},{4,0},{5,1},{6,2},{7,3},{8,4},{9,5},{1... | collective-permute-start | bytes 1843208 | tf_op jit(solution)/shard_map/ppermute | solution.py:288
  302.8 14.4 %copy-start.4 = (f32[128,960]{1,0:T(8,128)S(1)}, f32[128,960]{1,0:T(8,128)}, u32[]{:S(2)}) copy-start(f32[128,960]{1,0:T(8,128)} %copy-done.3) | copy-start | bytes 1474564
  302.8 14.4 %copy-start.27 = (bf16[128,960]{1,0:T(8,128)(2,1)S(1)}, bf16[128,960]{1,0:T(8,128)(2,1)}, u32[]{:S(2)}) copy-start(bf16[128,960]{1,0:T(8,128)(2,1)} %copy-done.24) | copy-start | bytes 737284
  302.8 14.4 %copy-start.31 = (f32[128,960]{1,0:T(8,128)S(1)}, f32[128,960]{1,0:T(8,128)}, u32[]{:S(2)}) copy-start(f32[128,960]{1,0:T(8,128)} %get-tuple-element.159) | copy-start | bytes 1474564
  302.8 14.4 %copy-start.38 = (f32[128,960]{1,0:T(8,128)S(1)}, f32[128,960]{1,0:T(8,128)}, u32[]{:S(2)}) copy-start(f32[128,960]{1,0:T(8,128)} %get-tuple-element.209) | copy-start | bytes 1474564
  302.8 14.4 %copy-start.55 = (f32[128]{0:T(128)S(1)}, f32[128]{0:T(128)}, u32[]{:S(2)}) copy-start(f32[128]{0:T(128)} %copy-done.54) | copy-start | bytes 1540
  306.5 11.7 %copy-start.46 = (bf16[160,960]{1,0:T(8,128)(2,1)S(1)}, bf16[160,960]{1,0:T(8,128)(2,1)}, u32[]{:S(2)}) copy-start(bf16[160,960]{1,0:T(8,128)(2,1)} %copy-done.45) | copy-start | bytes 921604
  306.5 11.7 %copy-start.48 = (bf16[160,960]{1,0:T(8,128)(2,1)S(1)}, bf16[160,960]{1,0:T(8,128)(2,1)}, u32[]{:S(2)}) copy-start(bf16[160,960]{1,0:T(8,128)(2,1)} %copy-done.47) | copy-start | bytes 921604
  306.5 11.7 %copy-start.50 = (bf16[160,960]{1,0:T(8,128)(2,1)S(1)}, bf16[160,960]{1,0:T(8,128)(2,1)}, u32[]{:S(2)}) copy-start(bf16[160,960]{1,0:T(8,128)(2,1)} %copy-done.49) | copy-start | bytes 921604
  306.5 25.6 %collective-permute-start.31 = (bf16[2,168,960]{2,1,0:T(8,128)(2,1)S(1)}, bf16[2,168,960]{2,1,0:T(8,128)(2,1)S(1)}, u32[]{:S(2)}, u32[]{:S(2)}) collective-permute-start(bf16[2,168,960]{2,1,0:T(8,128)(2,1)S(1)} %get-tuple-element.142), channel_id=1, source_target_pairs={{0,4},{1,5},{2,6},{3,7},{4,0},{5,1},{6,2},{7,3},{8,12},{9,13},{10,... | collective-permute-start | bytes 1935368 | tf_op jit(solution)/shard_map/ppermute | solution.py:249
  332.3 17.7 %collective-permute-start.33 = (bf16[168,960]{1,0:T(8,128)(2,1)S(1)}, bf16[168,960]{1,0:T(8,128)(2,1)S(1)}, u32[]{:S(2)}, u32[]{:S(2)}) collective-permute-start(bf16[168,960]{1,0:T(8,128)(2,1)S(1)} %fusion.67), channel_id=1, source_target_pairs={{0,8},{1,9},{2,10},{3,11},{4,12},{5,13},{6,14},{7,15},{8,0},{9,1},... | collective-permute-start | bytes 967688 | tf_op jit(solution)/shard_map/ppermute | solution.py:249
  (32 other events, 42.3 us)
Sparse Core Ops, SparseCore 0:
  10.2 111.5 all-gather.1

commit v9 on v8

--- a/solution.py
+++ b/solution.py
@@ -461,23 +461,23 @@
     dh1, dz, do, gain_two_grad = backward_mid(e, dm, state, weights)
     do, dz, both_y, down_one = tie((do, dz, both_y, down_one))
     both_c = cols_core(both, both_y, y, core)
+    both_c, down_two = tie((both_c, down_two))
     both_own, *both_sends = plane_product(both, both_y, both_c, [m_all], direct, ones)
     do, dz, both_sends = tie((do, dz, both_sends))
     both_one, both_two, both_three = direct_send(both_sends)
     dproj = backward_attention(do, state, tables)
-    dproj, down_two, down_three = tie((dproj, down_two, down_three))
+    dproj, down_three = tie((dproj, down_three))
     attn_cols = jnp.concatenate([dproj, o], axis=1).reshape(tokens, 4, 4, share)
     attn_cols = attn_cols.transpose(2, 0, 1, 3).reshape(4, 1, tokens, 4 * share)
     attn_y = cols_y(attn_cols, y)
     dz_y, dz_c = flip(dz, Y_BIT), flip(dz, CORE_BIT)
     du, gain_one_grad = backward_in(dproj, dh1, state, weights)
     gain_grad = jnp.concatenate([gain_one_grad, gain_two_grad])
-    gain_grad, attn_y, dz_y, dz_c, both_one = tie((gain_grad, attn_y, dz_y, dz_c, both_one))
     gain_grad = gain_grad + flip(gain_grad, CORE_BIT)
     gain_grad = gain_grad + flip(gain_grad, Y_BIT)
     dz_all = (dz, dz_y, dz_c, flip(dz_y, CORE_BIT))
     attn_c = cols_core(attn_cols, attn_y, y, core)
-    gain_grad, dz_all, attn_c, both_two = tie((gain_grad, dz_all, attn_c, both_two))
+    gain_grad, dz_all, attn_c, both_one = tie((gain_grad, dz_all, attn_c, both_one))
     gain_rows = at(gain_grad.reshape(4, 4, -1).transpose(1, 0, 2), y * 2 + core)[:, None]
     gain_share = gain_rows.shape[-1]
     gain_rows = jnp.pad(gain_rows, ((0, 0), (0, EXTRA_ROWS - 1), (0, width - gain_share)))
@@ -494,7 +494,9 @@
         gain_rows,
     )
     attn_received = flip(attn_send, Z1_BIT)
-    attn_own, attn_received, both_three = tie((attn_own, attn_received, both_three))
+    attn_own, attn_received, both_two, both_three = tie(
+        (attn_own, attn_received, both_two, both_three)
+    )
     attn = pair_second(attn_own, attn_received, z2)
     down = direct_total(down_own[0], (down_one, down_two, down_three))
     both = direct_total(both_own[0], (both_one, both_two, both_three))

time: 359 us -> 368 us (1.025)
  local copies, waits for them, and re-layouts: 14.9 us -> 21.6 us
    unnamed x122 -> x148, local copies, waits for them, and re-layouts: 3.98 us -> 11.6 us
    ppermute x6, starting transfers between devices: 17.4 us -> 22.4 us  [z_pairs(): lax.ppermute(x, 'dp', [(4 * a + i, 4 * b + i) for a, b in pairs for i in...]
  transfers between devices with their start and end apart: 35 -> 35, of which waited for: 19 -> 19; matrix products, arithmetic and copies ran while one was open for 6% -> 5% of each run, Pallas kernels for 10% -> 10%
where the time goes in v9:
time: 368 us; the launch traced here: 367 us
  waiting for transfers between devices  190 us (52%)
  starting transfers between devices  58.7 us (16%)
  Pallas kernels  47.2 us (13%)
  local copies, waits for them, and re-layouts  21.6 us (6%)
  matrix products  17.9 us (5%)
  other arithmetic  16.5 us (4%)
  between operations  15.4 us (4%)
    all_gather x1, waiting for transfers between devices, local(): lax.all_gather(own, 'dp', axis=0, tiled=True).reshape(4, 4, 4, share, width)  97.4 us
    ppermute x26, waiting for transfers between devices, flip(): return lax.ppermute(x, 'dp', [(i, i ^ bit) for i in range(size)])  39 us
    ppermute x6, waiting for transfers between devices, z_pairs(): lax.ppermute(x, 'dp', [(4 * a + i, 4 * b + i) for a, b in pairs for i in...  38.6 us
    pallas_call x4, Pallas kernels, ffn_call(): pl.pallas_call(kernel, grid=(steps,), in_specs=[whole] * len(wholes) + [b...  36.6 us
    ppermute x26, starting transfers between devices, flip(): return lax.ppermute(x, 'dp', [(i, i ^ bit) for i in range(size)])  31.3 us
    ppermute x6, starting transfers between devices, z_pairs(): lax.ppermute(x, 'dp', [(4 * a + i, 4 * b + i) for a, b in pairs for i in...  22.4 us
    unnamed x148, local copies, waits for them, and re-layouts  11.6 us
    pallas_call x3, Pallas kernels, plane_product(): pl.pallas_call(kernel, grid_spec=pltpu.PrefetchScalarGridSpec(num_scalar_...  10.6 us
  transfers between devices with their start and end apart: 35, of which 19 were waited for; matrix products, arithmetic and copies ran while one was open for 5% of the time, Pallas kernels for 10%

profile of v9, /device:TPU:0, one launch (start us, length us, event | category | flops | bytes accessed | tf_op | source)
XLA Modules:
  0.0 367.0 jit_solution(1394567849132804417)
XLA Ops:
  7.2 2.5 pad_maximum_fusion.1
  11.2 2.8 collective-permute-start.1
  14.2 1.4 collective-permute-done.1
  15.7 2.1 collective-permute-start.2
  17.9 1.4 collective-permute-done.2
  19.5 3.0 collective-permute-start.3
  22.8 1.3 collective-permute-done.3
  24.4 97.4 %all-gather.2.cloned.1.call-done = bf16[10240,960]{1,0:T(8,128)(2,1)} async-done(((bf16[640,960]{1,0:T(8,128)(2,1)}), bf16[10240,960]{1,0:T(8,128)(2,1)}) %all-gather.2.cloned.1.call-update) | async-done | bytes 19660816 | tf_op jit(solution)/shard_map/all_gather | solution.py:524
  121.8 3.4 slice.119
  125.2 1.1 fusion.6
  128.2 9.6 %shard_map.84 = (f32[4,128,640]{2,1,0:T(8,128)}, f32[4,128,640]{2,1,0:T(8,128)}, bf16[4,128,640]{2,1,0:T(8,128)(2,1)}, f32[128,960]{1,0:T(8,128)S(1)}) custom-call(bf16[128,960]{1,0:T(8,128)(2,1)S(1)} %multiply_convert_fusion.3.m_ref, f32[128,960]{1,0:T(8,128)S(1)} %get-tuple-element.192.h1_ref, bf16[4,4,4,160,960]{4,3,2,1,0:T(8,128)(2,1)} %bitcast.194, ...), custom_call_target="tpu_custom_call" | custom-call | flops 1887436800 | bytes 14745600 | tf_op jit(solution)/shard_map/pallas_call | solution.py:206
  137.9 3.6 collective-permute-start.4
  141.5 5.8 %collective-permute-done.4 = bf16[128,960]{1,0:T(8,128)(2,1)S(1)} collective-permute-done((bf16[128,960]{1,0:T(8,128)(2,1)S(1)}, bf16[128,960]{1,0:T(8,128)(2,1)S(1)}, u32[]{:S(2)}, u32[]{:S(2)}) %collective-permute-start.4) | collective-permute-done | bytes 245792 | tf_op jit(solution)/shard_map/ppermute | solution.py:539
  147.4 0.8 fusion.55.refs_4_
  148.3 3.0 fusion.4
  153.4 2.2 multiply_reduce_fusion.5
  156.0 0.8 multiply_convert_fusion.2.m_ref.refs_4_
  156.9 1.2 collective-permute-start.5
  158.9 8.3 %shard_map.85 = (f32[4,128,640]{2,1,0:T(8,128)S(1)}, f32[4,128,640]{2,1,0:T(8,128)S(1)}, bf16[4,128,640]{2,1,0:T(8,128)(2,1)S(1)}, f32[128,960]{1,0:T(8,128)S(1)}) custom-call(bf16[128,960]{1,0:T(8,128)(2,1)} %multiply_convert_fusion.2.m_ref.refs_4_, f32[128,960]{1,0:T(8,128)S(1)} %get-tuple-element.196.h1_ref, bf16[4,4,4,160,960]{4,3,2,1,0:T(8,128)(2,1)} %bitcast.197, ...), custom_call_target="tpu_custom_call" | custom-call | flops 1887436800 | bytes 14745600 | tf_op jit(solution)/shard_map/pallas_call | solution.py:206
  167.2 3.2 collective-permute-done.6.refs_5_
  171.2 1.2 collective-permute-start.7
  173.5 1.1 dynamic-slice_bitcast_fusion.2
  174.6 9.9 %shard_map.86 = (bf16[4,2,128,640]{3,2,1,0:T(8,128)(2,1)}, f32[128,960]{1,0:T(8,128)S(1)}) custom-call(bf16[128,960]{1,0:T(8,128)(2,1)S(1)} %bitcast.185, f32[4,128,640]{2,1,0:T(8,128)S(1)} %get-tuple-element.81.gate_ref, f32[4,128,640]{2,1,0:T(8,128)S(1)} %get-tuple-element.82.up_ref, bf16[4,4,4,160,960]{4,3,2,1,0:T(8,128)(2,1)} %bitcast.200, ...), custom_call_target="tpu_custom_call" | custom-call | flops 1887436800 | bytes 14745600 | tf_op jit(solution)/shard_map/pallas_call | solution.py:206
  188.0 0.9 constant_dynamic-slice_fusion.6
  190.7 1.3 collective-permute-start.13
  191.9 9.1 %collective-permute-done.13 = bf16[128,960]{1,0:T(8,128)(2,1)S(1)} collective-permute-done((bf16[128,960]{1,0:T(8,128)(2,1)S(1)}, bf16[128,960]{1,0:T(8,128)(2,1)S(1)}, u32[]{:S(2)}, u32[]{:S(2)}) %collective-permute-start.13) | collective-permute-done | bytes 245792 | tf_op jit(solution)/shard_map/ppermute | solution.py:543
  201.8 0.8 collective-permute-start.14
  202.7 8.8 %shard_map.87 = (bf16[4,2,128,640]{3,2,1,0:T(8,128)(2,1)S(1)}, f32[128,960]{1,0:T(8,128)S(1)}) custom-call(bf16[128,960]{1,0:T(8,128)(2,1)} %broadcast_select_fusion.eb_ref.refs_4_, f32[4,128,640]{2,1,0:T(8,128)S(1)} %get-tuple-element.81.gate_ref, f32[4,128,640]{2,1,0:T(8,128)S(1)} %get-tuple-element.82.up_ref, bf16[4,4,4,160,960]{4,3,2,1,0:T(8,128)(2,1)} %bitcast.203, ...), custom_call_target="tpu_custom_call" | custom-call | flops 1887436800 | bytes 14745600 | tf_op jit(solution)/shard_map/pallas_call | solution.py:206
  212.2 1.3 collective-permute-start.17
  213.5 2.8 shard_map.88
  216.5 1.8 collective-permute-start.18
  218.3 2.1 fusion.87
  220.4 2.4 fusion.33
  222.7 5.7 %collective-permute-done.18 = bf16[160,960]{1,0:T(8,128)(2,1)S(1)} collective-permute-done((bf16[160,960]{1,0:T(8,128)(2,1)S(1)}, bf16[160,960]{1,0:T(8,128)(2,1)S(1)}, u32[]{:S(2)}, u32[]{:S(2)}) %collective-permute-start.18) | collective-permute-done | bytes 307232 | tf_op jit(solution)/shard_map/ppermute | solution.py:288
  229.4 2.1 collective-permute-start.20
  231.6 1.5 collective-permute-start.21
  233.0 14.9 %collective-permute-done.20 = bf16[160,960]{1,0:T(8,128)(2,1)S(1)} collective-permute-done((bf16[160,960]{1,0:T(8,128)(2,1)S(1)}, bf16[160,960]{1,0:T(8,128)(2,1)S(1)}, u32[]{:S(2)}, u32[]{:S(2)}) %collective-permute-start.20) | collective-permute-done | bytes 307232 | tf_op jit(solution)/shard_map/ppermute | solution.py:288
  248.7 4.4 %shard_map.89 = (f32[1,320,960]{2,1,0:T(8,128)S(1)}, bf16[1,320,960]{2,1,0:T(8,128)(2,1)S(1)}, bf16[1,320,960]{2,1,0:T(8,128)(2,1)}, bf16[1,320,960]{2,1,0:T(8,128)(2,1)}) custom-call(s32[7]{0:T(128)S(1)} %stack.73.refs_0_, bf16[4,2,128,640]{3,2,1,0:T(8,128)(2,1)S(1)} %get-tuple-element.104.refs_1_, ...), custom_call_target="tpu_custom_call" | custom-call | flops 1258291200 | bytes 7208960 | tf_op jit(solution)/shard_map/pallas_call | solution.py:374
  256.6 0.9 copy.40
  257.5 1.3 collective-permute-start.22
  259.5 3.4 fusion.59
  263.3 6.7 %collective-permute-start.29 = (bf16[320,960]{1,0:T(8,128)(2,1)S(1)}, bf16[320,960]{1,0:T(8,128)(2,1)}, u32[]{:S(2)}, u32[]{:S(2)}) collective-permute-start(bf16[320,960]{1,0:T(8,128)(2,1)S(1)} %bitcast.189), channel_id=1, source_target_pairs={{0,4},{1,5},{2,6},{3,7},{4,8},{5,9},{6,10},{7,11},{8,12},{9,13},{1... | collective-permute-start | bytes 1843208 | tf_op jit(solution)/shard_map/ppermute | solution.py:288
  270.0 2.1 collective-permute-done.25.refs_9_
  272.9 1.3 collective-permute-done.23
  274.3 1.3 collective-permute-start.24
  275.6 2.3 collective-permute-done.24
  277.9 1.3 collective-permute-start.31
  280.0 8.9 %collective-permute-start.32 = (bf16[320,960]{1,0:T(8,128)(2,1)}, bf16[320,960]{1,0:T(8,128)(2,1)}, u32[]{:S(2)}, u32[]{:S(2)}) collective-permute-start(bf16[320,960]{1,0:T(8,128)(2,1)} %bitcast.88), channel_id=1, source_target_pairs={{0,12},{1,13},{2,14},{3,15},{4,0},{5,1},{6,2},{7,3},{8,4},{9,5},{1... | collective-permute-start | bytes 1843208 | tf_op jit(solution)/shard_map/ppermute | solution.py:288
  289.8 1.1 copy-done.6
  290.9 1.0 copy-done.14
  291.9 0.9 copy-done.18
  292.8 0.9 copy-done.24
  293.8 0.9 copy-done.26
  294.7 0.9 copy-done.28
  295.7 3.4 shard_map.90
  299.8 1.0 fusion.50
  301.0 15.6 %collective-permute-done.31 = bf16[320,960]{1,0:T(8,128)(2,1)} collective-permute-done((bf16[320,960]{1,0:T(8,128)(2,1)}, bf16[320,960]{1,0:T(8,128)(2,1)}, u32[]{:S(2)}, u32[]{:S(2)}) %collective-permute-start.31) | collective-permute-done | bytes 614432 | tf_op jit(solution)/shard_map/ppermute | solution.py:288
  316.6 2.4 collective-permute-done.32
  318.9 13.1 %collective-permute-done.30 = bf16[2,168,960]{2,1,0:T(8,128)(2,1)S(1)} collective-permute-done((bf16[2,168,960]{2,1,0:T(8,128)(2,1)S(1)}, bf16[2,168,960]{2,1,0:T(8,128)(2,1)S(1)}, u32[]{:S(2)}, u32[]{:S(2)}) %collective-permute-start.30) | collective-permute-done | bytes 645152 | tf_op jit(solution)/shard_map/ppermute | solution.py:249
  332.4 11.3 %collective-permute-start.33 = (bf16[168,960]{1,0:T(8,128)(2,1)S(1)}, bf16[168,960]{1,0:T(8,128)(2,1)S(1)}, u32[]{:S(2)}, u32[]{:S(2)}) collective-permute-start(bf16[168,960]{1,0:T(8,128)(2,1)S(1)} %fusion.67), channel_id=1, source_target_pairs={{0,8},{1,9},{2,10},{3,11},{4,12},{5,13},{6,14},{7,15},{8,0},{9,1},... | collective-permute-start | bytes 967688 | tf_op jit(solution)/shard_map/ppermute | solution.py:249
  343.7 1.9 bitcast_add_fusion
  345.6 1.4 pad_maximum_fusion
  347.0 11.6 %collective-permute-done.33 = bf16[168,960]{1,0:T(8,128)(2,1)S(1)} collective-permute-done((bf16[168,960]{1,0:T(8,128)(2,1)S(1)}, bf16[168,960]{1,0:T(8,128)(2,1)S(1)}, u32[]{:S(2)}, u32[]{:S(2)}) %collective-permute-start.33) | collective-permute-done | bytes 322592 | tf_op jit(solution)/shard_map/ppermute | solution.py:249
  358.7 0.9 slice_bitcast_fusion
  (285 shorter events, 26.5 us)
Async XLA Ops:
  7.2 114.6 %all-gather.2.cloned.1.call-start = ((), (), s32[]{:S(2)}) async-start(), calls=%async_computation | async-start | bytes 22282240 | tf_op jit(solution)/shard_map/all_gather | solution.py:524
  7.2 10.5 %copy-start = (bf16[1,2,64,960]{3,2,1,0:T(8,128)(2,1)S(1)}, bf16[1,2,64,960]{3,2,1,0:T(8,128)(2,1)}, u32[]{:S(2)}) copy-start(bf16[1,2,64,960]{3,2,1,0:T(8,128)(2,1)} %param.5) | copy-start | bytes 737284
  9.8 1.3 collective-permute-start
  11.2 4.3 %collective-permute-start.1 = (bf16[240]{0:T(256)(128)(2,1)S(1)}, bf16[240]{0:T(256)(128)(2,1)S(1)}, u32[]{:S(2)}, u32[]{:S(2)}) collective-permute-start(bf16[240]{0:T(256)(128)(2,1)S(1)} %pad_maximum_fusion.18), channel_id=1, source_target_pairs={{0,2},{1,3},{2,0},{3,1},{4,6},{5,7},{6,4},{7,5},{8,10},{9,11},{10,... | collective-permute-start | bytes 1448 | tf_op jit(solution)/shard_map/ppermute | solution.py:249
  15.7 3.6 collective-permute-start.2
  19.5 4.7 %collective-permute-start.3 = (bf16[960]{0:T(1024)(128)(2,1)S(1)}, bf16[960]{0:T(1024)(128)(2,1)S(1)}, u32[]{:S(2)}, u32[]{:S(2)}) collective-permute-start(bf16[960]{0:T(1024)(128)(2,1)S(1)} %pad_maximum_fusion.16), channel_id=1, source_target_pairs={{0,8},{1,9},{2,10},{3,11},{4,12},{5,13},{6,14},{7,15},{8,0},{9,1},... | collective-permute-start | bytes 5768 | tf_op jit(solution)/shard_map/ppermute | solution.py:249
  22.8 103.6 %copy-start.62 = (pred[128,128]{0,1:T(8,128)(4,1)}, pred[128,128]{0,1:T(8,128)(4,1)S(1)}, u32[]{:S(2)}) copy-start(pred[128,128]{0,1:T(8,128)(4,1)S(1)} %copy.24) | copy-start | bytes 49156
  137.9 9.4 %collective-permute-start.4 = (bf16[128,960]{1,0:T(8,128)(2,1)S(1)}, bf16[128,960]{1,0:T(8,128)(2,1)S(1)}, u32[]{:S(2)}, u32[]{:S(2)}) collective-permute-start(bf16[128,960]{1,0:T(8,128)(2,1)S(1)} %convert_element_type.150), channel_id=1, source_target_pairs={{0,16},{1,17},{2,18},{3,19},{4,20},{5,21},{6,22},{7,23},{8,24},{9,... | collective-permute-start | bytes 737288 | tf_op jit(solution)/shard_map/ppermute | solution.py:539
  147.4 5.9 %copy-start.36 = (bf16[128,960]{1,0:T(8,128)(2,1)}, bf16[128,960]{1,0:T(8,128)(2,1)S(1)}, u32[]{:S(2)}) copy-start(bf16[128,960]{1,0:T(8,128)(2,1)S(1)} %get-tuple-element.155) | copy-start | bytes 737284
  147.4 42.4 %copy-start.65 = (f32[128]{0:T(128)}, f32[128]{0:T(128)S(1)}, u32[]{:S(2)}) copy-start(f32[128]{0:T(128)S(1)} %get-tuple-element.186) | copy-start | bytes 1540
  147.4 42.4 %copy-start.67 = (f32[128]{0:T(128)}, f32[128]{0:T(128)S(1)}, u32[]{:S(2)}) copy-start(f32[128]{0:T(128)S(1)} %get-tuple-element.185) | copy-start | bytes 1540
  152.8 4.1 %copy-start.33 = (bf16[5,3,128,128]{2,3,1,0:T(8,128)(2,1)}, bf16[5,3,128,128]{2,3,1,0:T(8,128)(2,1)S(1)}, u32[]{:S(2)}) copy-start(bf16[5,3,128,128]{2,3,1,0:T(8,128)(2,1)S(1)} %fusion.60) | copy-start | bytes 1474564
  153.4 5.5 %copy-start.40 = (bf16[5,64,3,128]{3,1,2,0:T(8,128)(2,1)}, bf16[5,64,3,128]{3,1,2,0:T(8,128)(2,1)S(1)}, u32[]{:S(2)}) copy-start(bf16[5,64,3,128]{3,1,2,0:T(8,128)(2,1)S(1)} %convolution_convert_fusion) | copy-start | bytes 737284
  156.9 10.4 %collective-permute-start.5 = (bf16[128,960]{1,0:T(8,128)(2,1)}, bf16[128,960]{1,0:T(8,128)(2,1)}, u32[]{:S(2)}, u32[]{:S(2)}) collective-permute-start(bf16[128,960]{1,0:T(8,128)(2,1)} %multiply_convert_fusion.2.m_ref.refs_4_), channel_id=1, source_target_pairs={{0,2},{1,3},{2,0},{3,1},{4,6},{5,7},{6,4},{7,5},{8,10},{9,11},{10,... | collective-permute-start | bytes 737288 | tf_op jit(solution)/shard_map/ppermute | solution.py:249
  158.1 12.3 %collective-permute-start.6 = (bf16[128,960]{1,0:T(8,128)(2,1)}, bf16[128,960]{1,0:T(8,128)(2,1)}, u32[]{:S(2)}, u32[]{:S(2)}) collective-permute-start(bf16[128,960]{1,0:T(8,128)(2,1)} %fusion.55.refs_4_), channel_id=1, source_target_pairs={{0,2},{1,3},{2,0},{3,1},{4,6},{5,7},{6,4},{7,5},{8,10},{9,11},{10,... | collective-permute-start | bytes 737288 | tf_op jit(solution)/shard_map/ppermute | solution.py:249
  171.2 13.3 %collective-permute-start.7 = (bf16[2,1,128,640]{3,2,1,0:T(8,128)(2,1)}, bf16[2,1,128,640]{3,2,1,0:T(8,128)(2,1)}, u32[]{:S(2)}, u32[]{:S(2)}) collective-permute-start(bf16[2,1,128,640]{3,2,1,0:T(8,128)(2,1)} %dynamic-slice_bitcast_fusion.1), channel_id=1, source_target_pairs={{0,2},{1,3},{2,0},{3,1},{4,6},{5,7},{6,4},{7,5},{8,10},{9,11},{10,... | collective-permute-start | bytes 983048 | tf_op jit(solution)/shard_map/ppermute | solution.py:249
  172.5 12.0 %collective-permute-start.8 = (bf16[128,960]{1,0:T(8,128)(2,1)}, bf16[128,960]{1,0:T(8,128)(2,1)S(1)}, u32[]{:S(2)}, u32[]{:S(2)}) collective-permute-start(bf16[128,960]{1,0:T(8,128)(2,1)} %multiply_convert_fusion.2.m_ref.refs_4_), channel_id=1, source_target_pairs={{0,1},{1,0},{2,3},{3,2},{4,5},{5,4},{6,7},{7,6},{8,9},{9,8},{10,11... | collective-permute-start | bytes 737288 | tf_op jit(solution)/shard_map/ppermute | solution.py:249
  172.5 12.0 %collective-permute-start.10 = (bf16[128,960]{1,0:T(8,128)(2,1)}, bf16[128,960]{1,0:T(8,128)(2,1)S(1)}, u32[]{:S(2)}, u32[]{:S(2)}) collective-permute-start(bf16[128,960]{1,0:T(8,128)(2,1)} %fusion.55.refs_4_), channel_id=1, source_target_pairs={{0,1},{1,0},{2,3},{3,2},{4,5},{5,4},{6,7},{7,6},{8,9},{9,8},{10,11... | collective-permute-start | bytes 737288 | tf_op jit(solution)/shard_map/ppermute | solution.py:249
  173.0 11.5 %collective-permute-start.9 = (bf16[128,960]{1,0:T(8,128)(2,1)}, bf16[128,960]{1,0:T(8,128)(2,1)S(1)}, u32[]{:S(2)}, u32[]{:S(2)}) collective-permute-start(bf16[128,960]{1,0:T(8,128)(2,1)} %collective-permute-done.5.refs_5_), channel_id=1, source_target_pairs={{0,1},{1,0},{2,3},{3,2},{4,5},{5,4},{6,7},{7,6},{8,9},{9,8},{10,11... | collective-permute-start | bytes 737288 | tf_op jit(solution)/shard_map/ppermute | solution.py:249
  173.0 11.5 %collective-permute-start.11 = (bf16[128,960]{1,0:T(8,128)(2,1)}, bf16[128,960]{1,0:T(8,128)(2,1)S(1)}, u32[]{:S(2)}, u32[]{:S(2)}) collective-permute-start(bf16[128,960]{1,0:T(8,128)(2,1)} %collective-permute-done.6.refs_5_), channel_id=1, source_target_pairs={{0,1},{1,0},{2,3},{3,2},{4,5},{5,4},{6,7},{7,6},{8,9},{9,8},{10,11... | collective-permute-start | bytes 737288 | tf_op jit(solution)/shard_map/ppermute | solution.py:249
  173.5 11.4 %slice-start = ((s8[5242880]{0:T(1024)(128)(4,1)}), s8[4194304]{0:T(1024)(128)(4,1)S(1)}, s32[]{:S(2)}) async-start(s8[5242880]{0:T(1024)(128)(4,1)} %bitcast.212), calls=%async_computation.1 | async-start | bytes 8388608
  174.6 10.1 %copy-start.69 = (f32[128]{0:T(128)S(1)}, f32[128]{0:T(128)}, u32[]{:S(2)}) copy-start(f32[128]{0:T(128)} %get-tuple-element.187) | copy-start | bytes 1540
  174.6 10.3 %slice-start.1 = ((s8[5242880]{0:T(1024)(128)(4,1)}), s8[1048576]{0:T(1024)(128)(4,1)S(1)}, s32[]{:S(2)}) async-start(s8[5242880]{0:T(1024)(128)(4,1)} %bitcast.212), calls=%async_computation.2 | async-start | bytes 2097152
  189.0 1.7 collective-permute-start.12
  190.7 11.1 %copy-start.11 = (bf16[2,1,128,640]{3,2,1,0:T(8,128)(2,1)}, bf16[2,1,128,640]{3,2,1,0:T(8,128)(2,1)S(1)}, u32[]{:S(2)}) copy-start(bf16[2,1,128,640]{3,2,1,0:T(8,128)(2,1)S(1)} %collective-permute-done.12.refs_3_) | copy-start | bytes 983044
  190.7 10.4 %collective-permute-start.13 = (bf16[128,960]{1,0:T(8,128)(2,1)S(1)}, bf16[128,960]{1,0:T(8,128)(2,1)S(1)}, u32[]{:S(2)}, u32[]{:S(2)}) collective-permute-start(bf16[128,960]{1,0:T(8,128)(2,1)S(1)} %fusion.46), channel_id=1, source_target_pairs={{16,0},{17,1},{18,2},{19,3},{20,4},{21,5},{22,6},{23,7},{24,8},{25... | collective-permute-start | bytes 737288 | tf_op jit(solution)/shard_map/ppermute | solution.py:543
  201.8 9.7 %collective-permute-start.14 = (bf16[128,960]{1,0:T(8,128)(2,1)}, bf16[128,960]{1,0:T(8,128)(2,1)}, u32[]{:S(2)}, u32[]{:S(2)}) collective-permute-start(bf16[128,960]{1,0:T(8,128)(2,1)} %broadcast_select_fusion.eb_ref.refs_4_), channel_id=1, source_target_pairs={{0,2},{1,3},{2,0},{3,1},{4,6},{5,7},{6,4},{7,5},{8,10},{9,11},{10,... | collective-permute-start | bytes 737288 | tf_op jit(solution)/shard_map/ppermute | solution.py:249
  202.6 8.9 %collective-permute-start.15 = (bf16[128,960]{1,0:T(8,128)(2,1)}, bf16[128,960]{1,0:T(8,128)(2,1)}, u32[]{:S(2)}, u32[]{:S(2)}) collective-permute-start(bf16[128,960]{1,0:T(8,128)(2,1)} %broadcast_select_fusion.eb_ref.refs_4_), channel_id=1, source_target_pairs={{0,1},{1,0},{2,3},{3,2},{4,5},{5,4},{6,7},{7,6},{8,9},{9,8},{10,11... | collective-permute-start | bytes 737288 | tf_op jit(solution)/shard_map/ppermute | solution.py:249
  211.5 2.0 collective-permute-start.16
  212.1 6.1 %copy-start.70 = (f32[128]{0:T(128)S(1)}, f32[128]{0:T(128)}, u32[]{:S(2)}) copy-start(f32[128]{0:T(128)} %get-tuple-element.187) | copy-start | bytes 1540
  212.2 16.7 %collective-permute-start.17 = (bf16[2,2,128,640]{3,2,1,0:T(8,128)(2,1)S(1)}, bf16[2,2,128,640]{3,2,1,0:T(8,128)(2,1)S(1)}, u32[]{:S(2)}, u32[]{:S(2)}) collective-permute-start(bf16[2,2,128,640]{3,2,1,0:T(8,128)(2,1)S(1)} %dynamic-slice_bitcast_fusion), channel_id=1, source_target_pairs={{0,2},{1,3},{2,0},{3,1},{4,6},{5,7},{6,4},{7,5},{8,10},{9,11},{10,... | collective-permute-start | bytes 1966088 | tf_op jit(solution)/shard_map/ppermute | solution.py:249
  216.3 6.4 %copy-start.7 = (f32[1,160,960]{2,1,0:T(8,128)}, f32[1,160,960]{2,1,0:T(8,128)S(1)}, u32[]{:S(2)}) copy-start(f32[1,160,960]{2,1,0:T(8,128)S(1)} %get-tuple-element.144) | copy-start | bytes 1843204
  216.5 12.0 %collective-permute-start.18 = (bf16[160,960]{1,0:T(8,128)(2,1)S(1)}, bf16[160,960]{1,0:T(8,128)(2,1)S(1)}, u32[]{:S(2)}, u32[]{:S(2)}) collective-permute-start(bf16[160,960]{1,0:T(8,128)(2,1)S(1)} %bitcast.192), channel_id=1, source_target_pairs={{0,4},{1,5},{2,6},{3,7},{4,8},{5,9},{6,10},{7,11},{8,12},{9,13},{1... | collective-permute-start | bytes 921608 | tf_op jit(solution)/shard_map/ppermute | solution.py:288
  220.4 28.3 %copy-start.20 = (bf16[128,960]{1,0:T(8,128)(2,1)S(1)}, bf16[128,960]{1,0:T(8,128)(2,1)}, u32[]{:S(2)}) copy-start(bf16[128,960]{1,0:T(8,128)(2,1)} %copy-done.19) | copy-start | bytes 737284
  220.4 28.3 %copy-start.22 = (bf16[128,960]{1,0:T(8,128)(2,1)S(1)}, bf16[128,960]{1,0:T(8,128)(2,1)}, u32[]{:S(2)}) copy-start(bf16[128,960]{1,0:T(8,128)(2,1)} %copy-done.21) | copy-start | bytes 737284
  229.3 19.3 %collective-permute-start.19 = (bf16[2,2,128,640]{3,2,1,0:T(8,128)(2,1)S(1)}, bf16[2,2,128,640]{3,2,1,0:T(8,128)(2,1)S(1)}, u32[]{:S(2)}, u32[]{:S(2)}) collective-permute-start(bf16[2,2,128,640]{3,2,1,0:T(8,128)(2,1)S(1)} %pad_maximum_fusion.2), channel_id=1, source_target_pairs={{0,1},{1,0},{2,3},{3,2},{4,5},{5,4},{6,7},{7,6},{8,9},{9,8},{10,11... | collective-permute-start | bytes 1966088 | tf_op jit(solution)/shard_map/ppermute | solution.py:249
  229.4 18.5 %collective-permute-start.20 = (bf16[160,960]{1,0:T(8,128)(2,1)S(1)}, bf16[160,960]{1,0:T(8,128)(2,1)S(1)}, u32[]{:S(2)}, u32[]{:S(2)}) collective-permute-start(bf16[160,960]{1,0:T(8,128)(2,1)S(1)} %bitcast.191), channel_id=1, source_target_pairs={{0,8},{1,9},{2,10},{3,11},{4,12},{5,13},{6,14},{7,15},{8,0},{9,1},... | collective-permute-start | bytes 921608 | tf_op jit(solution)/shard_map/ppermute | solution.py:288
  231.5 21.6 %copy-start.35 = (bf16[5,3,128,128]{2,3,1,0:T(8,128)(2,1)S(1)}, bf16[5,3,128,128]{2,3,1,0:T(8,128)(2,1)}, u32[]{:S(2)}) copy-start(bf16[5,3,128,128]{2,3,1,0:T(8,128)(2,1)} %copy-done.33) | copy-start | bytes 1474564
  231.5 21.9 %copy-start.31 = (f32[5,3,128,128]{2,3,1,0:T(8,128)S(1)}, f32[5,3,128,128]{2,3,1,0:T(8,128)}, u32[]{:S(2)}) copy-start(f32[5,3,128,128]{2,3,1,0:T(8,128)} %copy-done.29) | copy-start | bytes 2949124
  231.6 23.8 %collective-permute-start.21 = (bf16[160,960]{1,0:T(8,128)(2,1)S(1)}, bf16[160,960]{1,0:T(8,128)(2,1)S(1)}, u32[]{:S(2)}, u32[]{:S(2)}) collective-permute-start(bf16[160,960]{1,0:T(8,128)(2,1)S(1)} %bitcast.190), channel_id=1, source_target_pairs={{0,12},{1,13},{2,14},{3,15},{4,0},{5,1},{6,2},{7,3},{8,4},{9,5},{1... | collective-permute-start | bytes 921608 | tf_op jit(solution)/shard_map/ppermute | solution.py:288
  255.3 4.2 %copy-start.38 = (bf16[128,960]{1,0:T(8,128)(2,1)S(1)}, bf16[128,960]{1,0:T(8,128)(2,1)}, u32[]{:S(2)}) copy-start(bf16[128,960]{1,0:T(8,128)(2,1)} %copy-done.36) | copy-start | bytes 737284
  255.4 4.2 %copy-start.66 = (f32[128]{0:T(128)S(1)}, f32[128]{0:T(128)}, u32[]{:S(2)}) copy-start(f32[128]{0:T(128)} %copy-done.65) | copy-start | bytes 1540
  257.5 14.7 %collective-permute-start.22 = (bf16[2,1,128,640]{3,2,1,0:T(8,128)(2,1)}, bf16[2,1,128,640]{3,2,1,0:T(8,128)(2,1)S(1)}, u32[]{:S(2)}, u32[]{:S(2)}) collective-permute-start(bf16[2,1,128,640]{3,2,1,0:T(8,128)(2,1)} %bitcast.85), channel_id=1, source_target_pairs={{0,2},{1,3},{2,0},{3,1},{4,6},{5,7},{6,4},{7,5},{8,10},{9,11},{10,... | collective-permute-start | bytes 983048 | tf_op jit(solution)/shard_map/ppermute | solution.py:249
  258.8 13.4 %collective-permute-start.25 = (bf16[128,960]{1,0:T(8,128)(2,1)}, bf16[128,960]{1,0:T(8,128)(2,1)S(1)}, u32[]{:S(2)}, u32[]{:S(2)}) collective-permute-start(bf16[128,960]{1,0:T(8,128)(2,1)} %get-tuple-element.129.refs_8_), channel_id=1, source_target_pairs={{0,2},{1,3},{2,0},{3,1},{4,6},{5,7},{6,4},{7,5},{8,10},{9,11},{10,... | collective-permute-start | bytes 737288 | tf_op jit(solution)/shard_map/ppermute | solution.py:249
  263.0 26.8 %copy-start.16 = (bf16[128,960]{1,0:T(8,128)(2,1)S(1)}, bf16[128,960]{1,0:T(8,128)(2,1)}, u32[]{:S(2)}) copy-start(bf16[128,960]{1,0:T(8,128)(2,1)} %copy-done.15) | copy-start | bytes 737284
  263.0 16.3 %collective-permute-start.26 = (bf16[128,960]{1,0:T(8,128)(2,1)}, bf16[128,960]{1,0:T(8,128)(2,1)S(1)}, u32[]{:S(2)}, u32[]{:S(2)}) collective-permute-start(bf16[128,960]{1,0:T(8,128)(2,1)} %get-tuple-element.129.refs_8_), channel_id=1, source_target_pairs={{0,1},{1,0},{2,3},{3,2},{4,5},{5,4},{6,7},{7,6},{8,9},{9,8},{10,11... | collective-permute-start | bytes 737288 | tf_op jit(solution)/shard_map/ppermute | solution.py:249
  263.3 26.5 %copy-start.5 = (bf16[4,1,128,640]{3,2,1,0:T(8,128)(2,1)}, bf16[4,1,128,640]{3,2,1,0:T(8,128)(2,1)S(1)}, u32[]{:S(2)}) copy-start(bf16[4,1,128,640]{3,2,1,0:T(8,128)(2,1)S(1)} %copy.43.refs_1_) | copy-start | bytes 1966084
  263.3 26.3 %collective-permute-start.29 = (bf16[320,960]{1,0:T(8,128)(2,1)S(1)}, bf16[320,960]{1,0:T(8,128)(2,1)}, u32[]{:S(2)}, u32[]{:S(2)}) collective-permute-start(bf16[320,960]{1,0:T(8,128)(2,1)S(1)} %bitcast.189), channel_id=1, source_target_pairs={{0,4},{1,5},{2,6},{3,7},{4,8},{5,9},{6,10},{7,11},{8,12},{9,13},{1... | collective-permute-start | bytes 1843208 | tf_op jit(solution)/shard_map/ppermute | solution.py:288
  272.2 17.6 %copy-start.23 = (bf16[128,960]{1,0:T(8,128)(2,1)}, bf16[128,960]{1,0:T(8,128)(2,1)S(1)}, u32[]{:S(2)}) copy-start(bf16[128,960]{1,0:T(8,128)(2,1)S(1)} %collective-permute-done.25.refs_9_) | copy-start | bytes 737284
  272.2 16.8 %collective-permute-start.27 = (bf16[128,960]{1,0:T(8,128)(2,1)S(1)}, bf16[128,960]{1,0:T(8,128)(2,1)S(1)}, u32[]{:S(2)}, u32[]{:S(2)}) collective-permute-start(bf16[128,960]{1,0:T(8,128)(2,1)S(1)} %collective-permute-done.25.refs_9_), channel_id=1, source_target_pairs={{0,1},{1,0},{2,3},{3,2},{4,5},{5,4},{6,7},{7,6},{8,9},{9,8},{10,11... | collective-permute-start | bytes 737288 | tf_op jit(solution)/shard_map/ppermute | solution.py:249
  272.2 17.6 %copy-start.13 = (bf16[2,1,128,640]{3,2,1,0:T(8,128)(2,1)}, bf16[2,1,128,640]{3,2,1,0:T(8,128)(2,1)S(1)}, u32[]{:S(2)}) copy-start(bf16[2,1,128,640]{3,2,1,0:T(8,128)(2,1)S(1)} %collective-permute-done.22.refs_2_) | copy-start | bytes 983044
  272.3 17.4 %collective-permute-start.28 = (bf16[2,1,128,640]{3,2,1,0:T(8,128)(2,1)S(1)}, bf16[2,1,128,640]{3,2,1,0:T(8,128)(2,1)S(1)}, u32[]{:S(2)}, u32[]{:S(2)}) collective-permute-start(bf16[2,1,128,640]{3,2,1,0:T(8,128)(2,1)S(1)} %pad_maximum_fusion.6), channel_id=1, source_target_pairs={{0,1},{1,0},{2,3},{3,2},{4,5},{5,4},{6,7},{7,6},{8,9},{9,8},{10,11... | collective-permute-start | bytes 983048 | tf_op jit(solution)/shard_map/ppermute | solution.py:249
  272.9 1.3 collective-permute-start.23
  274.3 3.7 collective-permute-start.24
  277.9 38.7 %collective-permute-start.31 = (bf16[320,960]{1,0:T(8,128)(2,1)}, bf16[320,960]{1,0:T(8,128)(2,1)}, u32[]{:S(2)}, u32[]{:S(2)}) collective-permute-start(bf16[320,960]{1,0:T(8,128)(2,1)} %bitcast.87), channel_id=1, source_target_pairs={{0,8},{1,9},{2,10},{3,11},{4,12},{5,13},{6,14},{7,15},{8,0},{9,1},... | collective-permute-start | bytes 1843208 | tf_op jit(solution)/shard_map/ppermute | solution.py:288
  280.0 39.0 %collective-permute-start.32 = (bf16[320,960]{1,0:T(8,128)(2,1)}, bf16[320,960]{1,0:T(8,128)(2,1)}, u32[]{:S(2)}, u32[]{:S(2)}) collective-permute-start(bf16[320,960]{1,0:T(8,128)(2,1)} %bitcast.88), channel_id=1, source_target_pairs={{0,12},{1,13},{2,14},{3,15},{4,0},{5,1},{6,2},{7,3},{8,4},{9,5},{1... | collective-permute-start | bytes 1843208 | tf_op jit(solution)/shard_map/ppermute | solution.py:288
  295.7 4.1 %copy-start.10 = (f32[128,960]{1,0:T(8,128)S(1)}, f32[128,960]{1,0:T(8,128)}, u32[]{:S(2)}) copy-start(f32[128,960]{1,0:T(8,128)} %copy-done.9) | copy-start | bytes 1474564
  295.7 4.1 %copy-start.39 = (bf16[128,960]{1,0:T(8,128)(2,1)S(1)}, bf16[128,960]{1,0:T(8,128)(2,1)}, u32[]{:S(2)}) copy-start(bf16[128,960]{1,0:T(8,128)(2,1)} %copy-done.36) | copy-start | bytes 737284
  295.7 4.1 %copy-start.42 = (f32[128,960]{1,0:T(8,128)S(1)}, f32[128,960]{1,0:T(8,128)}, u32[]{:S(2)}) copy-start(f32[128,960]{1,0:T(8,128)} %get-tuple-element.153) | copy-start | bytes 1474564
  295.7 4.1 %copy-start.49 = (f32[128,960]{1,0:T(8,128)S(1)}, f32[128,960]{1,0:T(8,128)}, u32[]{:S(2)}) copy-start(f32[128,960]{1,0:T(8,128)} %get-tuple-element.203) | copy-start | bytes 1474564
  295.7 4.1 %copy-start.68 = (f32[128]{0:T(128)S(1)}, f32[128]{0:T(128)}, u32[]{:S(2)}) copy-start(f32[128]{0:T(128)} %copy-done.67) | copy-start | bytes 1540
  299.1 33.0 %collective-permute-start.30 = (bf16[2,168,960]{2,1,0:T(8,128)(2,1)S(1)}, bf16[2,168,960]{2,1,0:T(8,128)(2,1)S(1)}, u32[]{:S(2)}, u32[]{:S(2)}) collective-permute-start(bf16[2,168,960]{2,1,0:T(8,128)(2,1)S(1)} %get-tuple-element.135), channel_id=1, source_target_pairs={{0,4},{1,5},{2,6},{3,7},{4,0},{5,1},{6,2},{7,3},{8,12},{9,13},{10,... | collective-permute-start | bytes 1935368 | tf_op jit(solution)/shard_map/ppermute | solution.py:249
  332.1 11.6 %copy-start.4 = (f32[1,320,960]{2,1,0:T(8,128)S(1)}, f32[1,320,960]{2,1,0:T(8,128)}, u32[]{:S(2)}) copy-start(f32[1,320,960]{2,1,0:T(8,128)} %copy-done.3) | copy-start | bytes 3686404
  332.4 26.2 %collective-permute-start.33 = (bf16[168,960]{1,0:T(8,128)(2,1)S(1)}, bf16[168,960]{1,0:T(8,128)(2,1)S(1)}, u32[]{:S(2)}, u32[]{:S(2)}) collective-permute-start(bf16[168,960]{1,0:T(8,128)(2,1)S(1)} %fusion.67), channel_id=1, source_target_pairs={{0,8},{1,9},{2,10},{3,11},{4,12},{5,13},{6,14},{7,15},{8,0},{9,1},... | collective-permute-start | bytes 967688 | tf_op jit(solution)/shard_map/ppermute | solution.py:249
  (45 other events, 60.6 us)
Sparse Core Ops, SparseCore 0:
  10.2 111.5 all-gather.1

commit v10 on v8

--- a/solution.py
+++ b/solution.py
@@ -393,23 +393,11 @@
 
 
 LINE = 4
-ORDER = (1, 2, 3)
-
-
-def direct_send(sends):
-    return [
-        z_pairs(send[0], [(a, (a + k) % LINE) for a in range(LINE)])
-        for k, send in zip(ORDER, sends)
-    ]
-
-
-def direct_total(own, received):
-    return own + sum(r.astype(f32) for r in received)
-
-
-def pair_second(own, received, z2):
+
+
+def pair_middle(own, received, z2):
     total = own + received.astype(f32)
-    return at(total, z2) + flip(at(total, 1 - z2).astype(bf16), Z2_BIT).astype(f32)
+    return at(total, z2), at(total, 1 - z2).astype(bf16)
 
 
 tie = lax.optimization_barrier
@@ -445,7 +433,6 @@
     tokens, width = o.shape[0], e.shape[1]
     share = act_c[0].shape[3] // LINE
     here = (2 * y + core, core)
-    others = [(z + k) % LINE for k in ORDER]
     eb = e.astype(bf16)
     eb_y, eb_c = flip(eb, Y_BIT), flip(eb, CORE_BIT)
     both, _, dm = backward_ffn(eb, state, weights)
@@ -453,31 +440,35 @@
     both_y = cols_y(both, y)
     eb_yc = flip(eb_y, CORE_BIT)
     dm, eb_yc = tie((dm, eb_yc))
-    direct = (*here, 0, z, *others)
-    ones = (1, 1, 1, 1)
-    down_own, *down_sends = plane_product(*act_c, [(eb, eb_y, eb_c, eb_yc)], direct, ones)
-    dm, down_sends = tie((dm, down_sends))
-    down_one, down_two, down_three = direct_send(down_sends)
+    pairs = (z1, 2 + z1, 1 - z1, 3 - z1)
+    down_own, down_send = plane_product(*act_c, [(eb, eb_y, eb_c, eb_yc)], (*here, 0, *pairs), (2, 2))
+    dm, down_own, down_send = tie((dm, down_own, down_send))
+    down_received = flip(down_send, Z1_BIT)
     dh1, dz, do, gain_two_grad = backward_mid(e, dm, state, weights)
-    do, dz, both_y, down_one = tie((do, dz, both_y, down_one))
+    do, dz, both_y, down_own, down_received = tie((do, dz, both_y, down_own, down_received))
     both_c = cols_core(both, both_y, y, core)
-    both_own, *both_sends = plane_product(both, both_y, both_c, [m_all], direct, ones)
-    do, dz, both_sends = tie((do, dz, both_sends))
-    both_one, both_two, both_three = direct_send(both_sends)
+    down, down_send = pair_middle(down_own, down_received, z2)
+    down_received = flip(down_send, Z2_BIT)
+    both_own, both_send = plane_product(both, both_y, both_c, [m_all], (*here, 0, *pairs), (2, 2))
+    do, dz, both_own, both_send = tie((do, dz, both_own, both_send))
+    both_received = flip(both_send, Z1_BIT)
     dproj = backward_attention(do, state, tables)
-    dproj, down_two, down_three = tie((dproj, down_two, down_three))
+    dproj, down_received = tie((dproj, down_received))
     attn_cols = jnp.concatenate([dproj, o], axis=1).reshape(tokens, 4, 4, share)
     attn_cols = attn_cols.transpose(2, 0, 1, 3).reshape(4, 1, tokens, 4 * share)
     attn_y = cols_y(attn_cols, y)
     dz_y, dz_c = flip(dz, Y_BIT), flip(dz, CORE_BIT)
     du, gain_one_grad = backward_in(dproj, dh1, state, weights)
     gain_grad = jnp.concatenate([gain_one_grad, gain_two_grad])
-    gain_grad, attn_y, dz_y, dz_c, both_one = tie((gain_grad, attn_y, dz_y, dz_c, both_one))
+    gain_grad, attn_y, dz_y, dz_c, both_own, both_received = tie(
+        (gain_grad, attn_y, dz_y, dz_c, both_own, both_received)
+    )
+    both, both_send = pair_middle(both_own, both_received, z2)
+    both_received = flip(both_send, Z2_BIT)
     gain_grad = gain_grad + flip(gain_grad, CORE_BIT)
     gain_grad = gain_grad + flip(gain_grad, Y_BIT)
     dz_all = (dz, dz_y, dz_c, flip(dz_y, CORE_BIT))
     attn_c = cols_core(attn_cols, attn_y, y, core)
-    gain_grad, dz_all, attn_c, both_two = tie((gain_grad, dz_all, attn_c, both_two))
     gain_rows = at(gain_grad.reshape(4, 4, -1).transpose(1, 0, 2), y * 2 + core)[:, None]
     gain_share = gain_rows.shape[-1]
     gain_rows = jnp.pad(gain_rows, ((0, 0), (0, EXTRA_ROWS - 1), (0, width - gain_share)))
@@ -488,16 +479,18 @@
         attn_y,
         attn_c,
         [n_all, dz_all],
-        (*here, is_qkv, z1, 2 + z1, 1 - z1, 3 - z1),
+        (*here, is_qkv, *pairs),
         (2, 2),
         (qkv_owners // 4, -(-qkv_owners // 4)),
         gain_rows,
     )
     attn_received = flip(attn_send, Z1_BIT)
-    attn_own, attn_received, both_three = tie((attn_own, attn_received, both_three))
-    attn = pair_second(attn_own, attn_received, z2)
-    down = direct_total(down_own[0], (down_one, down_two, down_three))
-    both = direct_total(both_own[0], (both_one, both_two, both_three))
+    attn_own, attn_received, both_received = tie((attn_own, attn_received, both_received))
+    attn, attn_send = pair_middle(attn_own, attn_received, z2)
+    attn_received = flip(attn_send, Z2_BIT)
+    down = down + down_received.astype(f32)
+    both = both + both_received.astype(f32)
+    attn = attn + attn_received.astype(f32)
     return (
         du,
         attn[:share],

time: 359 us -> 356 us (level)
  starting transfers between devices: 55.7 us -> 34.3 us
  local copies, waits for them, and re-layouts: 14.9 us -> 24.6 us
  other arithmetic: 16.8 us -> 20.5 us
    ppermute x26 -> x30, waiting for transfers between devices: 36.9 us -> 81.9 us  [flip(): return lax.ppermute(x, 'dp', [(i, i ^ bit) for i in range(size)])]
    ppermute x6 -> x0, waiting for transfers between devices: 41.8 us -> none  [z_pairs(): lax.ppermute(x, 'dp', [(4 * a + i, 4 * b + i) for a, b in pairs for i in...]
    ppermute x6 -> x0, starting transfers between devices: 17.4 us -> none  [z_pairs(): lax.ppermute(x, 'dp', [(4 * a + i, 4 * b + i) for a, b in pairs for i in...]
    unnamed x122 -> x142, local copies, waits for them, and re-layouts: 3.98 us -> 10 us
    ppermute x26 -> x30, starting transfers between devices: 33.4 us -> 29.2 us  [flip(): return lax.ppermute(x, 'dp', [(i, i ^ bit) for i in range(size)])]
  transfers between devices with their start and end apart: 35 -> 33, of which waited for: 19 -> 17; matrix products, arithmetic and copies ran while one was open for 6% -> 8% of each run, Pallas kernels for 10% -> 11%
where the time goes in v10:
time: 356 us; the launch traced here: 355 us
  waiting for transfers between devices  194 us (54%)
  Pallas kernels  47.7 us (13%)
  starting transfers between devices  34.3 us (10%)
  local copies, waits for them, and re-layouts  24.6 us (7%)
  other arithmetic  20.5 us (6%)
  matrix products  18.6 us (5%)
  between operations  15.4 us (4%)
    all_gather x1, waiting for transfers between devices, local(): lax.all_gather(own, 'dp', axis=0, tiled=True).reshape(4, 4, 4, share, width)  97.4 us
    ppermute x30, waiting for transfers between devices, flip(): return lax.ppermute(x, 'dp', [(i, i ^ bit) for i in range(size)])  81.9 us
    pallas_call x4, Pallas kernels, ffn_call(): pl.pallas_call(kernel, grid=(steps,), in_specs=[whole] * len(wholes) + [b...  36.6 us
    ppermute x30, starting transfers between devices, flip(): return lax.ppermute(x, 'dp', [(i, i ^ bit) for i in range(size)])  29.2 us
    pallas_call x3, Pallas kernels, plane_product(): pl.pallas_call(kernel, grid_spec=pltpu.PrefetchScalarGridSpec(num_scalar_...  11.1 us
    unnamed x142, local copies, waits for them, and re-layouts  10 us
    ppermute x1, waiting for transfers between devices, local(): received = lax.ppermute(first_grad, 'section', [(1, 0)])  8.84 us
    dot_general x4, matrix products, dot_nt(): lax.dot_general(a, b, (((1,), (1,)), ((), ())), preferred_element_type=f32)  7.85 us
  transfers between devices with their start and end apart: 33, of which 17 were waited for; matrix products, arithmetic and copies ran while one was open for 8% of the time, Pallas kernels for 11%

profile of v10, /device:TPU:0, one launch (start us, length us, event | category | flops | bytes accessed | tf_op | source)
XLA Modules:
  0.0 354.9 jit_solution(8088602372064082130)
XLA Ops:
  7.2 2.5 pad_maximum_fusion.1
  11.2 2.8 collective-permute-start.1
  14.2 1.4 collective-permute-done.1
  15.7 2.1 collective-permute-start.2
  17.9 1.4 collective-permute-done.2
  19.5 3.0 collective-permute-start.3
  22.8 1.3 collective-permute-done.3
  24.4 97.4 %all-gather.2.cloned.1.call-done = bf16[10240,960]{1,0:T(8,128)(2,1)} async-done(((bf16[640,960]{1,0:T(8,128)(2,1)}), bf16[10240,960]{1,0:T(8,128)(2,1)}) %all-gather.2.cloned.1.call-update) | async-done | bytes 19660816 | tf_op jit(solution)/shard_map/all_gather | solution.py:515
  121.8 3.4 slice.119
  125.2 1.1 fusion.6
  128.3 9.6 %shard_map.84 = (f32[4,128,640]{2,1,0:T(8,128)}, f32[4,128,640]{2,1,0:T(8,128)}, bf16[4,128,640]{2,1,0:T(8,128)(2,1)}, f32[128,960]{1,0:T(8,128)S(1)}) custom-call(bf16[128,960]{1,0:T(8,128)(2,1)S(1)} %multiply_convert_fusion.3.m_ref, f32[128,960]{1,0:T(8,128)S(1)} %get-tuple-element.174.h1_ref, bf16[4,4,4,160,960]{4,3,2,1,0:T(8,128)(2,1)} %bitcast.184, ...), custom_call_target="tpu_custom_call" | custom-call | flops 1887436800 | bytes 14745600 | tf_op jit(solution)/shard_map/pallas_call | solution.py:206
  137.9 3.6 %collective-permute-start.4 = (bf16[128,960]{1,0:T(8,128)(2,1)S(1)}, bf16[128,960]{1,0:T(8,128)(2,1)S(1)}, u32[]{:S(2)}, u32[]{:S(2)}) collective-permute-start(bf16[128,960]{1,0:T(8,128)(2,1)S(1)} %convert_element_type.156), channel_id=1, source_target_pairs={{0,16},{1,17},{2,18},{3,19},{4,20},{5,21},{6,22},{7,23},{8,24},{9,... | collective-permute-start | bytes 737288 | tf_op jit(solution)/shard_map/ppermute | solution.py:530
  141.5 5.8 %collective-permute-done.4 = bf16[128,960]{1,0:T(8,128)(2,1)S(1)} collective-permute-done((bf16[128,960]{1,0:T(8,128)(2,1)S(1)}, bf16[128,960]{1,0:T(8,128)(2,1)S(1)}, u32[]{:S(2)}, u32[]{:S(2)}) %collective-permute-start.4) | collective-permute-done | bytes 245792 | tf_op jit(solution)/shard_map/ppermute | solution.py:530
  148.3 3.0 fusion.4
  152.9 2.2 multiply_reduce_fusion.5
  156.5 1.2 collective-permute-start.5
  158.5 8.3 %shard_map.85 = (f32[4,128,640]{2,1,0:T(8,128)S(1)}, f32[4,128,640]{2,1,0:T(8,128)S(1)}, bf16[4,128,640]{2,1,0:T(8,128)(2,1)S(1)}, f32[128,960]{1,0:T(8,128)S(1)}) custom-call(bf16[128,960]{1,0:T(8,128)(2,1)} %multiply_convert_fusion.2.m_ref.refs_4_, f32[128,960]{1,0:T(8,128)S(1)} %get-tuple-element.178.h1_ref, bf16[4,4,4,160,960]{4,3,2,1,0:T(8,128)(2,1)} %bitcast.187, ...), custom_call_target="tpu_custom_call" | custom-call | flops 1887436800 | bytes 14745600 | tf_op jit(solution)/shard_map/pallas_call | solution.py:206
  166.9 3.2 collective-permute-done.6.refs_5_
  170.9 1.2 collective-permute-start.7
  173.1 1.1 dynamic-slice_bitcast_fusion.2
  174.2 9.9 %shard_map.86 = (bf16[4,2,128,640]{3,2,1,0:T(8,128)(2,1)}, f32[128,960]{1,0:T(8,128)S(1)}) custom-call(bf16[128,960]{1,0:T(8,128)(2,1)S(1)} %bitcast.179, f32[4,128,640]{2,1,0:T(8,128)S(1)} %get-tuple-element.72.gate_ref, f32[4,128,640]{2,1,0:T(8,128)S(1)} %get-tuple-element.73.up_ref, bf16[4,4,4,160,960]{4,3,2,1,0:T(8,128)(2,1)} %bitcast.190, ...), custom_call_target="tpu_custom_call" | custom-call | flops 1887436800 | bytes 14745600 | tf_op jit(solution)/shard_map/pallas_call | solution.py:206
  187.5 0.9 constant_dynamic-slice_fusion.6
  190.2 1.5 collective-permute-start.13
  191.7 8.8 %collective-permute-done.13 = bf16[128,960]{1,0:T(8,128)(2,1)S(1)} collective-permute-done((bf16[128,960]{1,0:T(8,128)(2,1)S(1)}, bf16[128,960]{1,0:T(8,128)(2,1)S(1)}, u32[]{:S(2)}, u32[]{:S(2)}) %collective-permute-start.13) | collective-permute-done | bytes 245792 | tf_op jit(solution)/shard_map/ppermute | solution.py:534
  202.3 8.8 %shard_map.87 = (bf16[4,2,128,640]{3,2,1,0:T(8,128)(2,1)S(1)}, f32[128,960]{1,0:T(8,128)S(1)}) custom-call(bf16[128,960]{1,0:T(8,128)(2,1)} %broadcast_select_fusion.eb_ref.refs_4_, f32[4,128,640]{2,1,0:T(8,128)S(1)} %get-tuple-element.72.gate_ref, f32[4,128,640]{2,1,0:T(8,128)S(1)} %get-tuple-element.73.up_ref, bf16[4,4,4,160,960]{4,3,2,1,0:T(8,128)(2,1)} %bitcast.193, ...), custom_call_target="tpu_custom_call" | custom-call | flops 1887436800 | bytes 14745600 | tf_op jit(solution)/shard_map/pallas_call | solution.py:206
  211.8 1.3 collective-permute-start.17
  213.1 2.8 shard_map.88
  216.1 1.6 collective-permute-start.18
  217.7 2.1 fusion.88
  219.8 3.0 fusion.33
  222.8 5.7 %collective-permute-done.17.refs_2_ = bf16[2,2,128,640]{3,2,1,0:T(8,128)(2,1)S(1)} collective-permute-done((bf16[2,2,128,640]{3,2,1,0:T(8,128)(2,1)S(1)}, bf16[2,2,128,640]{3,2,1,0:T(8,128)(2,1)S(1)}, u32[]{:S(2)}, u32[]{:S(2)}) %collective-permute-start.17) | collective-permute-done | bytes 655392 | tf_op jit(solution)/shard_map/ppermute | solution.py:249
  228.5 4.6 %collective-permute-done.18 = bf16[2,160,960]{2,1,0:T(8,128)(2,1)S(1)} collective-permute-done((bf16[2,160,960]{2,1,0:T(8,128)(2,1)S(1)}, bf16[2,160,960]{2,1,0:T(8,128)(2,1)S(1)}, u32[]{:S(2)}, u32[]{:S(2)}) %collective-permute-start.18) | collective-permute-done | bytes 614432 | tf_op jit(solution)/shard_map/ppermute | solution.py:249
  233.2 0.9 copy-done.11
  234.0 0.9 pad_maximum_fusion.2
  235.1 1.4 convert_add_fusion.2
  236.6 2.5 collective-permute-start.20
  239.9 1.1 copy-done.14
  241.0 4.5 %shard_map.89 = (f32[2,320,960]{2,1,0:T(8,128)S(1)}, bf16[2,320,960]{2,1,0:T(8,128)(2,1)}) custom-call(s32[7]{0:T(128)S(1)} %stack.65.refs_0_, bf16[4,2,128,640]{3,2,1,0:T(8,128)(2,1)S(1)} %copy-done.6, bf16[2,2,128,640]{3,2,1,0:T(8,128)(2,1)S(1)} %copy-done.12, bf16[2,2,128,640]{3,2,1,0:T(8,128)(2,1)S(1)} %copy-done.14, ...), custom_call_target="tpu_custom_call" | custom-call | flops 1258291200 | bytes 7208960 | tf_op jit(solution)/shard_map/pallas_call | solution.py:374
  247.4 1.3 collective-permute-start.22
  249.8 5.0 %collective-permute-done.20 = bf16[160,960]{1,0:T(8,128)(2,1)S(1)} collective-permute-done((bf16[160,960]{1,0:T(8,128)(2,1)S(1)}, bf16[160,960]{1,0:T(8,128)(2,1)S(1)}, u32[]{:S(2)}, u32[]{:S(2)}) %collective-permute-start.20) | collective-permute-done | bytes 307232 | tf_op jit(solution)/shard_map/ppermute | solution.py:249
  257.1 1.9 copy.41
  258.9 1.2 collective-permute-start.21
  260.2 3.4 fusion.60
  263.6 1.4 copy.43.refs_1_
  265.1 3.4 collective-permute-done.21.refs_2_
  268.5 14.3 %collective-permute-done.24 = bf16[2,320,960]{2,1,0:T(8,128)(2,1)} collective-permute-done((bf16[2,320,960]{2,1,0:T(8,128)(2,1)}, bf16[2,320,960]{2,1,0:T(8,128)(2,1)}, u32[]{:S(2)}, u32[]{:S(2)}) %collective-permute-start.24) | collective-permute-done | bytes 1228832 | tf_op jit(solution)/shard_map/ppermute | solution.py:249
  282.9 0.9 constant_dynamic-slice_fusion.1
  285.2 1.7 convert_add_fusion
  286.9 1.3 collective-permute-start.28
  288.4 0.9 fusion.42
  289.3 1.4 collective-permute-start.30
  290.9 1.1 copy-done.4
  292.0 0.9 copy-done.16
  292.9 0.9 copy-done.18
  293.9 3.8 %shard_map.90 = (f32[2,168,960]{2,1,0:T(8,128)S(1)}, bf16[2,168,960]{2,1,0:T(8,128)(2,1)S(1)}) custom-call(s32[7]{0:T(128)S(1)} %stack.69.refs_0_, bf16[4,1,128,640]{3,2,1,0:T(8,128)(2,1)S(1)} %copy-done.4, bf16[2,1,128,640]{3,2,1,0:T(8,128)(2,1)} %collective-permute-done.21.refs_2_, bf16[2,1,128,640]{3,2,1,0:T(8,128)(2,1)} %collective-permute-done.25.refs_3_, ...), custom_call_target="tpu_custom_call" | custom-call | flops 1258291200 | bytes 4096000 | tf_op jit(solution)/shard_map/pallas_call | solution.py:374
  297.7 2.5 collective-permute-start.29
  300.4 1.0 fusion.51
  301.4 20.3 %collective-permute-done.30 = bf16[320,960]{1,0:T(8,128)(2,1)} collective-permute-done((bf16[320,960]{1,0:T(8,128)(2,1)}, bf16[320,960]{1,0:T(8,128)(2,1)}, u32[]{:S(2)}, u32[]{:S(2)}) %collective-permute-start.30) | collective-permute-done | bytes 614432 | tf_op jit(solution)/shard_map/ppermute | solution.py:249
  321.8 7.6 %collective-permute-done.29 = bf16[2,168,960]{2,1,0:T(8,128)(2,1)S(1)} collective-permute-done((bf16[2,168,960]{2,1,0:T(8,128)(2,1)S(1)}, bf16[2,168,960]{2,1,0:T(8,128)(2,1)S(1)}, u32[]{:S(2)}, u32[]{:S(2)}) %collective-permute-start.29) | collective-permute-done | bytes 645152 | tf_op jit(solution)/shard_map/ppermute | solution.py:249
  330.1 1.0 copy-done.28
  331.1 1.3 bitcast_add_fusion
  332.4 1.5 pad_maximum_fusion
  333.8 12.7 %collective-permute-done.31 = bf16[168,960]{1,0:T(8,128)(2,1)S(1)} collective-permute-done((bf16[168,960]{1,0:T(8,128)(2,1)S(1)}, bf16[168,960]{1,0:T(8,128)(2,1)S(1)}, u32[]{:S(2)}, u32[]{:S(2)}) %collective-permute-start.31) | collective-permute-done | bytes 322592 | tf_op jit(solution)/shard_map/ppermute | solution.py:249
  346.7 0.9 slice_bitcast_fusion
  (279 shorter events, 27.7 us)
Async XLA Ops:
  7.2 114.6 %all-gather.2.cloned.1.call-start = ((), (), s32[]{:S(2)}) async-start(), calls=%async_computation | async-start | bytes 22282240 | tf_op jit(solution)/shard_map/all_gather | solution.py:515
  7.2 10.5 %copy-start = (bf16[1,2,64,960]{3,2,1,0:T(8,128)(2,1)S(1)}, bf16[1,2,64,960]{3,2,1,0:T(8,128)(2,1)}, u32[]{:S(2)}) copy-start(bf16[1,2,64,960]{3,2,1,0:T(8,128)(2,1)} %param.5) | copy-start | bytes 737284
  9.8 1.3 collective-permute-start
  11.2 4.3 %collective-permute-start.1 = (bf16[240]{0:T(256)(128)(2,1)S(1)}, bf16[240]{0:T(256)(128)(2,1)S(1)}, u32[]{:S(2)}, u32[]{:S(2)}) collective-permute-start(bf16[240]{0:T(256)(128)(2,1)S(1)} %pad_maximum_fusion.18), channel_id=1, source_target_pairs={{0,2},{1,3},{2,0},{3,1},{4,6},{5,7},{6,4},{7,5},{8,10},{9,11},{10,... | collective-permute-start | bytes 1448 | tf_op jit(solution)/shard_map/ppermute | solution.py:249
  15.7 3.6 %collective-permute-start.2 = (bf16[480]{0:T(512)(128)(2,1)S(1)}, bf16[480]{0:T(512)(128)(2,1)S(1)}, u32[]{:S(2)}, u32[]{:S(2)}) collective-permute-start(bf16[480]{0:T(512)(128)(2,1)S(1)} %pad_maximum_fusion.17), channel_id=1, source_target_pairs={{0,4},{1,5},{2,6},{3,7},{4,0},{5,1},{6,2},{7,3},{8,12},{9,13},{10,... | collective-permute-start | bytes 2888 | tf_op jit(solution)/shard_map/ppermute | solution.py:249
  19.5 4.7 %collective-permute-start.3 = (bf16[960]{0:T(1024)(128)(2,1)S(1)}, bf16[960]{0:T(1024)(128)(2,1)S(1)}, u32[]{:S(2)}, u32[]{:S(2)}) collective-permute-start(bf16[960]{0:T(1024)(128)(2,1)S(1)} %pad_maximum_fusion.16), channel_id=1, source_target_pairs={{0,8},{1,9},{2,10},{3,11},{4,12},{5,13},{6,14},{7,15},{8,0},{9,1},... | collective-permute-start | bytes 5768 | tf_op jit(solution)/shard_map/ppermute | solution.py:249
  137.9 9.4 %collective-permute-start.4 = (bf16[128,960]{1,0:T(8,128)(2,1)S(1)}, bf16[128,960]{1,0:T(8,128)(2,1)S(1)}, u32[]{:S(2)}, u32[]{:S(2)}) collective-permute-start(bf16[128,960]{1,0:T(8,128)(2,1)S(1)} %convert_element_type.156), channel_id=1, source_target_pairs={{0,16},{1,17},{2,18},{3,19},{4,20},{5,21},{6,22},{7,23},{8,24},{9,... | collective-permute-start | bytes 737288 | tf_op jit(solution)/shard_map/ppermute | solution.py:530
  147.5 5.5 %copy-start.32 = (bf16[128,960]{1,0:T(8,128)(2,1)}, bf16[128,960]{1,0:T(8,128)(2,1)S(1)}, u32[]{:S(2)}) copy-start(bf16[128,960]{1,0:T(8,128)(2,1)S(1)} %get-tuple-element.137) | copy-start | bytes 737284
  147.5 42.0 %copy-start.62 = (f32[128]{0:T(128)}, f32[128]{0:T(128)S(1)}, u32[]{:S(2)}) copy-start(f32[128]{0:T(128)S(1)} %get-tuple-element.168) | copy-start | bytes 1540
  147.5 42.0 %copy-start.64 = (f32[128]{0:T(128)}, f32[128]{0:T(128)S(1)}, u32[]{:S(2)}) copy-start(f32[128]{0:T(128)S(1)} %get-tuple-element.167) | copy-start | bytes 1540
  152.4 4.1 %copy-start.29 = (bf16[5,3,128,128]{2,3,1,0:T(8,128)(2,1)}, bf16[5,3,128,128]{2,3,1,0:T(8,128)(2,1)S(1)}, u32[]{:S(2)}) copy-start(bf16[5,3,128,128]{2,3,1,0:T(8,128)(2,1)S(1)} %fusion.61) | copy-start | bytes 1474564
  152.9 5.6 %copy-start.39 = (bf16[5,64,3,128]{3,1,2,0:T(8,128)(2,1)}, bf16[5,64,3,128]{3,1,2,0:T(8,128)(2,1)S(1)}, u32[]{:S(2)}) copy-start(bf16[5,64,3,128]{3,1,2,0:T(8,128)(2,1)S(1)} %convolution_convert_fusion) | copy-start | bytes 737284
  156.5 10.4 %collective-permute-start.5 = (bf16[128,960]{1,0:T(8,128)(2,1)}, bf16[128,960]{1,0:T(8,128)(2,1)}, u32[]{:S(2)}, u32[]{:S(2)}) collective-permute-start(bf16[128,960]{1,0:T(8,128)(2,1)} %multiply_convert_fusion.2.m_ref.refs_4_), channel_id=1, source_target_pairs={{0,2},{1,3},{2,0},{3,1},{4,6},{5,7},{6,4},{7,5},{8,10},{9,11},{10,... | collective-permute-start | bytes 737288 | tf_op jit(solution)/shard_map/ppermute | solution.py:249
  157.7 12.4 %collective-permute-start.6 = (bf16[128,960]{1,0:T(8,128)(2,1)}, bf16[128,960]{1,0:T(8,128)(2,1)}, u32[]{:S(2)}, u32[]{:S(2)}) collective-permute-start(bf16[128,960]{1,0:T(8,128)(2,1)} %fusion.56.refs_4_), channel_id=1, source_target_pairs={{0,2},{1,3},{2,0},{3,1},{4,6},{5,7},{6,4},{7,5},{8,10},{9,11},{10,... | collective-permute-start | bytes 737288 | tf_op jit(solution)/shard_map/ppermute | solution.py:249
  166.8 3.2 copy-start.1
  166.9 4.0 %copy-start.7 = (f32[128,960]{1,0:T(8,128)}, f32[128,960]{1,0:T(8,128)S(1)}, u32[]{:S(2)}) copy-start(f32[128,960]{1,0:T(8,128)S(1)} %get-tuple-element.110) | copy-start | bytes 1474564
  170.9 13.3 %collective-permute-start.7 = (bf16[2,1,128,640]{3,2,1,0:T(8,128)(2,1)}, bf16[2,1,128,640]{3,2,1,0:T(8,128)(2,1)}, u32[]{:S(2)}, u32[]{:S(2)}) collective-permute-start(bf16[2,1,128,640]{3,2,1,0:T(8,128)(2,1)} %dynamic-slice_bitcast_fusion.1), channel_id=1, source_target_pairs={{0,2},{1,3},{2,0},{3,1},{4,6},{5,7},{6,4},{7,5},{8,10},{9,11},{10,... | collective-permute-start | bytes 983048 | tf_op jit(solution)/shard_map/ppermute | solution.py:249
  172.1 12.0 %collective-permute-start.8 = (bf16[128,960]{1,0:T(8,128)(2,1)}, bf16[128,960]{1,0:T(8,128)(2,1)S(1)}, u32[]{:S(2)}, u32[]{:S(2)}) collective-permute-start(bf16[128,960]{1,0:T(8,128)(2,1)} %multiply_convert_fusion.2.m_ref.refs_4_), channel_id=1, source_target_pairs={{0,1},{1,0},{2,3},{3,2},{4,5},{5,4},{6,7},{7,6},{8,9},{9,8},{10,11... | collective-permute-start | bytes 737288 | tf_op jit(solution)/shard_map/ppermute | solution.py:249
  172.1 12.0 %collective-permute-start.10 = (bf16[128,960]{1,0:T(8,128)(2,1)}, bf16[128,960]{1,0:T(8,128)(2,1)S(1)}, u32[]{:S(2)}, u32[]{:S(2)}) collective-permute-start(bf16[128,960]{1,0:T(8,128)(2,1)} %fusion.56.refs_4_), channel_id=1, source_target_pairs={{0,1},{1,0},{2,3},{3,2},{4,5},{5,4},{6,7},{7,6},{8,9},{9,8},{10,11... | collective-permute-start | bytes 737288 | tf_op jit(solution)/shard_map/ppermute | solution.py:249
  172.6 11.5 %collective-permute-start.9 = (bf16[128,960]{1,0:T(8,128)(2,1)}, bf16[128,960]{1,0:T(8,128)(2,1)S(1)}, u32[]{:S(2)}, u32[]{:S(2)}) collective-permute-start(bf16[128,960]{1,0:T(8,128)(2,1)} %collective-permute-done.5.refs_5_), channel_id=1, source_target_pairs={{0,1},{1,0},{2,3},{3,2},{4,5},{5,4},{6,7},{7,6},{8,9},{9,8},{10,11... | collective-permute-start | bytes 737288 | tf_op jit(solution)/shard_map/ppermute | solution.py:249
  172.6 11.5 %collective-permute-start.11 = (bf16[128,960]{1,0:T(8,128)(2,1)}, bf16[128,960]{1,0:T(8,128)(2,1)S(1)}, u32[]{:S(2)}, u32[]{:S(2)}) collective-permute-start(bf16[128,960]{1,0:T(8,128)(2,1)} %collective-permute-done.6.refs_5_), channel_id=1, source_target_pairs={{0,1},{1,0},{2,3},{3,2},{4,5},{5,4},{6,7},{7,6},{8,9},{9,8},{10,11... | collective-permute-start | bytes 737288 | tf_op jit(solution)/shard_map/ppermute | solution.py:249
  173.1 11.4 %slice-start = ((s8[5242880]{0:T(1024)(128)(4,1)}), s8[4194304]{0:T(1024)(128)(4,1)S(1)}, s32[]{:S(2)}) async-start(s8[5242880]{0:T(1024)(128)(4,1)} %bitcast.202), calls=%async_computation.1 | async-start | bytes 8388608
  174.2 10.1 %copy-start.66 = (f32[128]{0:T(128)S(1)}, f32[128]{0:T(128)}, u32[]{:S(2)}) copy-start(f32[128]{0:T(128)} %get-tuple-element.169) | copy-start | bytes 1540
  174.2 10.3 %slice-start.1 = ((s8[5242880]{0:T(1024)(128)(4,1)}), s8[1048576]{0:T(1024)(128)(4,1)S(1)}, s32[]{:S(2)}) async-start(s8[5242880]{0:T(1024)(128)(4,1)} %bitcast.202), calls=%async_computation.2 | async-start | bytes 2097152
  188.5 1.7 collective-permute-start.12
  190.2 11.1 %copy-start.9 = (bf16[2,1,128,640]{3,2,1,0:T(8,128)(2,1)}, bf16[2,1,128,640]{3,2,1,0:T(8,128)(2,1)S(1)}, u32[]{:S(2)}) copy-start(bf16[2,1,128,640]{3,2,1,0:T(8,128)(2,1)S(1)} %collective-permute-done.12.refs_3_) | copy-start | bytes 983044
  190.2 10.4 %collective-permute-start.13 = (bf16[128,960]{1,0:T(8,128)(2,1)S(1)}, bf16[128,960]{1,0:T(8,128)(2,1)S(1)}, u32[]{:S(2)}, u32[]{:S(2)}) collective-permute-start(bf16[128,960]{1,0:T(8,128)(2,1)S(1)} %fusion.47), channel_id=1, source_target_pairs={{16,0},{17,1},{18,2},{19,3},{20,4},{21,5},{22,6},{23,7},{24,8},{25... | collective-permute-start | bytes 737288 | tf_op jit(solution)/shard_map/ppermute | solution.py:534
  201.4 9.8 %collective-permute-start.14 = (bf16[128,960]{1,0:T(8,128)(2,1)}, bf16[128,960]{1,0:T(8,128)(2,1)}, u32[]{:S(2)}, u32[]{:S(2)}) collective-permute-start(bf16[128,960]{1,0:T(8,128)(2,1)} %broadcast_select_fusion.eb_ref.refs_4_), channel_id=1, source_target_pairs={{0,2},{1,3},{2,0},{3,1},{4,6},{5,7},{6,4},{7,5},{8,10},{9,11},{10,... | collective-permute-start | bytes 737288 | tf_op jit(solution)/shard_map/ppermute | solution.py:249
  202.2 9.0 %collective-permute-start.15 = (bf16[128,960]{1,0:T(8,128)(2,1)}, bf16[128,960]{1,0:T(8,128)(2,1)}, u32[]{:S(2)}, u32[]{:S(2)}) collective-permute-start(bf16[128,960]{1,0:T(8,128)(2,1)} %broadcast_select_fusion.eb_ref.refs_4_), channel_id=1, source_target_pairs={{0,1},{1,0},{2,3},{3,2},{4,5},{5,4},{6,7},{7,6},{8,9},{9,8},{10,11... | collective-permute-start | bytes 737288 | tf_op jit(solution)/shard_map/ppermute | solution.py:249
  211.1 4.8 %copy-start.5 = (bf16[4,2,128,640]{3,2,1,0:T(8,128)(2,1)}, bf16[4,2,128,640]{3,2,1,0:T(8,128)(2,1)S(1)}, u32[]{:S(2)}) copy-start(bf16[4,2,128,640]{3,2,1,0:T(8,128)(2,1)S(1)} %get-tuple-element.94.refs_1_) | copy-start | bytes 3932164
  211.1 2.0 collective-permute-start.16
  211.8 5.9 %copy-start.67 = (f32[128]{0:T(128)S(1)}, f32[128]{0:T(128)}, u32[]{:S(2)}) copy-start(f32[128]{0:T(128)} %get-tuple-element.169) | copy-start | bytes 1540
  211.8 16.7 %collective-permute-start.17 = (bf16[2,2,128,640]{3,2,1,0:T(8,128)(2,1)S(1)}, bf16[2,2,128,640]{3,2,1,0:T(8,128)(2,1)S(1)}, u32[]{:S(2)}, u32[]{:S(2)}) collective-permute-start(bf16[2,2,128,640]{3,2,1,0:T(8,128)(2,1)S(1)} %dynamic-slice_bitcast_fusion), channel_id=1, source_target_pairs={{0,2},{1,3},{2,0},{3,1},{4,6},{5,7},{6,4},{7,5},{8,10},{9,11},{10,... | collective-permute-start | bytes 1966088 | tf_op jit(solution)/shard_map/ppermute | solution.py:249
  216.1 17.0 %collective-permute-start.18 = (bf16[2,160,960]{2,1,0:T(8,128)(2,1)S(1)}, bf16[2,160,960]{2,1,0:T(8,128)(2,1)S(1)}, u32[]{:S(2)}, u32[]{:S(2)}) collective-permute-start(bf16[2,160,960]{2,1,0:T(8,128)(2,1)S(1)} %get-tuple-element.96), channel_id=1, source_target_pairs={{0,4},{1,5},{2,6},{3,7},{4,0},{5,1},{6,2},{7,3},{8,12},{9,13},{10,... | collective-permute-start | bytes 1843208 | tf_op jit(solution)/shard_map/ppermute | solution.py:249
  235.0 4.1 %collective-permute-start.19 = (bf16[2,2,128,640]{3,2,1,0:T(8,128)(2,1)}, bf16[2,2,128,640]{3,2,1,0:T(8,128)(2,1)S(1)}, u32[]{:S(2)}, u32[]{:S(2)}) collective-permute-start(bf16[2,2,128,640]{3,2,1,0:T(8,128)(2,1)} %pad_maximum_fusion.2), channel_id=1, source_target_pairs={{0,1},{1,0},{2,3},{3,2},{4,5},{5,4},{6,7},{7,6},{8,9},{9,8},{10,11... | collective-permute-start | bytes 1966088 | tf_op jit(solution)/shard_map/ppermute | solution.py:249
  235.0 4.8 %copy-start.6 = (bf16[4,2,128,640]{3,2,1,0:T(8,128)(2,1)S(1)}, bf16[4,2,128,640]{3,2,1,0:T(8,128)(2,1)}, u32[]{:S(2)}) copy-start(bf16[4,2,128,640]{3,2,1,0:T(8,128)(2,1)} %copy-done.5) | copy-start | bytes 3932164
  235.1 4.8 %copy-start.12 = (bf16[2,2,128,640]{3,2,1,0:T(8,128)(2,1)S(1)}, bf16[2,2,128,640]{3,2,1,0:T(8,128)(2,1)}, u32[]{:S(2)}) copy-start(bf16[2,2,128,640]{3,2,1,0:T(8,128)(2,1)} %copy-done.11) | copy-start | bytes 1966084
  235.1 4.8 %copy-start.20 = (bf16[128,960]{1,0:T(8,128)(2,1)S(1)}, bf16[128,960]{1,0:T(8,128)(2,1)}, u32[]{:S(2)}) copy-start(bf16[128,960]{1,0:T(8,128)(2,1)} %copy-done.19) | copy-start | bytes 737284
  235.1 4.8 %copy-start.22 = (bf16[128,960]{1,0:T(8,128)(2,1)S(1)}, bf16[128,960]{1,0:T(8,128)(2,1)}, u32[]{:S(2)}) copy-start(bf16[128,960]{1,0:T(8,128)(2,1)} %copy-done.21) | copy-start | bytes 737284
  236.5 9.0 %copy-start.31 = (bf16[5,3,128,128]{2,3,1,0:T(8,128)(2,1)S(1)}, bf16[5,3,128,128]{2,3,1,0:T(8,128)(2,1)}, u32[]{:S(2)}) copy-start(bf16[5,3,128,128]{2,3,1,0:T(8,128)(2,1)} %copy-done.29) | copy-start | bytes 1474564
  236.6 18.2 %collective-permute-start.20 = (bf16[160,960]{1,0:T(8,128)(2,1)S(1)}, bf16[160,960]{1,0:T(8,128)(2,1)S(1)}, u32[]{:S(2)}, u32[]{:S(2)}) collective-permute-start(bf16[160,960]{1,0:T(8,128)(2,1)S(1)} %fusion.69), channel_id=1, source_target_pairs={{0,8},{1,9},{2,10},{3,11},{4,12},{5,13},{6,14},{7,15},{8,0},{9,1},... | collective-permute-start | bytes 921608 | tf_op jit(solution)/shard_map/ppermute | solution.py:249
  241.0 4.5 %copy-start.50 = (bf16[128,960]{0,1:T(8,128)(2,1)S(1)}, bf16[128,960]{0,1:T(8,128)(2,1)}, u32[]{:S(2)}) copy-start(bf16[128,960]{0,1:T(8,128)(2,1)} %fusion.33) | copy-start | bytes 737284
  241.0 4.8 %copy-start.25 = (f32[5,3,128,128]{2,3,1,0:T(8,128)S(1)}, f32[5,3,128,128]{2,3,1,0:T(8,128)}, u32[]{:S(2)}) copy-start(f32[5,3,128,128]{2,3,1,0:T(8,128)} %copy-done.23) | copy-start | bytes 2949124
  247.1 7.6 %copy-start.40 = (bf16[5,64,3,128]{3,1,2,0:T(8,128)(2,1)S(1)}, bf16[5,64,3,128]{3,1,2,0:T(8,128)(2,1)}, u32[]{:S(2)}) copy-start(bf16[5,64,3,128]{3,1,2,0:T(8,128)(2,1)} %copy-done.39) | copy-start | bytes 737284
  247.4 17.7 %collective-permute-start.22 = (bf16[128,960]{1,0:T(8,128)(2,1)}, bf16[128,960]{1,0:T(8,128)(2,1)}, u32[]{:S(2)}, u32[]{:S(2)}) collective-permute-start(bf16[128,960]{1,0:T(8,128)(2,1)} %get-tuple-element.111.refs_8_), channel_id=1, source_target_pairs={{0,2},{1,3},{2,0},{3,1},{4,6},{5,7},{6,4},{7,5},{8,10},{9,11},{10,... | collective-permute-start | bytes 737288 | tf_op jit(solution)/shard_map/ppermute | solution.py:249
  248.7 16.4 %collective-permute-start.23 = (bf16[128,960]{1,0:T(8,128)(2,1)}, bf16[128,960]{1,0:T(8,128)(2,1)}, u32[]{:S(2)}, u32[]{:S(2)}) collective-permute-start(bf16[128,960]{1,0:T(8,128)(2,1)} %get-tuple-element.111.refs_8_), channel_id=1, source_target_pairs={{0,1},{1,0},{2,3},{3,2},{4,5},{5,4},{6,7},{7,6},{8,9},{9,8},{10,11... | collective-permute-start | bytes 737288 | tf_op jit(solution)/shard_map/ppermute | solution.py:249
  248.8 34.0 %collective-permute-start.24 = (bf16[2,320,960]{2,1,0:T(8,128)(2,1)}, bf16[2,320,960]{2,1,0:T(8,128)(2,1)}, u32[]{:S(2)}, u32[]{:S(2)}) collective-permute-start(bf16[2,320,960]{2,1,0:T(8,128)(2,1)} %get-tuple-element.113), channel_id=1, source_target_pairs={{0,4},{1,5},{2,6},{3,7},{4,0},{5,1},{6,2},{7,3},{8,12},{9,13},{10,... | collective-permute-start | bytes 3686408 | tf_op jit(solution)/shard_map/ppermute | solution.py:249
  249.7 5.1 %copy-start.42 = (bf16[128,1600]{0,1:T(8,128)(2,1)}, bf16[128,1600]{0,1:T(8,128)(2,1)S(1)}, u32[]{:S(2)}) copy-start(bf16[128,1600]{0,1:T(8,128)(2,1)S(1)} %pad_maximum_fusion.4) | copy-start | bytes 1228804
  249.8 10.4 %copy-start.34 = (bf16[128,960]{1,0:T(8,128)(2,1)S(1)}, bf16[128,960]{1,0:T(8,128)(2,1)}, u32[]{:S(2)}) copy-start(bf16[128,960]{1,0:T(8,128)(2,1)} %copy-done.32) | copy-start | bytes 737284
  249.8 10.4 %copy-start.63 = (f32[128]{0:T(128)S(1)}, f32[128]{0:T(128)}, u32[]{:S(2)}) copy-start(f32[128]{0:T(128)} %copy-done.62) | copy-start | bytes 1540
  254.8 5.3 %copy-start.43 = (bf16[128,1600]{0,1:T(8,128)(2,1)S(1)}, bf16[128,1600]{0,1:T(8,128)(2,1)}, u32[]{:S(2)}) copy-start(bf16[128,1600]{0,1:T(8,128)(2,1)} %copy-done.42) | copy-start | bytes 1228804
  258.9 9.6 %collective-permute-start.21 = (bf16[2,1,128,640]{3,2,1,0:T(8,128)(2,1)}, bf16[2,1,128,640]{3,2,1,0:T(8,128)(2,1)}, u32[]{:S(2)}, u32[]{:S(2)}) collective-permute-start(bf16[2,1,128,640]{3,2,1,0:T(8,128)(2,1)} %bitcast.231), channel_id=1, source_target_pairs={{0,2},{1,3},{2,0},{3,1},{4,6},{5,7},{6,4},{7,5},{8,10},{9,11},{10,... | collective-permute-start | bytes 983048 | tf_op jit(solution)/shard_map/ppermute | solution.py:249
  265.0 21.9 %copy-start.3 = (bf16[4,1,128,640]{3,2,1,0:T(8,128)(2,1)}, bf16[4,1,128,640]{3,2,1,0:T(8,128)(2,1)S(1)}, u32[]{:S(2)}) copy-start(bf16[4,1,128,640]{3,2,1,0:T(8,128)(2,1)S(1)} %copy.43.refs_1_) | copy-start | bytes 1966084
  284.6 6.3 %collective-permute-start.25 = (bf16[2,1,128,640]{3,2,1,0:T(8,128)(2,1)}, bf16[2,1,128,640]{3,2,1,0:T(8,128)(2,1)}, u32[]{:S(2)}, u32[]{:S(2)}) collective-permute-start(bf16[2,1,128,640]{3,2,1,0:T(8,128)(2,1)} %pad_maximum_fusion.6), channel_id=1, source_target_pairs={{0,1},{1,0},{2,3},{3,2},{4,5},{5,4},{6,7},{7,6},{8,9},{9,8},{10,11... | collective-permute-start | bytes 983048 | tf_op jit(solution)/shard_map/ppermute | solution.py:249
  284.6 6.2 %collective-permute-start.26 = (bf16[128,960]{1,0:T(8,128)(2,1)}, bf16[128,960]{1,0:T(8,128)(2,1)}, u32[]{:S(2)}, u32[]{:S(2)}) collective-permute-start(bf16[128,960]{1,0:T(8,128)(2,1)} %collective-permute-done.22.refs_9_), channel_id=1, source_target_pairs={{0,1},{1,0},{2,3},{3,2},{4,5},{5,4},{6,7},{7,6},{8,9},{9,8},{10,11... | collective-permute-start | bytes 737288 | tf_op jit(solution)/shard_map/ppermute | solution.py:249
  285.1 1.8 collective-permute-start.27
  286.9 3.7 %collective-permute-start.28 = (f32[1920]{0:T(1024)S(1)}, f32[1920]{0:T(1024)S(1)}, u32[]{:S(2)}, u32[]{:S(2)}) collective-permute-start(f32[1920]{0:T(1024)S(1)} %add.213), channel_id=1, source_target_pairs={{0,2},{1,3},{2,0},{3,1},{4,6},{5,7},{6,4},{7,5},{8,10},{9,11},{10,... | collective-permute-start | bytes 23048 | tf_op jit(solution)/shard_map/ppermute | solution.py:249
  289.3 32.4 %collective-permute-start.30 = (bf16[320,960]{1,0:T(8,128)(2,1)}, bf16[320,960]{1,0:T(8,128)(2,1)}, u32[]{:S(2)}, u32[]{:S(2)}) collective-permute-start(bf16[320,960]{1,0:T(8,128)(2,1)} %fusion.42), channel_id=1, source_target_pairs={{0,8},{1,9},{2,10},{3,11},{4,12},{5,13},{6,14},{7,15},{8,0},{9,1},... | collective-permute-start | bytes 1843208 | tf_op jit(solution)/shard_map/ppermute | solution.py:249
  290.8 9.6 %copy-start.65 = (f32[128]{0:T(128)S(1)}, f32[128]{0:T(128)}, u32[]{:S(2)}) copy-start(f32[128]{0:T(128)} %copy-done.64) | copy-start | bytes 1540
  293.9 6.4 %copy-start.38 = (f32[2,160,960]{2,1,0:T(8,128)S(1)}, f32[2,160,960]{2,1,0:T(8,128)}, u32[]{:S(2)}) copy-start(f32[2,160,960]{2,1,0:T(8,128)} %copy-done.37) | copy-start | bytes 3686404
  293.9 6.4 %copy-start.60 = (bf16[160,960]{1,0:T(8,128)(2,1)S(1)}, bf16[160,960]{1,0:T(8,128)(2,1)}, u32[]{:S(2)}) copy-start(bf16[160,960]{1,0:T(8,128)(2,1)} %copy-done.59) | copy-start | bytes 921604
  293.9 6.5 %copy-start.35 = (bf16[128,960]{1,0:T(8,128)(2,1)S(1)}, bf16[128,960]{1,0:T(8,128)(2,1)}, u32[]{:S(2)}) copy-start(bf16[128,960]{1,0:T(8,128)(2,1)} %copy-done.32) | copy-start | bytes 737284
  297.7 31.6 %collective-permute-start.29 = (bf16[2,168,960]{2,1,0:T(8,128)(2,1)S(1)}, bf16[2,168,960]{2,1,0:T(8,128)(2,1)S(1)}, u32[]{:S(2)}, u32[]{:S(2)}) collective-permute-start(bf16[2,168,960]{2,1,0:T(8,128)(2,1)S(1)} %get-tuple-element.123), channel_id=1, source_target_pairs={{0,4},{1,5},{2,6},{3,7},{4,0},{5,1},{6,2},{7,3},{8,12},{9,13},{10,... | collective-permute-start | bytes 1935368 | tf_op jit(solution)/shard_map/ppermute | solution.py:249
  329.6 16.9 %collective-permute-start.31 = (bf16[168,960]{1,0:T(8,128)(2,1)S(1)}, bf16[168,960]{1,0:T(8,128)(2,1)S(1)}, u32[]{:S(2)}, u32[]{:S(2)}) collective-permute-start(bf16[168,960]{1,0:T(8,128)(2,1)S(1)} %fusion.68), channel_id=1, source_target_pairs={{0,8},{1,9},{2,10},{3,11},{4,12},{5,13},{6,14},{7,15},{8,0},{9,1},... | collective-permute-start | bytes 967688 | tf_op jit(solution)/shard_map/ppermute | solution.py:249
  (40 other events, 54.6 us)
Sparse Core Ops, SparseCore 0:
  10.2 111.5 all-gather.1

commit v11 on v10

--- a/solution.py
+++ b/solution.py
@@ -311,7 +311,7 @@
     return flip(jnp.stack([at(x, 2 * y + other), at(x_y, other)]), CORE_BIT)
 
 
-def plane_kernel(n_rows, split, n_own, picks_ref, *refs):
+def plane_kernel(n_rows, split, out_kinds, picks_ref, *refs):
     cols_ref, y_ref, core_ref = refs[:3]
     rows = [
         jnp.concatenate([r[...] for r in refs[3 + 4 * i : 7 + 4 * i]], axis=0) for i in range(n_rows)
@@ -351,26 +351,28 @@
         for i in range(ref.shape[0]):
             pick = picks_ref[slot]
             slot += 1
-            for j in range(kinds):
+            first = out_kinds[number][0]
+            for j in out_kinds[number]:
                 block = total[pl.ds(pl.multiple_of(j * height + pick * share, 8), share)]
-                ref[i, j * share : (j + 1) * share] = block.astype(ref.dtype)
+                ref[i, (j - first) * share : (j - first + 1) * share] = block.astype(ref.dtype)
             if extra_ref is not None:
                 ref[i, share:] = extra_ref[pick].astype(ref.dtype)
 
 
-def plane_product(cols, x_y, x_core, rows, picks, out_counts, split=None, extra=None):
+def plane_product(cols, x_y, x_core, rows, picks, split=None, extra=None):
     _, kinds, tokens, width_cols = cols.shape
     share, width = width_cols // LINE, rows[0][0].shape[1]
-    tall = kinds * share + (0 if extra is None else extra.shape[1])
+    out_kinds = [tuple(range(kinds)), *((j,) for j in range(kinds))]
+    more = 0 if extra is None else extra.shape[1]
     operands = [cols, x_y, x_core, *[r for chunk in rows for r in chunk]]
     if extra is not None:
         operands.append(extra)
     whole = lambda v: pl.BlockSpec(v.shape, lambda i, picks, n=v.ndim: (0,) * n)
     shapes = [
-        jax.ShapeDtypeStruct((count, tall, width), f32 if i == 0 else bf16)
-        for i, count in enumerate(out_counts)
+        jax.ShapeDtypeStruct((2, len(k) * share + more, width), f32 if i == 0 else bf16)
+        for i, k in enumerate(out_kinds)
     ]
-    kernel = lambda *refs: plane_kernel(len(rows), split, out_counts[0], *refs)
+    kernel = lambda *refs: plane_kernel(len(rows), split, out_kinds, *refs)
     return pl.pallas_call(
         kernel,
         grid_spec=pltpu.PrefetchScalarGridSpec(
@@ -441,7 +443,7 @@
     eb_yc = flip(eb_y, CORE_BIT)
     dm, eb_yc = tie((dm, eb_yc))
     pairs = (z1, 2 + z1, 1 - z1, 3 - z1)
-    down_own, down_send = plane_product(*act_c, [(eb, eb_y, eb_c, eb_yc)], (*here, 0, *pairs), (2, 2))
+    down_own, down_send = plane_product(*act_c, [(eb, eb_y, eb_c, eb_yc)], (*here, 0, *pairs))
     dm, down_own, down_send = tie((dm, down_own, down_send))
     down_received = flip(down_send, Z1_BIT)
     dh1, dz, do, gain_two_grad = backward_mid(e, dm, state, weights)
@@ -449,9 +451,11 @@
     both_c = cols_core(both, both_y, y, core)
     down, down_send = pair_middle(down_own, down_received, z2)
     down_received = flip(down_send, Z2_BIT)
-    both_own, both_send = plane_product(both, both_y, both_c, [m_all], (*here, 0, *pairs), (2, 2))
-    do, dz, both_own, both_send = tie((do, dz, both_own, both_send))
-    both_received = flip(both_send, Z1_BIT)
+    both_own, gate_send, up_send = plane_product(
+        both, both_y, both_c, [m_all], (*here, 0, *pairs, *pairs[2:])
+    )
+    do, dz, both_own, gate_send, up_send = tie((do, dz, both_own, gate_send, up_send))
+    gate_received, up_received = flip(gate_send, Z1_BIT), flip(up_send, Z1_BIT)
     dproj = backward_attention(do, state, tables)
     dproj, down_received = tie((dproj, down_received))
     attn_cols = jnp.concatenate([dproj, o], axis=1).reshape(tokens, 4, 4, share)
@@ -460,15 +464,20 @@
     dz_y, dz_c = flip(dz, Y_BIT), flip(dz, CORE_BIT)
     du, gain_one_grad = backward_in(dproj, dh1, state, weights)
     gain_grad = jnp.concatenate([gain_one_grad, gain_two_grad])
-    gain_grad, attn_y, dz_y, dz_c, both_own, both_received = tie(
-        (gain_grad, attn_y, dz_y, dz_c, both_own, both_received)
-    )
-    both, both_send = pair_middle(both_own, both_received, z2)
-    both_received = flip(both_send, Z2_BIT)
+    gain_grad, attn_y, dz_y, dz_c, both_own, gate_received = tie(
+        (gain_grad, attn_y, dz_y, dz_c, both_own, gate_received)
+    )
+    gate, gate_send = pair_middle(both_own[:, :share], gate_received, z2)
+    gate_received = flip(gate_send, Z2_BIT)
     gain_grad = gain_grad + flip(gain_grad, CORE_BIT)
     gain_grad = gain_grad + flip(gain_grad, Y_BIT)
     dz_all = (dz, dz_y, dz_c, flip(dz_y, CORE_BIT))
     attn_c = cols_core(attn_cols, attn_y, y, core)
+    gain_grad, dz_all, attn_c, both_own, up_received, gate_received = tie(
+        (gain_grad, dz_all, attn_c, both_own, up_received, gate_received)
+    )
+    up, up_send = pair_middle(both_own[:, share:], up_received, z2)
+    up_received = flip(up_send, Z2_BIT)
     gain_rows = at(gain_grad.reshape(4, 4, -1).transpose(1, 0, 2), y * 2 + core)[:, None]
     gain_share = gain_rows.shape[-1]
     gain_rows = jnp.pad(gain_rows, ((0, 0), (0, EXTRA_ROWS - 1), (0, width - gain_share)))
@@ -480,21 +489,21 @@
         attn_c,
         [n_all, dz_all],
         (*here, is_qkv, *pairs),
-        (2, 2),
         (qkv_owners // 4, -(-qkv_owners // 4)),
         gain_rows,
     )
     attn_received = flip(attn_send, Z1_BIT)
-    attn_own, attn_received, both_received = tie((attn_own, attn_received, both_received))
+    attn_own, attn_received, up_received = tie((attn_own, attn_received, up_received))
     attn, attn_send = pair_middle(attn_own, attn_received, z2)
     attn_received = flip(attn_send, Z2_BIT)
     down = down + down_received.astype(f32)
-    both = both + both_received.astype(f32)
+    gate = gate + gate_received.astype(f32)
+    up = up + up_received.astype(f32)
     attn = attn + attn_received.astype(f32)
     return (
         du,
         attn[:share],
-        jnp.concatenate([both, down]).reshape(3, share, width),
+        jnp.stack([gate, up, down]),
         attn[share : share + 1, :gain_share],
     )
 

time: 356 us -> 353 us (level)
  waiting for transfers between devices: 194 us -> 188 us
  starting transfers between devices: 34.3 us -> 38.7 us
    ppermute x30 -> x32, waiting for transfers between devices: 81.9 us -> 76.4 us  [flip(): return lax.ppermute(x, 'dp', [(i, i ^ bit) for i in range(size)])]
    ppermute x30 -> x32, starting transfers between devices: 29.2 us -> 33.6 us  [flip(): return lax.ppermute(x, 'dp', [(i, i ^ bit) for i in range(size)])]
    unnamed x142 -> x178, local copies, waits for them, and re-layouts: 10 us -> 11.1 us
  transfers between devices with their start and end apart: 33 -> 35, of which waited for: 17 -> 19; matrix products, arithmetic and copies ran while one was open for 8% -> 7% of each run, Pallas kernels for 11% -> 10%
where the time goes in v11:
time: 353 us; the launch traced here: 352 us
  waiting for transfers between devices  188 us (53%)
  Pallas kernels  47.3 us (13%)
  starting transfers between devices  38.7 us (11%)
  local copies, waits for them, and re-layouts  25 us (7%)
  other arithmetic  19 us (5%)
  matrix products  18.5 us (5%)
  between operations  15.6 us (4%)
    all_gather x1, waiting for transfers between devices, local(): lax.all_gather(own, 'dp', axis=0, tiled=True).reshape(4, 4, 4, share, width)  97.3 us
    ppermute x32, waiting for transfers between devices, flip(): return lax.ppermute(x, 'dp', [(i, i ^ bit) for i in range(size)])  76.4 us
    pallas_call x4, Pallas kernels, ffn_call(): pl.pallas_call(kernel, grid=(steps,), in_specs=[whole] * len(wholes) + [b...  36.6 us
    ppermute x32, starting transfers between devices, flip(): return lax.ppermute(x, 'dp', [(i, i ^ bit) for i in range(size)])  33.6 us
    unnamed x178, local copies, waits for them, and re-layouts  11.1 us
    pallas_call x3, Pallas kernels, plane_product(): pl.pallas_call(kernel, grid_spec=pltpu.PrefetchScalarGridSpec(num_scalar_...  10.7 us
    ppermute x1, waiting for transfers between devices, local(): received = lax.ppermute(first_grad, 'section', [(1, 0)])  8.84 us
    dot_general x4, matrix products, dot_nt(): lax.dot_general(a, b, (((1,), (1,)), ((), ())), preferred_element_type=f32)  7.84 us
  transfers between devices with their start and end apart: 35, of which 19 were waited for; matrix products, arithmetic and copies ran while one was open for 7% of the time, Pallas kernels for 10%

profile of v11, /device:TPU:0, one launch (start us, length us, event | category | flops | bytes accessed | tf_op | source)
XLA Modules:
  0.0 352.5 jit_solution(4190963135301366520)
XLA Ops:
  7.2 2.5 pad_maximum_fusion
  11.2 2.8 collective-permute-start.1
  14.2 1.4 collective-permute-done.1
  15.7 2.1 collective-permute-start.2
  17.9 1.4 collective-permute-done.2
  19.5 3.0 collective-permute-start.3
  22.8 1.3 collective-permute-done.3
  24.4 97.3 %all-gather.2.cloned.1.call-done = bf16[10240,960]{1,0:T(8,128)(2,1)} async-done(((bf16[640,960]{1,0:T(8,128)(2,1)}), bf16[10240,960]{1,0:T(8,128)(2,1)}) %all-gather.2.cloned.1.call-update) | async-done | bytes 19660816 | tf_op jit(solution)/shard_map/all_gather | solution.py:524
  121.8 3.4 slice.127
  125.2 1.1 fusion.6
  128.2 9.6 %shard_map.84 = (f32[4,128,640]{2,1,0:T(8,128)}, f32[4,128,640]{2,1,0:T(8,128)}, bf16[4,128,640]{2,1,0:T(8,128)(2,1)}, f32[128,960]{1,0:T(8,128)S(1)}) custom-call(bf16[128,960]{1,0:T(8,128)(2,1)S(1)} %multiply_convert_fusion.3.m_ref, f32[128,960]{1,0:T(8,128)S(1)} %get-tuple-element.196.h1_ref, bf16[4,4,4,160,960]{4,3,2,1,0:T(8,128)(2,1)} %bitcast.199, ...), custom_call_target="tpu_custom_call" | custom-call | flops 1887436800 | bytes 14745600 | tf_op jit(solution)/shard_map/pallas_call | solution.py:206
  137.9 3.6 %collective-permute-start.4 = (bf16[128,960]{1,0:T(8,128)(2,1)S(1)}, bf16[128,960]{1,0:T(8,128)(2,1)S(1)}, u32[]{:S(2)}, u32[]{:S(2)}) collective-permute-start(bf16[128,960]{1,0:T(8,128)(2,1)S(1)} %convert_element_type.168), channel_id=1, source_target_pairs={{0,16},{1,17},{2,18},{3,19},{4,20},{5,21},{6,22},{7,23},{8,24},{9,... | collective-permute-start | bytes 737288 | tf_op jit(solution)/shard_map/ppermute | solution.py:539
  141.5 5.8 %collective-permute-done.4 = bf16[128,960]{1,0:T(8,128)(2,1)S(1)} collective-permute-done((bf16[128,960]{1,0:T(8,128)(2,1)S(1)}, bf16[128,960]{1,0:T(8,128)(2,1)S(1)}, u32[]{:S(2)}, u32[]{:S(2)}) %collective-permute-start.4) | collective-permute-done | bytes 245792 | tf_op jit(solution)/shard_map/ppermute | solution.py:539
  148.9 3.0 fusion.4
  153.8 2.2 multiply_reduce_fusion.5
  156.9 1.2 collective-permute-start.5
  158.9 8.3 %shard_map.85 = (f32[4,128,640]{2,1,0:T(8,128)S(1)}, f32[4,128,640]{2,1,0:T(8,128)S(1)}, bf16[4,128,640]{2,1,0:T(8,128)(2,1)S(1)}, f32[128,960]{1,0:T(8,128)S(1)}) custom-call(bf16[128,960]{1,0:T(8,128)(2,1)} %multiply_convert_fusion.2.m_ref.refs_4_, f32[128,960]{1,0:T(8,128)S(1)} %get-tuple-element.200.h1_ref, bf16[4,4,4,160,960]{4,3,2,1,0:T(8,128)(2,1)} %bitcast.202, ...), custom_call_target="tpu_custom_call" | custom-call | flops 1887436800 | bytes 14745600 | tf_op jit(solution)/shard_map/pallas_call | solution.py:206
  167.2 3.3 collective-permute-done.6.refs_5_
  171.3 1.2 collective-permute-start.7
  173.5 1.1 dynamic-slice_bitcast_fusion.2
  174.6 9.9 %shard_map.86 = (bf16[4,2,128,640]{3,2,1,0:T(8,128)(2,1)}, f32[128,960]{1,0:T(8,128)S(1)}) custom-call(bf16[128,960]{1,0:T(8,128)(2,1)S(1)} %bitcast.194, f32[4,128,640]{2,1,0:T(8,128)S(1)} %get-tuple-element.83.gate_ref, f32[4,128,640]{2,1,0:T(8,128)S(1)} %get-tuple-element.84.up_ref, bf16[4,4,4,160,960]{4,3,2,1,0:T(8,128)(2,1)} %bitcast.205, ...), custom_call_target="tpu_custom_call" | custom-call | flops 1887436800 | bytes 14745600 | tf_op jit(solution)/shard_map/pallas_call | solution.py:206
  188.7 0.9 constant_dynamic-slice_fusion.6
  191.4 1.5 collective-permute-start.13
  192.9 8.8 %collective-permute-done.13 = bf16[128,960]{1,0:T(8,128)(2,1)S(1)} collective-permute-done((bf16[128,960]{1,0:T(8,128)(2,1)S(1)}, bf16[128,960]{1,0:T(8,128)(2,1)S(1)}, u32[]{:S(2)}, u32[]{:S(2)}) %collective-permute-start.13) | collective-permute-done | bytes 245792 | tf_op jit(solution)/shard_map/ppermute | solution.py:543
  203.4 8.8 %shard_map.87 = (bf16[4,2,128,640]{3,2,1,0:T(8,128)(2,1)S(1)}, f32[128,960]{1,0:T(8,128)S(1)}) custom-call(bf16[128,960]{1,0:T(8,128)(2,1)} %broadcast_select_fusion.eb_ref.refs_4_, f32[4,128,640]{2,1,0:T(8,128)S(1)} %get-tuple-element.83.gate_ref, f32[4,128,640]{2,1,0:T(8,128)S(1)} %get-tuple-element.84.up_ref, bf16[4,4,4,160,960]{4,3,2,1,0:T(8,128)(2,1)} %bitcast.208, ...), custom_call_target="tpu_custom_call" | custom-call | flops 1887436800 | bytes 14745600 | tf_op jit(solution)/shard_map/pallas_call | solution.py:206
  212.9 1.3 collective-permute-start.17
  214.2 2.8 shard_map.88
  217.2 1.6 collective-permute-start.18
  218.8 2.0 fusion.92
  220.8 3.0 fusion.33
  223.9 5.8 %collective-permute-done.17.refs_2_ = bf16[2,2,128,640]{3,2,1,0:T(8,128)(2,1)S(1)} collective-permute-done((bf16[2,2,128,640]{3,2,1,0:T(8,128)(2,1)S(1)}, bf16[2,2,128,640]{3,2,1,0:T(8,128)(2,1)S(1)}, u32[]{:S(2)}, u32[]{:S(2)}) %collective-permute-start.17) | collective-permute-done | bytes 655392 | tf_op jit(solution)/shard_map/ppermute | solution.py:249
  229.6 4.6 %collective-permute-done.18 = bf16[2,160,960]{2,1,0:T(8,128)(2,1)S(1)} collective-permute-done((bf16[2,160,960]{2,1,0:T(8,128)(2,1)S(1)}, bf16[2,160,960]{2,1,0:T(8,128)(2,1)S(1)}, u32[]{:S(2)}, u32[]{:S(2)}) %collective-permute-start.18) | collective-permute-done | bytes 614432 | tf_op jit(solution)/shard_map/ppermute | solution.py:249
  234.3 1.0 pad_maximum_fusion.1
  235.5 1.4 convert_add_fusion.3
  237.0 2.5 collective-permute-start.20
  240.3 1.1 copy-done.11
  241.4 4.3 %shard_map.89 = (f32[2,320,960]{2,1,0:T(8,128)S(1)}, bf16[2,160,960]{2,1,0:T(8,128)(2,1)}, bf16[2,160,960]{2,1,0:T(8,128)(2,1)S(1)}) custom-call(s32[9]{0:T(128)S(1)} %stack.82.refs_0_, bf16[4,2,128,640]{3,2,1,0:T(8,128)(2,1)S(1)} %copy-done.4, bf16[2,2,128,640]{3,2,1,0:T(8,128)(2,1)S(1)} %collective-permute-done.17.refs_2_, ...), custom_call_target="tpu_custom_call" | custom-call | flops 1258291200 | bytes 7208960 | tf_op jit(solution)/shard_map/pallas_call | solution.py:376
  247.6 1.3 collective-permute-start.22
  249.2 5.9 %collective-permute-done.20 = bf16[160,960]{1,0:T(8,128)(2,1)S(1)} collective-permute-done((bf16[160,960]{1,0:T(8,128)(2,1)S(1)}, bf16[160,960]{1,0:T(8,128)(2,1)S(1)}, u32[]{:S(2)}, u32[]{:S(2)}) %collective-permute-start.20) | collective-permute-done | bytes 307232 | tf_op jit(solution)/shard_map/ppermute | solution.py:249
  257.4 1.9 copy.41
  259.2 1.2 collective-permute-start.21
  260.5 3.4 fusion.62
  263.9 1.4 copy.43.refs_1_
  265.3 1.3 collective-permute-start.29
  266.7 2.2 collective-permute-done.21.refs_2_
  268.9 4.8 %collective-permute-done.24 = bf16[2,160,960]{2,1,0:T(8,128)(2,1)} collective-permute-done((bf16[2,160,960]{2,1,0:T(8,128)(2,1)}, bf16[2,160,960]{2,1,0:T(8,128)(2,1)}, u32[]{:S(2)}, u32[]{:S(2)}) %collective-permute-start.24) | collective-permute-done | bytes 614432 | tf_op jit(solution)/shard_map/ppermute | solution.py:249
  273.7 0.9 constant_dynamic-slice_fusion.1
  275.4 1.2 convert_add_fusion.2
  276.7 1.8 collective-permute-start.30
  279.2 1.0 fusion.53
  280.2 2.0 collective-permute-done.26
  282.2 11.2 %collective-permute-done.29 = bf16[2,160,960]{2,1,0:T(8,128)(2,1)S(1)} collective-permute-done((bf16[2,160,960]{2,1,0:T(8,128)(2,1)}, bf16[2,160,960]{2,1,0:T(8,128)(2,1)S(1)}, u32[]{:S(2)}, u32[]{:S(2)}) %collective-permute-start.29) | collective-permute-done | bytes 614432 | tf_op jit(solution)/shard_map/ppermute | solution.py:249
  295.9 1.0 copy-done.13
  296.9 0.9 copy-done.15
  297.9 0.9 copy-done.17
  298.8 0.9 copy-done.23
  299.8 3.6 %shard_map.90 = (f32[2,168,960]{2,1,0:T(8,128)S(1)}, bf16[2,168,960]{2,1,0:T(8,128)(2,1)S(1)}) custom-call(s32[7]{0:T(128)S(1)} %stack.86.refs_0_, bf16[4,1,128,640]{3,2,1,0:T(8,128)(2,1)S(1)} %copy.43.refs_1_, bf16[2,1,128,640]{3,2,1,0:T(8,128)(2,1)} %collective-permute-done.21.refs_2_, bf16[2,1,128,640]{3,2,1,0:T(8,128)(2,1)S(1)} %copy-done.13, ...), custom_call_target="tpu_custom_call" | custom-call | flops 1258291200 | bytes 4096000 | tf_op jit(solution)/shard_map/pallas_call | solution.py:376
  303.4 1.5 collective-permute-start.31
  305.2 2.5 collective-permute-start.32
  307.9 18.4 %collective-permute-done.32 = bf16[160,960]{1,0:T(8,128)(2,1)S(1)} collective-permute-done((bf16[160,960]{1,0:T(8,128)(2,1)S(1)}, bf16[160,960]{1,0:T(8,128)(2,1)S(1)}, u32[]{:S(2)}, u32[]{:S(2)}) %collective-permute-start.32) | collective-permute-done | bytes 307232 | tf_op jit(solution)/shard_map/ppermute | solution.py:249
  327.3 2.7 collective-permute-start.33
  330.1 1.5 maximum_bitcast_fusion
  331.6 12.5 %collective-permute-done.33 = bf16[168,960]{1,0:T(8,128)(2,1)S(1)} collective-permute-done((bf16[168,960]{1,0:T(8,128)(2,1)S(1)}, bf16[168,960]{1,0:T(8,128)(2,1)S(1)}, u32[]{:S(2)}, u32[]{:S(2)}) %collective-permute-start.33) | collective-permute-done | bytes 322592 | tf_op jit(solution)/shard_map/ppermute | solution.py:249
  344.2 0.9 slice_bitcast_fusion
  (323 shorter events, 30.9 us)
Async XLA Ops:
  7.2 114.6 %all-gather.2.cloned.1.call-start = ((), (), s32[]{:S(2)}) async-start(), calls=%async_computation | async-start | bytes 22282240 | tf_op jit(solution)/shard_map/all_gather | solution.py:524
  7.2 10.5 %copy-start = (bf16[1,2,64,960]{3,2,1,0:T(8,128)(2,1)S(1)}, bf16[1,2,64,960]{3,2,1,0:T(8,128)(2,1)}, u32[]{:S(2)}) copy-start(bf16[1,2,64,960]{3,2,1,0:T(8,128)(2,1)} %param.5) | copy-start | bytes 737284
  9.8 1.3 collective-permute-start
  11.2 4.3 %collective-permute-start.1 = (bf16[240]{0:T(256)(128)(2,1)S(1)}, bf16[240]{0:T(256)(128)(2,1)S(1)}, u32[]{:S(2)}, u32[]{:S(2)}) collective-permute-start(bf16[240]{0:T(256)(128)(2,1)S(1)} %pad_maximum_fusion.17), channel_id=1, source_target_pairs={{0,2},{1,3},{2,0},{3,1},{4,6},{5,7},{6,4},{7,5},{8,10},{9,11},{10,... | collective-permute-start | bytes 1448 | tf_op jit(solution)/shard_map/ppermute | solution.py:249
  14.2 173.7 %copy-start.56 = (f32[128,32]{0,1:T(8,128)}, f32[128,32]{0,1:T(8,128)S(1)}, u32[]{:S(2)}) copy-start(f32[128,32]{0,1:T(8,128)S(1)} %get-tuple-element.182) | copy-start | bytes 49156
  15.7 3.6 %collective-permute-start.2 = (bf16[480]{0:T(512)(128)(2,1)S(1)}, bf16[480]{0:T(512)(128)(2,1)S(1)}, u32[]{:S(2)}, u32[]{:S(2)}) collective-permute-start(bf16[480]{0:T(512)(128)(2,1)S(1)} %pad_maximum_fusion.16), channel_id=1, source_target_pairs={{0,4},{1,5},{2,6},{3,7},{4,0},{5,1},{6,2},{7,3},{8,12},{9,13},{10,... | collective-permute-start | bytes 2888 | tf_op jit(solution)/shard_map/ppermute | solution.py:249
  19.5 4.7 %collective-permute-start.3 = (bf16[960]{0:T(1024)(128)(2,1)S(1)}, bf16[960]{0:T(1024)(128)(2,1)S(1)}, u32[]{:S(2)}, u32[]{:S(2)}) collective-permute-start(bf16[960]{0:T(1024)(128)(2,1)S(1)} %pad_maximum_fusion.15), channel_id=1, source_target_pairs={{0,8},{1,9},{2,10},{3,11},{4,12},{5,13},{6,14},{7,15},{8,0},{9,1},... | collective-permute-start | bytes 5768 | tf_op jit(solution)/shard_map/ppermute | solution.py:249
  24.4 123.7 %copy-start.72 = (f32[960]{0:T(1024)}, f32[960]{0:T(1024)S(1)}, u32[]{:S(2)}) copy-start(f32[960]{0:T(1024)S(1)} %get-tuple-element.177) | copy-start | bytes 11524
  24.4 160.3 %copy-start.70 = (f32[960]{0:T(1024)}, f32[960]{0:T(1024)S(1)}, u32[]{:S(2)}) copy-start(f32[960]{0:T(1024)S(1)} %get-tuple-element.176) | copy-start | bytes 11524
  137.9 9.4 %collective-permute-start.4 = (bf16[128,960]{1,0:T(8,128)(2,1)S(1)}, bf16[128,960]{1,0:T(8,128)(2,1)S(1)}, u32[]{:S(2)}, u32[]{:S(2)}) collective-permute-start(bf16[128,960]{1,0:T(8,128)(2,1)S(1)} %convert_element_type.168), channel_id=1, source_target_pairs={{0,16},{1,17},{2,18},{3,19},{4,20},{5,21},{6,22},{7,23},{8,24},{9,... | collective-permute-start | bytes 737288 | tf_op jit(solution)/shard_map/ppermute | solution.py:539
  147.4 6.4 %copy-start.31 = (bf16[128,960]{1,0:T(8,128)(2,1)}, bf16[128,960]{1,0:T(8,128)(2,1)S(1)}, u32[]{:S(2)}) copy-start(bf16[128,960]{1,0:T(8,128)(2,1)S(1)} %get-tuple-element.159) | copy-start | bytes 737284
  151.9 34.3 %copy-start.43 = (bf16[128,320]{0,1:T(8,128)(2,1)}, bf16[128,320]{0,1:T(8,128)(2,1)S(1)}, u32[]{:S(2)}) copy-start(bf16[128,320]{0,1:T(8,128)(2,1)S(1)} %slice.218) | copy-start | bytes 245764
  152.9 33.8 %copy-start.58 = (f32[5,3,128]{2,1,0:T(4,128)}, f32[5,3,128]{2,1,0:T(4,128)S(1)}, u32[]{:S(2)}) copy-start(f32[5,3,128]{2,1,0:T(4,128)S(1)} %log_add_fusion) | copy-start | bytes 23044
  156.0 28.7 %copy-start.76 = (f32[128]{0:T(128)}, f32[128]{0:T(128)S(1)}, u32[]{:S(2)}) copy-start(f32[128]{0:T(128)S(1)} %get-tuple-element.192) | copy-start | bytes 1540
  156.1 28.7 %copy-start.84 = (f32[128]{0:T(128)}, f32[128]{0:T(128)S(1)}, u32[]{:S(2)}) copy-start(f32[128]{0:T(128)S(1)} %get-tuple-element.191) | copy-start | bytes 1540
  156.9 10.3 %collective-permute-start.5 = (bf16[128,960]{1,0:T(8,128)(2,1)}, bf16[128,960]{1,0:T(8,128)(2,1)}, u32[]{:S(2)}, u32[]{:S(2)}) collective-permute-start(bf16[128,960]{1,0:T(8,128)(2,1)} %multiply_convert_fusion.2.m_ref.refs_4_), channel_id=1, source_target_pairs={{0,2},{1,3},{2,0},{3,1},{4,6},{5,7},{6,4},{7,5},{8,10},{9,11},{10,... | collective-permute-start | bytes 737288 | tf_op jit(solution)/shard_map/ppermute | solution.py:249
  158.1 12.4 %collective-permute-start.6 = (bf16[128,960]{1,0:T(8,128)(2,1)}, bf16[128,960]{1,0:T(8,128)(2,1)}, u32[]{:S(2)}, u32[]{:S(2)}) collective-permute-start(bf16[128,960]{1,0:T(8,128)(2,1)} %fusion.58.refs_4_), channel_id=1, source_target_pairs={{0,2},{1,3},{2,0},{3,1},{4,6},{5,7},{6,4},{7,5},{8,10},{9,11},{10,... | collective-permute-start | bytes 737288 | tf_op jit(solution)/shard_map/ppermute | solution.py:249
  171.3 13.3 %collective-permute-start.7 = (bf16[2,1,128,640]{3,2,1,0:T(8,128)(2,1)}, bf16[2,1,128,640]{3,2,1,0:T(8,128)(2,1)}, u32[]{:S(2)}, u32[]{:S(2)}) collective-permute-start(bf16[2,1,128,640]{3,2,1,0:T(8,128)(2,1)} %dynamic-slice_bitcast_fusion.1), channel_id=1, source_target_pairs={{0,2},{1,3},{2,0},{3,1},{4,6},{5,7},{6,4},{7,5},{8,10},{9,11},{10,... | collective-permute-start | bytes 983048 | tf_op jit(solution)/shard_map/ppermute | solution.py:249
  172.5 12.0 %collective-permute-start.8 = (bf16[128,960]{1,0:T(8,128)(2,1)}, bf16[128,960]{1,0:T(8,128)(2,1)S(1)}, u32[]{:S(2)}, u32[]{:S(2)}) collective-permute-start(bf16[128,960]{1,0:T(8,128)(2,1)} %multiply_convert_fusion.2.m_ref.refs_4_), channel_id=1, source_target_pairs={{0,1},{1,0},{2,3},{3,2},{4,5},{5,4},{6,7},{7,6},{8,9},{9,8},{10,11... | collective-permute-start | bytes 737288 | tf_op jit(solution)/shard_map/ppermute | solution.py:249
  172.5 12.0 %collective-permute-start.10 = (bf16[128,960]{1,0:T(8,128)(2,1)}, bf16[128,960]{1,0:T(8,128)(2,1)S(1)}, u32[]{:S(2)}, u32[]{:S(2)}) collective-permute-start(bf16[128,960]{1,0:T(8,128)(2,1)} %fusion.58.refs_4_), channel_id=1, source_target_pairs={{0,1},{1,0},{2,3},{3,2},{4,5},{5,4},{6,7},{7,6},{8,9},{9,8},{10,11... | collective-permute-start | bytes 737288 | tf_op jit(solution)/shard_map/ppermute | solution.py:249
  173.0 11.5 %collective-permute-start.9 = (bf16[128,960]{1,0:T(8,128)(2,1)}, bf16[128,960]{1,0:T(8,128)(2,1)S(1)}, u32[]{:S(2)}, u32[]{:S(2)}) collective-permute-start(bf16[128,960]{1,0:T(8,128)(2,1)} %collective-permute-done.5.refs_5_), channel_id=1, source_target_pairs={{0,1},{1,0},{2,3},{3,2},{4,5},{5,4},{6,7},{7,6},{8,9},{9,8},{10,11... | collective-permute-start | bytes 737288 | tf_op jit(solution)/shard_map/ppermute | solution.py:249
  173.0 11.5 %collective-permute-start.11 = (bf16[128,960]{1,0:T(8,128)(2,1)}, bf16[128,960]{1,0:T(8,128)(2,1)S(1)}, u32[]{:S(2)}, u32[]{:S(2)}) collective-permute-start(bf16[128,960]{1,0:T(8,128)(2,1)} %collective-permute-done.6.refs_5_), channel_id=1, source_target_pairs={{0,1},{1,0},{2,3},{3,2},{4,5},{5,4},{6,7},{7,6},{8,9},{9,8},{10,11... | collective-permute-start | bytes 737288 | tf_op jit(solution)/shard_map/ppermute | solution.py:249
  173.5 11.4 %slice-start = ((s8[5242880]{0:T(1024)(128)(4,1)}), s8[4194304]{0:T(1024)(128)(4,1)S(1)}, s32[]{:S(2)}) async-start(s8[5242880]{0:T(1024)(128)(4,1)} %bitcast.217), calls=%async_computation.1 | async-start | bytes 8388608
  174.6 10.4 %slice-start.1 = ((s8[5242880]{0:T(1024)(128)(4,1)}), s8[1048576]{0:T(1024)(128)(4,1)S(1)}, s32[]{:S(2)}) async-start(s8[5242880]{0:T(1024)(128)(4,1)} %bitcast.217), calls=%async_computation.2 | async-start | bytes 2097152
  189.7 1.7 collective-permute-start.12
  191.4 11.1 %copy-start.7 = (bf16[2,1,128,640]{3,2,1,0:T(8,128)(2,1)}, bf16[2,1,128,640]{3,2,1,0:T(8,128)(2,1)S(1)}, u32[]{:S(2)}) copy-start(bf16[2,1,128,640]{3,2,1,0:T(8,128)(2,1)S(1)} %collective-permute-done.12.refs_3_) | copy-start | bytes 983044
  191.4 10.4 %collective-permute-start.13 = (bf16[128,960]{1,0:T(8,128)(2,1)S(1)}, bf16[128,960]{1,0:T(8,128)(2,1)S(1)}, u32[]{:S(2)}, u32[]{:S(2)}) collective-permute-start(bf16[128,960]{1,0:T(8,128)(2,1)S(1)} %fusion.49), channel_id=1, source_target_pairs={{16,0},{17,1},{18,2},{19,3},{20,4},{21,5},{22,6},{23,7},{24,8},{25... | collective-permute-start | bytes 737288 | tf_op jit(solution)/shard_map/ppermute | solution.py:543
  202.5 9.7 %collective-permute-start.14 = (bf16[128,960]{1,0:T(8,128)(2,1)}, bf16[128,960]{1,0:T(8,128)(2,1)}, u32[]{:S(2)}, u32[]{:S(2)}) collective-permute-start(bf16[128,960]{1,0:T(8,128)(2,1)} %broadcast_select_fusion.eb_ref.refs_4_), channel_id=1, source_target_pairs={{0,2},{1,3},{2,0},{3,1},{4,6},{5,7},{6,4},{7,5},{8,10},{9,11},{10,... | collective-permute-start | bytes 737288 | tf_op jit(solution)/shard_map/ppermute | solution.py:249
  203.3 8.9 %collective-permute-start.15 = (bf16[128,960]{1,0:T(8,128)(2,1)}, bf16[128,960]{1,0:T(8,128)(2,1)}, u32[]{:S(2)}, u32[]{:S(2)}) collective-permute-start(bf16[128,960]{1,0:T(8,128)(2,1)} %broadcast_select_fusion.eb_ref.refs_4_), channel_id=1, source_target_pairs={{0,1},{1,0},{2,3},{3,2},{4,5},{5,4},{6,7},{7,6},{8,9},{9,8},{10,11... | collective-permute-start | bytes 737288 | tf_op jit(solution)/shard_map/ppermute | solution.py:249
  212.2 4.8 %copy-start.3 = (bf16[4,2,128,640]{3,2,1,0:T(8,128)(2,1)}, bf16[4,2,128,640]{3,2,1,0:T(8,128)(2,1)S(1)}, u32[]{:S(2)}) copy-start(bf16[4,2,128,640]{3,2,1,0:T(8,128)(2,1)S(1)} %get-tuple-element.105.refs_1_) | copy-start | bytes 3932164
  212.2 2.0 collective-permute-start.16
  212.9 5.9 %copy-start.85 = (f32[128]{0:T(128)S(1)}, f32[128]{0:T(128)}, u32[]{:S(2)}) copy-start(f32[128]{0:T(128)} %copy-done.84) | copy-start | bytes 1540
  212.9 16.7 %collective-permute-start.17 = (bf16[2,2,128,640]{3,2,1,0:T(8,128)(2,1)S(1)}, bf16[2,2,128,640]{3,2,1,0:T(8,128)(2,1)S(1)}, u32[]{:S(2)}, u32[]{:S(2)}) collective-permute-start(bf16[2,2,128,640]{3,2,1,0:T(8,128)(2,1)S(1)} %dynamic-slice_bitcast_fusion), channel_id=1, source_target_pairs={{0,2},{1,3},{2,0},{3,1},{4,6},{5,7},{6,4},{7,5},{8,10},{9,11},{10,... | collective-permute-start | bytes 1966088 | tf_op jit(solution)/shard_map/ppermute | solution.py:249
  217.2 17.0 %collective-permute-start.18 = (bf16[2,160,960]{2,1,0:T(8,128)(2,1)S(1)}, bf16[2,160,960]{2,1,0:T(8,128)(2,1)S(1)}, u32[]{:S(2)}, u32[]{:S(2)}) collective-permute-start(bf16[2,160,960]{2,1,0:T(8,128)(2,1)S(1)} %get-tuple-element.107), channel_id=1, source_target_pairs={{0,4},{1,5},{2,6},{3,7},{4,0},{5,1},{6,2},{7,3},{8,12},{9,13},{10,... | collective-permute-start | bytes 1843208 | tf_op jit(solution)/shard_map/ppermute | solution.py:249
  235.3 4.1 %collective-permute-start.19 = (bf16[2,2,128,640]{3,2,1,0:T(8,128)(2,1)}, bf16[2,2,128,640]{3,2,1,0:T(8,128)(2,1)S(1)}, u32[]{:S(2)}, u32[]{:S(2)}) collective-permute-start(bf16[2,2,128,640]{3,2,1,0:T(8,128)(2,1)} %pad_maximum_fusion.1), channel_id=1, source_target_pairs={{0,1},{1,0},{2,3},{3,2},{4,5},{5,4},{6,7},{7,6},{8,9},{9,8},{10,11... | collective-permute-start | bytes 1966088 | tf_op jit(solution)/shard_map/ppermute | solution.py:249
  235.5 4.8 %copy-start.4 = (bf16[4,2,128,640]{3,2,1,0:T(8,128)(2,1)S(1)}, bf16[4,2,128,640]{3,2,1,0:T(8,128)(2,1)}, u32[]{:S(2)}) copy-start(bf16[4,2,128,640]{3,2,1,0:T(8,128)(2,1)} %copy-done.3) | copy-start | bytes 3932164
  235.5 4.8 %copy-start.19 = (bf16[128,960]{1,0:T(8,128)(2,1)S(1)}, bf16[128,960]{1,0:T(8,128)(2,1)}, u32[]{:S(2)}) copy-start(bf16[128,960]{1,0:T(8,128)(2,1)} %copy-done.18) | copy-start | bytes 737284
  235.5 4.8 %copy-start.21 = (bf16[128,960]{1,0:T(8,128)(2,1)S(1)}, bf16[128,960]{1,0:T(8,128)(2,1)}, u32[]{:S(2)}) copy-start(bf16[128,960]{1,0:T(8,128)(2,1)} %copy-done.20) | copy-start | bytes 737284
  236.9 8.8 %copy-start.30 = (bf16[5,3,128,128]{2,3,1,0:T(8,128)(2,1)S(1)}, bf16[5,3,128,128]{2,3,1,0:T(8,128)(2,1)}, u32[]{:S(2)}) copy-start(bf16[5,3,128,128]{2,3,1,0:T(8,128)(2,1)} %copy-done.28) | copy-start | bytes 1474564
  236.9 9.1 %copy-start.44 = (bf16[128,320]{0,1:T(8,128)(2,1)S(1)}, bf16[128,320]{0,1:T(8,128)(2,1)}, u32[]{:S(2)}) copy-start(bf16[128,320]{0,1:T(8,128)(2,1)} %copy-done.43) | copy-start | bytes 245764
  236.9 9.1 %copy-start.59 = (f32[5,3,128]{2,1,0:T(4,128)S(1)}, f32[5,3,128]{2,1,0:T(4,128)}, u32[]{:S(2)}) copy-start(f32[5,3,128]{2,1,0:T(4,128)} %copy-done.58) | copy-start | bytes 23044
  237.0 18.1 %collective-permute-start.20 = (bf16[160,960]{1,0:T(8,128)(2,1)S(1)}, bf16[160,960]{1,0:T(8,128)(2,1)S(1)}, u32[]{:S(2)}, u32[]{:S(2)}) collective-permute-start(bf16[160,960]{1,0:T(8,128)(2,1)S(1)} %fusion.71), channel_id=1, source_target_pairs={{0,8},{1,9},{2,10},{3,11},{4,12},{5,13},{6,14},{7,15},{8,0},{9,1},... | collective-permute-start | bytes 921608 | tf_op jit(solution)/shard_map/ppermute | solution.py:249
  241.4 4.7 %copy-start.26 = (f32[5,3,128,128]{2,3,1,0:T(8,128)S(1)}, f32[5,3,128,128]{2,3,1,0:T(8,128)}, u32[]{:S(2)}) copy-start(f32[5,3,128,128]{2,3,1,0:T(8,128)} %copy-done.24) | copy-start | bytes 2949124
  247.4 7.7 %copy-start.41 = (bf16[5,64,3,128]{3,1,2,0:T(8,128)(2,1)S(1)}, bf16[5,64,3,128]{3,1,2,0:T(8,128)(2,1)}, u32[]{:S(2)}) copy-start(bf16[5,64,3,128]{3,1,2,0:T(8,128)(2,1)} %copy-done.40) | copy-start | bytes 737284
  247.6 19.0 %collective-permute-start.22 = (bf16[128,960]{1,0:T(8,128)(2,1)}, bf16[128,960]{1,0:T(8,128)(2,1)}, u32[]{:S(2)}, u32[]{:S(2)}) collective-permute-start(bf16[128,960]{1,0:T(8,128)(2,1)} %get-tuple-element.138.refs_8_), channel_id=1, source_target_pairs={{0,2},{1,3},{2,0},{3,1},{4,6},{5,7},{6,4},{7,5},{8,10},{9,11},{10,... | collective-permute-start | bytes 737288 | tf_op jit(solution)/shard_map/ppermute | solution.py:249
  248.9 17.7 %collective-permute-start.23 = (bf16[128,960]{1,0:T(8,128)(2,1)}, bf16[128,960]{1,0:T(8,128)(2,1)}, u32[]{:S(2)}, u32[]{:S(2)}) collective-permute-start(bf16[128,960]{1,0:T(8,128)(2,1)} %get-tuple-element.138.refs_8_), channel_id=1, source_target_pairs={{0,1},{1,0},{2,3},{3,2},{4,5},{5,4},{6,7},{7,6},{8,9},{9,8},{10,11... | collective-permute-start | bytes 737288 | tf_op jit(solution)/shard_map/ppermute | solution.py:249
  249.1 11.3 %copy-start.33 = (bf16[128,960]{1,0:T(8,128)(2,1)S(1)}, bf16[128,960]{1,0:T(8,128)(2,1)}, u32[]{:S(2)}) copy-start(bf16[128,960]{1,0:T(8,128)(2,1)} %copy-done.31) | copy-start | bytes 737284
  249.1 11.3 %copy-start.74 = (f32[960]{0:T(1024)S(1)}, f32[960]{0:T(1024)}, u32[]{:S(2)}) copy-start(f32[960]{0:T(1024)} %copy-done.72) | copy-start | bytes 11524
  249.1 11.3 %copy-start.80 = (f32[128]{0:T(128)S(1)}, f32[128]{0:T(128)}, u32[]{:S(2)}) copy-start(f32[128]{0:T(128)} %copy-done.78) | copy-start | bytes 1540
  255.8 18.0 %collective-permute-start.24 = (bf16[2,160,960]{2,1,0:T(8,128)(2,1)}, bf16[2,160,960]{2,1,0:T(8,128)(2,1)}, u32[]{:S(2)}, u32[]{:S(2)}) collective-permute-start(bf16[2,160,960]{2,1,0:T(8,128)(2,1)} %get-tuple-element.125), channel_id=1, source_target_pairs={{0,4},{1,5},{2,6},{3,7},{4,0},{5,1},{6,2},{7,3},{8,12},{9,13},{10,... | collective-permute-start | bytes 1843208 | tf_op jit(solution)/shard_map/ppermute | solution.py:249
  259.2 9.7 %collective-permute-start.21 = (bf16[2,1,128,640]{3,2,1,0:T(8,128)(2,1)}, bf16[2,1,128,640]{3,2,1,0:T(8,128)(2,1)}, u32[]{:S(2)}, u32[]{:S(2)}) collective-permute-start(bf16[2,1,128,640]{3,2,1,0:T(8,128)(2,1)} %bitcast.245), channel_id=1, source_target_pairs={{0,2},{1,3},{2,0},{3,1},{4,6},{5,7},{6,4},{7,5},{8,10},{9,11},{10,... | collective-permute-start | bytes 983048 | tf_op jit(solution)/shard_map/ppermute | solution.py:249
  265.3 28.2 %collective-permute-start.29 = (bf16[2,160,960]{2,1,0:T(8,128)(2,1)}, bf16[2,160,960]{2,1,0:T(8,128)(2,1)S(1)}, u32[]{:S(2)}, u32[]{:S(2)}) collective-permute-start(bf16[2,160,960]{2,1,0:T(8,128)(2,1)} %copy-done.9), channel_id=1, source_target_pairs={{0,4},{1,5},{2,6},{3,7},{4,0},{5,1},{6,2},{7,3},{8,12},{9,13},{10,... | collective-permute-start | bytes 1843208 | tf_op jit(solution)/shard_map/ppermute | solution.py:249
  273.7 4.8 %collective-permute-start.25 = (f32[1920]{0:T(1024)S(1)}, f32[1920]{0:T(1024)S(1)}, u32[]{:S(2)}, u32[]{:S(2)}) collective-permute-start(f32[1920]{0:T(1024)S(1)} %pad_maximum_fusion.14), channel_id=1, source_target_pairs={{0,1},{1,0},{2,3},{3,2},{4,5},{5,4},{6,7},{7,6},{8,9},{9,8},{10,11... | collective-permute-start | bytes 23048 | tf_op jit(solution)/shard_map/ppermute | solution.py:249
  274.7 4.5 %copy-start.6 = (f32[128,960]{1,0:T(8,128)S(1)}, f32[128,960]{1,0:T(8,128)}, u32[]{:S(2)}) copy-start(f32[128,960]{1,0:T(8,128)} %copy-done.5) | copy-start | bytes 1474564
  274.7 4.5 %copy-start.34 = (bf16[128,960]{1,0:T(8,128)(2,1)S(1)}, bf16[128,960]{1,0:T(8,128)(2,1)}, u32[]{:S(2)}) copy-start(bf16[128,960]{1,0:T(8,128)(2,1)} %copy-done.31) | copy-start | bytes 737284
  274.8 20.3 %collective-permute-start.28 = (bf16[2,1,128,640]{3,2,1,0:T(8,128)(2,1)S(1)}, bf16[2,1,128,640]{3,2,1,0:T(8,128)(2,1)S(1)}, u32[]{:S(2)}, u32[]{:S(2)}) collective-permute-start(bf16[2,1,128,640]{3,2,1,0:T(8,128)(2,1)S(1)} %pad_maximum_fusion.5), channel_id=1, source_target_pairs={{0,1},{1,0},{2,3},{3,2},{4,5},{5,4},{6,7},{7,6},{8,9},{9,8},{10,11... | collective-permute-start | bytes 983048 | tf_op jit(solution)/shard_map/ppermute | solution.py:249
  276.6 16.8 %copy-start.38 = (f32[2,160,960]{2,1,0:T(8,128)}, f32[2,160,960]{2,1,0:T(8,128)S(1)}, u32[]{:S(2)}) copy-start(f32[2,160,960]{2,1,0:T(8,128)S(1)} %convert_add_fusion.2) | copy-start | bytes 3686404
  276.7 17.5 %collective-permute-start.30 = (bf16[160,960]{1,0:T(8,128)(2,1)S(1)}, bf16[160,960]{1,0:T(8,128)(2,1)S(1)}, u32[]{:S(2)}, u32[]{:S(2)}) collective-permute-start(bf16[160,960]{1,0:T(8,128)(2,1)S(1)} %fusion.72), channel_id=1, source_target_pairs={{0,8},{1,9},{2,10},{3,11},{4,12},{5,13},{6,14},{7,15},{8,0},{9,1},... | collective-permute-start | bytes 921608 | tf_op jit(solution)/shard_map/ppermute | solution.py:249
  278.5 14.9 %collective-permute-start.27 = (bf16[128,960]{1,0:T(8,128)(2,1)}, bf16[128,960]{1,0:T(8,128)(2,1)S(1)}, u32[]{:S(2)}, u32[]{:S(2)}) collective-permute-start(bf16[128,960]{1,0:T(8,128)(2,1)} %collective-permute-done.22.refs_9_), channel_id=1, source_target_pairs={{0,1},{1,0},{2,3},{3,2},{4,5},{5,4},{6,7},{7,6},{8,9},{9,8},{10,11... | collective-permute-start | bytes 737288 | tf_op jit(solution)/shard_map/ppermute | solution.py:249
  278.5 3.7 %collective-permute-start.26 = (f32[1920]{0:T(1024)S(1)}, f32[1920]{0:T(1024)S(1)}, u32[]{:S(2)}, u32[]{:S(2)}) collective-permute-start(f32[1920]{0:T(1024)S(1)} %add.220), channel_id=1, source_target_pairs={{0,2},{1,3},{2,0},{3,1},{4,6},{5,7},{6,4},{7,5},{8,10},{9,11},{10,... | collective-permute-start | bytes 23048 | tf_op jit(solution)/shard_map/ppermute | solution.py:249
  299.8 5.2 %copy-start.53 = (bf16[2,160,960]{2,1,0:T(8,128)(2,1)S(1)}, bf16[2,160,960]{2,1,0:T(8,128)(2,1)}, u32[]{:S(2)}) copy-start(bf16[2,160,960]{2,1,0:T(8,128)(2,1)} %copy-done.52) | copy-start | bytes 1843204
  303.4 23.6 %collective-permute-start.31 = (bf16[2,168,960]{2,1,0:T(8,128)(2,1)S(1)}, bf16[2,168,960]{2,1,0:T(8,128)(2,1)S(1)}, u32[]{:S(2)}, u32[]{:S(2)}) collective-permute-start(bf16[2,168,960]{2,1,0:T(8,128)(2,1)S(1)} %get-tuple-element.144), channel_id=1, source_target_pairs={{0,4},{1,5},{2,6},{3,7},{4,0},{5,1},{6,2},{7,3},{8,12},{9,13},{10,... | collective-permute-start | bytes 1935368 | tf_op jit(solution)/shard_map/ppermute | solution.py:249
  305.2 21.1 %collective-permute-start.32 = (bf16[160,960]{1,0:T(8,128)(2,1)S(1)}, bf16[160,960]{1,0:T(8,128)(2,1)S(1)}, u32[]{:S(2)}, u32[]{:S(2)}) collective-permute-start(bf16[160,960]{1,0:T(8,128)(2,1)S(1)} %fusion.73), channel_id=1, source_target_pairs={{0,8},{1,9},{2,10},{3,11},{4,12},{5,13},{6,14},{7,15},{8,0},{9,1},... | collective-permute-start | bytes 921608 | tf_op jit(solution)/shard_map/ppermute | solution.py:249
  327.3 16.8 %collective-permute-start.33 = (bf16[168,960]{1,0:T(8,128)(2,1)S(1)}, bf16[168,960]{1,0:T(8,128)(2,1)S(1)}, u32[]{:S(2)}, u32[]{:S(2)}) collective-permute-start(bf16[168,960]{1,0:T(8,128)(2,1)S(1)} %fusion.70), channel_id=1, source_target_pairs={{0,8},{1,9},{2,10},{3,11},{4,12},{5,13},{6,14},{7,15},{8,0},{9,1},... | collective-permute-start | bytes 967688 | tf_op jit(solution)/shard_map/ppermute | solution.py:249
  (60 other events, 112.5 us)
Sparse Core Ops, SparseCore 0:
  10.2 111.5 all-gather.1

commit v12 on v11

--- a/solution.py
+++ b/solution.py
@@ -213,7 +213,7 @@
         out_shape=[jax.ShapeDtypeStruct((steps, *shape), t) for shape, t in out_blocks]
         + [jax.ShapeDtypeStruct((tokens, width), f32)],
         compiler_params=pltpu.CompilerParams(
-            dimension_semantics=("arbitrary",), vmem_limit_bytes=40 * 1024 * 1024
+            dimension_semantics=("arbitrary",), vmem_limit_bytes=60 * 1024 * 1024
         ),
         cost_estimate=pl.CostEstimate(
             flops=6 * tokens * steps * cols * width,
@@ -384,7 +384,7 @@
         ),
         out_shape=shapes,
         compiler_params=pltpu.CompilerParams(
-            dimension_semantics=("arbitrary",), vmem_limit_bytes=32 * 1024 * 1024
+            dimension_semantics=("arbitrary",), vmem_limit_bytes=60 * 1024 * 1024
         ),
         cost_estimate=pl.CostEstimate(
             flops=8 * tokens * kinds * width_cols * width * len(rows),
@@ -473,11 +473,6 @@
     gain_grad = gain_grad + flip(gain_grad, Y_BIT)
     dz_all = (dz, dz_y, dz_c, flip(dz_y, CORE_BIT))
     attn_c = cols_core(attn_cols, attn_y, y, core)
-    gain_grad, dz_all, attn_c, both_own, up_received, gate_received = tie(
-        (gain_grad, dz_all, attn_c, both_own, up_received, gate_received)
-    )
-    up, up_send = pair_middle(both_own[:, share:], up_received, z2)
-    up_received = flip(up_send, Z2_BIT)
     gain_rows = at(gain_grad.reshape(4, 4, -1).transpose(1, 0, 2), y * 2 + core)[:, None]
     gain_share = gain_rows.shape[-1]
     gain_rows = jnp.pad(gain_rows, ((0, 0), (0, EXTRA_ROWS - 1), (0, width - gain_share)))
@@ -492,6 +487,11 @@
         (qkv_owners // 4, -(-qkv_owners // 4)),
         gain_rows,
     )
+    attn_own, attn_send, both_own, up_received, gate_received = tie(
+        (attn_own, attn_send, both_own, up_received, gate_received)
+    )
+    up, up_send = pair_middle(both_own[:, share:], up_received, z2)
+    up_received = flip(up_send, Z2_BIT)
     attn_received = flip(attn_send, Z1_BIT)
     attn_own, attn_received, up_received = tie((attn_own, attn_received, up_received))
     attn, attn_send = pair_middle(attn_own, attn_received, z2)

time: 353 us -> 361 us (1.023)
  Pallas kernels: 47.3 us -> 56.9 us
    unnamed x178 -> x118, local copies, waits for them, and re-layouts: 11.1 us -> 2.87 us
    pallas_call x3, Pallas kernels: 10.7 us -> 16.3 us  [plane_product(): pl.pallas_call(kernel, grid_spec=pltpu.PrefetchScalarGridSpec(num_scalar_...]
    pallas_call x4, Pallas kernels: 36.6 us -> 40.6 us  [ffn_call(): pl.pallas_call(kernel, grid=(steps,), in_specs=[whole] * len(wholes) + [b...]
  transfers between devices with their start and end apart: 35 -> 35, of which waited for: 19 -> 19; matrix products, arithmetic and copies ran while one was open for 7% -> 8% of each run, Pallas kernels for 10% -> 13%
where the time goes in v12:
time: 361 us; the launch traced here: 360 us
  waiting for transfers between devices  187 us (52%)
  Pallas kernels  56.9 us (16%)
  starting transfers between devices  38.7 us (11%)
  other arithmetic  22.2 us (6%)
  local copies, waits for them, and re-layouts  21.9 us (6%)
  matrix products  18.6 us (5%)
  between operations  15.3 us (4%)
    all_gather x1, waiting for transfers between devices, local(): lax.all_gather(own, 'dp', axis=0, tiled=True).reshape(4, 4, 4, share, width)  97.3 us
    ppermute x32, waiting for transfers between devices, flip(): return lax.ppermute(x, 'dp', [(i, i ^ bit) for i in range(size)])  74.7 us
    pallas_call x4, Pallas kernels, ffn_call(): pl.pallas_call(kernel, grid=(steps,), in_specs=[whole] * len(wholes) + [b...  40.6 us
    ppermute x32, starting transfers between devices, flip(): return lax.ppermute(x, 'dp', [(i, i ^ bit) for i in range(size)])  33.6 us
    pallas_call x3, Pallas kernels, plane_product(): pl.pallas_call(kernel, grid_spec=pltpu.PrefetchScalarGridSpec(num_scalar_...  16.3 us
    ppermute x1, waiting for transfers between devices, local(): received = lax.ppermute(first_grad, 'section', [(1, 0)])  8.84 us
    dot_general x4, matrix products, dot_nt(): lax.dot_general(a, b, (((1,), (1,)), ((), ())), preferred_element_type=f32)  8.7 us
  transfers between devices with their start and end apart: 35, of which 19 were waited for; matrix products, arithmetic and copies ran while one was open for 8% of the time, Pallas kernels for 13%

profile of v12, /device:TPU:0, one launch (start us, length us, event | category | flops | bytes accessed | tf_op | source)
XLA Modules:
  0.0 360.2 jit_solution(16578350324842434420)
XLA Ops:
  7.2 2.5 pad_maximum_fusion
  11.2 2.8 collective-permute-start.1
  14.2 1.3 collective-permute-done.1
  15.7 2.1 collective-permute-start.2
  17.9 1.4 collective-permute-done.2
  19.5 3.0 collective-permute-start.3
  22.8 1.3 collective-permute-done.3
  24.4 97.3 %all-gather.2.cloned.1.call-done = bf16[10240,960]{1,0:T(8,128)(2,1)} async-done(((bf16[640,960]{1,0:T(8,128)(2,1)}), bf16[10240,960]{1,0:T(8,128)(2,1)}) %all-gather.2.cloned.1.call-update) | async-done | bytes 19660816 | tf_op jit(solution)/shard_map/all_gather | solution.py:524
  121.8 3.4 slice.127
  125.2 1.1 fusion.6
  129.0 10.0 %shard_map.84 = (f32[4,128,640]{2,1,0:T(8,128)}, f32[4,128,640]{2,1,0:T(8,128)}, bf16[4,128,640]{2,1,0:T(8,128)(2,1)}, f32[128,960]{1,0:T(8,128)}) custom-call(bf16[128,960]{1,0:T(8,128)(2,1)} %multiply_convert_fusion.3.m_ref, f32[128,960]{1,0:T(8,128)} %copy-done.5, bf16[4,4,4,160,960]{4,3,2,1,0:T(8,128)(2,1)} %bitcast.193, ...), custom_call_target="tpu_custom_call" | custom-call | flops 1887436800 | bytes 14745600 | tf_op jit(solution)/shard_map/pallas_call | solution.py:206
  139.0 1.1 convert_element_type.168
  140.0 3.6 collective-permute-start.4
  143.6 5.8 %collective-permute-done.4 = bf16[128,960]{1,0:T(8,128)(2,1)S(1)} collective-permute-done((bf16[128,960]{1,0:T(8,128)(2,1)S(1)}, bf16[128,960]{1,0:T(8,128)(2,1)S(1)}, u32[]{:S(2)}, u32[]{:S(2)}) %collective-permute-start.4) | collective-permute-done | bytes 245792 | tf_op jit(solution)/shard_map/ppermute | solution.py:539
  150.9 3.0 fusion.4
  155.2 2.1 multiply_reduce_fusion.5
  157.5 1.3 collective-permute-start.5
  159.6 10.0 %shard_map.85 = (f32[4,128,640]{2,1,0:T(8,128)}, f32[4,128,640]{2,1,0:T(8,128)}, bf16[4,128,640]{2,1,0:T(8,128)(2,1)}, f32[128,960]{1,0:T(8,128)}) custom-call(bf16[128,960]{1,0:T(8,128)(2,1)} %copy-done.18, f32[128,960]{1,0:T(8,128)} %copy-done, bf16[4,4,4,160,960]{4,3,2,1,0:T(8,128)(2,1)} %bitcast.196, bf16[4,4,4,160,960]{4,3,2,1,0:T(8,128)(2,1)} %bitcast.197, ...), custom_call_target="tpu_custom_call" | custom-call | flops 1887436800 | bytes 14745600 | tf_op jit(solution)/shard_map/pallas_call | solution.py:206
  169.6 1.4 collective-permute-done.6.refs_5_
  170.9 1.7 dynamic-slice_bitcast_fusion.1
  172.7 1.2 collective-permute-start.7
  174.9 0.9 dynamic-slice_bitcast_fusion.2
  175.9 10.3 %shard_map.86 = (bf16[4,2,128,640]{3,2,1,0:T(8,128)(2,1)}, f32[128,960]{1,0:T(8,128)}) custom-call(bf16[128,960]{1,0:T(8,128)(2,1)} %bitcast.215, f32[4,128,640]{2,1,0:T(8,128)} %get-tuple-element.79.gate_ref, f32[4,128,640]{2,1,0:T(8,128)} %get-tuple-element.80.up_ref, bf16[4,4,4,160,960]{4,3,2,1,0:T(8,128)(2,1)} %bitcast.199, ...), custom_call_target="tpu_custom_call" | custom-call | flops 1887436800 | bytes 14745600 | tf_op jit(solution)/shard_map/pallas_call | solution.py:206
  186.3 1.4 multiply_reduce_fusion.4
  187.8 1.4 convert_add_fusion.5
  189.1 2.2 fusion.30
  195.0 1.5 collective-permute-start.13
  196.6 8.8 %collective-permute-done.13 = bf16[128,960]{1,0:T(8,128)(2,1)S(1)} collective-permute-done((bf16[128,960]{1,0:T(8,128)(2,1)S(1)}, bf16[128,960]{1,0:T(8,128)(2,1)S(1)}, u32[]{:S(2)}, u32[]{:S(2)}) %collective-permute-start.13) | collective-permute-done | bytes 245792 | tf_op jit(solution)/shard_map/ppermute | solution.py:543
  207.0 10.3 %shard_map.87 = (bf16[4,2,128,640]{3,2,1,0:T(8,128)(2,1)}, f32[128,960]{1,0:T(8,128)}) custom-call(bf16[128,960]{1,0:T(8,128)(2,1)} %copy-done.6, f32[4,128,640]{2,1,0:T(8,128)} %get-tuple-element.79.gate_ref, f32[4,128,640]{2,1,0:T(8,128)} %get-tuple-element.80.up_ref, bf16[4,4,4,160,960]{4,3,2,1,0:T(8,128)(2,1)} %bitcast.202, ...), custom_call_target="tpu_custom_call" | custom-call | flops 1887436800 | bytes 14745600 | tf_op jit(solution)/shard_map/pallas_call | solution.py:206
  218.1 2.1 dynamic-slice_bitcast_fusion
  220.2 1.2 collective-permute-start.17
  221.4 1.7 constant_dynamic-slice_fusion.5
  223.9 4.5 %shard_map.88 = (f32[2,160,960]{2,1,0:T(8,128)}, bf16[2,160,960]{2,1,0:T(8,128)(2,1)}) custom-call(s32[7]{0:T(128)} %stack.81.refs_0_, bf16[4,1,128,640]{3,2,1,0:T(8,128)(2,1)} %bitcast.225, bf16[2,1,128,640]{3,2,1,0:T(8,128)(2,1)} %copy-done.19, bf16[2,1,128,640]{3,2,1,0:T(8,128)(2,1)} %copy-done.32, bf16[128,960]{1,0:T(8,128)(2,1)} %copy-done.6, ...), custom_call_target="tpu_custom_call" | custom-call | flops 629145600 | bytes 4096000 | tf_op jit(solution)/shard_map/pallas_call | solution.py:376
  229.1 1.5 collective-permute-start.18
  230.8 2.3 fusion.33
  233.2 4.5 %collective-permute-done.17.refs_2_ = bf16[2,2,128,640]{3,2,1,0:T(8,128)(2,1)} collective-permute-done((bf16[2,2,128,640]{3,2,1,0:T(8,128)(2,1)}, bf16[2,2,128,640]{3,2,1,0:T(8,128)(2,1)}, u32[]{:S(2)}, u32[]{:S(2)}) %collective-permute-start.17) | collective-permute-done | bytes 655392 | tf_op jit(solution)/shard_map/ppermute | solution.py:249
  237.6 8.5 %collective-permute-done.18 = bf16[2,160,960]{2,1,0:T(8,128)(2,1)S(1)} collective-permute-done((bf16[2,160,960]{2,1,0:T(8,128)(2,1)}, bf16[2,160,960]{2,1,0:T(8,128)(2,1)S(1)}, u32[]{:S(2)}, u32[]{:S(2)}) %collective-permute-start.18) | collective-permute-done | bytes 614432 | tf_op jit(solution)/shard_map/ppermute | solution.py:249
  246.2 1.2 constant_dynamic-slice_fusion.4
  247.4 0.9 pad_maximum_fusion.1
  249.6 1.6 convert_add_fusion.3
  251.3 1.1 copy-done.8
  252.4 2.5 collective-permute-start.20
  254.9 6.2 %shard_map.89 = (f32[2,320,960]{2,1,0:T(8,128)}, bf16[2,160,960]{2,1,0:T(8,128)(2,1)}, bf16[2,160,960]{2,1,0:T(8,128)(2,1)}) custom-call(s32[9]{0:T(128)} %stack.82.refs_0_, bf16[4,2,128,640]{3,2,1,0:T(8,128)(2,1)} %get-tuple-element.101.refs_1_, bf16[2,2,128,640]{3,2,1,0:T(8,128)(2,1)} %collective-permute-done.17.refs_2_, ...), custom_call_target="tpu_custom_call" | custom-call | flops 1258291200 | bytes 7208960 | tf_op jit(solution)/shard_map/pallas_call | solution.py:376
  263.9 6.7 %collective-permute-done.20 = bf16[160,960]{1,0:T(8,128)(2,1)} collective-permute-done((bf16[160,960]{1,0:T(8,128)(2,1)S(1)}, bf16[160,960]{1,0:T(8,128)(2,1)}, u32[]{:S(2)}, u32[]{:S(2)}) %collective-permute-start.20) | collective-permute-done | bytes 307232 | tf_op jit(solution)/shard_map/ppermute | solution.py:249
  270.8 1.1 copy.43.refs_1_
  273.3 0.9 constant_dynamic-slice_fusion.2
  274.3 1.7 collective-permute-start.29
  276.0 2.7 fusion.62
  278.8 2.6 collective-permute-done.21.refs_2_
  281.5 9.3 %collective-permute-done.24 = bf16[2,160,960]{2,1,0:T(8,128)(2,1)S(1)} collective-permute-done((bf16[2,160,960]{2,1,0:T(8,128)(2,1)}, bf16[2,160,960]{2,1,0:T(8,128)(2,1)S(1)}, u32[]{:S(2)}, u32[]{:S(2)}) %collective-permute-start.24) | collective-permute-done | bytes 614432 | tf_op jit(solution)/shard_map/ppermute | solution.py:249
  292.6 1.8 collective-permute-start.30
  295.0 1.0 fusion.53
  295.9 2.0 collective-permute-done.28
  298.8 5.6 %shard_map.90 = (f32[2,168,960]{2,1,0:T(8,128)}, bf16[2,168,960]{2,1,0:T(8,128)(2,1)}) custom-call(s32[7]{0:T(128)} %stack.86.refs_0_, bf16[4,1,128,640]{3,2,1,0:T(8,128)(2,1)} %copy.43.refs_1_, bf16[2,1,128,640]{3,2,1,0:T(8,128)(2,1)} %copy-done.40, bf16[2,1,128,640]{3,2,1,0:T(8,128)(2,1)} %collective-permute-done.25.refs_3_, ...), custom_call_target="tpu_custom_call" | custom-call | flops 1258291200 | bytes 4096000 | tf_op jit(solution)/shard_map/pallas_call | solution.py:376
  304.4 5.9 %collective-permute-done.29 = bf16[2,160,960]{2,1,0:T(8,128)(2,1)S(1)} collective-permute-done((bf16[2,160,960]{2,1,0:T(8,128)(2,1)}, bf16[2,160,960]{2,1,0:T(8,128)(2,1)S(1)}, u32[]{:S(2)}, u32[]{:S(2)}) %collective-permute-start.29) | collective-permute-done | bytes 614432 | tf_op jit(solution)/shard_map/ppermute | solution.py:249
  310.3 2.5 collective-permute-start.31
  312.8 1.5 convert_add_fusion.1
  314.3 2.0 collective-permute-start.32
  316.4 1.1 fusion.42
  317.4 1.0 fusion.44
  318.5 15.5 %collective-permute-done.32 = bf16[160,960]{1,0:T(8,128)(2,1)S(1)} collective-permute-done((bf16[160,960]{1,0:T(8,128)(2,1)S(1)}, bf16[160,960]{1,0:T(8,128)(2,1)S(1)}, u32[]{:S(2)}, u32[]{:S(2)}) %collective-permute-start.32) | collective-permute-done | bytes 307232 | tf_op jit(solution)/shard_map/ppermute | solution.py:249
  335.1 2.7 collective-permute-start.33
  337.9 1.5 maximum_bitcast_fusion
  339.4 12.5 %collective-permute-done.33 = bf16[168,960]{1,0:T(8,128)(2,1)S(1)} collective-permute-done((bf16[168,960]{1,0:T(8,128)(2,1)S(1)}, bf16[168,960]{1,0:T(8,128)(2,1)S(1)}, u32[]{:S(2)}, u32[]{:S(2)}) %collective-permute-start.33) | collective-permute-done | bytes 322592 | tf_op jit(solution)/shard_map/ppermute | solution.py:249
  (263 shorter events, 28.8 us)
Async XLA Ops:
  7.2 114.6 %all-gather.2.cloned.1.call-start = ((), (), s32[]{:S(2)}) async-start(), calls=%async_computation | async-start | bytes 22282240 | tf_op jit(solution)/shard_map/all_gather | solution.py:524
  7.2 10.5 %copy-start.3 = (bf16[1,2,64,960]{3,2,1,0:T(8,128)(2,1)S(1)}, bf16[1,2,64,960]{3,2,1,0:T(8,128)(2,1)}, u32[]{:S(2)}) copy-start(bf16[1,2,64,960]{3,2,1,0:T(8,128)(2,1)} %param.5) | copy-start | bytes 737284
  9.8 1.3 collective-permute-start
  11.2 4.3 %collective-permute-start.1 = (bf16[240]{0:T(256)(128)(2,1)S(1)}, bf16[240]{0:T(256)(128)(2,1)S(1)}, u32[]{:S(2)}, u32[]{:S(2)}) collective-permute-start(bf16[240]{0:T(256)(128)(2,1)S(1)} %pad_maximum_fusion.17), channel_id=1, source_target_pairs={{0,2},{1,3},{2,0},{3,1},{4,6},{5,7},{6,4},{7,5},{8,10},{9,11},{10,... | collective-permute-start | bytes 1448 | tf_op jit(solution)/shard_map/ppermute | solution.py:249
  14.2 179.0 %copy-start.13 = (f32[128,32]{0,1:T(8,128)}, f32[128,32]{0,1:T(8,128)S(1)}, u32[]{:S(2)}) copy-start(f32[128,32]{0,1:T(8,128)S(1)} %get-tuple-element.176) | copy-start | bytes 49156
  14.2 179.0 %copy-start.22 = (f32[128,32]{0,1:T(8,128)}, f32[128,32]{0,1:T(8,128)S(1)}, u32[]{:S(2)}) copy-start(f32[128,32]{0,1:T(8,128)S(1)} %get-tuple-element.174) | copy-start | bytes 49156
  15.7 3.6 %collective-permute-start.2 = (bf16[480]{0:T(512)(128)(2,1)S(1)}, bf16[480]{0:T(512)(128)(2,1)S(1)}, u32[]{:S(2)}, u32[]{:S(2)}) collective-permute-start(bf16[480]{0:T(512)(128)(2,1)S(1)} %pad_maximum_fusion.16), channel_id=1, source_target_pairs={{0,4},{1,5},{2,6},{3,7},{4,0},{5,1},{6,2},{7,3},{8,12},{9,13},{10,... | collective-permute-start | bytes 2888 | tf_op jit(solution)/shard_map/ppermute | solution.py:249
  19.5 4.7 %collective-permute-start.3 = (bf16[960]{0:T(1024)(128)(2,1)S(1)}, bf16[960]{0:T(1024)(128)(2,1)S(1)}, u32[]{:S(2)}, u32[]{:S(2)}) collective-permute-start(bf16[960]{0:T(1024)(128)(2,1)S(1)} %pad_maximum_fusion.15), channel_id=1, source_target_pairs={{0,8},{1,9},{2,10},{3,11},{4,12},{5,13},{6,14},{7,15},{8,0},{9,1},... | collective-permute-start | bytes 5768 | tf_op jit(solution)/shard_map/ppermute | solution.py:249
  24.4 163.3 %copy-start.38 = (f32[960]{0:T(1024)}, f32[960]{0:T(1024)S(1)}, u32[]{:S(2)}) copy-start(f32[960]{0:T(1024)S(1)} %get-tuple-element.168) | copy-start | bytes 11524
  24.4 169.1 %copy-start.41 = (f32[960]{0:T(1024)}, f32[960]{0:T(1024)S(1)}, u32[]{:S(2)}) copy-start(f32[960]{0:T(1024)S(1)} %get-tuple-element.169) | copy-start | bytes 11524
  140.0 9.4 %collective-permute-start.4 = (bf16[128,960]{1,0:T(8,128)(2,1)S(1)}, bf16[128,960]{1,0:T(8,128)(2,1)S(1)}, u32[]{:S(2)}, u32[]{:S(2)}) collective-permute-start(bf16[128,960]{1,0:T(8,128)(2,1)S(1)} %convert_element_type.168), channel_id=1, source_target_pairs={{0,16},{1,17},{2,18},{3,19},{4,20},{5,21},{6,22},{7,23},{8,24},{9,... | collective-permute-start | bytes 737288 | tf_op jit(solution)/shard_map/ppermute | solution.py:539
  154.0 37.7 %copy-start.15 = (bf16[128,320]{0,1:T(8,128)(2,1)}, bf16[128,320]{0,1:T(8,128)(2,1)S(1)}, u32[]{:S(2)}) copy-start(bf16[128,320]{0,1:T(8,128)(2,1)S(1)} %slice.218) | copy-start | bytes 245764
  154.8 37.3 %copy-start.24 = (f32[5,3,128]{2,1,0:T(4,128)}, f32[5,3,128]{2,1,0:T(4,128)S(1)}, u32[]{:S(2)}) copy-start(f32[5,3,128]{2,1,0:T(4,128)S(1)} %log_add_fusion) | copy-start | bytes 23044
  157.3 30.4 %copy-start.45 = (f32[128]{0:T(128)}, f32[128]{0:T(128)S(1)}, u32[]{:S(2)}) copy-start(f32[128]{0:T(128)S(1)} %get-tuple-element.184) | copy-start | bytes 1540
  157.4 30.4 %copy-start.52 = (f32[128]{0:T(128)}, f32[128]{0:T(128)S(1)}, u32[]{:S(2)}) copy-start(f32[128]{0:T(128)S(1)} %get-tuple-element.183) | copy-start | bytes 1540
  157.5 12.1 %collective-permute-start.5 = (bf16[128,960]{1,0:T(8,128)(2,1)S(1)}, bf16[128,960]{1,0:T(8,128)(2,1)}, u32[]{:S(2)}, u32[]{:S(2)}) collective-permute-start(bf16[128,960]{1,0:T(8,128)(2,1)S(1)} %multiply_convert_fusion.2.m_ref.refs_4_), channel_id=1, source_target_pairs={{0,2},{1,3},{2,0},{3,1},{4,6},{5,7},{6,4},{7,5},{8,10},{9,11},{10,... | collective-permute-start | bytes 737288 | tf_op jit(solution)/shard_map/ppermute | solution.py:249
  158.8 12.1 %collective-permute-start.6 = (bf16[128,960]{1,0:T(8,128)(2,1)}, bf16[128,960]{1,0:T(8,128)(2,1)}, u32[]{:S(2)}, u32[]{:S(2)}) collective-permute-start(bf16[128,960]{1,0:T(8,128)(2,1)} %fusion.58.refs_4_), channel_id=1, source_target_pairs={{0,2},{1,3},{2,0},{3,1},{4,6},{5,7},{6,4},{7,5},{8,10},{9,11},{10,... | collective-permute-start | bytes 737288 | tf_op jit(solution)/shard_map/ppermute | solution.py:249
  172.7 13.6 %collective-permute-start.7 = (bf16[2,1,128,640]{3,2,1,0:T(8,128)(2,1)}, bf16[2,1,128,640]{3,2,1,0:T(8,128)(2,1)S(1)}, u32[]{:S(2)}, u32[]{:S(2)}) collective-permute-start(bf16[2,1,128,640]{3,2,1,0:T(8,128)(2,1)} %dynamic-slice_bitcast_fusion.1), channel_id=1, source_target_pairs={{0,2},{1,3},{2,0},{3,1},{4,6},{5,7},{6,4},{7,5},{8,10},{9,11},{10,... | collective-permute-start | bytes 983048 | tf_op jit(solution)/shard_map/ppermute | solution.py:249
  173.9 12.3 %collective-permute-start.8 = (bf16[128,960]{1,0:T(8,128)(2,1)}, bf16[128,960]{1,0:T(8,128)(2,1)}, u32[]{:S(2)}, u32[]{:S(2)}) collective-permute-start(bf16[128,960]{1,0:T(8,128)(2,1)} %copy-done.18), channel_id=1, source_target_pairs={{0,1},{1,0},{2,3},{3,2},{4,5},{5,4},{6,7},{7,6},{8,9},{9,8},{10,11... | collective-permute-start | bytes 737288 | tf_op jit(solution)/shard_map/ppermute | solution.py:249
  173.9 12.3 %collective-permute-start.10 = (bf16[128,960]{1,0:T(8,128)(2,1)}, bf16[128,960]{1,0:T(8,128)(2,1)S(1)}, u32[]{:S(2)}, u32[]{:S(2)}) collective-permute-start(bf16[128,960]{1,0:T(8,128)(2,1)} %fusion.58.refs_4_), channel_id=1, source_target_pairs={{0,1},{1,0},{2,3},{3,2},{4,5},{5,4},{6,7},{7,6},{8,9},{9,8},{10,11... | collective-permute-start | bytes 737288 | tf_op jit(solution)/shard_map/ppermute | solution.py:249
  174.4 11.8 %collective-permute-start.9 = (bf16[128,960]{1,0:T(8,128)(2,1)}, bf16[128,960]{1,0:T(8,128)(2,1)}, u32[]{:S(2)}, u32[]{:S(2)}) collective-permute-start(bf16[128,960]{1,0:T(8,128)(2,1)} %collective-permute-done.5.refs_5_), channel_id=1, source_target_pairs={{0,1},{1,0},{2,3},{3,2},{4,5},{5,4},{6,7},{7,6},{8,9},{9,8},{10,11... | collective-permute-start | bytes 737288 | tf_op jit(solution)/shard_map/ppermute | solution.py:249
  174.4 11.8 %collective-permute-start.11 = (bf16[128,960]{1,0:T(8,128)(2,1)}, bf16[128,960]{1,0:T(8,128)(2,1)}, u32[]{:S(2)}, u32[]{:S(2)}) collective-permute-start(bf16[128,960]{1,0:T(8,128)(2,1)} %collective-permute-done.6.refs_5_), channel_id=1, source_target_pairs={{0,1},{1,0},{2,3},{3,2},{4,5},{5,4},{6,7},{7,6},{8,9},{9,8},{10,11... | collective-permute-start | bytes 737288 | tf_op jit(solution)/shard_map/ppermute | solution.py:249
  175.9 10.4 %copy-start.1 = (f32[128,960]{1,0:T(8,128)S(1)}, f32[128,960]{1,0:T(8,128)}, u32[]{:S(2)}) copy-start(f32[128,960]{1,0:T(8,128)} %copy-done) | copy-start | bytes 1474564
  175.9 11.9 %copy-start.4 = (bf16[1,2,64,960]{3,2,1,0:T(8,128)(2,1)S(1)}, bf16[1,2,64,960]{3,2,1,0:T(8,128)(2,1)}, u32[]{:S(2)}) copy-start(bf16[1,2,64,960]{3,2,1,0:T(8,128)(2,1)} %param.5) | copy-start | bytes 737284
  186.3 7.0 %copy-start.19 = (bf16[2,1,128,640]{3,2,1,0:T(8,128)(2,1)}, bf16[2,1,128,640]{3,2,1,0:T(8,128)(2,1)S(1)}, u32[]{:S(2)}) copy-start(bf16[2,1,128,640]{3,2,1,0:T(8,128)(2,1)S(1)} %collective-permute-done.7.refs_2_) | copy-start | bytes 983044
  186.3 7.2 %slice-start = ((s8[5242880]{0:T(1024)(128)(4,1)}), s8[4194304]{0:T(1024)(128)(4,1)S(1)}, s32[]{:S(2)}) async-start(s8[5242880]{0:T(1024)(128)(4,1)} %bitcast.212), calls=%async_computation.1 | async-start | bytes 8388608
  193.4 1.7 collective-permute-start.12
  195.0 10.4 %copy-start.32 = (bf16[2,1,128,640]{3,2,1,0:T(8,128)(2,1)}, bf16[2,1,128,640]{3,2,1,0:T(8,128)(2,1)S(1)}, u32[]{:S(2)}) copy-start(bf16[2,1,128,640]{3,2,1,0:T(8,128)(2,1)S(1)} %collective-permute-done.12.refs_3_) | copy-start | bytes 983044
  195.0 10.4 %collective-permute-start.13 = (bf16[128,960]{1,0:T(8,128)(2,1)S(1)}, bf16[128,960]{1,0:T(8,128)(2,1)S(1)}, u32[]{:S(2)}, u32[]{:S(2)}) collective-permute-start(bf16[128,960]{1,0:T(8,128)(2,1)S(1)} %fusion.49), channel_id=1, source_target_pairs={{16,0},{17,1},{18,2},{19,3},{20,4},{21,5},{22,6},{23,7},{24,8},{25... | collective-permute-start | bytes 737288 | tf_op jit(solution)/shard_map/ppermute | solution.py:543
  205.5 11.9 %collective-permute-start.14 = (bf16[128,960]{1,0:T(8,128)(2,1)S(1)}, bf16[128,960]{1,0:T(8,128)(2,1)S(1)}, u32[]{:S(2)}, u32[]{:S(2)}) collective-permute-start(bf16[128,960]{1,0:T(8,128)(2,1)S(1)} %broadcast_select_fusion.eb_ref.refs_4_), channel_id=1, source_target_pairs={{0,2},{1,3},{2,0},{3,1},{4,6},{5,7},{6,4},{7,5},{8,10},{9,11},{10,... | collective-permute-start | bytes 737288 | tf_op jit(solution)/shard_map/ppermute | solution.py:249
  206.3 11.0 %collective-permute-start.15 = (bf16[128,960]{1,0:T(8,128)(2,1)S(1)}, bf16[128,960]{1,0:T(8,128)(2,1)S(1)}, u32[]{:S(2)}, u32[]{:S(2)}) collective-permute-start(bf16[128,960]{1,0:T(8,128)(2,1)S(1)} %broadcast_select_fusion.eb_ref.refs_4_), channel_id=1, source_target_pairs={{0,1},{1,0},{2,3},{3,2},{4,5},{5,4},{6,7},{7,6},{8,9},{9,8},{10,11... | collective-permute-start | bytes 737288 | tf_op jit(solution)/shard_map/ppermute | solution.py:249
  217.3 5.8 %copy-start.35 = (bf16[128,960]{1,0:T(8,128)(2,1)}, bf16[128,960]{1,0:T(8,128)(2,1)S(1)}, u32[]{:S(2)}) copy-start(bf16[128,960]{1,0:T(8,128)(2,1)S(1)} %collective-permute-done.14.refs_5_) | copy-start | bytes 737284
  217.4 5.8 %collective-permute-start.16 = (bf16[128,960]{1,0:T(8,128)(2,1)S(1)}, bf16[128,960]{1,0:T(8,128)(2,1)S(1)}, u32[]{:S(2)}, u32[]{:S(2)}) collective-permute-start(bf16[128,960]{1,0:T(8,128)(2,1)S(1)} %collective-permute-done.14.refs_5_), channel_id=1, source_target_pairs={{0,1},{1,0},{2,3},{3,2},{4,5},{5,4},{6,7},{7,6},{8,9},{9,8},{10,11... | collective-permute-start | bytes 737288 | tf_op jit(solution)/shard_map/ppermute | solution.py:249
  218.1 10.2 %copy-start.11 = (f32[128,960]{1,0:T(8,128)S(1)}, f32[128,960]{1,0:T(8,128)}, u32[]{:S(2)}) copy-start(f32[128,960]{1,0:T(8,128)} %get-tuple-element.100) | copy-start | bytes 1474564
  218.1 10.2 %copy-start.39 = (f32[960]{0:T(1024)S(1)}, f32[960]{0:T(1024)}, u32[]{:S(2)}) copy-start(f32[960]{0:T(1024)} %copy-done.38) | copy-start | bytes 11524
  218.1 10.2 %copy-start.46 = (f32[128]{0:T(128)S(1)}, f32[128]{0:T(128)}, u32[]{:S(2)}) copy-start(f32[128]{0:T(128)} %copy-done.45) | copy-start | bytes 1540
  220.2 10.4 %copy-start.7 = (bf16[128,960]{1,0:T(8,128)(2,1)S(1)}, bf16[128,960]{1,0:T(8,128)(2,1)}, u32[]{:S(2)}) copy-start(bf16[128,960]{1,0:T(8,128)(2,1)} %copy-done.6) | copy-start | bytes 737284
  220.2 10.4 %copy-start.53 = (f32[128]{0:T(128)S(1)}, f32[128]{0:T(128)}, u32[]{:S(2)}) copy-start(f32[128]{0:T(128)} %copy-done.52) | copy-start | bytes 1540
  220.2 17.4 %collective-permute-start.17 = (bf16[2,2,128,640]{3,2,1,0:T(8,128)(2,1)}, bf16[2,2,128,640]{3,2,1,0:T(8,128)(2,1)}, u32[]{:S(2)}, u32[]{:S(2)}) collective-permute-start(bf16[2,2,128,640]{3,2,1,0:T(8,128)(2,1)} %dynamic-slice_bitcast_fusion), channel_id=1, source_target_pairs={{0,2},{1,3},{2,0},{3,1},{4,6},{5,7},{6,4},{7,5},{8,10},{9,11},{10,... | collective-permute-start | bytes 1966088 | tf_op jit(solution)/shard_map/ppermute | solution.py:249
  229.1 17.1 %collective-permute-start.18 = (bf16[2,160,960]{2,1,0:T(8,128)(2,1)}, bf16[2,160,960]{2,1,0:T(8,128)(2,1)S(1)}, u32[]{:S(2)}, u32[]{:S(2)}) collective-permute-start(bf16[2,160,960]{2,1,0:T(8,128)(2,1)} %get-tuple-element.103), channel_id=1, source_target_pairs={{0,4},{1,5},{2,6},{3,7},{4,0},{5,1},{6,2},{7,3},{8,12},{9,13},{10,... | collective-permute-start | bytes 1843208 | tf_op jit(solution)/shard_map/ppermute | solution.py:249
  230.8 17.5 %copy-start.33 = (bf16[128,960]{1,0:T(8,128)(2,1)}, bf16[128,960]{1,0:T(8,128)(2,1)S(1)}, u32[]{:S(2)}) copy-start(bf16[128,960]{1,0:T(8,128)(2,1)S(1)} %get-tuple-element.119.refs_8_) | copy-start | bytes 737284
  230.8 16.6 %copy-start.17 = (bf16[1,2,128,640]{3,2,1,0:T(8,128)(2,1)S(1)}, bf16[1,2,128,640]{3,2,1,0:T(8,128)(2,1)}, u32[]{:S(2)}) copy-start(bf16[1,2,128,640]{3,2,1,0:T(8,128)(2,1)} %constant_dynamic-slice_fusion.5) | copy-start | bytes 983044
  248.3 6.6 %collective-permute-start.19 = (bf16[2,2,128,640]{3,2,1,0:T(8,128)(2,1)}, bf16[2,2,128,640]{3,2,1,0:T(8,128)(2,1)}, u32[]{:S(2)}, u32[]{:S(2)}) collective-permute-start(bf16[2,2,128,640]{3,2,1,0:T(8,128)(2,1)} %pad_maximum_fusion.1), channel_id=1, source_target_pairs={{0,1},{1,0},{2,3},{3,2},{4,5},{5,4},{6,7},{7,6},{8,9},{9,8},{10,11... | collective-permute-start | bytes 1966088 | tf_op jit(solution)/shard_map/ppermute | solution.py:249
  252.4 9.0 %copy-start.16 = (bf16[128,320]{0,1:T(8,128)(2,1)S(1)}, bf16[128,320]{0,1:T(8,128)(2,1)}, u32[]{:S(2)}) copy-start(bf16[128,320]{0,1:T(8,128)(2,1)} %copy-done.15) | copy-start | bytes 245764
  252.4 9.0 %copy-start.25 = (f32[5,3,128]{2,1,0:T(4,128)S(1)}, f32[5,3,128]{2,1,0:T(4,128)}, u32[]{:S(2)}) copy-start(f32[5,3,128]{2,1,0:T(4,128)} %copy-done.24) | copy-start | bytes 23044
  252.4 18.2 %collective-permute-start.20 = (bf16[160,960]{1,0:T(8,128)(2,1)S(1)}, bf16[160,960]{1,0:T(8,128)(2,1)}, u32[]{:S(2)}, u32[]{:S(2)}) collective-permute-start(bf16[160,960]{1,0:T(8,128)(2,1)S(1)} %fusion.71), channel_id=1, source_target_pairs={{0,8},{1,9},{2,10},{3,11},{4,12},{5,13},{6,14},{7,15},{8,0},{9,1},... | collective-permute-start | bytes 921608 | tf_op jit(solution)/shard_map/ppermute | solution.py:249
  262.9 16.0 %collective-permute-start.22 = (bf16[128,960]{1,0:T(8,128)(2,1)S(1)}, bf16[128,960]{1,0:T(8,128)(2,1)S(1)}, u32[]{:S(2)}, u32[]{:S(2)}) collective-permute-start(bf16[128,960]{1,0:T(8,128)(2,1)S(1)} %copy-done.34), channel_id=1, source_target_pairs={{0,2},{1,3},{2,0},{3,1},{4,6},{5,7},{6,4},{7,5},{8,10},{9,11},{10,... | collective-permute-start | bytes 737288 | tf_op jit(solution)/shard_map/ppermute | solution.py:249
  263.7 15.1 %collective-permute-start.23 = (bf16[128,960]{1,0:T(8,128)(2,1)S(1)}, bf16[128,960]{1,0:T(8,128)(2,1)}, u32[]{:S(2)}, u32[]{:S(2)}) collective-permute-start(bf16[128,960]{1,0:T(8,128)(2,1)S(1)} %copy-done.34), channel_id=1, source_target_pairs={{0,1},{1,0},{2,3},{3,2},{4,5},{5,4},{6,7},{7,6},{8,9},{9,8},{10,11... | collective-permute-start | bytes 737288 | tf_op jit(solution)/shard_map/ppermute | solution.py:249
  272.1 9.4 %collective-permute-start.21 = (bf16[2,1,128,640]{3,2,1,0:T(8,128)(2,1)S(1)}, bf16[2,1,128,640]{3,2,1,0:T(8,128)(2,1)S(1)}, u32[]{:S(2)}, u32[]{:S(2)}) collective-permute-start(bf16[2,1,128,640]{3,2,1,0:T(8,128)(2,1)S(1)} %bitcast.245), channel_id=1, source_target_pairs={{0,2},{1,3},{2,0},{3,1},{4,6},{5,7},{6,4},{7,5},{8,10},{9,11},{10,... | collective-permute-start | bytes 983048 | tf_op jit(solution)/shard_map/ppermute | solution.py:249
  272.9 17.9 %collective-permute-start.24 = (bf16[2,160,960]{2,1,0:T(8,128)(2,1)}, bf16[2,160,960]{2,1,0:T(8,128)(2,1)S(1)}, u32[]{:S(2)}, u32[]{:S(2)}) collective-permute-start(bf16[2,160,960]{2,1,0:T(8,128)(2,1)} %get-tuple-element.121), channel_id=1, source_target_pairs={{0,4},{1,5},{2,6},{3,7},{4,0},{5,1},{6,2},{7,3},{8,12},{9,13},{10,... | collective-permute-start | bytes 1843208 | tf_op jit(solution)/shard_map/ppermute | solution.py:249
  274.3 17.3 %copy-start.10 = (f32[2,320,960]{2,1,0:T(8,128)S(1)}, f32[2,320,960]{2,1,0:T(8,128)}, u32[]{:S(2)}) copy-start(f32[2,320,960]{2,1,0:T(8,128)} %get-tuple-element.137) | copy-start | bytes 7372804
  274.3 36.0 %collective-permute-start.29 = (bf16[2,160,960]{2,1,0:T(8,128)(2,1)}, bf16[2,160,960]{2,1,0:T(8,128)(2,1)S(1)}, u32[]{:S(2)}, u32[]{:S(2)}) collective-permute-start(bf16[2,160,960]{2,1,0:T(8,128)(2,1)} %get-tuple-element.133), channel_id=1, source_target_pairs={{0,4},{1,5},{2,6},{3,7},{4,0},{5,1},{6,2},{7,3},{8,12},{9,13},{10,... | collective-permute-start | bytes 1843208 | tf_op jit(solution)/shard_map/ppermute | solution.py:249
  278.8 12.0 %copy-start.56 = (bf16[128,960]{1,0:T(8,128)(2,1)}, bf16[128,960]{1,0:T(8,128)(2,1)S(1)}, u32[]{:S(2)}) copy-start(bf16[128,960]{1,0:T(8,128)(2,1)S(1)} %collective-permute-done.22.refs_9_) | copy-start | bytes 737284
  281.5 10.3 %copy-start.40 = (bf16[2,1,128,640]{3,2,1,0:T(8,128)(2,1)}, bf16[2,1,128,640]{3,2,1,0:T(8,128)(2,1)S(1)}, u32[]{:S(2)}) copy-start(bf16[2,1,128,640]{3,2,1,0:T(8,128)(2,1)S(1)} %collective-permute-done.21.refs_2_) | copy-start | bytes 983044
  290.9 7.9 %collective-permute-start.25 = (bf16[2,1,128,640]{3,2,1,0:T(8,128)(2,1)S(1)}, bf16[2,1,128,640]{3,2,1,0:T(8,128)(2,1)}, u32[]{:S(2)}, u32[]{:S(2)}) collective-permute-start(bf16[2,1,128,640]{3,2,1,0:T(8,128)(2,1)S(1)} %pad_maximum_fusion.5), channel_id=1, source_target_pairs={{0,1},{1,0},{2,3},{3,2},{4,5},{5,4},{6,7},{7,6},{8,9},{9,8},{10,11... | collective-permute-start | bytes 983048 | tf_op jit(solution)/shard_map/ppermute | solution.py:249
  291.0 7.8 %collective-permute-start.26 = (bf16[128,960]{1,0:T(8,128)(2,1)}, bf16[128,960]{1,0:T(8,128)(2,1)}, u32[]{:S(2)}, u32[]{:S(2)}) collective-permute-start(bf16[128,960]{1,0:T(8,128)(2,1)} %copy-done.56), channel_id=1, source_target_pairs={{0,1},{1,0},{2,3},{3,2},{4,5},{5,4},{6,7},{7,6},{8,9},{9,8},{10,11... | collective-permute-start | bytes 737288 | tf_op jit(solution)/shard_map/ppermute | solution.py:249
  291.5 2.9 collective-permute-start.27
  292.6 17.7 %collective-permute-start.30 = (bf16[160,960]{1,0:T(8,128)(2,1)}, bf16[160,960]{1,0:T(8,128)(2,1)}, u32[]{:S(2)}, u32[]{:S(2)}) collective-permute-start(bf16[160,960]{1,0:T(8,128)(2,1)} %fusion.72), channel_id=1, source_target_pairs={{0,8},{1,9},{2,10},{3,11},{4,12},{5,13},{6,14},{7,15},{8,0},{9,1},... | collective-permute-start | bytes 921608 | tf_op jit(solution)/shard_map/ppermute | solution.py:249
  294.3 3.7 %collective-permute-start.28 = (f32[1920]{0:T(1024)S(1)}, f32[1920]{0:T(1024)S(1)}, u32[]{:S(2)}, u32[]{:S(2)}) collective-permute-start(f32[1920]{0:T(1024)S(1)} %add.220), channel_id=1, source_target_pairs={{0,2},{1,3},{2,0},{3,1},{4,6},{5,7},{6,4},{7,5},{8,10},{9,11},{10,... | collective-permute-start | bytes 23048 | tf_op jit(solution)/shard_map/ppermute | solution.py:249
  310.3 6.1 %copy-start.9 = (f32[2,160,960]{2,1,0:T(8,128)S(1)}, f32[2,160,960]{2,1,0:T(8,128)}, u32[]{:S(2)}) copy-start(f32[2,160,960]{2,1,0:T(8,128)} %copy-done.8) | copy-start | bytes 3686404
  310.3 24.5 %collective-permute-start.31 = (bf16[2,168,960]{2,1,0:T(8,128)(2,1)}, bf16[2,168,960]{2,1,0:T(8,128)(2,1)S(1)}, u32[]{:S(2)}, u32[]{:S(2)}) collective-permute-start(bf16[2,168,960]{2,1,0:T(8,128)(2,1)} %get-tuple-element.136), channel_id=1, source_target_pairs={{0,4},{1,5},{2,6},{3,7},{4,0},{5,1},{6,2},{7,3},{8,12},{9,13},{10,... | collective-permute-start | bytes 1935368 | tf_op jit(solution)/shard_map/ppermute | solution.py:249
  314.3 20.5 %copy-start.12 = (f32[2,168,960]{2,1,0:T(8,128)S(1)}, f32[2,168,960]{2,1,0:T(8,128)}, u32[]{:S(2)}) copy-start(f32[2,168,960]{2,1,0:T(8,128)} %get-tuple-element.139) | copy-start | bytes 3870724
  314.3 19.7 %collective-permute-start.32 = (bf16[160,960]{1,0:T(8,128)(2,1)S(1)}, bf16[160,960]{1,0:T(8,128)(2,1)S(1)}, u32[]{:S(2)}, u32[]{:S(2)}) collective-permute-start(bf16[160,960]{1,0:T(8,128)(2,1)S(1)} %fusion.73), channel_id=1, source_target_pairs={{0,8},{1,9},{2,10},{3,11},{4,12},{5,13},{6,14},{7,15},{8,0},{9,1},... | collective-permute-start | bytes 921608 | tf_op jit(solution)/shard_map/ppermute | solution.py:249
  335.1 16.8 %collective-permute-start.33 = (bf16[168,960]{1,0:T(8,128)(2,1)S(1)}, bf16[168,960]{1,0:T(8,128)(2,1)S(1)}, u32[]{:S(2)}, u32[]{:S(2)}) collective-permute-start(bf16[168,960]{1,0:T(8,128)(2,1)S(1)} %fusion.70), channel_id=1, source_target_pairs={{0,8},{1,9},{2,10},{3,11},{4,12},{5,13},{6,14},{7,15},{8,0},{9,1},... | collective-permute-start | bytes 967688 | tf_op jit(solution)/shard_map/ppermute | solution.py:249
  (30 other events, 60.6 us)
Sparse Core Ops, SparseCore 0:
  10.2 111.5 all-gather.1

commit v13 on v12

--- a/solution.py
+++ b/solution.py
@@ -213,7 +213,7 @@
         out_shape=[jax.ShapeDtypeStruct((steps, *shape), t) for shape, t in out_blocks]
         + [jax.ShapeDtypeStruct((tokens, width), f32)],
         compiler_params=pltpu.CompilerParams(
-            dimension_semantics=("arbitrary",), vmem_limit_bytes=60 * 1024 * 1024
+            dimension_semantics=("arbitrary",), vmem_limit_bytes=40 * 1024 * 1024
         ),
         cost_estimate=pl.CostEstimate(
             flops=6 * tokens * steps * cols * width,
@@ -384,7 +384,7 @@
         ),
         out_shape=shapes,
         compiler_params=pltpu.CompilerParams(
-            dimension_semantics=("arbitrary",), vmem_limit_bytes=60 * 1024 * 1024
+            dimension_semantics=("arbitrary",), vmem_limit_bytes=32 * 1024 * 1024
         ),
         cost_estimate=pl.CostEstimate(
             flops=8 * tokens * kinds * width_cols * width * len(rows),

time: 361 us -> 350 us (0.970)
  Pallas kernels: 56.9 us -> 46.5 us
    pallas_call x3, Pallas kernels: 16.3 us -> 9.9 us  [plane_product(): pl.pallas_call(kernel, grid_spec=pltpu.PrefetchScalarGridSpec(num_scalar_...]
    pallas_call x4, Pallas kernels: 40.6 us -> 36.6 us  [ffn_call(): pl.pallas_call(kernel, grid=(steps,), in_specs=[whole] * len(wholes) + [b...]
    unnamed x118 -> x162, local copies, waits for them, and re-layouts: 2.87 us -> 6.91 us
  transfers between devices with their start and end apart: 35 -> 35, of which waited for: 19 -> 20; matrix products, arithmetic and copies ran while one was open for 8% -> 8% of each run, Pallas kernels for 13% -> 11%
where the time goes in v13:
time: 350 us; the launch traced here: 349 us
  waiting for transfers between devices  187 us (53%)
  Pallas kernels  46.5 us (13%)
  starting transfers between devices  38.3 us (11%)
  local copies, waits for them, and re-layouts  22.3 us (6%)
  other arithmetic  20.9 us (6%)
  matrix products  18 us (5%)
  between operations  15.5 us (4%)
    all_gather x1, waiting for transfers between devices, local(): lax.all_gather(own, 'dp', axis=0, tiled=True).reshape(4, 4, 4, share, width)  97.3 us
    ppermute x32, waiting for transfers between devices, flip(): return lax.ppermute(x, 'dp', [(i, i ^ bit) for i in range(size)])  75.4 us
    pallas_call x4, Pallas kernels, ffn_call(): pl.pallas_call(kernel, grid=(steps,), in_specs=[whole] * len(wholes) + [b...  36.6 us
    ppermute x32, starting transfers between devices, flip(): return lax.ppermute(x, 'dp', [(i, i ^ bit) for i in range(size)])  33.2 us
    pallas_call x3, Pallas kernels, plane_product(): pl.pallas_call(kernel, grid_spec=pltpu.PrefetchScalarGridSpec(num_scalar_...  9.9 us
    ppermute x1, waiting for transfers between devices, local(): received = lax.ppermute(first_grad, 'section', [(1, 0)])  8.84 us
    dot_general x4, matrix products, dot_nt(): lax.dot_general(a, b, (((1,), (1,)), ((), ())), preferred_element_type=f32)  7.86 us
  transfers between devices with their start and end apart: 35, of which 20 were waited for; matrix products, arithmetic and copies ran while one was open for 8% of the time, Pallas kernels for 11%

profile of v13, /device:TPU:0, one launch (start us, length us, event | category | flops | bytes accessed | tf_op | source)
XLA Modules:
  0.0 348.9 jit_solution(13559131077418493875)
XLA Ops:
  7.2 2.5 pad_maximum_fusion
  11.2 2.8 collective-permute-start.1
  14.2 1.4 collective-permute-done.1
  15.7 2.1 collective-permute-start.2
  17.9 1.4 collective-permute-done.2
  19.5 3.0 collective-permute-start.3
  22.8 1.3 collective-permute-done.3
  24.4 97.3 %all-gather.2.cloned.1.call-done = bf16[10240,960]{1,0:T(8,128)(2,1)} async-done(((bf16[640,960]{1,0:T(8,128)(2,1)}), bf16[10240,960]{1,0:T(8,128)(2,1)}) %all-gather.2.cloned.1.call-update) | async-done | bytes 19660816 | tf_op jit(solution)/shard_map/all_gather | solution.py:524
  121.8 3.3 slice.127
  125.0 1.1 fusion.6
  128.1 9.6 %shard_map.84 = (f32[4,128,640]{2,1,0:T(8,128)}, f32[4,128,640]{2,1,0:T(8,128)}, bf16[4,128,640]{2,1,0:T(8,128)(2,1)}, f32[128,960]{1,0:T(8,128)S(1)}) custom-call(bf16[128,960]{1,0:T(8,128)(2,1)S(1)} %multiply_convert_fusion.3.m_ref, f32[128,960]{1,0:T(8,128)S(1)} %get-tuple-element.188.h1_ref, bf16[4,4,4,160,960]{4,3,2,1,0:T(8,128)(2,1)} %bitcast.199, ...), custom_call_target="tpu_custom_call" | custom-call | flops 1887436800 | bytes 14745600 | tf_op jit(solution)/shard_map/pallas_call | solution.py:206
  137.8 3.6 %collective-permute-start.4 = (bf16[128,960]{1,0:T(8,128)(2,1)S(1)}, bf16[128,960]{1,0:T(8,128)(2,1)S(1)}, u32[]{:S(2)}, u32[]{:S(2)}) collective-permute-start(bf16[128,960]{1,0:T(8,128)(2,1)S(1)} %convert_element_type.168), channel_id=1, source_target_pairs={{0,16},{1,17},{2,18},{3,19},{4,20},{5,21},{6,22},{7,23},{8,24},{9,... | collective-permute-start | bytes 737288 | tf_op jit(solution)/shard_map/ppermute | solution.py:539
  141.3 5.8 %collective-permute-done.4 = bf16[128,960]{1,0:T(8,128)(2,1)S(1)} collective-permute-done((bf16[128,960]{1,0:T(8,128)(2,1)S(1)}, bf16[128,960]{1,0:T(8,128)(2,1)S(1)}, u32[]{:S(2)}, u32[]{:S(2)}) %collective-permute-start.4) | collective-permute-done | bytes 245792 | tf_op jit(solution)/shard_map/ppermute | solution.py:539
  148.7 3.0 fusion.4
  153.7 2.2 multiply_reduce_fusion.5
  156.8 1.2 collective-permute-start.5
  158.8 8.3 %shard_map.85 = (f32[4,128,640]{2,1,0:T(8,128)S(1)}, f32[4,128,640]{2,1,0:T(8,128)S(1)}, bf16[4,128,640]{2,1,0:T(8,128)(2,1)S(1)}, f32[128,960]{1,0:T(8,128)S(1)}) custom-call(bf16[128,960]{1,0:T(8,128)(2,1)} %multiply_convert_fusion.2.m_ref.refs_4_, f32[128,960]{1,0:T(8,128)S(1)} %get-tuple-element.192.h1_ref, bf16[4,4,4,160,960]{4,3,2,1,0:T(8,128)(2,1)} %bitcast.202, ...), custom_call_target="tpu_custom_call" | custom-call | flops 1887436800 | bytes 14745600 | tf_op jit(solution)/shard_map/pallas_call | solution.py:206
  167.1 3.2 collective-permute-done.6.refs_5_
  171.1 1.2 collective-permute-start.7
  173.4 1.1 dynamic-slice_bitcast_fusion.2
  174.5 9.9 %shard_map.86 = (bf16[4,2,128,640]{3,2,1,0:T(8,128)(2,1)}, f32[128,960]{1,0:T(8,128)S(1)}) custom-call(bf16[128,960]{1,0:T(8,128)(2,1)S(1)} %bitcast.194, f32[4,128,640]{2,1,0:T(8,128)S(1)} %get-tuple-element.79.gate_ref, f32[4,128,640]{2,1,0:T(8,128)S(1)} %get-tuple-element.80.up_ref, bf16[4,4,4,160,960]{4,3,2,1,0:T(8,128)(2,1)} %bitcast.205, ...), custom_call_target="tpu_custom_call" | custom-call | flops 1887436800 | bytes 14745600 | tf_op jit(solution)/shard_map/pallas_call | solution.py:206
  188.6 0.9 constant_dynamic-slice_fusion.6
  191.3 1.5 collective-permute-start.13
  192.8 8.8 %collective-permute-done.13 = bf16[128,960]{1,0:T(8,128)(2,1)S(1)} collective-permute-done((bf16[128,960]{1,0:T(8,128)(2,1)S(1)}, bf16[128,960]{1,0:T(8,128)(2,1)S(1)}, u32[]{:S(2)}, u32[]{:S(2)}) %collective-permute-start.13) | collective-permute-done | bytes 245792 | tf_op jit(solution)/shard_map/ppermute | solution.py:543
  203.3 8.8 %shard_map.87 = (bf16[4,2,128,640]{3,2,1,0:T(8,128)(2,1)S(1)}, f32[128,960]{1,0:T(8,128)S(1)}) custom-call(bf16[128,960]{1,0:T(8,128)(2,1)} %broadcast_select_fusion.eb_ref.refs_4_, f32[4,128,640]{2,1,0:T(8,128)S(1)} %get-tuple-element.79.gate_ref, f32[4,128,640]{2,1,0:T(8,128)S(1)} %get-tuple-element.80.up_ref, bf16[4,4,4,160,960]{4,3,2,1,0:T(8,128)(2,1)} %bitcast.208, ...), custom_call_target="tpu_custom_call" | custom-call | flops 1887436800 | bytes 14745600 | tf_op jit(solution)/shard_map/pallas_call | solution.py:206
  212.8 1.3 collective-permute-start.17
  214.2 2.8 shard_map.88
  217.1 1.6 collective-permute-start.18
  218.7 2.1 fusion.92
  220.8 3.0 fusion.33
  223.8 5.7 %collective-permute-done.17.refs_2_ = bf16[2,2,128,640]{3,2,1,0:T(8,128)(2,1)S(1)} collective-permute-done((bf16[2,2,128,640]{3,2,1,0:T(8,128)(2,1)S(1)}, bf16[2,2,128,640]{3,2,1,0:T(8,128)(2,1)S(1)}, u32[]{:S(2)}, u32[]{:S(2)}) %collective-permute-start.17) | collective-permute-done | bytes 655392 | tf_op jit(solution)/shard_map/ppermute | solution.py:249
  229.5 4.6 %collective-permute-done.18 = bf16[2,160,960]{2,1,0:T(8,128)(2,1)S(1)} collective-permute-done((bf16[2,160,960]{2,1,0:T(8,128)(2,1)S(1)}, bf16[2,160,960]{2,1,0:T(8,128)(2,1)S(1)}, u32[]{:S(2)}, u32[]{:S(2)}) %collective-permute-start.18) | collective-permute-done | bytes 614432 | tf_op jit(solution)/shard_map/ppermute | solution.py:249
  234.2 1.0 pad_maximum_fusion.1
  235.4 1.4 convert_add_fusion.3
  236.9 2.5 collective-permute-start.20
  240.2 1.1 copy-done.14
  241.3 3.4 shard_map.89
  246.7 1.3 collective-permute-start.22
  248.2 6.7 %collective-permute-done.20 = bf16[160,960]{1,0:T(8,128)(2,1)S(1)} collective-permute-done((bf16[160,960]{1,0:T(8,128)(2,1)S(1)}, bf16[160,960]{1,0:T(8,128)(2,1)S(1)}, u32[]{:S(2)}, u32[]{:S(2)}) %collective-permute-start.20) | collective-permute-done | bytes 307232 | tf_op jit(solution)/shard_map/ppermute | solution.py:249
  255.9 1.4 copy.43.refs_1_
  257.3 1.7 constant_dynamic-slice_fusion.3
  259.0 1.9 copy.41
  260.9 1.3 collective-permute-start.21
  262.2 2.1 collective-permute-start.29
  264.3 2.9 fusion.62
  267.2 3.2 collective-permute-done.21.refs_2_
  270.5 9.6 %collective-permute-done.24 = bf16[2,160,960]{2,1,0:T(8,128)(2,1)S(1)} collective-permute-done((bf16[2,160,960]{2,1,0:T(8,128)(2,1)}, bf16[2,160,960]{2,1,0:T(8,128)(2,1)S(1)}, u32[]{:S(2)}, u32[]{:S(2)}) %collective-permute-start.24) | collective-permute-done | bytes 614432 | tf_op jit(solution)/shard_map/ppermute | solution.py:249
  282.6 1.1 collective-permute-start.30
  283.7 1.4 collective-permute-start.28
  285.1 1.0 fusion.53
  286.1 1.2 collective-permute-done.28
  287.5 1.0 copy-done.10
  288.5 0.9 copy-done.16
  289.4 0.9 copy-done.18
  290.4 3.7 %shard_map.90 = (f32[2,168,960]{2,1,0:T(8,128)S(1)}, bf16[2,168,960]{2,1,0:T(8,128)(2,1)S(1)}) custom-call(s32[7]{0:T(128)S(1)} %stack.86.refs_0_, bf16[4,1,128,640]{3,2,1,0:T(8,128)(2,1)S(1)} %copy.43.refs_1_, bf16[2,1,128,640]{3,2,1,0:T(8,128)(2,1)S(1)} %copy-done.10, bf16[2,1,128,640]{3,2,1,0:T(8,128)(2,1)} %collective-permute-done.25.refs_3_, ...), custom_call_target="tpu_custom_call" | custom-call | flops 1258291200 | bytes 4096000 | tf_op jit(solution)/shard_map/pallas_call | solution.py:376
  294.1 5.2 %collective-permute-done.29 = bf16[2,160,960]{2,1,0:T(8,128)(2,1)} collective-permute-done((bf16[2,160,960]{2,1,0:T(8,128)(2,1)}, bf16[2,160,960]{2,1,0:T(8,128)(2,1)}, u32[]{:S(2)}, u32[]{:S(2)}) %collective-permute-start.29) | collective-permute-done | bytes 614432 | tf_op jit(solution)/shard_map/ppermute | solution.py:249
  299.3 1.6 collective-permute-done.30
  301.2 1.4 convert_add_fusion.1
  302.6 2.9 collective-permute-start.32
  305.6 1.1 fusion.44
  306.7 15.6 %collective-permute-done.32 = bf16[160,960]{1,0:T(8,128)(2,1)S(1)} collective-permute-done((bf16[160,960]{1,0:T(8,128)(2,1)S(1)}, bf16[160,960]{1,0:T(8,128)(2,1)S(1)}, u32[]{:S(2)}, u32[]{:S(2)}) %collective-permute-start.32) | collective-permute-done | bytes 307232 | tf_op jit(solution)/shard_map/ppermute | solution.py:249
  323.3 2.7 collective-permute-start.33
  326.1 1.5 maximum_bitcast_fusion
  327.6 13.0 %collective-permute-done.33 = bf16[168,960]{1,0:T(8,128)(2,1)S(1)} collective-permute-done((bf16[168,960]{1,0:T(8,128)(2,1)S(1)}, bf16[168,960]{1,0:T(8,128)(2,1)S(1)}, u32[]{:S(2)}, u32[]{:S(2)}) %collective-permute-start.33) | collective-permute-done | bytes 322592 | tf_op jit(solution)/shard_map/ppermute | solution.py:249
  (307 shorter events, 29.2 us)
Async XLA Ops:
  7.2 114.6 %all-gather.2.cloned.1.call-start = ((), (), s32[]{:S(2)}) async-start(), calls=%async_computation | async-start | bytes 22282240 | tf_op jit(solution)/shard_map/all_gather | solution.py:524
  7.2 10.5 %copy-start = (bf16[1,2,64,960]{3,2,1,0:T(8,128)(2,1)S(1)}, bf16[1,2,64,960]{3,2,1,0:T(8,128)(2,1)}, u32[]{:S(2)}) copy-start(bf16[1,2,64,960]{3,2,1,0:T(8,128)(2,1)} %param.5) | copy-start | bytes 737284
  9.8 1.3 collective-permute-start
  11.2 4.3 %collective-permute-start.1 = (bf16[240]{0:T(256)(128)(2,1)S(1)}, bf16[240]{0:T(256)(128)(2,1)S(1)}, u32[]{:S(2)}, u32[]{:S(2)}) collective-permute-start(bf16[240]{0:T(256)(128)(2,1)S(1)} %pad_maximum_fusion.17), channel_id=1, source_target_pairs={{0,2},{1,3},{2,0},{3,1},{4,6},{5,7},{6,4},{7,5},{8,10},{9,11},{10,... | collective-permute-start | bytes 1448 | tf_op jit(solution)/shard_map/ppermute | solution.py:249
  14.2 173.6 %copy-start.51 = (f32[128,32]{0,1:T(8,128)}, f32[128,32]{0,1:T(8,128)S(1)}, u32[]{:S(2)}) copy-start(f32[128,32]{0,1:T(8,128)S(1)} %get-tuple-element.174) | copy-start | bytes 49156
  15.7 3.6 %collective-permute-start.2 = (bf16[480]{0:T(512)(128)(2,1)S(1)}, bf16[480]{0:T(512)(128)(2,1)S(1)}, u32[]{:S(2)}, u32[]{:S(2)}) collective-permute-start(bf16[480]{0:T(512)(128)(2,1)S(1)} %pad_maximum_fusion.16), channel_id=1, source_target_pairs={{0,4},{1,5},{2,6},{3,7},{4,0},{5,1},{6,2},{7,3},{8,12},{9,13},{10,... | collective-permute-start | bytes 2888 | tf_op jit(solution)/shard_map/ppermute | solution.py:249
  19.5 4.7 %collective-permute-start.3 = (bf16[960]{0:T(1024)(128)(2,1)S(1)}, bf16[960]{0:T(1024)(128)(2,1)S(1)}, u32[]{:S(2)}, u32[]{:S(2)}) collective-permute-start(bf16[960]{0:T(1024)(128)(2,1)S(1)} %pad_maximum_fusion.15), channel_id=1, source_target_pairs={{0,8},{1,9},{2,10},{3,11},{4,12},{5,13},{6,14},{7,15},{8,0},{9,1},... | collective-permute-start | bytes 5768 | tf_op jit(solution)/shard_map/ppermute | solution.py:249
  24.4 123.5 %copy-start.65 = (f32[960]{0:T(1024)}, f32[960]{0:T(1024)S(1)}, u32[]{:S(2)}) copy-start(f32[960]{0:T(1024)S(1)} %get-tuple-element.169) | copy-start | bytes 11524
  24.4 160.2 %copy-start.63 = (f32[960]{0:T(1024)}, f32[960]{0:T(1024)S(1)}, u32[]{:S(2)}) copy-start(f32[960]{0:T(1024)S(1)} %get-tuple-element.168) | copy-start | bytes 11524
  137.8 9.4 %collective-permute-start.4 = (bf16[128,960]{1,0:T(8,128)(2,1)S(1)}, bf16[128,960]{1,0:T(8,128)(2,1)S(1)}, u32[]{:S(2)}, u32[]{:S(2)}) collective-permute-start(bf16[128,960]{1,0:T(8,128)(2,1)S(1)} %convert_element_type.168), channel_id=1, source_target_pairs={{0,16},{1,17},{2,18},{3,19},{4,20},{5,21},{6,22},{7,23},{8,24},{9,... | collective-permute-start | bytes 737288 | tf_op jit(solution)/shard_map/ppermute | solution.py:539
  147.3 6.4 %copy-start.30 = (bf16[128,960]{1,0:T(8,128)(2,1)}, bf16[128,960]{1,0:T(8,128)(2,1)S(1)}, u32[]{:S(2)}) copy-start(bf16[128,960]{1,0:T(8,128)(2,1)S(1)} %get-tuple-element.151) | copy-start | bytes 737284
  151.8 34.3 %copy-start.41 = (bf16[128,320]{0,1:T(8,128)(2,1)}, bf16[128,320]{0,1:T(8,128)(2,1)S(1)}, u32[]{:S(2)}) copy-start(bf16[128,320]{0,1:T(8,128)(2,1)S(1)} %slice.218) | copy-start | bytes 245764
  152.7 33.8 %copy-start.53 = (f32[5,3,128]{2,1,0:T(4,128)}, f32[5,3,128]{2,1,0:T(4,128)S(1)}, u32[]{:S(2)}) copy-start(f32[5,3,128]{2,1,0:T(4,128)S(1)} %log_add_fusion) | copy-start | bytes 23044
  155.9 28.7 %copy-start.69 = (f32[128]{0:T(128)}, f32[128]{0:T(128)S(1)}, u32[]{:S(2)}) copy-start(f32[128]{0:T(128)S(1)} %get-tuple-element.184) | copy-start | bytes 1540
  155.9 28.7 %copy-start.76 = (f32[128]{0:T(128)}, f32[128]{0:T(128)S(1)}, u32[]{:S(2)}) copy-start(f32[128]{0:T(128)S(1)} %get-tuple-element.183) | copy-start | bytes 1540
  156.8 10.3 %collective-permute-start.5 = (bf16[128,960]{1,0:T(8,128)(2,1)}, bf16[128,960]{1,0:T(8,128)(2,1)}, u32[]{:S(2)}, u32[]{:S(2)}) collective-permute-start(bf16[128,960]{1,0:T(8,128)(2,1)} %multiply_convert_fusion.2.m_ref.refs_4_), channel_id=1, source_target_pairs={{0,2},{1,3},{2,0},{3,1},{4,6},{5,7},{6,4},{7,5},{8,10},{9,11},{10,... | collective-permute-start | bytes 737288 | tf_op jit(solution)/shard_map/ppermute | solution.py:249
  158.0 12.3 %collective-permute-start.6 = (bf16[128,960]{1,0:T(8,128)(2,1)}, bf16[128,960]{1,0:T(8,128)(2,1)}, u32[]{:S(2)}, u32[]{:S(2)}) collective-permute-start(bf16[128,960]{1,0:T(8,128)(2,1)} %fusion.58.refs_4_), channel_id=1, source_target_pairs={{0,2},{1,3},{2,0},{3,1},{4,6},{5,7},{6,4},{7,5},{8,10},{9,11},{10,... | collective-permute-start | bytes 737288 | tf_op jit(solution)/shard_map/ppermute | solution.py:249
  171.1 13.3 %collective-permute-start.7 = (bf16[2,1,128,640]{3,2,1,0:T(8,128)(2,1)}, bf16[2,1,128,640]{3,2,1,0:T(8,128)(2,1)}, u32[]{:S(2)}, u32[]{:S(2)}) collective-permute-start(bf16[2,1,128,640]{3,2,1,0:T(8,128)(2,1)} %dynamic-slice_bitcast_fusion.1), channel_id=1, source_target_pairs={{0,2},{1,3},{2,0},{3,1},{4,6},{5,7},{6,4},{7,5},{8,10},{9,11},{10,... | collective-permute-start | bytes 983048 | tf_op jit(solution)/shard_map/ppermute | solution.py:249
  172.4 12.0 %collective-permute-start.8 = (bf16[128,960]{1,0:T(8,128)(2,1)}, bf16[128,960]{1,0:T(8,128)(2,1)S(1)}, u32[]{:S(2)}, u32[]{:S(2)}) collective-permute-start(bf16[128,960]{1,0:T(8,128)(2,1)} %multiply_convert_fusion.2.m_ref.refs_4_), channel_id=1, source_target_pairs={{0,1},{1,0},{2,3},{3,2},{4,5},{5,4},{6,7},{7,6},{8,9},{9,8},{10,11... | collective-permute-start | bytes 737288 | tf_op jit(solution)/shard_map/ppermute | solution.py:249
  172.4 12.0 %collective-permute-start.10 = (bf16[128,960]{1,0:T(8,128)(2,1)}, bf16[128,960]{1,0:T(8,128)(2,1)S(1)}, u32[]{:S(2)}, u32[]{:S(2)}) collective-permute-start(bf16[128,960]{1,0:T(8,128)(2,1)} %fusion.58.refs_4_), channel_id=1, source_target_pairs={{0,1},{1,0},{2,3},{3,2},{4,5},{5,4},{6,7},{7,6},{8,9},{9,8},{10,11... | collective-permute-start | bytes 737288 | tf_op jit(solution)/shard_map/ppermute | solution.py:249
  172.9 11.5 %collective-permute-start.9 = (bf16[128,960]{1,0:T(8,128)(2,1)}, bf16[128,960]{1,0:T(8,128)(2,1)S(1)}, u32[]{:S(2)}, u32[]{:S(2)}) collective-permute-start(bf16[128,960]{1,0:T(8,128)(2,1)} %collective-permute-done.5.refs_5_), channel_id=1, source_target_pairs={{0,1},{1,0},{2,3},{3,2},{4,5},{5,4},{6,7},{7,6},{8,9},{9,8},{10,11... | collective-permute-start | bytes 737288 | tf_op jit(solution)/shard_map/ppermute | solution.py:249
  172.9 11.5 %collective-permute-start.11 = (bf16[128,960]{1,0:T(8,128)(2,1)}, bf16[128,960]{1,0:T(8,128)(2,1)S(1)}, u32[]{:S(2)}, u32[]{:S(2)}) collective-permute-start(bf16[128,960]{1,0:T(8,128)(2,1)} %collective-permute-done.6.refs_5_), channel_id=1, source_target_pairs={{0,1},{1,0},{2,3},{3,2},{4,5},{5,4},{6,7},{7,6},{8,9},{9,8},{10,11... | collective-permute-start | bytes 737288 | tf_op jit(solution)/shard_map/ppermute | solution.py:249
  173.4 11.4 %slice-start = ((s8[5242880]{0:T(1024)(128)(4,1)}), s8[4194304]{0:T(1024)(128)(4,1)S(1)}, s32[]{:S(2)}) async-start(s8[5242880]{0:T(1024)(128)(4,1)} %bitcast.217), calls=%async_computation.1 | async-start | bytes 8388608
  174.5 10.4 %slice-start.1 = ((s8[5242880]{0:T(1024)(128)(4,1)}), s8[1048576]{0:T(1024)(128)(4,1)S(1)}, s32[]{:S(2)}) async-start(s8[5242880]{0:T(1024)(128)(4,1)} %bitcast.217), calls=%async_computation.2 | async-start | bytes 2097152
  189.6 1.7 collective-permute-start.12
  191.3 11.1 %copy-start.7 = (bf16[2,1,128,640]{3,2,1,0:T(8,128)(2,1)}, bf16[2,1,128,640]{3,2,1,0:T(8,128)(2,1)S(1)}, u32[]{:S(2)}) copy-start(bf16[2,1,128,640]{3,2,1,0:T(8,128)(2,1)S(1)} %collective-permute-done.12.refs_3_) | copy-start | bytes 983044
  191.3 10.4 %collective-permute-start.13 = (bf16[128,960]{1,0:T(8,128)(2,1)S(1)}, bf16[128,960]{1,0:T(8,128)(2,1)S(1)}, u32[]{:S(2)}, u32[]{:S(2)}) collective-permute-start(bf16[128,960]{1,0:T(8,128)(2,1)S(1)} %fusion.49), channel_id=1, source_target_pairs={{16,0},{17,1},{18,2},{19,3},{20,4},{21,5},{22,6},{23,7},{24,8},{25... | collective-permute-start | bytes 737288 | tf_op jit(solution)/shard_map/ppermute | solution.py:543
  202.4 9.7 %collective-permute-start.14 = (bf16[128,960]{1,0:T(8,128)(2,1)}, bf16[128,960]{1,0:T(8,128)(2,1)}, u32[]{:S(2)}, u32[]{:S(2)}) collective-permute-start(bf16[128,960]{1,0:T(8,128)(2,1)} %broadcast_select_fusion.eb_ref.refs_4_), channel_id=1, source_target_pairs={{0,2},{1,3},{2,0},{3,1},{4,6},{5,7},{6,4},{7,5},{8,10},{9,11},{10,... | collective-permute-start | bytes 737288 | tf_op jit(solution)/shard_map/ppermute | solution.py:249
  203.2 8.9 %collective-permute-start.15 = (bf16[128,960]{1,0:T(8,128)(2,1)}, bf16[128,960]{1,0:T(8,128)(2,1)}, u32[]{:S(2)}, u32[]{:S(2)}) collective-permute-start(bf16[128,960]{1,0:T(8,128)(2,1)} %broadcast_select_fusion.eb_ref.refs_4_), channel_id=1, source_target_pairs={{0,1},{1,0},{2,3},{3,2},{4,5},{5,4},{6,7},{7,6},{8,9},{9,8},{10,11... | collective-permute-start | bytes 737288 | tf_op jit(solution)/shard_map/ppermute | solution.py:249
  212.1 4.9 %copy-start.3 = (bf16[4,2,128,640]{3,2,1,0:T(8,128)(2,1)}, bf16[4,2,128,640]{3,2,1,0:T(8,128)(2,1)S(1)}, u32[]{:S(2)}) copy-start(bf16[4,2,128,640]{3,2,1,0:T(8,128)(2,1)S(1)} %get-tuple-element.101.refs_1_) | copy-start | bytes 3932164
  212.1 2.0 collective-permute-start.16
  212.8 6.0 %copy-start.77 = (f32[128]{0:T(128)S(1)}, f32[128]{0:T(128)}, u32[]{:S(2)}) copy-start(f32[128]{0:T(128)} %copy-done.76) | copy-start | bytes 1540
  212.8 16.7 %collective-permute-start.17 = (bf16[2,2,128,640]{3,2,1,0:T(8,128)(2,1)S(1)}, bf16[2,2,128,640]{3,2,1,0:T(8,128)(2,1)S(1)}, u32[]{:S(2)}, u32[]{:S(2)}) collective-permute-start(bf16[2,2,128,640]{3,2,1,0:T(8,128)(2,1)S(1)} %dynamic-slice_bitcast_fusion), channel_id=1, source_target_pairs={{0,2},{1,3},{2,0},{3,1},{4,6},{5,7},{6,4},{7,5},{8,10},{9,11},{10,... | collective-permute-start | bytes 1966088 | tf_op jit(solution)/shard_map/ppermute | solution.py:249
  217.1 17.0 %collective-permute-start.18 = (bf16[2,160,960]{2,1,0:T(8,128)(2,1)S(1)}, bf16[2,160,960]{2,1,0:T(8,128)(2,1)S(1)}, u32[]{:S(2)}, u32[]{:S(2)}) collective-permute-start(bf16[2,160,960]{2,1,0:T(8,128)(2,1)S(1)} %get-tuple-element.103), channel_id=1, source_target_pairs={{0,4},{1,5},{2,6},{3,7},{4,0},{5,1},{6,2},{7,3},{8,12},{9,13},{10,... | collective-permute-start | bytes 1843208 | tf_op jit(solution)/shard_map/ppermute | solution.py:249
  235.2 4.2 %collective-permute-start.19 = (bf16[2,2,128,640]{3,2,1,0:T(8,128)(2,1)}, bf16[2,2,128,640]{3,2,1,0:T(8,128)(2,1)S(1)}, u32[]{:S(2)}, u32[]{:S(2)}) collective-permute-start(bf16[2,2,128,640]{3,2,1,0:T(8,128)(2,1)} %pad_maximum_fusion.1), channel_id=1, source_target_pairs={{0,1},{1,0},{2,3},{3,2},{4,5},{5,4},{6,7},{7,6},{8,9},{9,8},{10,11... | collective-permute-start | bytes 1966088 | tf_op jit(solution)/shard_map/ppermute | solution.py:249
  235.4 4.8 %copy-start.4 = (bf16[4,2,128,640]{3,2,1,0:T(8,128)(2,1)S(1)}, bf16[4,2,128,640]{3,2,1,0:T(8,128)(2,1)}, u32[]{:S(2)}) copy-start(bf16[4,2,128,640]{3,2,1,0:T(8,128)(2,1)} %copy-done.3) | copy-start | bytes 3932164
  235.4 4.8 %copy-start.20 = (bf16[128,960]{1,0:T(8,128)(2,1)S(1)}, bf16[128,960]{1,0:T(8,128)(2,1)}, u32[]{:S(2)}) copy-start(bf16[128,960]{1,0:T(8,128)(2,1)} %copy-done.19) | copy-start | bytes 737284
  235.4 4.8 %copy-start.22 = (bf16[128,960]{1,0:T(8,128)(2,1)S(1)}, bf16[128,960]{1,0:T(8,128)(2,1)}, u32[]{:S(2)}) copy-start(bf16[128,960]{1,0:T(8,128)(2,1)} %copy-done.21) | copy-start | bytes 737284
  236.8 8.0 %copy-start.29 = (bf16[5,3,128,128]{2,3,1,0:T(8,128)(2,1)S(1)}, bf16[5,3,128,128]{2,3,1,0:T(8,128)(2,1)}, u32[]{:S(2)}) copy-start(bf16[5,3,128,128]{2,3,1,0:T(8,128)(2,1)} %copy-done.27) | copy-start | bytes 1474564
  236.8 8.3 %copy-start.42 = (bf16[128,320]{0,1:T(8,128)(2,1)S(1)}, bf16[128,320]{0,1:T(8,128)(2,1)}, u32[]{:S(2)}) copy-start(bf16[128,320]{0,1:T(8,128)(2,1)} %copy-done.41) | copy-start | bytes 245764
  236.8 8.3 %copy-start.54 = (f32[5,3,128]{2,1,0:T(4,128)S(1)}, f32[5,3,128]{2,1,0:T(4,128)}, u32[]{:S(2)}) copy-start(f32[5,3,128]{2,1,0:T(4,128)} %copy-done.53) | copy-start | bytes 23044
  236.9 18.1 %collective-permute-start.20 = (bf16[160,960]{1,0:T(8,128)(2,1)S(1)}, bf16[160,960]{1,0:T(8,128)(2,1)S(1)}, u32[]{:S(2)}, u32[]{:S(2)}) collective-permute-start(bf16[160,960]{1,0:T(8,128)(2,1)S(1)} %fusion.71), channel_id=1, source_target_pairs={{0,8},{1,9},{2,10},{3,11},{4,12},{5,13},{6,14},{7,15},{8,0},{9,1},... | collective-permute-start | bytes 921608 | tf_op jit(solution)/shard_map/ppermute | solution.py:249
  246.5 8.5 %copy-start.38 = (bf16[5,64,3,128]{3,1,2,0:T(8,128)(2,1)S(1)}, bf16[5,64,3,128]{3,1,2,0:T(8,128)(2,1)}, u32[]{:S(2)}) copy-start(bf16[5,64,3,128]{3,1,2,0:T(8,128)(2,1)} %copy-done.37) | copy-start | bytes 737284
  246.7 20.5 %collective-permute-start.22 = (bf16[128,960]{1,0:T(8,128)(2,1)}, bf16[128,960]{1,0:T(8,128)(2,1)}, u32[]{:S(2)}, u32[]{:S(2)}) collective-permute-start(bf16[128,960]{1,0:T(8,128)(2,1)} %get-tuple-element.119.refs_8_), channel_id=1, source_target_pairs={{0,2},{1,3},{2,0},{3,1},{4,6},{5,7},{6,4},{7,5},{8,10},{9,11},{10,... | collective-permute-start | bytes 737288 | tf_op jit(solution)/shard_map/ppermute | solution.py:249
  248.0 19.2 %collective-permute-start.23 = (bf16[128,960]{1,0:T(8,128)(2,1)}, bf16[128,960]{1,0:T(8,128)(2,1)}, u32[]{:S(2)}, u32[]{:S(2)}) collective-permute-start(bf16[128,960]{1,0:T(8,128)(2,1)} %get-tuple-element.119.refs_8_), channel_id=1, source_target_pairs={{0,1},{1,0},{2,3},{3,2},{4,5},{5,4},{6,7},{7,6},{8,9},{9,8},{10,11... | collective-permute-start | bytes 737288 | tf_op jit(solution)/shard_map/ppermute | solution.py:249
  248.2 7.7 %copy-start.40 = (bf16[128,1600]{0,1:T(8,128)(2,1)}, bf16[128,1600]{0,1:T(8,128)(2,1)S(1)}, u32[]{:S(2)}) copy-start(bf16[128,1600]{0,1:T(8,128)(2,1)S(1)} %pad_maximum_fusion.3) | copy-start | bytes 1228804
  255.0 9.3 %copy-start.67 = (f32[960]{0:T(1024)S(1)}, f32[960]{0:T(1024)}, u32[]{:S(2)}) copy-start(f32[960]{0:T(1024)} %copy-done.65) | copy-start | bytes 11524
  255.0 9.2 %copy-start.73 = (f32[128]{0:T(128)S(1)}, f32[128]{0:T(128)}, u32[]{:S(2)}) copy-start(f32[128]{0:T(128)} %copy-done.71) | copy-start | bytes 1540
  260.9 9.6 %collective-permute-start.21 = (bf16[2,1,128,640]{3,2,1,0:T(8,128)(2,1)}, bf16[2,1,128,640]{3,2,1,0:T(8,128)(2,1)S(1)}, u32[]{:S(2)}, u32[]{:S(2)}) collective-permute-start(bf16[2,1,128,640]{3,2,1,0:T(8,128)(2,1)} %bitcast.245), channel_id=1, source_target_pairs={{0,2},{1,3},{2,0},{3,1},{4,6},{5,7},{6,4},{7,5},{8,10},{9,11},{10,... | collective-permute-start | bytes 983048 | tf_op jit(solution)/shard_map/ppermute | solution.py:249
  262.2 17.9 %collective-permute-start.24 = (bf16[2,160,960]{2,1,0:T(8,128)(2,1)}, bf16[2,160,960]{2,1,0:T(8,128)(2,1)S(1)}, u32[]{:S(2)}, u32[]{:S(2)}) collective-permute-start(bf16[2,160,960]{2,1,0:T(8,128)(2,1)} %copy-done.12), channel_id=1, source_target_pairs={{0,4},{1,5},{2,6},{3,7},{4,0},{5,1},{6,2},{7,3},{8,12},{9,13},{10,... | collective-permute-start | bytes 1843208 | tf_op jit(solution)/shard_map/ppermute | solution.py:249
  262.2 37.1 %collective-permute-start.29 = (bf16[2,160,960]{2,1,0:T(8,128)(2,1)}, bf16[2,160,960]{2,1,0:T(8,128)(2,1)}, u32[]{:S(2)}, u32[]{:S(2)}) collective-permute-start(bf16[2,160,960]{2,1,0:T(8,128)(2,1)} %copy-done.11), channel_id=1, source_target_pairs={{0,4},{1,5},{2,6},{3,7},{4,0},{5,1},{6,2},{7,3},{8,12},{9,13},{10,... | collective-permute-start | bytes 1843208 | tf_op jit(solution)/shard_map/ppermute | solution.py:249
  270.5 11.2 %copy-start.9 = (bf16[2,1,128,640]{3,2,1,0:T(8,128)(2,1)}, bf16[2,1,128,640]{3,2,1,0:T(8,128)(2,1)S(1)}, u32[]{:S(2)}) copy-start(bf16[2,1,128,640]{3,2,1,0:T(8,128)(2,1)S(1)} %collective-permute-done.21.refs_2_) | copy-start | bytes 983044
  280.8 4.3 %copy-start.75 = (f32[128]{0:T(128)S(1)}, f32[128]{0:T(128)}, u32[]{:S(2)}) copy-start(f32[128]{0:T(128)} %get-tuple-element.181) | copy-start | bytes 1540
  280.8 6.7 %collective-permute-start.25 = (bf16[2,1,128,640]{3,2,1,0:T(8,128)(2,1)}, bf16[2,1,128,640]{3,2,1,0:T(8,128)(2,1)}, u32[]{:S(2)}, u32[]{:S(2)}) collective-permute-start(bf16[2,1,128,640]{3,2,1,0:T(8,128)(2,1)} %pad_maximum_fusion.5), channel_id=1, source_target_pairs={{0,1},{1,0},{2,3},{3,2},{4,5},{5,4},{6,7},{7,6},{8,9},{9,8},{10,11... | collective-permute-start | bytes 983048 | tf_op jit(solution)/shard_map/ppermute | solution.py:249
  280.9 6.6 %collective-permute-start.26 = (bf16[128,960]{1,0:T(8,128)(2,1)}, bf16[128,960]{1,0:T(8,128)(2,1)}, u32[]{:S(2)}, u32[]{:S(2)}) collective-permute-start(bf16[128,960]{1,0:T(8,128)(2,1)} %collective-permute-done.22.refs_9_), channel_id=1, source_target_pairs={{0,1},{1,0},{2,3},{3,2},{4,5},{5,4},{6,7},{7,6},{8,9},{9,8},{10,11... | collective-permute-start | bytes 737288 | tf_op jit(solution)/shard_map/ppermute | solution.py:249
  281.4 2.3 collective-permute-start.27
  281.7 4.4 %copy-start.35 = (f32[2,160,960]{2,1,0:T(8,128)}, f32[2,160,960]{2,1,0:T(8,128)S(1)}, u32[]{:S(2)}) copy-start(f32[2,160,960]{2,1,0:T(8,128)S(1)} %convert_add_fusion.2) | copy-start | bytes 3686404
  282.6 18.3 %collective-permute-start.30 = (bf16[160,960]{1,0:T(8,128)(2,1)}, bf16[160,960]{1,0:T(8,128)(2,1)}, u32[]{:S(2)}, u32[]{:S(2)}) collective-permute-start(bf16[160,960]{1,0:T(8,128)(2,1)} %fusion.72), channel_id=1, source_target_pairs={{0,8},{1,9},{2,10},{3,11},{4,12},{5,13},{6,14},{7,15},{8,0},{9,1},... | collective-permute-start | bytes 921608 | tf_op jit(solution)/shard_map/ppermute | solution.py:249
  283.7 3.7 %collective-permute-start.28 = (f32[1920]{0:T(1024)S(1)}, f32[1920]{0:T(1024)S(1)}, u32[]{:S(2)}, u32[]{:S(2)}) collective-permute-start(f32[1920]{0:T(1024)S(1)} %add.220), channel_id=1, source_target_pairs={{0,2},{1,3},{2,0},{3,1},{4,6},{5,7},{6,4},{7,5},{8,10},{9,11},{10,... | collective-permute-start | bytes 23048 | tf_op jit(solution)/shard_map/ppermute | solution.py:249
  300.9 4.6 %copy-start.34 = (f32[2,160,960]{2,1,0:T(8,128)S(1)}, f32[2,160,960]{2,1,0:T(8,128)}, u32[]{:S(2)}) copy-start(f32[2,160,960]{2,1,0:T(8,128)} %copy-done.33) | copy-start | bytes 3686404
  300.9 4.6 %copy-start.62 = (bf16[160,960]{1,0:T(8,128)(2,1)S(1)}, bf16[160,960]{1,0:T(8,128)(2,1)}, u32[]{:S(2)}) copy-start(bf16[160,960]{1,0:T(8,128)(2,1)} %copy-done.61) | copy-start | bytes 921604
  300.9 22.1 %collective-permute-start.31 = (bf16[2,168,960]{2,1,0:T(8,128)(2,1)S(1)}, bf16[2,168,960]{2,1,0:T(8,128)(2,1)S(1)}, u32[]{:S(2)}, u32[]{:S(2)}) collective-permute-start(bf16[2,168,960]{2,1,0:T(8,128)(2,1)S(1)} %get-tuple-element.136), channel_id=1, source_target_pairs={{0,4},{1,5},{2,6},{3,7},{4,0},{5,1},{6,2},{7,3},{8,12},{9,13},{10,... | collective-permute-start | bytes 1935368 | tf_op jit(solution)/shard_map/ppermute | solution.py:249
  302.6 19.6 %collective-permute-start.32 = (bf16[160,960]{1,0:T(8,128)(2,1)S(1)}, bf16[160,960]{1,0:T(8,128)(2,1)S(1)}, u32[]{:S(2)}, u32[]{:S(2)}) collective-permute-start(bf16[160,960]{1,0:T(8,128)(2,1)S(1)} %fusion.73), channel_id=1, source_target_pairs={{0,8},{1,9},{2,10},{3,11},{4,12},{5,13},{6,14},{7,15},{8,0},{9,1},... | collective-permute-start | bytes 921608 | tf_op jit(solution)/shard_map/ppermute | solution.py:249
  323.3 17.3 %collective-permute-start.33 = (bf16[168,960]{1,0:T(8,128)(2,1)S(1)}, bf16[168,960]{1,0:T(8,128)(2,1)S(1)}, u32[]{:S(2)}, u32[]{:S(2)}) collective-permute-start(bf16[168,960]{1,0:T(8,128)(2,1)S(1)} %fusion.70), channel_id=1, source_target_pairs={{0,8},{1,9},{2,10},{3,11},{4,12},{5,13},{6,14},{7,15},{8,0},{9,1},... | collective-permute-start | bytes 967688 | tf_op jit(solution)/shard_map/ppermute | solution.py:249
  (52 other events, 96.4 us)
Sparse Core Ops, SparseCore 0:
  10.2 111.5 all-gather.1

commit v14 on v13

--- a/solution.py
+++ b/solution.py
@@ -213,7 +213,7 @@
         out_shape=[jax.ShapeDtypeStruct((steps, *shape), t) for shape, t in out_blocks]
         + [jax.ShapeDtypeStruct((tokens, width), f32)],
         compiler_params=pltpu.CompilerParams(
-            dimension_semantics=("arbitrary",), vmem_limit_bytes=40 * 1024 * 1024
+            dimension_semantics=("arbitrary",), vmem_limit_bytes=24 * 1024 * 1024
         ),
         cost_estimate=pl.CostEstimate(
             flops=6 * tokens * steps * cols * width,
@@ -384,7 +384,7 @@
         ),
         out_shape=shapes,
         compiler_params=pltpu.CompilerParams(
-            dimension_semantics=("arbitrary",), vmem_limit_bytes=32 * 1024 * 1024
+            dimension_semantics=("arbitrary",), vmem_limit_bytes=20 * 1024 * 1024
         ),
         cost_estimate=pl.CostEstimate(
             flops=8 * tokens * kinds * width_cols * width * len(rows),

time: 350 us -> 371 us (1.060)
  local copies, waits for them, and re-layouts: 22.3 us -> 50.7 us
  Pallas kernels: 46.5 us -> 39.1 us
    unnamed x162 -> x166, local copies, waits for them, and re-layouts: 6.91 us -> 35.3 us
    pallas_call x4, Pallas kernels: 36.6 us -> 29.2 us  [ffn_call(): pl.pallas_call(kernel, grid=(steps,), in_specs=[whole] * len(wholes) + [b...]
    ppermute x32, waiting for transfers between devices: 75.4 us -> 71.6 us  [flip(): return lax.ppermute(x, 'dp', [(i, i ^ bit) for i in range(size)])]
  transfers between devices with their start and end apart: 35 -> 35, of which waited for: 20 -> 18; matrix products, arithmetic and copies ran while one was open for 8% -> 8% of each run, Pallas kernels for 11% -> 9%
where the time goes in v14:
time: 371 us; the launch traced here: 370 us
  waiting for transfers between devices  184 us (50%)
  local copies, waits for them, and re-layouts  50.7 us (14%)
  Pallas kernels  39.1 us (11%)
  starting transfers between devices  38.4 us (10%)
  matrix products  21.6 us (6%)
  other arithmetic  21 us (6%)
  between operations  15.5 us (4%)
    all_gather x1, waiting for transfers between devices, local(): lax.all_gather(own, 'dp', axis=0, tiled=True).reshape(4, 4, 4, share, width)  97.3 us
    ppermute x32, waiting for transfers between devices, flip(): return lax.ppermute(x, 'dp', [(i, i ^ bit) for i in range(size)])  71.6 us
    unnamed x166, local copies, waits for them, and re-layouts  35.3 us
    ppermute x32, starting transfers between devices, flip(): return lax.ppermute(x, 'dp', [(i, i ^ bit) for i in range(size)])  33.2 us
    pallas_call x4, Pallas kernels, ffn_call(): pl.pallas_call(kernel, grid=(steps,), in_specs=[whole] * len(wholes) + [b...  29.2 us
    pallas_call x3, Pallas kernels, plane_product(): pl.pallas_call(kernel, grid_spec=pltpu.PrefetchScalarGridSpec(num_scalar_...  9.9 us
    dot_general x4, matrix products, dot_nt(): lax.dot_general(a, b, (((1,), (1,)), ((), ())), preferred_element_type=f32)  9.51 us
    ppermute x1, waiting for transfers between devices, local(): received = lax.ppermute(first_grad, 'section', [(1, 0)])  9.2 us
  transfers between devices with their start and end apart: 35, of which 18 were waited for; matrix products, arithmetic and copies ran while one was open for 8% of the time, Pallas kernels for 9%

profile of v14, /device:TPU:0, one launch (start us, length us, event | category | flops | bytes accessed | tf_op | source)
XLA Modules:
  0.0 370.2 jit_solution(7765736807940664856)
XLA Ops:
  7.2 2.5 pad_maximum_fusion
  11.2 2.8 collective-permute-start.1
  14.2 1.4 collective-permute-done.1
  15.7 2.1 collective-permute-start.2
  17.9 1.4 collective-permute-done.2
  19.5 3.0 collective-permute-start.3
  22.8 1.3 collective-permute-done.3
  24.4 97.3 %all-gather.2.cloned.1.call-done = bf16[10240,960]{1,0:T(8,128)(2,1)} async-done(((bf16[640,960]{1,0:T(8,128)(2,1)}), bf16[10240,960]{1,0:T(8,128)(2,1)}) %all-gather.2.cloned.1.call-update) | async-done | bytes 19660816 | tf_op jit(solution)/shard_map/all_gather | solution.py:524
  121.8 3.4 slice.127
  125.2 1.1 fusion.6
  128.3 7.0 %copy-done = bf16[10240,960]{1,0:T(8,128)(2,1)S(1)} copy-done((bf16[10240,960]{1,0:T(8,128)(2,1)S(1)}, bf16[10240,960]{1,0:T(8,128)(2,1)}, u32[]{:S(2)}) %copy-start) | copy-done | bytes 19660824
  135.2 7.2 %shard_map.84 = (f32[4,128,640]{2,1,0:T(8,128)}, f32[4,128,640]{2,1,0:T(8,128)}, bf16[4,128,640]{2,1,0:T(8,128)(2,1)}, f32[128,960]{1,0:T(8,128)S(1)}) custom-call(bf16[128,960]{1,0:T(8,128)(2,1)S(1)} %multiply_convert_fusion.3.m_ref, f32[128,960]{1,0:T(8,128)S(1)} %get-tuple-element.188.h1_ref, bf16[4,4,4,160,960]{4,3,2,1,0:T(8,128)(2,1)S(1)} %bitcast.193, ...), custom_call_target="tpu_custom_call" | custom-call | flops 1887436800 | bytes 14745600 | tf_op jit(solution)/shard_map/pallas_call | solution.py:206
  142.4 3.6 collective-permute-start.4
  146.0 5.8 %collective-permute-done.4 = bf16[128,960]{1,0:T(8,128)(2,1)S(1)} collective-permute-done((bf16[128,960]{1,0:T(8,128)(2,1)S(1)}, bf16[128,960]{1,0:T(8,128)(2,1)S(1)}, u32[]{:S(2)}, u32[]{:S(2)}) %collective-permute-start.4) | collective-permute-done | bytes 245792 | tf_op jit(solution)/shard_map/ppermute | solution.py:539
  153.4 3.0 fusion.4
  158.4 2.2 multiply_reduce_fusion.5
  161.4 1.3 collective-permute-start.5
  163.5 7.0 %copy-done.1 = bf16[10240,960]{1,0:T(8,128)(2,1)S(1)} copy-done((bf16[10240,960]{1,0:T(8,128)(2,1)S(1)}, bf16[10240,960]{1,0:T(8,128)(2,1)}, u32[]{:S(2)}) %copy-start.1) | copy-done | bytes 19660824
  170.4 6.8 %shard_map.85 = (f32[4,128,640]{2,1,0:T(8,128)S(1)}, f32[4,128,640]{2,1,0:T(8,128)S(1)}, bf16[4,128,640]{2,1,0:T(8,128)(2,1)S(1)}, f32[128,960]{1,0:T(8,128)S(1)}) custom-call(bf16[128,960]{1,0:T(8,128)(2,1)} %multiply_convert_fusion.2.m_ref.refs_4_, f32[128,960]{1,0:T(8,128)S(1)} %get-tuple-element.192.h1_ref, bf16[4,4,4,160,960]{4,3,2,1,0:T(8,128)(2,1)S(1)} %bitcast.196, ...), custom_call_target="tpu_custom_call" | custom-call | flops 1887436800 | bytes 14745600 | tf_op jit(solution)/shard_map/pallas_call | solution.py:206
  178.9 1.2 collective-permute-start.7
  182.1 7.0 %copy-done.2 = bf16[10240,960]{1,0:T(8,128)(2,1)S(1)} copy-done((bf16[10240,960]{1,0:T(8,128)(2,1)S(1)}, bf16[10240,960]{1,0:T(8,128)(2,1)}, u32[]{:S(2)}) %copy-start.2) | copy-done | bytes 19660824
  189.1 7.6 %shard_map.86 = (bf16[4,2,128,640]{3,2,1,0:T(8,128)(2,1)}, f32[128,960]{1,0:T(8,128)S(1)}) custom-call(bf16[128,960]{1,0:T(8,128)(2,1)S(1)} %bitcast.207, f32[4,128,640]{2,1,0:T(8,128)S(1)} %get-tuple-element.79.gate_ref, f32[4,128,640]{2,1,0:T(8,128)S(1)} %get-tuple-element.80.up_ref, bf16[4,4,4,160,960]{4,3,2,1,0:T(8,128)(2,1)S(1)} %bitcast.199, ...), custom_call_target="tpu_custom_call" | custom-call | flops 1887436800 | bytes 14745600 | tf_op jit(solution)/shard_map/pallas_call | solution.py:206
  197.1 2.3 fusion.30
  203.4 2.7 fusion.59
  206.4 1.5 collective-permute-start.13
  207.9 9.2 %collective-permute-done.13 = bf16[128,960]{1,0:T(8,128)(2,1)S(1)} collective-permute-done((bf16[128,960]{1,0:T(8,128)(2,1)S(1)}, bf16[128,960]{1,0:T(8,128)(2,1)S(1)}, u32[]{:S(2)}, u32[]{:S(2)}) %collective-permute-start.13) | collective-permute-done | bytes 245792 | tf_op jit(solution)/shard_map/ppermute | solution.py:543
  218.7 7.0 %copy-done.3 = bf16[10240,960]{1,0:T(8,128)(2,1)S(1)} copy-done((bf16[10240,960]{1,0:T(8,128)(2,1)S(1)}, bf16[10240,960]{1,0:T(8,128)(2,1)}, u32[]{:S(2)}) %copy-start.3) | copy-done | bytes 19660824
  225.7 7.6 %shard_map.87 = (bf16[4,2,128,640]{3,2,1,0:T(8,128)(2,1)S(1)}, f32[128,960]{1,0:T(8,128)S(1)}) custom-call(bf16[128,960]{1,0:T(8,128)(2,1)} %broadcast_select_fusion.eb_ref.refs_4_, f32[4,128,640]{2,1,0:T(8,128)S(1)} %get-tuple-element.79.gate_ref, f32[4,128,640]{2,1,0:T(8,128)S(1)} %get-tuple-element.80.up_ref, bf16[4,4,4,160,960]{4,3,2,1,0:T(8,128)(2,1)S(1)} %bitcast.202, ...), custom_call_target="tpu_custom_call" | custom-call | flops 1887436800 | bytes 14745600 | tf_op jit(solution)/shard_map/pallas_call | solution.py:206
  234.0 1.3 collective-permute-start.17
  235.4 2.8 shard_map.88
  238.4 1.6 collective-permute-start.18
  240.0 2.1 fusion.92
  242.0 3.0 fusion.33
  245.1 5.7 %collective-permute-done.17.refs_2_ = bf16[2,2,128,640]{3,2,1,0:T(8,128)(2,1)S(1)} collective-permute-done((bf16[2,2,128,640]{3,2,1,0:T(8,128)(2,1)S(1)}, bf16[2,2,128,640]{3,2,1,0:T(8,128)(2,1)S(1)}, u32[]{:S(2)}, u32[]{:S(2)}) %collective-permute-start.17) | collective-permute-done | bytes 655392 | tf_op jit(solution)/shard_map/ppermute | solution.py:249
  250.7 4.6 %collective-permute-done.18 = bf16[2,160,960]{2,1,0:T(8,128)(2,1)S(1)} collective-permute-done((bf16[2,160,960]{2,1,0:T(8,128)(2,1)S(1)}, bf16[2,160,960]{2,1,0:T(8,128)(2,1)S(1)}, u32[]{:S(2)}, u32[]{:S(2)}) %collective-permute-start.18) | collective-permute-done | bytes 614432 | tf_op jit(solution)/shard_map/ppermute | solution.py:249
  255.4 1.0 pad_maximum_fusion.1
  256.6 1.4 convert_add_fusion.3
  258.1 2.5 collective-permute-start.20
  261.4 1.1 copy-done.18
  262.5 3.4 shard_map.89
  268.0 1.3 collective-permute-start.22
  269.5 6.7 %collective-permute-done.20 = bf16[160,960]{1,0:T(8,128)(2,1)S(1)} collective-permute-done((bf16[160,960]{1,0:T(8,128)(2,1)S(1)}, bf16[160,960]{1,0:T(8,128)(2,1)S(1)}, u32[]{:S(2)}, u32[]{:S(2)}) %collective-permute-start.20) | collective-permute-done | bytes 307232 | tf_op jit(solution)/shard_map/ppermute | solution.py:249
  277.2 1.4 copy.43.refs_1_
  278.5 1.7 constant_dynamic-slice_fusion.3
  280.3 1.9 copy.41
  282.1 1.3 collective-permute-start.21
  283.4 2.1 collective-permute-start.29
  285.5 2.9 fusion.62
  288.5 3.2 collective-permute-done.21.refs_2_
  291.7 9.6 %collective-permute-done.24 = bf16[2,160,960]{2,1,0:T(8,128)(2,1)S(1)} collective-permute-done((bf16[2,160,960]{2,1,0:T(8,128)(2,1)}, bf16[2,160,960]{2,1,0:T(8,128)(2,1)S(1)}, u32[]{:S(2)}, u32[]{:S(2)}) %collective-permute-start.24) | collective-permute-done | bytes 614432 | tf_op jit(solution)/shard_map/ppermute | solution.py:249
  303.8 1.1 collective-permute-start.30
  304.9 1.4 collective-permute-start.28
  306.4 1.0 fusion.53
  307.4 1.2 collective-permute-done.28
  311.6 3.7 %shard_map.90 = (f32[2,168,960]{2,1,0:T(8,128)S(1)}, bf16[2,168,960]{2,1,0:T(8,128)(2,1)S(1)}) custom-call(s32[7]{0:T(128)S(1)} %stack.86.refs_0_, bf16[4,1,128,640]{3,2,1,0:T(8,128)(2,1)S(1)} %copy.43.refs_1_, bf16[2,1,128,640]{3,2,1,0:T(8,128)(2,1)S(1)} %copy-done.14, bf16[2,1,128,640]{3,2,1,0:T(8,128)(2,1)} %collective-permute-done.25.refs_3_, ...), custom_call_target="tpu_custom_call" | custom-call | flops 1258291200 | bytes 4096000 | tf_op jit(solution)/shard_map/pallas_call | solution.py:376
  315.3 5.2 %collective-permute-done.29 = bf16[2,160,960]{2,1,0:T(8,128)(2,1)} collective-permute-done((bf16[2,160,960]{2,1,0:T(8,128)(2,1)}, bf16[2,160,960]{2,1,0:T(8,128)(2,1)}, u32[]{:S(2)}, u32[]{:S(2)}) %collective-permute-start.29) | collective-permute-done | bytes 614432 | tf_op jit(solution)/shard_map/ppermute | solution.py:249
  320.5 1.6 collective-permute-done.30
  322.4 1.4 convert_add_fusion.1
  323.8 2.9 collective-permute-start.32
  326.8 1.1 fusion.44
  327.9 15.6 %collective-permute-done.32 = bf16[160,960]{1,0:T(8,128)(2,1)S(1)} collective-permute-done((bf16[160,960]{1,0:T(8,128)(2,1)S(1)}, bf16[160,960]{1,0:T(8,128)(2,1)S(1)}, u32[]{:S(2)}, u32[]{:S(2)}) %collective-permute-start.32) | collective-permute-done | bytes 307232 | tf_op jit(solution)/shard_map/ppermute | solution.py:249
  344.5 2.7 collective-permute-start.33
  347.3 1.5 maximum_bitcast_fusion
  348.8 13.0 %collective-permute-done.33 = bf16[168,960]{1,0:T(8,128)(2,1)S(1)} collective-permute-done((bf16[168,960]{1,0:T(8,128)(2,1)S(1)}, bf16[168,960]{1,0:T(8,128)(2,1)S(1)}, u32[]{:S(2)}, u32[]{:S(2)}) %collective-permute-start.33) | collective-permute-done | bytes 322592 | tf_op jit(solution)/shard_map/ppermute | solution.py:249
  (310 shorter events, 32.6 us)
Async XLA Ops:
  7.2 114.6 %all-gather.2.cloned.1.call-start = ((), (), s32[]{:S(2)}) async-start(), calls=%async_computation | async-start | bytes 22282240 | tf_op jit(solution)/shard_map/all_gather | solution.py:524
  7.2 10.5 %copy-start.4 = (bf16[1,2,64,960]{3,2,1,0:T(8,128)(2,1)S(1)}, bf16[1,2,64,960]{3,2,1,0:T(8,128)(2,1)}, u32[]{:S(2)}) copy-start(bf16[1,2,64,960]{3,2,1,0:T(8,128)(2,1)} %param.5) | copy-start | bytes 737284
  9.8 1.3 collective-permute-start
  11.2 4.3 %collective-permute-start.1 = (bf16[240]{0:T(256)(128)(2,1)S(1)}, bf16[240]{0:T(256)(128)(2,1)S(1)}, u32[]{:S(2)}, u32[]{:S(2)}) collective-permute-start(bf16[240]{0:T(256)(128)(2,1)S(1)} %pad_maximum_fusion.17), channel_id=1, source_target_pairs={{0,2},{1,3},{2,0},{3,1},{4,6},{5,7},{6,4},{7,5},{8,10},{9,11},{10,... | collective-permute-start | bytes 1448 | tf_op jit(solution)/shard_map/ppermute | solution.py:249
  14.2 187.3 %copy-start.55 = (f32[128,32]{0,1:T(8,128)}, f32[128,32]{0,1:T(8,128)S(1)}, u32[]{:S(2)}) copy-start(f32[128,32]{0,1:T(8,128)S(1)} %get-tuple-element.174) | copy-start | bytes 49156
  15.7 3.6 collective-permute-start.2
  19.5 4.7 %collective-permute-start.3 = (bf16[960]{0:T(1024)(128)(2,1)S(1)}, bf16[960]{0:T(1024)(128)(2,1)S(1)}, u32[]{:S(2)}, u32[]{:S(2)}) collective-permute-start(bf16[960]{0:T(1024)(128)(2,1)S(1)} %pad_maximum_fusion.15), channel_id=1, source_target_pairs={{0,8},{1,9},{2,10},{3,11},{4,12},{5,13},{6,14},{7,15},{8,0},{9,1},... | collective-permute-start | bytes 5768 | tf_op jit(solution)/shard_map/ppermute | solution.py:249
  24.4 128.2 %copy-start.69 = (f32[960]{0:T(1024)}, f32[960]{0:T(1024)S(1)}, u32[]{:S(2)}) copy-start(f32[960]{0:T(1024)S(1)} %get-tuple-element.169) | copy-start | bytes 11524
  24.4 172.5 %copy-start.67 = (f32[960]{0:T(1024)}, f32[960]{0:T(1024)S(1)}, u32[]{:S(2)}) copy-start(f32[960]{0:T(1024)S(1)} %get-tuple-element.168) | copy-start | bytes 11524
  128.3 7.0 %copy-start = (bf16[10240,960]{1,0:T(8,128)(2,1)S(1)}, bf16[10240,960]{1,0:T(8,128)(2,1)}, u32[]{:S(2)}) copy-start(bf16[10240,960]{1,0:T(8,128)(2,1)} %all-gather.2.cloned.1.call-done) | copy-start | bytes 58982404
  142.4 9.3 %collective-permute-start.4 = (bf16[128,960]{1,0:T(8,128)(2,1)S(1)}, bf16[128,960]{1,0:T(8,128)(2,1)S(1)}, u32[]{:S(2)}, u32[]{:S(2)}) collective-permute-start(bf16[128,960]{1,0:T(8,128)(2,1)S(1)} %convert_element_type.168), channel_id=1, source_target_pairs={{0,16},{1,17},{2,18},{3,19},{4,20},{5,21},{6,22},{7,23},{8,24},{9,... | collective-permute-start | bytes 737288 | tf_op jit(solution)/shard_map/ppermute | solution.py:539
  152.0 6.4 %copy-start.34 = (bf16[128,960]{1,0:T(8,128)(2,1)}, bf16[128,960]{1,0:T(8,128)(2,1)S(1)}, u32[]{:S(2)}) copy-start(bf16[128,960]{1,0:T(8,128)(2,1)S(1)} %get-tuple-element.151) | copy-start | bytes 737284
  156.5 43.4 %copy-start.45 = (bf16[128,320]{0,1:T(8,128)(2,1)}, bf16[128,320]{0,1:T(8,128)(2,1)S(1)}, u32[]{:S(2)}) copy-start(bf16[128,320]{0,1:T(8,128)(2,1)S(1)} %slice.218) | copy-start | bytes 245764
  157.4 42.9 %copy-start.57 = (f32[5,3,128]{2,1,0:T(4,128)}, f32[5,3,128]{2,1,0:T(4,128)S(1)}, u32[]{:S(2)}) copy-start(f32[5,3,128]{2,1,0:T(4,128)S(1)} %log_add_fusion) | copy-start | bytes 23044
  160.6 36.3 %copy-start.73 = (f32[128]{0:T(128)}, f32[128]{0:T(128)S(1)}, u32[]{:S(2)}) copy-start(f32[128]{0:T(128)S(1)} %get-tuple-element.184) | copy-start | bytes 1540
  160.6 36.3 %copy-start.80 = (f32[128]{0:T(128)}, f32[128]{0:T(128)S(1)}, u32[]{:S(2)}) copy-start(f32[128]{0:T(128)S(1)} %get-tuple-element.183) | copy-start | bytes 1540
  161.4 15.9 %collective-permute-start.5 = (bf16[128,960]{1,0:T(8,128)(2,1)}, bf16[128,960]{1,0:T(8,128)(2,1)}, u32[]{:S(2)}, u32[]{:S(2)}) collective-permute-start(bf16[128,960]{1,0:T(8,128)(2,1)} %multiply_convert_fusion.2.m_ref.refs_4_), channel_id=1, source_target_pairs={{0,2},{1,3},{2,0},{3,1},{4,6},{5,7},{6,4},{7,5},{8,10},{9,11},{10,... | collective-permute-start | bytes 737288 | tf_op jit(solution)/shard_map/ppermute | solution.py:249
  162.7 14.6 %collective-permute-start.6 = (bf16[128,960]{1,0:T(8,128)(2,1)}, bf16[128,960]{1,0:T(8,128)(2,1)}, u32[]{:S(2)}, u32[]{:S(2)}) collective-permute-start(bf16[128,960]{1,0:T(8,128)(2,1)} %fusion.58.refs_4_), channel_id=1, source_target_pairs={{0,2},{1,3},{2,0},{3,1},{4,6},{5,7},{6,4},{7,5},{8,10},{9,11},{10,... | collective-permute-start | bytes 737288 | tf_op jit(solution)/shard_map/ppermute | solution.py:249
  163.5 7.0 %copy-start.1 = (bf16[10240,960]{1,0:T(8,128)(2,1)S(1)}, bf16[10240,960]{1,0:T(8,128)(2,1)}, u32[]{:S(2)}) copy-start(bf16[10240,960]{1,0:T(8,128)(2,1)} %all-gather.2.cloned.1.call-done) | copy-start | bytes 58982404
  178.9 17.8 %collective-permute-start.7 = (bf16[2,1,128,640]{3,2,1,0:T(8,128)(2,1)}, bf16[2,1,128,640]{3,2,1,0:T(8,128)(2,1)}, u32[]{:S(2)}, u32[]{:S(2)}) collective-permute-start(bf16[2,1,128,640]{3,2,1,0:T(8,128)(2,1)} %dynamic-slice_bitcast_fusion.1), channel_id=1, source_target_pairs={{0,2},{1,3},{2,0},{3,1},{4,6},{5,7},{6,4},{7,5},{8,10},{9,11},{10,... | collective-permute-start | bytes 983048 | tf_op jit(solution)/shard_map/ppermute | solution.py:249
  180.1 16.5 %collective-permute-start.8 = (bf16[128,960]{1,0:T(8,128)(2,1)}, bf16[128,960]{1,0:T(8,128)(2,1)S(1)}, u32[]{:S(2)}, u32[]{:S(2)}) collective-permute-start(bf16[128,960]{1,0:T(8,128)(2,1)} %multiply_convert_fusion.2.m_ref.refs_4_), channel_id=1, source_target_pairs={{0,1},{1,0},{2,3},{3,2},{4,5},{5,4},{6,7},{7,6},{8,9},{9,8},{10,11... | collective-permute-start | bytes 737288 | tf_op jit(solution)/shard_map/ppermute | solution.py:249
  180.1 16.5 %collective-permute-start.10 = (bf16[128,960]{1,0:T(8,128)(2,1)}, bf16[128,960]{1,0:T(8,128)(2,1)S(1)}, u32[]{:S(2)}, u32[]{:S(2)}) collective-permute-start(bf16[128,960]{1,0:T(8,128)(2,1)} %fusion.58.refs_4_), channel_id=1, source_target_pairs={{0,1},{1,0},{2,3},{3,2},{4,5},{5,4},{6,7},{7,6},{8,9},{9,8},{10,11... | collective-permute-start | bytes 737288 | tf_op jit(solution)/shard_map/ppermute | solution.py:249
  180.6 16.0 %collective-permute-start.9 = (bf16[128,960]{1,0:T(8,128)(2,1)}, bf16[128,960]{1,0:T(8,128)(2,1)S(1)}, u32[]{:S(2)}, u32[]{:S(2)}) collective-permute-start(bf16[128,960]{1,0:T(8,128)(2,1)} %collective-permute-done.5.refs_5_), channel_id=1, source_target_pairs={{0,1},{1,0},{2,3},{3,2},{4,5},{5,4},{6,7},{7,6},{8,9},{9,8},{10,11... | collective-permute-start | bytes 737288 | tf_op jit(solution)/shard_map/ppermute | solution.py:249
  180.6 16.1 %collective-permute-start.11 = (bf16[128,960]{1,0:T(8,128)(2,1)}, bf16[128,960]{1,0:T(8,128)(2,1)S(1)}, u32[]{:S(2)}, u32[]{:S(2)}) collective-permute-start(bf16[128,960]{1,0:T(8,128)(2,1)} %collective-permute-done.6.refs_5_), channel_id=1, source_target_pairs={{0,1},{1,0},{2,3},{3,2},{4,5},{5,4},{6,7},{7,6},{8,9},{9,8},{10,11... | collective-permute-start | bytes 737288 | tf_op jit(solution)/shard_map/ppermute | solution.py:249
  182.1 7.0 %copy-start.2 = (bf16[10240,960]{1,0:T(8,128)(2,1)S(1)}, bf16[10240,960]{1,0:T(8,128)(2,1)}, u32[]{:S(2)}) copy-start(bf16[10240,960]{1,0:T(8,128)(2,1)} %all-gather.2.cloned.1.call-done) | copy-start | bytes 58982404
  203.3 3.1 collective-permute-start.12
  206.4 11.5 %copy-start.11 = (bf16[2,1,128,640]{3,2,1,0:T(8,128)(2,1)}, bf16[2,1,128,640]{3,2,1,0:T(8,128)(2,1)S(1)}, u32[]{:S(2)}) copy-start(bf16[2,1,128,640]{3,2,1,0:T(8,128)(2,1)S(1)} %collective-permute-done.12.refs_3_) | copy-start | bytes 983044
  206.4 10.7 %collective-permute-start.13 = (bf16[128,960]{1,0:T(8,128)(2,1)S(1)}, bf16[128,960]{1,0:T(8,128)(2,1)S(1)}, u32[]{:S(2)}, u32[]{:S(2)}) collective-permute-start(bf16[128,960]{1,0:T(8,128)(2,1)S(1)} %fusion.49), channel_id=1, source_target_pairs={{16,0},{17,1},{18,2},{19,3},{20,4},{21,5},{22,6},{23,7},{24,8},{25... | collective-permute-start | bytes 737288 | tf_op jit(solution)/shard_map/ppermute | solution.py:543
  217.9 15.5 %collective-permute-start.14 = (bf16[128,960]{1,0:T(8,128)(2,1)}, bf16[128,960]{1,0:T(8,128)(2,1)}, u32[]{:S(2)}, u32[]{:S(2)}) collective-permute-start(bf16[128,960]{1,0:T(8,128)(2,1)} %broadcast_select_fusion.eb_ref.refs_4_), channel_id=1, source_target_pairs={{0,2},{1,3},{2,0},{3,1},{4,6},{5,7},{6,4},{7,5},{8,10},{9,11},{10,... | collective-permute-start | bytes 737288 | tf_op jit(solution)/shard_map/ppermute | solution.py:249
  218.6 14.7 %collective-permute-start.15 = (bf16[128,960]{1,0:T(8,128)(2,1)}, bf16[128,960]{1,0:T(8,128)(2,1)}, u32[]{:S(2)}, u32[]{:S(2)}) collective-permute-start(bf16[128,960]{1,0:T(8,128)(2,1)} %broadcast_select_fusion.eb_ref.refs_4_), channel_id=1, source_target_pairs={{0,1},{1,0},{2,3},{3,2},{4,5},{5,4},{6,7},{7,6},{8,9},{9,8},{10,11... | collective-permute-start | bytes 737288 | tf_op jit(solution)/shard_map/ppermute | solution.py:249
  218.7 7.0 %copy-start.3 = (bf16[10240,960]{1,0:T(8,128)(2,1)S(1)}, bf16[10240,960]{1,0:T(8,128)(2,1)}, u32[]{:S(2)}) copy-start(bf16[10240,960]{1,0:T(8,128)(2,1)} %all-gather.2.cloned.1.call-done) | copy-start | bytes 58982404
  233.3 4.9 %copy-start.7 = (bf16[4,2,128,640]{3,2,1,0:T(8,128)(2,1)}, bf16[4,2,128,640]{3,2,1,0:T(8,128)(2,1)S(1)}, u32[]{:S(2)}) copy-start(bf16[4,2,128,640]{3,2,1,0:T(8,128)(2,1)S(1)} %get-tuple-element.101.refs_1_) | copy-start | bytes 3932164
  233.3 2.0 collective-permute-start.16
  234.0 6.0 %copy-start.81 = (f32[128]{0:T(128)S(1)}, f32[128]{0:T(128)}, u32[]{:S(2)}) copy-start(f32[128]{0:T(128)} %copy-done.80) | copy-start | bytes 1540
  234.0 16.7 %collective-permute-start.17 = (bf16[2,2,128,640]{3,2,1,0:T(8,128)(2,1)S(1)}, bf16[2,2,128,640]{3,2,1,0:T(8,128)(2,1)S(1)}, u32[]{:S(2)}, u32[]{:S(2)}) collective-permute-start(bf16[2,2,128,640]{3,2,1,0:T(8,128)(2,1)S(1)} %dynamic-slice_bitcast_fusion), channel_id=1, source_target_pairs={{0,2},{1,3},{2,0},{3,1},{4,6},{5,7},{6,4},{7,5},{8,10},{9,11},{10,... | collective-permute-start | bytes 1966088 | tf_op jit(solution)/shard_map/ppermute | solution.py:249
  238.4 17.0 %collective-permute-start.18 = (bf16[2,160,960]{2,1,0:T(8,128)(2,1)S(1)}, bf16[2,160,960]{2,1,0:T(8,128)(2,1)S(1)}, u32[]{:S(2)}, u32[]{:S(2)}) collective-permute-start(bf16[2,160,960]{2,1,0:T(8,128)(2,1)S(1)} %get-tuple-element.103), channel_id=1, source_target_pairs={{0,4},{1,5},{2,6},{3,7},{4,0},{5,1},{6,2},{7,3},{8,12},{9,13},{10,... | collective-permute-start | bytes 1843208 | tf_op jit(solution)/shard_map/ppermute | solution.py:249
  256.4 4.2 %collective-permute-start.19 = (bf16[2,2,128,640]{3,2,1,0:T(8,128)(2,1)}, bf16[2,2,128,640]{3,2,1,0:T(8,128)(2,1)S(1)}, u32[]{:S(2)}, u32[]{:S(2)}) collective-permute-start(bf16[2,2,128,640]{3,2,1,0:T(8,128)(2,1)} %pad_maximum_fusion.1), channel_id=1, source_target_pairs={{0,1},{1,0},{2,3},{3,2},{4,5},{5,4},{6,7},{7,6},{8,9},{9,8},{10,11... | collective-permute-start | bytes 1966088 | tf_op jit(solution)/shard_map/ppermute | solution.py:249
  256.6 4.8 %copy-start.8 = (bf16[4,2,128,640]{3,2,1,0:T(8,128)(2,1)S(1)}, bf16[4,2,128,640]{3,2,1,0:T(8,128)(2,1)}, u32[]{:S(2)}) copy-start(bf16[4,2,128,640]{3,2,1,0:T(8,128)(2,1)} %copy-done.7) | copy-start | bytes 3932164
  256.6 4.8 %copy-start.24 = (bf16[128,960]{1,0:T(8,128)(2,1)S(1)}, bf16[128,960]{1,0:T(8,128)(2,1)}, u32[]{:S(2)}) copy-start(bf16[128,960]{1,0:T(8,128)(2,1)} %copy-done.23) | copy-start | bytes 737284
  256.6 4.8 %copy-start.26 = (bf16[128,960]{1,0:T(8,128)(2,1)S(1)}, bf16[128,960]{1,0:T(8,128)(2,1)}, u32[]{:S(2)}) copy-start(bf16[128,960]{1,0:T(8,128)(2,1)} %copy-done.25) | copy-start | bytes 737284
  258.0 8.0 %copy-start.33 = (bf16[5,3,128,128]{2,3,1,0:T(8,128)(2,1)S(1)}, bf16[5,3,128,128]{2,3,1,0:T(8,128)(2,1)}, u32[]{:S(2)}) copy-start(bf16[5,3,128,128]{2,3,1,0:T(8,128)(2,1)} %copy-done.31) | copy-start | bytes 1474564
  258.0 8.3 %copy-start.46 = (bf16[128,320]{0,1:T(8,128)(2,1)S(1)}, bf16[128,320]{0,1:T(8,128)(2,1)}, u32[]{:S(2)}) copy-start(bf16[128,320]{0,1:T(8,128)(2,1)} %copy-done.45) | copy-start | bytes 245764
  258.0 8.3 %copy-start.58 = (f32[5,3,128]{2,1,0:T(4,128)S(1)}, f32[5,3,128]{2,1,0:T(4,128)}, u32[]{:S(2)}) copy-start(f32[5,3,128]{2,1,0:T(4,128)} %copy-done.57) | copy-start | bytes 23044
  258.1 18.1 %collective-permute-start.20 = (bf16[160,960]{1,0:T(8,128)(2,1)S(1)}, bf16[160,960]{1,0:T(8,128)(2,1)S(1)}, u32[]{:S(2)}, u32[]{:S(2)}) collective-permute-start(bf16[160,960]{1,0:T(8,128)(2,1)S(1)} %fusion.71), channel_id=1, source_target_pairs={{0,8},{1,9},{2,10},{3,11},{4,12},{5,13},{6,14},{7,15},{8,0},{9,1},... | collective-permute-start | bytes 921608 | tf_op jit(solution)/shard_map/ppermute | solution.py:249
  267.7 8.5 %copy-start.42 = (bf16[5,64,3,128]{3,1,2,0:T(8,128)(2,1)S(1)}, bf16[5,64,3,128]{3,1,2,0:T(8,128)(2,1)}, u32[]{:S(2)}) copy-start(bf16[5,64,3,128]{3,1,2,0:T(8,128)(2,1)} %copy-done.41) | copy-start | bytes 737284
  268.0 20.5 %collective-permute-start.22 = (bf16[128,960]{1,0:T(8,128)(2,1)}, bf16[128,960]{1,0:T(8,128)(2,1)}, u32[]{:S(2)}, u32[]{:S(2)}) collective-permute-start(bf16[128,960]{1,0:T(8,128)(2,1)} %get-tuple-element.119.refs_8_), channel_id=1, source_target_pairs={{0,2},{1,3},{2,0},{3,1},{4,6},{5,7},{6,4},{7,5},{8,10},{9,11},{10,... | collective-permute-start | bytes 737288 | tf_op jit(solution)/shard_map/ppermute | solution.py:249
  269.3 19.2 %collective-permute-start.23 = (bf16[128,960]{1,0:T(8,128)(2,1)}, bf16[128,960]{1,0:T(8,128)(2,1)}, u32[]{:S(2)}, u32[]{:S(2)}) collective-permute-start(bf16[128,960]{1,0:T(8,128)(2,1)} %get-tuple-element.119.refs_8_), channel_id=1, source_target_pairs={{0,1},{1,0},{2,3},{3,2},{4,5},{5,4},{6,7},{7,6},{8,9},{9,8},{10,11... | collective-permute-start | bytes 737288 | tf_op jit(solution)/shard_map/ppermute | solution.py:249
  269.5 7.7 %copy-start.44 = (bf16[128,1600]{0,1:T(8,128)(2,1)}, bf16[128,1600]{0,1:T(8,128)(2,1)S(1)}, u32[]{:S(2)}) copy-start(bf16[128,1600]{0,1:T(8,128)(2,1)S(1)} %pad_maximum_fusion.3) | copy-start | bytes 1228804
  276.2 9.3 %copy-start.71 = (f32[960]{0:T(1024)S(1)}, f32[960]{0:T(1024)}, u32[]{:S(2)}) copy-start(f32[960]{0:T(1024)} %copy-done.69) | copy-start | bytes 11524
  276.2 9.3 %copy-start.77 = (f32[128]{0:T(128)S(1)}, f32[128]{0:T(128)}, u32[]{:S(2)}) copy-start(f32[128]{0:T(128)} %copy-done.75) | copy-start | bytes 1540
  282.1 9.6 %collective-permute-start.21 = (bf16[2,1,128,640]{3,2,1,0:T(8,128)(2,1)}, bf16[2,1,128,640]{3,2,1,0:T(8,128)(2,1)S(1)}, u32[]{:S(2)}, u32[]{:S(2)}) collective-permute-start(bf16[2,1,128,640]{3,2,1,0:T(8,128)(2,1)} %bitcast.243), channel_id=1, source_target_pairs={{0,2},{1,3},{2,0},{3,1},{4,6},{5,7},{6,4},{7,5},{8,10},{9,11},{10,... | collective-permute-start | bytes 983048 | tf_op jit(solution)/shard_map/ppermute | solution.py:249
  283.4 17.9 %collective-permute-start.24 = (bf16[2,160,960]{2,1,0:T(8,128)(2,1)}, bf16[2,160,960]{2,1,0:T(8,128)(2,1)S(1)}, u32[]{:S(2)}, u32[]{:S(2)}) collective-permute-start(bf16[2,160,960]{2,1,0:T(8,128)(2,1)} %copy-done.16), channel_id=1, source_target_pairs={{0,4},{1,5},{2,6},{3,7},{4,0},{5,1},{6,2},{7,3},{8,12},{9,13},{10,... | collective-permute-start | bytes 1843208 | tf_op jit(solution)/shard_map/ppermute | solution.py:249
  283.4 37.1 %collective-permute-start.29 = (bf16[2,160,960]{2,1,0:T(8,128)(2,1)}, bf16[2,160,960]{2,1,0:T(8,128)(2,1)}, u32[]{:S(2)}, u32[]{:S(2)}) collective-permute-start(bf16[2,160,960]{2,1,0:T(8,128)(2,1)} %copy-done.15), channel_id=1, source_target_pairs={{0,4},{1,5},{2,6},{3,7},{4,0},{5,1},{6,2},{7,3},{8,12},{9,13},{10,... | collective-permute-start | bytes 1843208 | tf_op jit(solution)/shard_map/ppermute | solution.py:249
  291.7 11.2 %copy-start.13 = (bf16[2,1,128,640]{3,2,1,0:T(8,128)(2,1)}, bf16[2,1,128,640]{3,2,1,0:T(8,128)(2,1)S(1)}, u32[]{:S(2)}) copy-start(bf16[2,1,128,640]{3,2,1,0:T(8,128)(2,1)S(1)} %collective-permute-done.21.refs_2_) | copy-start | bytes 983044
  302.1 6.7 %collective-permute-start.25 = (bf16[2,1,128,640]{3,2,1,0:T(8,128)(2,1)}, bf16[2,1,128,640]{3,2,1,0:T(8,128)(2,1)}, u32[]{:S(2)}, u32[]{:S(2)}) collective-permute-start(bf16[2,1,128,640]{3,2,1,0:T(8,128)(2,1)} %pad_maximum_fusion.5), channel_id=1, source_target_pairs={{0,1},{1,0},{2,3},{3,2},{4,5},{5,4},{6,7},{7,6},{8,9},{9,8},{10,11... | collective-permute-start | bytes 983048 | tf_op jit(solution)/shard_map/ppermute | solution.py:249
  302.1 6.6 %collective-permute-start.26 = (bf16[128,960]{1,0:T(8,128)(2,1)}, bf16[128,960]{1,0:T(8,128)(2,1)}, u32[]{:S(2)}, u32[]{:S(2)}) collective-permute-start(bf16[128,960]{1,0:T(8,128)(2,1)} %collective-permute-done.22.refs_9_), channel_id=1, source_target_pairs={{0,1},{1,0},{2,3},{3,2},{4,5},{5,4},{6,7},{7,6},{8,9},{9,8},{10,11... | collective-permute-start | bytes 737288 | tf_op jit(solution)/shard_map/ppermute | solution.py:249
  302.6 2.3 collective-permute-start.27
  303.8 18.3 %collective-permute-start.30 = (bf16[160,960]{1,0:T(8,128)(2,1)}, bf16[160,960]{1,0:T(8,128)(2,1)}, u32[]{:S(2)}, u32[]{:S(2)}) collective-permute-start(bf16[160,960]{1,0:T(8,128)(2,1)} %fusion.72), channel_id=1, source_target_pairs={{0,8},{1,9},{2,10},{3,11},{4,12},{5,13},{6,14},{7,15},{8,0},{9,1},... | collective-permute-start | bytes 921608 | tf_op jit(solution)/shard_map/ppermute | solution.py:249
  304.9 3.7 collective-permute-start.28
  322.1 4.6 %copy-start.38 = (f32[2,160,960]{2,1,0:T(8,128)S(1)}, f32[2,160,960]{2,1,0:T(8,128)}, u32[]{:S(2)}) copy-start(f32[2,160,960]{2,1,0:T(8,128)} %copy-done.37) | copy-start | bytes 3686404
  322.1 4.6 %copy-start.66 = (bf16[160,960]{1,0:T(8,128)(2,1)S(1)}, bf16[160,960]{1,0:T(8,128)(2,1)}, u32[]{:S(2)}) copy-start(bf16[160,960]{1,0:T(8,128)(2,1)} %copy-done.65) | copy-start | bytes 921604
  322.1 22.1 %collective-permute-start.31 = (bf16[2,168,960]{2,1,0:T(8,128)(2,1)S(1)}, bf16[2,168,960]{2,1,0:T(8,128)(2,1)S(1)}, u32[]{:S(2)}, u32[]{:S(2)}) collective-permute-start(bf16[2,168,960]{2,1,0:T(8,128)(2,1)S(1)} %get-tuple-element.136), channel_id=1, source_target_pairs={{0,4},{1,5},{2,6},{3,7},{4,0},{5,1},{6,2},{7,3},{8,12},{9,13},{10,... | collective-permute-start | bytes 1935368 | tf_op jit(solution)/shard_map/ppermute | solution.py:249
  323.8 19.7 %collective-permute-start.32 = (bf16[160,960]{1,0:T(8,128)(2,1)S(1)}, bf16[160,960]{1,0:T(8,128)(2,1)S(1)}, u32[]{:S(2)}, u32[]{:S(2)}) collective-permute-start(bf16[160,960]{1,0:T(8,128)(2,1)S(1)} %fusion.73), channel_id=1, source_target_pairs={{0,8},{1,9},{2,10},{3,11},{4,12},{5,13},{6,14},{7,15},{8,0},{9,1},... | collective-permute-start | bytes 921608 | tf_op jit(solution)/shard_map/ppermute | solution.py:249
  344.5 17.3 %collective-permute-start.33 = (bf16[168,960]{1,0:T(8,128)(2,1)S(1)}, bf16[168,960]{1,0:T(8,128)(2,1)S(1)}, u32[]{:S(2)}, u32[]{:S(2)}) collective-permute-start(bf16[168,960]{1,0:T(8,128)(2,1)S(1)} %fusion.70), channel_id=1, source_target_pairs={{0,8},{1,9},{2,10},{3,11},{4,12},{5,13},{6,14},{7,15},{8,0},{9,1},... | collective-permute-start | bytes 967688 | tf_op jit(solution)/shard_map/ppermute | solution.py:249
  (54 other events, 113.5 us)
Sparse Core Ops, SparseCore 0:
  10.2 111.5 all-gather.1
